TPU v7x, 256 devices: a whole 4x4x8 slice. The times are simulated.
256 devices in a mesh: task: 16 (over z_lo, y, core), rows: 16 (over z_hi, x).
Axes of the slice: x: 4, y: 4, z: 8 (z_hi: 4, z_lo: 2; z = z_hi * 2 + z_lo), core: 2. Of those that a mesh axis runs over, the one named last changes fastest.
Arguments:
- probes: bfloat16 [16, 384, 8192], P('task', None, 'rows'), may hold values from -48 to 48
- task_weights: bfloat16 [16, 8192, 128], P('task', 'rows'), may hold values from -6 to 6
Outputs:
- merged: float32 [8192, 128], P(('rows', 'task'))
- residual: float32 [8192, 128], P(('rows', 'task'))
All inputs are finite; a program needn't handle non-finite values.
Results may differ from a plain program's by a relative error of at most 0.0003.
Values may be sent and summed in bfloat16 or wider, within the bound.
No kernel may reach another device: no remote copies, remote signals or barrier semaphores. Data moves between devices by JAX's collectives and lax.ppermute only.
A program may use at most 128 MiB of HBM per device.

v0:
```python
import jax
import jax.numpy as jnp
from jax import lax
from jax.sharding import PartitionSpec as P

PROBE = 384
ITERS = 2


ALPHA = 0.9
EPS = 1e-06


def column_squares(vector):
    return lax.psum(jnp.sum(vector * vector, axis=0), ("task", "rows"))


def on_device(probes, task_weights):
    local_x = probes[0]
    local_w = task_weights[0]
    tasks = lax.axis_size("task")
    width = local_x.shape[1]
    share = width // tasks
    cols = local_w.shape[1]
    offset = lax.axis_index("rows") * width
    scale = 1.0 / (PROBE * tasks)
    exact_x = local_x.astype(jnp.float32)
    diag_local = jnp.sum(exact_x * exact_x, axis=0)
    partial_value = jnp.dot(local_x, local_w, preferred_element_type=jnp.float32)
    outputs = lax.psum(partial_value, "rows")
    b_term = ALPHA * jnp.einsum("pd,pc->dc", exact_x, outputs, precision=lax.Precision.HIGHEST)
    b_term = scale * (b_term + (1.0 - ALPHA) * diag_local[:, None] * local_w.astype(jnp.float32))
    raw = jnp.einsum(
        "pd,pe->de",
        local_x,
        lax.all_gather(local_x, "rows", axis=1, tiled=True),
        preferred_element_type=jnp.float32,
    )
    g_term = ALPHA * scale * raw
    square = lax.dynamic_slice_in_dim(g_term, offset, width, 1)
    square = square + jnp.diag((1.0 - ALPHA) * scale * diag_local)
    g_term = lax.dynamic_update_slice_in_dim(g_term, square, offset, 1)
    system, targets = (
        lax.psum_scatter(g_term, "task", scatter_dimension=0, tiled=True),
        lax.psum_scatter(b_term, "task", scatter_dimension=0, tiled=True),
    )
    merged = jnp.zeros((share, cols), jnp.float32)
    residual = targets
    direction = targets
    norm_now = column_squares(residual)
    for step in range(ITERS):
        block = lax.all_gather(direction, "task", axis=0, tiled=True)
        image = jnp.dot(
            system,
            lax.all_gather(block, "rows", axis=0, tiled=True),
            precision=lax.Precision.HIGHEST,
            preferred_element_type=jnp.float32,
        )
        curve = lax.psum(jnp.sum(direction * image, axis=0), ("task", "rows"))
        alpha = norm_now / curve
        merged = merged + alpha * direction
        residual = residual - alpha * image
        norm_next = column_squares(residual)
        direction = residual + norm_next / (norm_now + EPS) * direction
        norm_now = norm_next
    return (merged, residual)


def solution(mesh):
    in_specs = (P("task", None, "rows"), P("task", "rows", None))
    out_specs = (P(("rows", "task"), None), P(("rows", "task"), None))
    return jax.shard_map(
        on_device, mesh=mesh, in_specs=in_specs, out_specs=out_specs, check_vma=False
    )
```

profile of v0, /device:TPU:1, one launch (start us, length us, event | category | flops | bytes accessed | tf_op | source)
XLA Modules:
  0.0 856.5 jit_solution(6923377379118053543)
XLA Ops:
  7.2 0.0 all-reduce.3.cloned.1.call-start
  7.2 2.0 fusion.6
  9.2 0.0 all-reduce.3.cloned.1.call-update
  9.2 0.0 reduce-scatter.7.cloned.1.call-start
  9.2 1.1 multiply_reduce_fusion
  10.4 1.0 copy.11
  11.4 152.3 %all-reduce.3.cloned.1.call-done = f32[384,128]{1,0:T(8,128)} async-done(((f32[384,128]{1,0:T(8,128)}), f32[384,128]{1,0:T(8,128)}) %all-reduce.3.cloned.1.call-update) | async-done | bytes 196624 | tf_op jit(solution)/shard_map/psum | solution.py:30
  163.7 1.5 fusion.3
  165.2 0.8 copy.17
  166.0 0.0 reduce-scatter.7.cloned.1.call-update
  166.1 0.0 all-gather.9.cloned.1.call-start
  166.1 0.7 all-gather.9.cloned.1.call-update
  166.8 0.0 all-gather.5.cloned.1.call-start
  166.8 68.9 %reduce-scatter.7.cloned.1.call-done = f32[32,128]{1,0:T(8,128)} async-done(((f32[512,128]{1,0:T(8,128)}), f32[32,128]{1,0:T(8,128)}) %reduce-scatter.7.cloned.1.call-update) | async-done | bytes 16400 | tf_op jit(solution)/shard_map/reduce_scatter | solution.py:45
  235.7 22.1 %all_gather.16 = f32[512,128]{1,0:T(8,128)} all-gather(f32[32,128]{1,0:T(8,128)} %reduce-scatter.7.cloned.1.call-done), channel_id=1, replica_groups=mesh['task'=16,'rows'=16] {'task'}, dimensions={0}, use_global_device_ids=true | all-gather | bytes 278528 | tf_op jit(solution)/shard_map/all_gather | solution.py:52
  257.8 0.0 all-gather.5.cloned.1.call-update
  257.9 0.0 reduce-scatter.5.cloned.1.call-start
  257.9 84.4 %all-gather.9.cloned.1.call-done = bf16[1,384,8192]{2,1,0:T(8,128)(2,1)} async-done(((bf16[1,384,512]{2,1,0:T(8,128)(2,1)}), bf16[1,384,8192]{2,1,0:T(8,128)(2,1)}) %all-gather.9.cloned.1.call-update) | async-done | bytes 6291472 | tf_op jit(solution)/shard_map/all_gather | solution.py:36
  342.3 13.2 %convolution_multiply_fusion = f32[512,8192]{1,0:T(8,128)} fusion(bf16[1,384,8192]{2,1,0:T(8,128)(2,1)} %all-gather.9.cloned.1.call-done, bf16[1,384,512]{2,1,0:T(8,128)(2,1)} %param.2), kind=kOutput, calls=%fused_computation | convolution fusion | flops 3225419776 | bytes 23461888 | tf_op jit(solution)/shard_map/pd,pe->de/dot_general | solution.py:33
  355.5 2.4 add_dynamic-update-slice_fusion
  357.9 0.0 copy-start.1
  357.9 0.0 reduce-scatter.5.cloned.1.call-update
  358.0 0.0 all-gather.7.cloned.1.call-start
  358.0 0.6 copy-done.1
  358.7 0.1 copy.18
  358.8 0.1 multiply_reduce_fusion.1
  358.9 59.2 %all-gather.5.cloned.1.call-done = f32[8192,128]{1,0:T(8,128)} async-done(((f32[512,128]{1,0:T(8,128)}), f32[8192,128]{1,0:T(8,128)}) %all-gather.5.cloned.1.call-update) | async-done | bytes 4194320 | tf_op jit(solution)/shard_map/all_gather | solution.py:55
  418.1 102.8 %reduce-scatter.5.cloned.1.call-done = f32[32,8192]{1,0:T(8,128)} async-done(((f32[512,8192]{1,0:T(8,128)}), f32[32,8192]{1,0:T(8,128)}) %reduce-scatter.5.cloned.1.call-update) | async-done | bytes 1048592 | tf_op jit(solution)/shard_map/reduce_scatter | solution.py:44
  520.8 0.0 copy-start
  520.8 4.9 multiply_reduce_fusion.4
  525.7 77.6 %all-reduce = (f32[128]{0:T(128)S(1)}, f32[128]{0:T(128)S(1)}) all-reduce(f32[128]{0:T(128)S(1)} %multiply_reduce_fusion.1, f32[128]{0:T(128)S(1)} %get-tuple-element.10), channel_id=1, replica_groups=mesh['task'=16,'rows'=16] {'task','rows'}, use_global_device_ids=true, to_apply=%region_4.5 | all-reduce | flops 256 | bytes 2048 | tf_op jit(solution)/shard_map/psum | solution.py:15
  603.4 73.2 %psum.38 = f32[128]{0:T(128)S(1)} all-reduce(f32[128]{0:T(128)S(1)} %multiply_reduce_fusion.3), channel_id=1, replica_groups=mesh['task'=16,'rows'=16] {'task','rows'}, use_global_device_ids=true, to_apply=%region_9.10 | all-reduce | flops 128 | bytes 1024 | tf_op jit(solution)/shard_map/psum | solution.py:15
  676.5 21.1 %all_gather.18 = f32[512,128]{1,0:T(8,128)} all-gather(f32[32,128]{1,0:T(8,128)S(1)} %multiply_add_fusion.1), channel_id=1, replica_groups=mesh['task'=16,'rows'=16] {'task'}, dimensions={0}, use_global_device_ids=true | all-gather | bytes 278528 | tf_op jit(solution)/shard_map/all_gather | solution.py:52
  697.6 0.0 all-gather.7.cloned.1.call-update
  697.7 68.8 %all-gather.7.cloned.1.call-done = f32[8192,128]{1,0:T(8,128)} async-done(((f32[512,128]{1,0:T(8,128)}), f32[8192,128]{1,0:T(8,128)}) %all-gather.7.cloned.1.call-update) | async-done | bytes 4194320 | tf_op jit(solution)/shard_map/all_gather | solution.py:55
  766.5 0.0 copy-done
  766.5 4.0 multiply_reduce_fusion.2
  770.5 78.4 %psum.39 = f32[128]{0:T(128)S(1)} all-reduce(f32[128]{0:T(128)S(1)} %get-tuple-element.12), channel_id=1, replica_groups=mesh['task'=16,'rows'=16] {'task','rows'}, use_global_device_ids=true, to_apply=%region_11.12 | all-reduce | flops 128 | bytes 1024 | tf_op jit(solution)/shard_map/psum | solution.py:59
  849.0 0.6 multiply_subtract_fusion
  (6 shorter events, 0.1 us)
Async XLA Ops:
  7.2 156.5 %all-reduce.3.cloned.1.call-start = ((), (), s32[]{:S(2)}) async-start(), calls=%async_computation.2 | async-start | bytes 393216 | tf_op jit(solution)/shard_map/psum | solution.py:30
  9.2 226.5 %reduce-scatter.7.cloned.1.call-start = ((), (), s32[]{:S(2)}) async-start(), calls=%async_computation.7 | async-start | bytes 278528 | tf_op jit(solution)/shard_map/reduce_scatter | solution.py:45
  166.1 176.3 %all-gather.9.cloned.1.call-start = ((), (), s32[]{:S(2)}) async-start(), calls=%async_computation.6 | async-start | bytes 6684672 | tf_op jit(solution)/shard_map/all_gather | solution.py:36
  166.8 251.3 %all-gather.5.cloned.1.call-start = ((), (), s32[]{:S(2)}) async-start(), calls=%async_computation.4 | async-start | bytes 4456448 | tf_op jit(solution)/shard_map/all_gather | solution.py:55
  257.9 263.0 %reduce-scatter.5.cloned.1.call-start = ((), (), s32[]{:S(2)}) async-start(), calls=%async_computation.3 | async-start | bytes 17825792 | tf_op jit(solution)/shard_map/reduce_scatter | solution.py:44
  357.9 0.7 copy-start.1
  358.0 408.5 %all-gather.7.cloned.1.call-start = ((), (), s32[]{:S(2)}) async-start(), calls=%async_computation.5 | async-start | bytes 4456448 | tf_op jit(solution)/shard_map/all_gather | solution.py:55
  520.8 245.6 %copy-start = (f32[32,8192]{1,0:T(8,128)S(1)}, f32[32,8192]{1,0:T(8,128)}, u32[]{:S(2)}) copy-start(f32[32,8192]{1,0:T(8,128)} %reduce-scatter.5.cloned.1.call-done) | copy-start | bytes 3145732
Sparse Core Ops, SparseCore 0:
  10.6 153.0 all-reduce.2
  166.2 69.4 reduce-scatter.6
  238.1 104.1 all-gather.8
  344.6 73.4 all-gather.4
  420.5 100.3 reduce-scatter.4
  697.8 68.6 all-gather.6
where the time goes:
time: 857 us; the launch traced here: 856 us
  waiting for transfers between devices  537 us (63%)
  blocking collectives  272 us (32%)
  matrix products  25.6 us (3%)
  between operations  14.2 us (2%)
    psum x1, waiting for transfers between devices, on_device(): outputs = lax.psum(partial_value, 'rows')  152 us
    psum x2, blocking collectives, column_squares(): return lax.psum(jnp.sum(vector * vector, axis=0), ('task', 'rows'))  151 us
    all_gather x2, waiting for transfers between devices, on_device(): lax.all_gather(block, 'rows', axis=0, tiled=True)  128 us
    reduce_scatter x1, waiting for transfers between devices, on_device(): lax.psum_scatter(g_term, 'task', scatter_dimension=0, tiled=True)  103 us
    all_gather x1, waiting for transfers between devices, on_device(): lax.all_gather(local_x, 'rows', axis=1, tiled=True)  84.4 us
    psum x1, blocking collectives, on_device(): curve = lax.psum(jnp.sum(direction * image, axis=0), ('task', 'rows'))  78.4 us
    reduce_scatter x1, waiting for transfers between devices, on_device(): lax.psum_scatter(b_term, 'task', scatter_dimension=0, tiled=True)  68.9 us
    all_gather x2, blocking collectives, on_device(): block = lax.all_gather(direction, 'task', axis=0, tiled=True)  43.2 us
  transfers between devices with their start and end apart: 6, of which 6 were waited for; matrix products, arithmetic and copies ran while one was open for 2% of the time, Pallas kernels for 0%

commit v1 on v0

v1 whole, which is shorter than its diff:
```python
import jax
import jax.numpy as jnp
from jax import lax
from jax.sharding import PartitionSpec as P

ALPHA = 0.9
EPS = 1e-06


def scatter_sum(chunks, axis):
    return jnp.sum(lax.all_to_all(chunks, axis, 0, 0), axis=0)


def gather(chunk, axis):
    n = lax.axis_size(axis)
    copies = jnp.broadcast_to(chunk[None], (n,) + chunk.shape)
    return lax.all_to_all(copies, axis, 0, 0).reshape(n * chunk.shape[0], chunk.shape[1])


def pieces(value):
    high = lax.reduce_precision(value, 8, 7)
    low = value - high
    return jnp.concatenate([high.astype(jnp.bfloat16), low.astype(jnp.bfloat16)], axis=1)


def times(x, value, dim):
    cols = value.shape[1]
    wide = lax.dot_general(x, pieces(value), (((dim,), (0,)), ((), ())), preferred_element_type=jnp.float32)
    return wide[:, :cols] + wide[:, cols:]


def with_rows(value, axis, rows):
    n = lax.axis_size(axis)
    chunks = value.reshape(n, value.shape[0] // n, value.shape[1])
    extra = jnp.concatenate([r[None] for r in rows] + [jnp.zeros((8 - len(rows), value.shape[1]), jnp.float32)])
    return jnp.concatenate([chunks, jnp.broadcast_to(extra[None], (n,) + extra.shape)], axis=1)


def on_device(probes, task_weights):
    x = probes[0]
    w = task_weights[0]
    tokens, width = x.shape
    tasks = lax.axis_size("task")
    scale = 1.0 / (tokens * tasks)
    gram_scale, diag_scale = ALPHA * scale, (1.0 - ALPHA) * scale
    wide_x = x.astype(jnp.float32)
    diag = diag_scale * jnp.sum(wide_x * wide_x, axis=0)[:, None]

    def columns(value):
        return jnp.sum(value, axis=0)

    first = jnp.dot(x, w, preferred_element_type=jnp.float32)
    first = scatter_sum(first.reshape(-1, tokens // lax.axis_size("rows"), first.shape[1]), "rows")
    outputs = gather(first, "rows")
    part = gram_scale * times(x, outputs, 0) + diag * w.astype(jnp.float32)
    target_chunk = scatter_sum(part.reshape(tasks, width // tasks, part.shape[1]), "task")
    target = gather(target_chunk, "task")

    share = tokens // lax.axis_size("rows")
    rows = with_rows(times(x, target, 1), "rows", [columns(target * target), columns(diag * target * target)])
    rows = scatter_sum(rows, "rows")
    norm0, weigh0 = rows[share], rows[share + 1]
    image0 = gather(rows[:share], "rows")
    part = gram_scale * times(x, image0, 0) + diag * target
    curve = gram_scale * columns(image0 * image0) + weigh0
    part = scatter_sum(with_rows(part, "task", [curve]), "task")
    depth = width // tasks
    alpha0 = norm0 / part[depth]
    residual_chunk = target_chunk - alpha0 * part[:depth]
    residual = gather(residual_chunk, "task")

    rows = with_rows(
        times(x, residual, 1),
        "rows",
        [columns(residual * residual), columns(diag * residual * residual), columns(diag * residual * target)],
    )
    rows = scatter_sum(rows, "rows")
    norm1, weigh1, cross = rows[share], rows[share + 1], rows[share + 2]
    beta = norm1 / (norm0 + EPS)
    image1 = gather(rows[:share], "rows") + beta * image0
    direction = residual + beta * target
    part = gram_scale * times(x, image1, 0) + diag * direction
    curve = gram_scale * columns(image1 * image1) + weigh1 + 2.0 * beta * cross + beta * beta * weigh0
    part = scatter_sum(with_rows(part, "task", [curve]), "task")
    alpha1 = norm1 / part[depth]
    merged = alpha0 * target_chunk + alpha1 * (residual_chunk + beta * target_chunk)
    return merged, residual_chunk - alpha1 * part[:depth]


def solution(mesh):
    in_specs = (P("task", None, "rows"), P("task", "rows", None))
    out_specs = (P(("rows", "task"), None), P(("rows", "task"), None))
    return jax.shard_map(
        on_device, mesh=mesh, in_specs=in_specs, out_specs=out_specs, check_vma=False
    )
```

time: 857 us -> 169 us (0.20)
  waiting for transfers between devices: 537 us -> 42.9 us
  blocking collectives: 272 us -> 90 us
  starting transfers between devices: 0.24 us -> 24.5 us
  matrix products: 25.6 us -> 2.94 us
  between operations: 14.2 us -> 0.96 us
    psum x3 -> x0, blocking collectives: 229 us -> none  [the longest x2 151 us: column_squares(): return lax.psum(jnp.sum(vector * vector, axis=0), ('task', 'rows'))]
    all_gather x3 -> x0, waiting for transfers between devices: 212 us -> none  [the longest x2 128 us: on_device(): lax.all_gather(block, 'rows', axis=0, tiled=True)]
    reduce_scatter x2 -> x0, waiting for transfers between devices: 172 us -> none  [the longest x1 103 us: on_device(): lax.psum_scatter(g_term, 'task', scatter_dimension=0, tiled=True)]
    psum x1 -> x0, waiting for transfers between devices: 152 us -> none  [on_device(): outputs = lax.psum(partial_value, 'rows')]
    all_to_all x0 -> x6, blocking collectives: none -> 90 us  [scatter_sum(): return jnp.sum(lax.all_to_all(chunks, axis, 0, 0), axis=0)]
    all_gather x2 -> x0, blocking collectives: 43.2 us -> none  [on_device(): block = lax.all_gather(direction, 'task', axis=0, tiled=True)]
    all_to_all x0 -> x5, waiting for transfers between devices: none -> 42.9 us  [gather(): lax.all_to_all(copies, axis, 0, 0)]
    all_to_all x0 -> x5, starting transfers between devices: none -> 24.5 us  [gather(): lax.all_to_all(copies, axis, 0, 0)]
  transfers between devices with their start and end apart: 6 -> 5, of which waited for: 6 -> 5; matrix products, arithmetic and copies ran while one was open for 2% -> 0% of each run, Pallas kernels for 0% -> 0%
where the time goes in v1:
time: 169 us; the launch traced here: 168 us
  blocking collectives  90 us (53%)
  waiting for transfers between devices  42.9 us (25%)
  starting transfers between devices  24.5 us (14%)
  local copies, waits for them, and re-layouts  4.76 us (3%)
  matrix products  2.94 us (2%)
  other arithmetic  2.12 us (1%)
    all_to_all x6, blocking collectives, scatter_sum(): return jnp.sum(lax.all_to_all(chunks, axis, 0, 0), axis=0)  90 us
    all_to_all x5, waiting for transfers between devices, gather(): lax.all_to_all(copies, axis, 0, 0)  42.9 us
    all_to_all x5, starting transfers between devices, gather(): lax.all_to_all(copies, axis, 0, 0)  24.5 us
    broadcast_in_dim x5, local copies, waits for them, and re-layouts, gather(): copies = jnp.broadcast_to(chunk[None], (n,) + chunk.shape)  3.49 us
  transfers between devices with their start and end apart: 5, of which 5 were waited for; matrix products, arithmetic and copies ran while one was open for 0% of the time, Pallas kernels for 0%

profile of v1, /device:TPU:1, one launch (start us, length us, event | category | flops | bytes accessed | tf_op | source)
XLA Modules:
  0.0 168.2 jit_solution(5149066570826503854)
XLA Ops:
  0.6 1.3 fusion.34
  1.9 21.2 %all_to_all.55 = f32[16,24,128]{2,1,0:T(8,128)S(1)} all-to-all(f32[16,24,128]{2,1,0:T(8,128)S(1)} %fusion.34), channel_id=1, replica_groups=mesh['task'=16,'rows'=16] {'rows'}, dimensions={0} | all-to-all | bytes 393216 | tf_op jit(solution)/shard_map/all_to_all | solution.py:11
  23.1 0.7 broadcast_in_dim.32
  23.8 4.4 %all-to-all-start.1 = ((f32[16,24,128]{2,1,0:T(8,128)}), f32[16,24,128]{2,1,0:T(8,128)S(1)}, u32[]{:S(2)}, u32[]{:S(2)}) async-start(f32[16,24,128]{2,1,0:T(8,128)} %broadcast_in_dim.32), calls=%async_computation.1 | async-start | bytes 393216 | tf_op jit(solution)/shard_map/all_to_all | solution.py:17
  28.2 0.1 copy.25
  28.4 0.1 multiply_reduce_fusion
  28.5 9.5 %all-to-all-done.1 = f32[16,24,128]{2,1,0:T(8,128)S(1)} async-done(((f32[16,24,128]{2,1,0:T(8,128)}), f32[16,24,128]{2,1,0:T(8,128)S(1)}, u32[]{:S(2)}, u32[]{:S(2)}) %all-to-all-start.1) | async-done | bytes 196640 | tf_op jit(solution)/shard_map/all_to_all | solution.py:17
  38.1 0.3 convolution_bitcast_fusion.2
  38.5 0.1 copy.27
  38.6 14.9 %all_to_all.56 = f32[16,32,128]{2,1,0:T(8,128)S(1)} all-to-all(f32[16,32,128]{2,1,0:T(8,128)S(1)} %bitcast.80), channel_id=1, replica_groups=mesh['task'=16,'rows'=16] {'task'}, dimensions={0} | all-to-all | bytes 524288 | tf_op jit(solution)/shard_map/all_to_all | solution.py:11
  53.5 0.7 broadcast_in_dim.33
  54.2 4.2 %all-to-all-start.3 = ((f32[16,32,128]{2,1,0:T(8,128)}), f32[16,32,128]{2,1,0:T(8,128)S(1)}, u32[]{:S(2)}, u32[]{:S(2)}) async-start(f32[16,32,128]{2,1,0:T(8,128)} %broadcast_in_dim.33), calls=%async_computation.3 | async-start | bytes 524288 | tf_op jit(solution)/shard_map/all_to_all | solution.py:17
  58.5 0.1 mul.211
  58.5 0.1 pad.22.clone
  58.6 7.1 %all-to-all-done.3 = f32[16,32,128]{2,1,0:T(8,128)S(1)} async-done(((f32[16,32,128]{2,1,0:T(8,128)}), f32[16,32,128]{2,1,0:T(8,128)S(1)}, u32[]{:S(2)}, u32[]{:S(2)}) %all-to-all-start.3) | async-done | bytes 262176 | tf_op jit(solution)/shard_map/all_to_all | solution.py:17
  65.8 0.4 convolution_bitcast_fusion.4
  66.2 0.1 copy.28
  66.3 0.2 multiply_reduce_fusion.2
  66.5 0.1 maximum_maximum_fusion
  66.6 13.5 %all_to_all.57 = f32[16,32,128]{2,1,0:T(8,128)S(1)} all-to-all(f32[16,32,128]{2,1,0:T(8,128)S(1)} %pad_maximum_fusion.2), channel_id=1, replica_groups=mesh['task'=16,'rows'=16] {'rows'}, dimensions={0} | all-to-all | bytes 524288 | tf_op jit(solution)/shard_map/all_to_all | solution.py:11
  80.1 0.7 broadcast_in_dim.38
  80.8 5.7 %all-to-all-start.5 = ((f32[16,24,128]{2,1,0:T(8,128)}), f32[16,24,128]{2,1,0:T(8,128)S(1)}, u32[]{:S(2)}, u32[]{:S(2)}) async-start(f32[16,24,128]{2,1,0:T(8,128)} %broadcast_in_dim.38), calls=%async_computation.5 | async-start | bytes 393216 | tf_op jit(solution)/shard_map/all_to_all | solution.py:17
  86.5 0.1 copy.29
  86.6 9.5 %all-to-all-done.5 = f32[16,24,128]{2,1,0:T(8,128)S(1)} async-done(((f32[16,24,128]{2,1,0:T(8,128)}), f32[16,24,128]{2,1,0:T(8,128)S(1)}, u32[]{:S(2)}, u32[]{:S(2)}) %all-to-all-start.5) | async-done | bytes 196640 | tf_op jit(solution)/shard_map/all_to_all | solution.py:17
  96.1 0.1 multiply_reduce_fusion.4
  96.3 0.3 convolution_bitcast_fusion.1
  96.6 0.1 fusion.13
  96.7 0.1 copy.30
  96.8 13.7 %all_to_all.58 = f32[16,40,128]{2,1,0:T(8,128)S(1)} all-to-all(f32[16,40,128]{2,1,0:T(8,128)S(1)} %pad_maximum_fusion), channel_id=1, replica_groups=mesh['task'=16,'rows'=16] {'task'}, dimensions={0} | all-to-all | bytes 655360 | tf_op jit(solution)/shard_map/all_to_all | solution.py:11
  110.6 0.7 broadcast_in_dim.40
  111.3 4.5 %all-to-all-start.7 = ((f32[16,32,128]{2,1,0:T(8,128)}), f32[16,32,128]{2,1,0:T(8,128)S(1)}, u32[]{:S(2)}, u32[]{:S(2)}) async-start(f32[16,32,128]{2,1,0:T(8,128)} %broadcast_in_dim.40), calls=%async_computation.7 | async-start | bytes 524288 | tf_op jit(solution)/shard_map/all_to_all | solution.py:17
  115.8 0.1 pad.11.clone
  115.9 7.2 %all-to-all-done.7 = f32[16,32,128]{2,1,0:T(8,128)S(1)} async-done(((f32[16,32,128]{2,1,0:T(8,128)}), f32[16,32,128]{2,1,0:T(8,128)S(1)}, u32[]{:S(2)}, u32[]{:S(2)}) %all-to-all-start.7) | async-done | bytes 262176 | tf_op jit(solution)/shard_map/all_to_all | solution.py:17
  123.1 0.3 convolution_bitcast_fusion.3
  123.5 0.1 copy.31
  123.6 0.2 fusion.7
  123.8 0.1 maximum_maximum_fusion.1
  123.9 13.1 %all_to_all.59 = f32[16,32,128]{2,1,0:T(8,128)S(1)} all-to-all(f32[16,32,128]{2,1,0:T(8,128)S(1)} %pad_maximum_fusion.3), channel_id=1, replica_groups=mesh['task'=16,'rows'=16] {'rows'}, dimensions={0} | all-to-all | bytes 524288 | tf_op jit(solution)/shard_map/all_to_all | solution.py:11
  137.0 0.7 broadcast_in_dim.46
  137.7 5.7 %all-to-all-start.9 = ((f32[16,24,128]{2,1,0:T(8,128)}), f32[16,24,128]{2,1,0:T(8,128)S(1)}, u32[]{:S(2)}, u32[]{:S(2)}) async-start(f32[16,24,128]{2,1,0:T(8,128)} %broadcast_in_dim.46), calls=%async_computation.9 | async-start | bytes 393216 | tf_op jit(solution)/shard_map/all_to_all | solution.py:17
  143.4 0.1 copy.33
  143.6 9.5 %all-to-all-done.9 = f32[16,24,128]{2,1,0:T(8,128)S(1)} async-done(((f32[16,24,128]{2,1,0:T(8,128)}), f32[16,24,128]{2,1,0:T(8,128)S(1)}, u32[]{:S(2)}, u32[]{:S(2)}) %all-to-all-start.9) | async-done | bytes 196640 | tf_op jit(solution)/shard_map/all_to_all | solution.py:17
  153.1 0.1 multiply_reduce_fusion.3
  153.2 0.3 convolution_bitcast_fusion
  153.5 0.1 fusion.11
  153.7 0.1 copy.34
  153.8 13.7 %all_to_all.60 = f32[16,40,128]{2,1,0:T(8,128)S(1)} all-to-all(f32[16,40,128]{2,1,0:T(8,128)S(1)} %pad_maximum_fusion.1), channel_id=1, replica_groups=mesh['task'=16,'rows'=16] {'task'}, dimensions={0} | all-to-all | bytes 655360 | tf_op jit(solution)/shard_map/all_to_all | solution.py:11
  167.6 0.6 fusion.36
  (39 shorter events, 0.7 us)
Async XLA Ops:
  23.1 5.3 %copy-start = (bf16[1,384,512]{2,1,0:T(8,128)(2,1)S(1)}, bf16[1,384,512]{2,1,0:T(8,128)(2,1)}, u32[]{:S(2)}) copy-start(bf16[1,384,512]{2,1,0:T(8,128)(2,1)} %param.2) | copy-start | bytes 1179652
  23.8 4.4 %copy-start.1 = (bf16[1,512,128]{2,1,0:T(8,128)(2,1)S(1)}, bf16[1,512,128]{2,1,0:T(8,128)(2,1)}, u32[]{:S(2)}) copy-start(bf16[1,512,128]{2,1,0:T(8,128)(2,1)} %param.3) | copy-start | bytes 393220
  23.8 14.2 %all-to-all-start.1 = ((f32[16,24,128]{2,1,0:T(8,128)}), f32[16,24,128]{2,1,0:T(8,128)S(1)}, u32[]{:S(2)}, u32[]{:S(2)}) async-start(f32[16,24,128]{2,1,0:T(8,128)} %broadcast_in_dim.32), calls=%async_computation.1 | async-start | bytes 393216 | tf_op jit(solution)/shard_map/all_to_all | solution.py:17
  54.2 11.5 %all-to-all-start.3 = ((f32[16,32,128]{2,1,0:T(8,128)}), f32[16,32,128]{2,1,0:T(8,128)S(1)}, u32[]{:S(2)}, u32[]{:S(2)}) async-start(f32[16,32,128]{2,1,0:T(8,128)} %broadcast_in_dim.33), calls=%async_computation.3 | async-start | bytes 524288 | tf_op jit(solution)/shard_map/all_to_all | solution.py:17
  80.8 15.4 %all-to-all-start.5 = ((f32[16,24,128]{2,1,0:T(8,128)}), f32[16,24,128]{2,1,0:T(8,128)S(1)}, u32[]{:S(2)}, u32[]{:S(2)}) async-start(f32[16,24,128]{2,1,0:T(8,128)} %broadcast_in_dim.38), calls=%async_computation.5 | async-start | bytes 393216 | tf_op jit(solution)/shard_map/all_to_all | solution.py:17
  111.3 11.7 %all-to-all-start.7 = ((f32[16,32,128]{2,1,0:T(8,128)}), f32[16,32,128]{2,1,0:T(8,128)S(1)}, u32[]{:S(2)}, u32[]{:S(2)}) async-start(f32[16,32,128]{2,1,0:T(8,128)} %broadcast_in_dim.40), calls=%async_computation.7 | async-start | bytes 524288 | tf_op jit(solution)/shard_map/all_to_all | solution.py:17
  137.7 15.4 %all-to-all-start.9 = ((f32[16,24,128]{2,1,0:T(8,128)}), f32[16,24,128]{2,1,0:T(8,128)S(1)}, u32[]{:S(2)}, u32[]{:S(2)}) async-start(f32[16,24,128]{2,1,0:T(8,128)} %broadcast_in_dim.46), calls=%async_computation.9 | async-start | bytes 393216 | tf_op jit(solution)/shard_map/all_to_all | solution.py:17

commit v2 on v1

v2 whole, which is shorter than its diff:
```python
import jax
import jax.numpy as jnp
from jax import lax
from jax.sharding import PartitionSpec as P


ALPHA = 0.9
EPS = 1e-06


def moved(value, axis, to):
    return lax.ppermute(value, axis, [(i, to(i)) for i in range(16)])


def x_move(value, k):
    return moved(value, "rows", lambda r: r - r % 4 + (r + k) % 4)


def zhi_sum(value):
    return value + sum(moved(value, "rows", lambda r, k=k: (r + 4 * k) % 16) for k in (1, 3, 2))


def core_move(value):
    return moved(value, "task", lambda t: t ^ 1)


def zlo_move(value):
    return moved(value, "task", lambda t: t ^ 8)


def y_move(value, k):
    return moved(value, "task", lambda t: (t & 9) | ((((t >> 1) & 3) + k) % 4) << 1)


def pick(value, index, dim=0):
    return lax.dynamic_index_in_dim(value, index, dim, keepdims=False)


def pieces(value):
    high = lax.reduce_precision(value, 8, 7)
    low = value - high
    return jnp.concatenate([high.astype(jnp.bfloat16), low.astype(jnp.bfloat16)], axis=0)


def product(value, x, dim):
    n = value.shape[0]
    wide = lax.dot_general(pieces(value), x, (((1,), (dim,)), ((), ())), preferred_element_type=jnp.float32)
    return wide[:n] + wide[n:]


def blocks_of(value):
    return value.reshape(value.shape[0], -1, 128).transpose(1, 0, 2)


def flat(blocks):
    return blocks.transpose(1, 0, 2).reshape(blocks.shape[1], -1)


def halves(blocks, core):
    grid = blocks.reshape((2, 2, 4) + blocks.shape[1:])
    own, other = pick(grid, core, 1), pick(grid, 1 - core, 1)
    return own.reshape((8,) + blocks.shape[1:]), other.reshape((8,) + blocks.shape[1:])


def whole(own, core):
    other = core_move(own)
    shape = own.shape[1:]
    own, other = own.reshape((2, 1, 4) + shape), other.reshape((2, 1, 4) + shape)
    pair = jnp.where(core == 0, jnp.concatenate([own, other], 1), jnp.concatenate([other, own], 1))
    return pair.reshape((16,) + shape)


def task_half_sum(blocks, extra, core):
    own, other = halves(blocks, core)
    if extra is not None:
        own, other = jnp.concatenate([own, extra[None]]), jnp.concatenate([other, extra[None]])
    own = own + core_move(other)
    own = own + zlo_move(own)
    return own + y_move(own, 1) + y_move(own, 3) + y_move(own, 2)


def with_scalars(value, scalars):
    lane = lax.broadcasted_iota(jnp.int32, (value.shape[0], 128), 1)
    extra = jnp.zeros((value.shape[0], 128), jnp.float32)
    for i, s in enumerate(scalars):
        extra = jnp.where(lane == i, s, extra)
    return jnp.concatenate([value, extra], axis=1)


def total(value):
    return jnp.sum(value, axis=1, keepdims=True)


def on_device(probes, task_weights):
    own_x = probes[0]
    w = task_weights[0]
    tokens, width = own_x.shape
    tasks = lax.axis_size("task")
    row = lax.axis_index("rows")
    task = lax.axis_index("task")
    x, core, ylow, yhigh, zlo = row % 4, task % 2, (task // 2) % 2, (task // 4) % 2, task // 8
    scale = 1.0 / (tokens * tasks)
    gram_scale, diag_scale = ALPHA * scale, (1.0 - ALPHA) * scale

    half = tokens // 2
    from_left = x_move(own_x, 1)
    from_right = x_move(own_x, 3)

    first = lax.dot_general(w, own_x, (((0,), (1,)), ((), ())), preferred_element_type=jnp.float32)
    first = first.reshape(4, 32, tokens)
    mine = pick(first, x)
    for k in (1, 3, 2):
        mine = mine + x_move(pick(first, (x + k) % 4), k)
    turned = w.T.reshape(4, 32, width)
    weights = [pick(turned, x)]
    for k in (1, 2, 3):
        weights.append(x_move(pick(turned, (x + k) % 4), k))
    outputs = mine
    for k in (1, 3, 2):
        outputs = outputs + moved(mine, "rows", lambda r, k=k: (r + 4 * k) % 16)
    far_left = x_move(from_left[:half], 1)
    far_right = x_move(from_right[half:], 3)

    xs = jnp.concatenate([own_x, from_left, jnp.concatenate([far_left, far_right]), from_right], axis=1)
    ws = jnp.concatenate(weights, axis=1)
    wide_x = xs.astype(jnp.float32)
    diag = diag_scale * jnp.sum(wide_x * wide_x, axis=0, keepdims=True)

    def image_part(y, vector):
        return blocks_of(gram_scale * product(y, xs, 0) + diag * vector)

    part = task_half_sum(image_part(outputs, ws.astype(jnp.float32)), None, core)
    target_blocks = whole(part, core)
    target = flat(target_blocks)

    scalars = [total(target * target), total(diag * target * target)]
    rows = zhi_sum(with_scalars(product(target, xs, 1), scalars))
    image0, norm0, weigh0 = rows[:, :tokens], rows[:, tokens : tokens + 1], rows[:, tokens + 1 : tokens + 2]
    curve = jnp.broadcast_to(gram_scale * total(image0 * image0) + weigh0, (32, 128))
    part = task_half_sum(image_part(image0, target), curve, core)
    alpha0 = norm0 / part[8][:, :1]
    residual_half = halves(target_blocks, core)[0] - alpha0[None] * part[:8]
    residual_blocks = whole(residual_half, core)
    residual = flat(residual_blocks)

    scalars = [total(residual * residual), total(diag * residual * residual), total(diag * residual * target)]
    rows = zhi_sum(with_scalars(product(residual, xs, 1), scalars))
    norm1, weigh1, cross = (rows[:, tokens + i : tokens + i + 1] for i in range(3))
    beta = norm1 / (norm0 + EPS)
    image1 = rows[:, :tokens] + beta * image0
    direction = residual + beta * target
    curve = gram_scale * total(image1 * image1) + weigh1 + 2.0 * beta * cross + beta * beta * weigh0
    curve = jnp.broadcast_to(curve, (1, 32, 128))

    part = image_part(image1, direction)
    own = jnp.concatenate([part, curve])
    own = (own + core_move(own)).reshape(17, 32, 128)
    grid, curve = own[:16].reshape(4, 2, 2, 32, 128), own[16:]
    own, other = pick(grid, zlo, 1).reshape(8, 32, 128), pick(grid, 1 - zlo, 1).reshape(8, 32, 128)
    own = jnp.concatenate([own, curve]) + zlo_move(jnp.concatenate([other, curve]))
    grid, curve = own[:8].reshape(4, 2, 32, 128), own[8:]
    y = 2 * yhigh + ylow

    def for_y(k):
        return jnp.concatenate([pick(grid, ((y + k) % 4) // 2, 1), curve])

    own = for_y(0) + y_move(for_y(1), 1) + y_move(for_y(3), 3) + y_move(for_y(2), 2)
    alpha1 = norm1 / own[4][:, :1]

    def mine_of(blocks):
        return pick(blocks.reshape(4, 4, 32, 128), 2 * zlo + yhigh, 1)

    my_target, my_residual = mine_of(target_blocks), mine_of(residual_blocks)
    merged = alpha0 * my_target + alpha1 * (my_residual + beta * my_target)
    both = jnp.concatenate([merged, my_residual - alpha1 * own[:4]], axis=1)
    both = lax.dynamic_slice_in_dim(both, 32 * (2 * ylow + core), 32, 2)

    groups = jnp.stack([both[0]] + [x_move(both[k], 4 - k) for k in (1, 2, 3)])
    groups = lax.dynamic_slice_in_dim(jnp.concatenate([groups, groups]), (4 - x) % 4, 4, 0)
    return groups[:, :32].reshape(128, 32).T, groups[:, 32:].reshape(128, 32).T


def solution(mesh):
    in_specs = (P("task", None, "rows"), P("task", "rows", None))
    out_specs = (P(("rows", "task"), None), P(("rows", "task"), None))

    return jax.shard_map(on_device, mesh=mesh, in_specs=in_specs, out_specs=out_specs, check_vma=False)
```

time: 169 us -> 131 us (0.78)
  blocking collectives: 90 us -> 0 us
  starting transfers between devices: 24.5 us -> 63 us
  waiting for transfers between devices: 42.9 us -> 54.1 us
    all_to_all x6 -> x0, blocking collectives: 90 us -> none  [scatter_sum(): return jnp.sum(lax.all_to_all(chunks, axis, 0, 0), axis=0)]
    ppermute x0 -> x39, starting transfers between devices: none -> 63 us  [moved(): return lax.ppermute(value, axis, [(i, to(i)) for i in range(16)])]
    ppermute x0 -> x39, waiting for transfers between devices: none -> 54.1 us  [moved(): return lax.ppermute(value, axis, [(i, to(i)) for i in range(16)])]
    all_to_all x5 -> x0, waiting for transfers between devices: 42.9 us -> none  [gather(): lax.all_to_all(copies, axis, 0, 0)]
    all_to_all x5 -> x0, starting transfers between devices: 24.5 us -> none  [gather(): lax.all_to_all(copies, axis, 0, 0)]
    broadcast_in_dim x11 -> x1, local copies, waits for them, and re-layouts: 3.52 us -> 0.07 us  [on_device(): curve = jnp.broadcast_to(curve, (1, 32, 128))]
  transfers between devices with their start and end apart: 5 -> 39, of which waited for: 5 -> 28; matrix products, arithmetic and copies ran while one was open for 0% -> 1% of each run, Pallas kernels for 0% -> 0%
where the time goes in v2:
time: 131 us; the launch traced here: 129 us
  starting transfers between devices  63 us (48%)
  waiting for transfers between devices  54.1 us (41%)
  matrix products  3.69 us (3%)
  other arithmetic  3.66 us (3%)
  local copies, waits for them, and re-layouts  3.52 us (3%)
    ppermute x39, starting transfers between devices, moved(): return lax.ppermute(value, axis, [(i, to(i)) for i in range(16)])  63 us
    ppermute x39, waiting for transfers between devices, moved(): return lax.ppermute(value, axis, [(i, to(i)) for i in range(16)])  54.1 us
  transfers between devices with their start and end apart: 39, of which 28 were waited for; matrix products, arithmetic and copies ran while one was open for 1% of the time, Pallas kernels for 0%

profile of v2, /device:TPU:1, one launch (start us, length us, event | category | flops | bytes accessed | tf_op | source)
XLA Modules:
  0.0 129.2 jit_solution(11829358335800184056)
XLA Ops:
  0.7 1.0 copy.32
  1.8 1.3 fusion
  3.1 3.6 %collective-permute-start.2 = (f32[32,384]{1,0:T(8,128)S(1)}, f32[32,384]{1,0:T(8,128)S(1)}, u32[]{:S(2)}, u32[]{:S(2)}) collective-permute-start(f32[32,384]{1,0:T(8,128)S(1)} %get-tuple-element.28), channel_id=1, source_target_pairs={{0,2},{1,3},{2,0},{3,1},{4,6},{5,7},{6,4},{7,5},{8,10},{9,11},{10,... | collective-permute-start | bytes 147464 | tf_op jit(solution)/shard_map/ppermute | solution.py:12
  6.7 0.9 collective-permute-start.1
  8.2 2.1 %collective-permute-start.8 = (bf16[384,512]{1,0:T(8,128)(2,1)}, bf16[384,512]{1,0:T(8,128)(2,1)S(1)}, u32[]{:S(2)}, u32[]{:S(2)}) collective-permute-start(bf16[384,512]{1,0:T(8,128)(2,1)} %bitcast.164), channel_id=1, source_target_pairs={{0,3},{1,0},{2,1},{3,2},{4,7},{5,4},{6,5},{7,6},{8,11},{9,8},{10,9... | collective-permute-start | bytes 1179656 | tf_op jit(solution)/shard_map/ppermute | solution.py:12
  10.3 1.5 %collective-permute-done = f32[32,384]{1,0:T(8,128)S(1)} collective-permute-done((f32[32,384]{1,0:T(8,128)S(1)}, f32[32,384]{1,0:T(8,128)S(1)}, u32[]{:S(2)}, u32[]{:S(2)}) %collective-permute-start) | collective-permute-done | bytes 49184 | tf_op jit(solution)/shard_map/ppermute | solution.py:12
  11.8 6.9 %collective-permute-start.5 = (f32[32,384]{1,0:T(8,128)S(1)}, f32[32,384]{1,0:T(8,128)S(1)}, u32[]{:S(2)}, u32[]{:S(2)}) collective-permute-start(f32[32,384]{1,0:T(8,128)S(1)} %fusion.50), channel_id=1, source_target_pairs={{0,8},{1,9},{2,10},{3,11},{4,12},{5,13},{6,14},{7,15},{8,0},{9,1},... | collective-permute-start | bytes 147464 | tf_op jit(solution)/shard_map/ppermute | solution.py:12
  18.8 2.4 %collective-permute-start.3 = (f32[32,384]{1,0:T(8,128)S(1)}, f32[32,384]{1,0:T(8,128)S(1)}, u32[]{:S(2)}, u32[]{:S(2)}) collective-permute-start(f32[32,384]{1,0:T(8,128)S(1)} %fusion.50), channel_id=1, source_target_pairs={{0,4},{1,5},{2,6},{3,7},{4,8},{5,9},{6,10},{7,11},{8,12},{9,13},{1... | collective-permute-start | bytes 147464 | tf_op jit(solution)/shard_map/ppermute | solution.py:12
  21.2 1.3 %collective-permute-start.12 = (bf16[32,512]{1,0:T(8,128)(2,1)S(1)}, bf16[32,512]{1,0:T(8,128)(2,1)S(1)}, u32[]{:S(2)}, u32[]{:S(2)}) collective-permute-start(bf16[32,512]{1,0:T(8,128)(2,1)S(1)} %get-tuple-element.39), channel_id=1, source_target_pairs={{0,3},{1,0},{2,1},{3,2},{4,7},{5,4},{6,5},{7,6},{8,11},{9,8},{10,9... | collective-permute-start | bytes 98312 | tf_op jit(solution)/shard_map/ppermute | solution.py:12
  24.6 2.1 %collective-permute-start.9 = (bf16[192,512]{1,0:T(8,128)(2,1)S(1)}, bf16[192,512]{1,0:T(8,128)(2,1)S(1)}, u32[]{:S(2)}, u32[]{:S(2)}) collective-permute-start(bf16[192,512]{1,0:T(8,128)(2,1)S(1)} %slice.141), channel_id=1, source_target_pairs={{0,3},{1,0},{2,1},{3,2},{4,7},{5,4},{6,5},{7,6},{8,11},{9,8},{10,9... | collective-permute-start | bytes 589832 | tf_op jit(solution)/shard_map/ppermute | solution.py:12
  26.8 2.7 %collective-permute-done.9 = bf16[192,512]{1,0:T(8,128)(2,1)S(1)} collective-permute-done((bf16[192,512]{1,0:T(8,128)(2,1)S(1)}, bf16[192,512]{1,0:T(8,128)(2,1)S(1)}, u32[]{:S(2)}, u32[]{:S(2)}) %collective-permute-start.9) | collective-permute-done | bytes 196640 | tf_op jit(solution)/shard_map/ppermute | solution.py:12
  29.6 3.7 %collective-permute-done.7 = bf16[192,512]{1,0:T(8,128)(2,1)S(1)} collective-permute-done((bf16[192,512]{1,0:T(8,128)(2,1)S(1)}, bf16[192,512]{1,0:T(8,128)(2,1)S(1)}, u32[]{:S(2)}, u32[]{:S(2)}) %collective-permute-start.7) | collective-permute-done | bytes 196640 | tf_op jit(solution)/shard_map/ppermute | solution.py:12
  34.2 4.9 %collective-permute-start.13 = (f32[8,32,128]{2,1,0:T(8,128)S(1)}, f32[8,32,128]{2,1,0:T(8,128)S(1)}, u32[]{:S(2)}, u32[]{:S(2)}) collective-permute-start(f32[8,32,128]{2,1,0:T(8,128)S(1)} %bitcast.185), channel_id=1, source_target_pairs={{0,16},{16,0},{32,48},{48,32},{64,80},{80,64},{96,112},{112,96},{1... | collective-permute-start | bytes 393224 | tf_op jit(solution)/shard_map/ppermute | solution.py:12
  39.1 1.0 collective-permute-done.13
  40.1 1.8 %collective-permute-start.14 = (f32[8,32,128]{2,1,0:T(8,128)S(1)}, f32[8,32,128]{2,1,0:T(8,128)S(1)}, u32[]{:S(2)}, u32[]{:S(2)}) collective-permute-start(f32[8,32,128]{2,1,0:T(8,128)S(1)} %bitcast_add_fusion.1), channel_id=1, source_target_pairs={{0,128},{16,144},{32,160},{48,176},{64,192},{80,208},{96,224},{112... | collective-permute-start | bytes 393224 | tf_op jit(solution)/shard_map/ppermute | solution.py:12
  41.8 3.4 %collective-permute-done.14 = f32[8,32,128]{2,1,0:T(8,128)S(1)} collective-permute-done((f32[8,32,128]{2,1,0:T(8,128)S(1)}, f32[8,32,128]{2,1,0:T(8,128)S(1)}, u32[]{:S(2)}, u32[]{:S(2)}) %collective-permute-start.14) | collective-permute-done | bytes 131104 | tf_op jit(solution)/shard_map/ppermute | solution.py:12
  45.3 3.2 %collective-permute-start.17 = (f32[8,32,128]{2,1,0:T(8,128)S(1)}, f32[8,32,128]{2,1,0:T(8,128)S(1)}, u32[]{:S(2)}, u32[]{:S(2)}) collective-permute-start(f32[8,32,128]{2,1,0:T(8,128)S(1)} %add.297), channel_id=1, source_target_pairs={{0,64},{16,80},{32,96},{48,112},{64,0},{80,16},{96,32},{112,48},{1... | collective-permute-start | bytes 393224 | tf_op jit(solution)/shard_map/ppermute | solution.py:12
  49.9 0.9 collective-permute-done.17
  50.9 3.1 %collective-permute-done.16 = f32[8,32,128]{2,1,0:T(8,128)S(1)} collective-permute-done((f32[8,32,128]{2,1,0:T(8,128)S(1)}, f32[8,32,128]{2,1,0:T(8,128)S(1)}, u32[]{:S(2)}, u32[]{:S(2)}) %collective-permute-start.16) | collective-permute-done | bytes 131104 | tf_op jit(solution)/shard_map/ppermute | solution.py:12
  54.4 2.7 %collective-permute-start.18 = (f32[8,32,128]{2,1,0:T(8,128)S(1)}, f32[8,32,128]{2,1,0:T(8,128)S(1)}, u32[]{:S(2)}, u32[]{:S(2)}) collective-permute-start(f32[8,32,128]{2,1,0:T(8,128)S(1)} %add_add_fusion.1), channel_id=1, source_target_pairs={{0,16},{16,0},{32,48},{48,32},{64,80},{80,64},{96,112},{112,96},{1... | collective-permute-start | bytes 393224 | tf_op jit(solution)/shard_map/ppermute | solution.py:12
  57.1 1.0 collective-permute-done.18
  59.4 4.7 %collective-permute-start.21 = (f32[32,512]{1,0:T(8,128)S(1)}, f32[32,512]{1,0:T(8,128)S(1)}, u32[]{:S(2)}, u32[]{:S(2)}) collective-permute-start(f32[32,512]{1,0:T(8,128)S(1)} %pad_maximum_fusion.10), channel_id=1, source_target_pairs={{0,8},{1,9},{2,10},{3,11},{4,12},{5,13},{6,14},{7,15},{8,0},{9,1},... | collective-permute-start | bytes 196616 | tf_op jit(solution)/shard_map/ppermute | solution.py:12
  64.1 3.6 %collective-permute-start.20 = (f32[32,512]{1,0:T(8,128)S(1)}, f32[32,512]{1,0:T(8,128)S(1)}, u32[]{:S(2)}, u32[]{:S(2)}) collective-permute-start(f32[32,512]{1,0:T(8,128)S(1)} %pad_maximum_fusion.10), channel_id=1, source_target_pairs={{0,12},{1,13},{2,14},{3,15},{4,0},{5,1},{6,2},{7,3},{8,4},{9,5},{1... | collective-permute-start | bytes 196616 | tf_op jit(solution)/shard_map/ppermute | solution.py:12
  67.7 1.7 %collective-permute-done.19 = f32[32,512]{1,0:T(8,128)S(1)} collective-permute-done((f32[32,512]{1,0:T(8,128)S(1)}, f32[32,512]{1,0:T(8,128)S(1)}, u32[]{:S(2)}, u32[]{:S(2)}) %collective-permute-start.19) | collective-permute-done | bytes 65568 | tf_op jit(solution)/shard_map/ppermute | solution.py:12
  69.4 1.7 %collective-permute-done.20 = f32[32,512]{1,0:T(8,128)S(1)} collective-permute-done((f32[32,512]{1,0:T(8,128)S(1)}, f32[32,512]{1,0:T(8,128)S(1)}, u32[]{:S(2)}, u32[]{:S(2)}) %collective-permute-start.20) | collective-permute-done | bytes 65568 | tf_op jit(solution)/shard_map/ppermute | solution.py:12
  73.1 1.0 collective-permute-done.22
  74.1 1.7 %collective-permute-start.23 = (f32[9,32,128]{2,1,0:T(8,128)S(1)}, f32[9,32,128]{2,1,0:T(8,128)S(1)}, u32[]{:S(2)}, u32[]{:S(2)}) collective-permute-start(f32[9,32,128]{2,1,0:T(8,128)S(1)} %fusion.26), channel_id=1, source_target_pairs={{0,128},{16,144},{32,160},{48,176},{64,192},{80,208},{96,224},{112... | collective-permute-start | bytes 442376 | tf_op jit(solution)/shard_map/ppermute | solution.py:12
  75.8 3.7 %collective-permute-done.23 = f32[9,32,128]{2,1,0:T(8,128)S(1)} collective-permute-done((f32[9,32,128]{2,1,0:T(8,128)S(1)}, f32[9,32,128]{2,1,0:T(8,128)S(1)}, u32[]{:S(2)}, u32[]{:S(2)}) %collective-permute-start.23) | collective-permute-done | bytes 147488 | tf_op jit(solution)/shard_map/ppermute | solution.py:12
  79.5 1.5 %collective-permute-start.26 = (f32[9,32,128]{2,1,0:T(8,128)S(1)}, f32[9,32,128]{2,1,0:T(8,128)S(1)}, u32[]{:S(2)}, u32[]{:S(2)}) collective-permute-start(f32[9,32,128]{2,1,0:T(8,128)S(1)} %add.309), channel_id=1, source_target_pairs={{0,64},{16,80},{32,96},{48,112},{64,0},{80,16},{96,32},{112,48},{1... | collective-permute-start | bytes 442376 | tf_op jit(solution)/shard_map/ppermute | solution.py:12
  81.0 1.0 collective-permute-start.25
  82.5 2.9 %collective-permute-done.26 = f32[9,32,128]{2,1,0:T(8,128)S(1)} collective-permute-done((f32[9,32,128]{2,1,0:T(8,128)S(1)}, f32[9,32,128]{2,1,0:T(8,128)S(1)}, u32[]{:S(2)}, u32[]{:S(2)}) %collective-permute-start.26) | collective-permute-done | bytes 147488 | tf_op jit(solution)/shard_map/ppermute | solution.py:12
  85.4 1.9 %collective-permute-done.25 = f32[9,32,128]{2,1,0:T(8,128)S(1)} collective-permute-done((f32[9,32,128]{2,1,0:T(8,128)S(1)}, f32[9,32,128]{2,1,0:T(8,128)S(1)}, u32[]{:S(2)}, u32[]{:S(2)}) %collective-permute-start.25) | collective-permute-done | bytes 147488 | tf_op jit(solution)/shard_map/ppermute | solution.py:12
  87.3 1.9 %collective-permute-done.24 = f32[9,32,128]{2,1,0:T(8,128)S(1)} collective-permute-done((f32[9,32,128]{2,1,0:T(8,128)S(1)}, f32[9,32,128]{2,1,0:T(8,128)S(1)}, u32[]{:S(2)}, u32[]{:S(2)}) %collective-permute-start.24) | collective-permute-done | bytes 147488 | tf_op jit(solution)/shard_map/ppermute | solution.py:12
  89.5 1.6 %collective-permute-start.27 = (f32[8,32,128]{2,1,0:T(8,128)S(1)}, f32[8,32,128]{2,1,0:T(8,128)S(1)}, u32[]{:S(2)}, u32[]{:S(2)}) collective-permute-start(f32[8,32,128]{2,1,0:T(8,128)S(1)} %fusion.27), channel_id=1, source_target_pairs={{0,16},{16,0},{32,48},{48,32},{64,80},{80,64},{96,112},{112,96},{1... | collective-permute-start | bytes 393224 | tf_op jit(solution)/shard_map/ppermute | solution.py:12
  91.1 1.0 collective-permute-done.27
  93.4 3.8 %collective-permute-start.30 = (f32[32,512]{1,0:T(8,128)S(1)}, f32[32,512]{1,0:T(8,128)S(1)}, u32[]{:S(2)}, u32[]{:S(2)}) collective-permute-start(f32[32,512]{1,0:T(8,128)S(1)} %pad_maximum_fusion.11), channel_id=1, source_target_pairs={{0,8},{1,9},{2,10},{3,11},{4,12},{5,13},{6,14},{7,15},{8,0},{9,1},... | collective-permute-start | bytes 196616 | tf_op jit(solution)/shard_map/ppermute | solution.py:12
  97.3 2.2 %collective-permute-start.28 = (f32[32,512]{1,0:T(8,128)S(1)}, f32[32,512]{1,0:T(8,128)S(1)}, u32[]{:S(2)}, u32[]{:S(2)}) collective-permute-start(f32[32,512]{1,0:T(8,128)S(1)} %pad_maximum_fusion.11), channel_id=1, source_target_pairs={{0,4},{1,5},{2,6},{3,7},{4,8},{5,9},{6,10},{7,11},{8,12},{9,13},{1... | collective-permute-start | bytes 196616 | tf_op jit(solution)/shard_map/ppermute | solution.py:12
  99.5 1.4 %collective-permute-start.29 = (f32[32,512]{1,0:T(8,128)S(1)}, f32[32,512]{1,0:T(8,128)S(1)}, u32[]{:S(2)}, u32[]{:S(2)}) collective-permute-start(f32[32,512]{1,0:T(8,128)S(1)} %pad_maximum_fusion.11), channel_id=1, source_target_pairs={{0,12},{1,13},{2,14},{3,15},{4,0},{5,1},{6,2},{7,3},{8,4},{9,5},{1... | collective-permute-start | bytes 196616 | tf_op jit(solution)/shard_map/ppermute | solution.py:12
  100.9 4.6 %collective-permute-done.28 = f32[32,512]{1,0:T(8,128)S(1)} collective-permute-done((f32[32,512]{1,0:T(8,128)S(1)}, f32[32,512]{1,0:T(8,128)S(1)}, u32[]{:S(2)}, u32[]{:S(2)}) %collective-permute-start.28) | collective-permute-done | bytes 65568 | tf_op jit(solution)/shard_map/ppermute | solution.py:12
  108.1 1.2 collective-permute-done.31
  109.9 4.6 %collective-permute-done.32 = f32[9,32,128]{2,1,0:T(8,128)S(1)} collective-permute-done((f32[9,32,128]{2,1,0:T(8,128)S(1)}, f32[9,32,128]{2,1,0:T(8,128)S(1)}, u32[]{:S(2)}, u32[]{:S(2)}) %collective-permute-start.32) | collective-permute-done | bytes 147488 | tf_op jit(solution)/shard_map/ppermute | solution.py:12
  114.7 1.2 collective-permute-start.35
  115.8 1.0 collective-permute-start.34
  117.4 2.2 %collective-permute-done.35 = f32[5,32,128]{2,1,0:T(8,128)S(1)} collective-permute-done((f32[5,32,128]{2,1,0:T(8,128)S(1)}, f32[5,32,128]{2,1,0:T(8,128)S(1)}, u32[]{:S(2)}, u32[]{:S(2)}) %collective-permute-start.35) | collective-permute-done | bytes 81952 | tf_op jit(solution)/shard_map/ppermute | solution.py:12
  119.5 2.6 %collective-permute-done.33 = f32[5,32,128]{2,1,0:T(8,128)S(1)} collective-permute-done((f32[5,32,128]{2,1,0:T(8,128)S(1)}, f32[5,32,128]{2,1,0:T(8,128)S(1)}, u32[]{:S(2)}, u32[]{:S(2)}) %collective-permute-start.33) | collective-permute-done | bytes 81952 | tf_op jit(solution)/shard_map/ppermute | solution.py:12
  123.0 1.1 collective-permute-start.38
  124.1 1.3 %collective-permute-done.36 = f32[64,32]{1,0:T(8,128)S(1)} collective-permute-done((f32[64,32]{1,0:T(8,128)S(1)}, f32[64,32]{1,0:T(8,128)S(1)}, u32[]{:S(2)}, u32[]{:S(2)}) %collective-permute-start.36) | collective-permute-done | bytes 8224 | tf_op jit(solution)/shard_map/ppermute | solution.py:12
  125.4 1.6 %collective-permute-done.37 = f32[64,32]{1,0:T(8,128)S(1)} collective-permute-done((f32[64,32]{1,0:T(8,128)S(1)}, f32[64,32]{1,0:T(8,128)S(1)}, u32[]{:S(2)}, u32[]{:S(2)}) %collective-permute-start.37) | collective-permute-done | bytes 8224 | tf_op jit(solution)/shard_map/ppermute | solution.py:12
  (126 shorter events, 17.9 us)
Async XLA Ops:
  0.6 32.6 %copy-start = (bf16[1,384,512]{2,1,0:T(8,128)(2,1)S(1)}, bf16[1,384,512]{2,1,0:T(8,128)(2,1)}, u32[]{:S(2)}) copy-start(bf16[1,384,512]{2,1,0:T(8,128)(2,1)} %param.2) | copy-start | bytes 1179652
  3.1 7.2 %collective-permute-start.2 = (f32[32,384]{1,0:T(8,128)S(1)}, f32[32,384]{1,0:T(8,128)S(1)}, u32[]{:S(2)}, u32[]{:S(2)}) collective-permute-start(f32[32,384]{1,0:T(8,128)S(1)} %get-tuple-element.28), channel_id=1, source_target_pairs={{0,2},{1,3},{2,0},{3,1},{4,6},{5,7},{6,4},{7,5},{8,10},{9,11},{10,... | collective-permute-start | bytes 147464 | tf_op jit(solution)/shard_map/ppermute | solution.py:12
  6.7 3.5 %collective-permute-start.1 = (f32[32,384]{1,0:T(8,128)S(1)}, f32[32,384]{1,0:T(8,128)S(1)}, u32[]{:S(2)}, u32[]{:S(2)}) collective-permute-start(f32[32,384]{1,0:T(8,128)S(1)} %get-tuple-element.29), channel_id=1, source_target_pairs={{0,3},{1,0},{2,1},{3,2},{4,7},{5,4},{6,5},{7,6},{8,11},{9,8},{10,9... | collective-permute-start | bytes 147464 | tf_op jit(solution)/shard_map/ppermute | solution.py:12
  7.6 4.2 %collective-permute-start = (f32[32,384]{1,0:T(8,128)S(1)}, f32[32,384]{1,0:T(8,128)S(1)}, u32[]{:S(2)}, u32[]{:S(2)}) collective-permute-start(f32[32,384]{1,0:T(8,128)S(1)} %get-tuple-element.27), channel_id=1, source_target_pairs={{0,1},{1,2},{2,3},{3,0},{4,5},{5,6},{6,7},{7,4},{8,9},{9,10},{10,1... | collective-permute-start | bytes 147464 | tf_op jit(solution)/shard_map/ppermute | solution.py:12
  8.2 16.4 %collective-permute-start.8 = (bf16[384,512]{1,0:T(8,128)(2,1)}, bf16[384,512]{1,0:T(8,128)(2,1)S(1)}, u32[]{:S(2)}, u32[]{:S(2)}) collective-permute-start(bf16[384,512]{1,0:T(8,128)(2,1)} %bitcast.164), channel_id=1, source_target_pairs={{0,3},{1,0},{2,1},{3,2},{4,7},{5,4},{6,5},{7,6},{8,11},{9,8},{10,9... | collective-permute-start | bytes 1179656 | tf_op jit(solution)/shard_map/ppermute | solution.py:12
  10.3 16.4 %collective-permute-start.6 = (bf16[384,512]{1,0:T(8,128)(2,1)}, bf16[384,512]{1,0:T(8,128)(2,1)S(1)}, u32[]{:S(2)}, u32[]{:S(2)}) collective-permute-start(bf16[384,512]{1,0:T(8,128)(2,1)} %bitcast.165), channel_id=1, source_target_pairs={{0,1},{1,2},{2,3},{3,0},{4,5},{5,6},{6,7},{7,4},{8,9},{9,10},{10,1... | collective-permute-start | bytes 1179656 | tf_op jit(solution)/shard_map/ppermute | solution.py:12
  11.8 9.3 %collective-permute-start.5 = (f32[32,384]{1,0:T(8,128)S(1)}, f32[32,384]{1,0:T(8,128)S(1)}, u32[]{:S(2)}, u32[]{:S(2)}) collective-permute-start(f32[32,384]{1,0:T(8,128)S(1)} %fusion.50), channel_id=1, source_target_pairs={{0,8},{1,9},{2,10},{3,11},{4,12},{5,13},{6,14},{7,15},{8,0},{9,1},... | collective-permute-start | bytes 147464 | tf_op jit(solution)/shard_map/ppermute | solution.py:12
  18.8 4.1 %collective-permute-start.4 = (f32[32,384]{1,0:T(8,128)S(1)}, f32[32,384]{1,0:T(8,128)S(1)}, u32[]{:S(2)}, u32[]{:S(2)}) collective-permute-start(f32[32,384]{1,0:T(8,128)S(1)} %fusion.50), channel_id=1, source_target_pairs={{0,12},{1,13},{2,14},{3,15},{4,0},{5,1},{6,2},{7,3},{8,4},{9,5},{1... | collective-permute-start | bytes 147464 | tf_op jit(solution)/shard_map/ppermute | solution.py:12
  18.8 5.2 %collective-permute-start.3 = (f32[32,384]{1,0:T(8,128)S(1)}, f32[32,384]{1,0:T(8,128)S(1)}, u32[]{:S(2)}, u32[]{:S(2)}) collective-permute-start(f32[32,384]{1,0:T(8,128)S(1)} %fusion.50), channel_id=1, source_target_pairs={{0,4},{1,5},{2,6},{3,7},{4,8},{5,9},{6,10},{7,11},{8,12},{9,13},{1... | collective-permute-start | bytes 147464 | tf_op jit(solution)/shard_map/ppermute | solution.py:12
  21.2 12.9 %collective-permute-start.12 = (bf16[32,512]{1,0:T(8,128)(2,1)S(1)}, bf16[32,512]{1,0:T(8,128)(2,1)S(1)}, u32[]{:S(2)}, u32[]{:S(2)}) collective-permute-start(bf16[32,512]{1,0:T(8,128)(2,1)S(1)} %get-tuple-element.39), channel_id=1, source_target_pairs={{0,3},{1,0},{2,1},{3,2},{4,7},{5,4},{6,5},{7,6},{8,11},{9,8},{10,9... | collective-permute-start | bytes 98312 | tf_op jit(solution)/shard_map/ppermute | solution.py:12
  22.9 11.2 %collective-permute-start.11 = (bf16[32,512]{1,0:T(8,128)(2,1)S(1)}, bf16[32,512]{1,0:T(8,128)(2,1)S(1)}, u32[]{:S(2)}, u32[]{:S(2)}) collective-permute-start(bf16[32,512]{1,0:T(8,128)(2,1)S(1)} %get-tuple-element.40), channel_id=1, source_target_pairs={{0,2},{1,3},{2,0},{3,1},{4,6},{5,7},{6,4},{7,5},{8,10},{9,11},{10,... | collective-permute-start | bytes 98312 | tf_op jit(solution)/shard_map/ppermute | solution.py:12
  23.9 10.2 %collective-permute-start.10 = (bf16[32,512]{1,0:T(8,128)(2,1)S(1)}, bf16[32,512]{1,0:T(8,128)(2,1)S(1)}, u32[]{:S(2)}, u32[]{:S(2)}) collective-permute-start(bf16[32,512]{1,0:T(8,128)(2,1)S(1)} %get-tuple-element.41), channel_id=1, source_target_pairs={{0,1},{1,2},{2,3},{3,0},{4,5},{5,6},{6,7},{7,4},{8,9},{9,10},{10,1... | collective-permute-start | bytes 98312 | tf_op jit(solution)/shard_map/ppermute | solution.py:12
  24.6 4.9 %collective-permute-start.9 = (bf16[192,512]{1,0:T(8,128)(2,1)S(1)}, bf16[192,512]{1,0:T(8,128)(2,1)S(1)}, u32[]{:S(2)}, u32[]{:S(2)}) collective-permute-start(bf16[192,512]{1,0:T(8,128)(2,1)S(1)} %slice.141), channel_id=1, source_target_pairs={{0,3},{1,0},{2,1},{3,2},{4,7},{5,4},{6,5},{7,6},{8,11},{9,8},{10,9... | collective-permute-start | bytes 589832 | tf_op jit(solution)/shard_map/ppermute | solution.py:12
  26.7 6.5 %collective-permute-start.7 = (bf16[192,512]{1,0:T(8,128)(2,1)S(1)}, bf16[192,512]{1,0:T(8,128)(2,1)S(1)}, u32[]{:S(2)}, u32[]{:S(2)}) collective-permute-start(bf16[192,512]{1,0:T(8,128)(2,1)S(1)} %slice.140), channel_id=1, source_target_pairs={{0,1},{1,2},{2,3},{3,0},{4,5},{5,6},{6,7},{7,4},{8,9},{9,10},{10,1... | collective-permute-start | bytes 589832 | tf_op jit(solution)/shard_map/ppermute | solution.py:12
  34.2 5.8 %collective-permute-start.13 = (f32[8,32,128]{2,1,0:T(8,128)S(1)}, f32[8,32,128]{2,1,0:T(8,128)S(1)}, u32[]{:S(2)}, u32[]{:S(2)}) collective-permute-start(f32[8,32,128]{2,1,0:T(8,128)S(1)} %bitcast.185), channel_id=1, source_target_pairs={{0,16},{16,0},{32,48},{48,32},{64,80},{80,64},{96,112},{112,96},{1... | collective-permute-start | bytes 393224 | tf_op jit(solution)/shard_map/ppermute | solution.py:12
  40.1 5.2 %collective-permute-start.14 = (f32[8,32,128]{2,1,0:T(8,128)S(1)}, f32[8,32,128]{2,1,0:T(8,128)S(1)}, u32[]{:S(2)}, u32[]{:S(2)}) collective-permute-start(f32[8,32,128]{2,1,0:T(8,128)S(1)} %bitcast_add_fusion.1), channel_id=1, source_target_pairs={{0,128},{16,144},{32,160},{48,176},{64,192},{80,208},{96,224},{112... | collective-permute-start | bytes 393224 | tf_op jit(solution)/shard_map/ppermute | solution.py:12
  45.3 5.6 %collective-permute-start.17 = (f32[8,32,128]{2,1,0:T(8,128)S(1)}, f32[8,32,128]{2,1,0:T(8,128)S(1)}, u32[]{:S(2)}, u32[]{:S(2)}) collective-permute-start(f32[8,32,128]{2,1,0:T(8,128)S(1)} %add.297), channel_id=1, source_target_pairs={{0,64},{16,80},{32,96},{48,112},{64,0},{80,16},{96,32},{112,48},{1... | collective-permute-start | bytes 393224 | tf_op jit(solution)/shard_map/ppermute | solution.py:12
  48.5 5.5 %collective-permute-start.16 = (f32[8,32,128]{2,1,0:T(8,128)S(1)}, f32[8,32,128]{2,1,0:T(8,128)S(1)}, u32[]{:S(2)}, u32[]{:S(2)}) collective-permute-start(f32[8,32,128]{2,1,0:T(8,128)S(1)} %add.297), channel_id=1, source_target_pairs={{0,96},{16,112},{32,0},{48,16},{64,32},{80,48},{96,64},{112,80},{1... | collective-permute-start | bytes 393224 | tf_op jit(solution)/shard_map/ppermute | solution.py:12
  49.2 5.1 %collective-permute-start.15 = (f32[8,32,128]{2,1,0:T(8,128)S(1)}, f32[8,32,128]{2,1,0:T(8,128)S(1)}, u32[]{:S(2)}, u32[]{:S(2)}) collective-permute-start(f32[8,32,128]{2,1,0:T(8,128)S(1)} %add.297), channel_id=1, source_target_pairs={{0,32},{16,48},{32,64},{48,80},{64,96},{80,112},{96,0},{112,16},{1... | collective-permute-start | bytes 393224 | tf_op jit(solution)/shard_map/ppermute | solution.py:12
  54.4 3.7 %collective-permute-start.18 = (f32[8,32,128]{2,1,0:T(8,128)S(1)}, f32[8,32,128]{2,1,0:T(8,128)S(1)}, u32[]{:S(2)}, u32[]{:S(2)}) collective-permute-start(f32[8,32,128]{2,1,0:T(8,128)S(1)} %add_add_fusion.1), channel_id=1, source_target_pairs={{0,16},{16,0},{32,48},{48,32},{64,80},{80,64},{96,112},{112,96},{1... | collective-permute-start | bytes 393224 | tf_op jit(solution)/shard_map/ppermute | solution.py:12
  59.4 8.3 %collective-permute-start.21 = (f32[32,512]{1,0:T(8,128)S(1)}, f32[32,512]{1,0:T(8,128)S(1)}, u32[]{:S(2)}, u32[]{:S(2)}) collective-permute-start(f32[32,512]{1,0:T(8,128)S(1)} %pad_maximum_fusion.10), channel_id=1, source_target_pairs={{0,8},{1,9},{2,10},{3,11},{4,12},{5,13},{6,14},{7,15},{8,0},{9,1},... | collective-permute-start | bytes 196616 | tf_op jit(solution)/shard_map/ppermute | solution.py:12
  64.1 5.3 %collective-permute-start.19 = (f32[32,512]{1,0:T(8,128)S(1)}, f32[32,512]{1,0:T(8,128)S(1)}, u32[]{:S(2)}, u32[]{:S(2)}) collective-permute-start(f32[32,512]{1,0:T(8,128)S(1)} %pad_maximum_fusion.10), channel_id=1, source_target_pairs={{0,4},{1,5},{2,6},{3,7},{4,8},{5,9},{6,10},{7,11},{8,12},{9,13},{1... | collective-permute-start | bytes 196616 | tf_op jit(solution)/shard_map/ppermute | solution.py:12
  64.1 7.0 %collective-permute-start.20 = (f32[32,512]{1,0:T(8,128)S(1)}, f32[32,512]{1,0:T(8,128)S(1)}, u32[]{:S(2)}, u32[]{:S(2)}) collective-permute-start(f32[32,512]{1,0:T(8,128)S(1)} %pad_maximum_fusion.10), channel_id=1, source_target_pairs={{0,12},{1,13},{2,14},{3,15},{4,0},{5,1},{6,2},{7,3},{8,4},{9,5},{1... | collective-permute-start | bytes 196616 | tf_op jit(solution)/shard_map/ppermute | solution.py:12
  72.3 1.7 %collective-permute-start.22 = (f32[9,32,128]{2,1,0:T(8,128)S(1)}, f32[9,32,128]{2,1,0:T(8,128)S(1)}, u32[]{:S(2)}, u32[]{:S(2)}) collective-permute-start(f32[9,32,128]{2,1,0:T(8,128)S(1)} %pad_maximum_fusion.2), channel_id=1, source_target_pairs={{0,16},{16,0},{32,48},{48,32},{64,80},{80,64},{96,112},{112,96},{1... | collective-permute-start | bytes 442376 | tf_op jit(solution)/shard_map/ppermute | solution.py:12
  74.1 5.4 %collective-permute-start.23 = (f32[9,32,128]{2,1,0:T(8,128)S(1)}, f32[9,32,128]{2,1,0:T(8,128)S(1)}, u32[]{:S(2)}, u32[]{:S(2)}) collective-permute-start(f32[9,32,128]{2,1,0:T(8,128)S(1)} %fusion.26), channel_id=1, source_target_pairs={{0,128},{16,144},{32,160},{48,176},{64,192},{80,208},{96,224},{112... | collective-permute-start | bytes 442376 | tf_op jit(solution)/shard_map/ppermute | solution.py:12
  79.5 5.9 %collective-permute-start.26 = (f32[9,32,128]{2,1,0:T(8,128)S(1)}, f32[9,32,128]{2,1,0:T(8,128)S(1)}, u32[]{:S(2)}, u32[]{:S(2)}) collective-permute-start(f32[9,32,128]{2,1,0:T(8,128)S(1)} %add.309), channel_id=1, source_target_pairs={{0,64},{16,80},{32,96},{48,112},{64,0},{80,16},{96,32},{112,48},{1... | collective-permute-start | bytes 442376 | tf_op jit(solution)/shard_map/ppermute | solution.py:12
  81.0 6.3 %collective-permute-start.25 = (f32[9,32,128]{2,1,0:T(8,128)S(1)}, f32[9,32,128]{2,1,0:T(8,128)S(1)}, u32[]{:S(2)}, u32[]{:S(2)}) collective-permute-start(f32[9,32,128]{2,1,0:T(8,128)S(1)} %add.309), channel_id=1, source_target_pairs={{0,96},{16,112},{32,0},{48,16},{64,32},{80,48},{96,64},{112,80},{1... | collective-permute-start | bytes 442376 | tf_op jit(solution)/shard_map/ppermute | solution.py:12
  82.0 7.3 %collective-permute-start.24 = (f32[9,32,128]{2,1,0:T(8,128)S(1)}, f32[9,32,128]{2,1,0:T(8,128)S(1)}, u32[]{:S(2)}, u32[]{:S(2)}) collective-permute-start(f32[9,32,128]{2,1,0:T(8,128)S(1)} %add.309), channel_id=1, source_target_pairs={{0,32},{16,48},{32,64},{48,80},{64,96},{80,112},{96,0},{112,16},{1... | collective-permute-start | bytes 442376 | tf_op jit(solution)/shard_map/ppermute | solution.py:12
  89.5 2.6 %collective-permute-start.27 = (f32[8,32,128]{2,1,0:T(8,128)S(1)}, f32[8,32,128]{2,1,0:T(8,128)S(1)}, u32[]{:S(2)}, u32[]{:S(2)}) collective-permute-start(f32[8,32,128]{2,1,0:T(8,128)S(1)} %fusion.27), channel_id=1, source_target_pairs={{0,16},{16,0},{32,48},{48,32},{64,80},{80,64},{96,112},{112,96},{1... | collective-permute-start | bytes 393224 | tf_op jit(solution)/shard_map/ppermute | solution.py:12
  93.4 7.4 %collective-permute-start.30 = (f32[32,512]{1,0:T(8,128)S(1)}, f32[32,512]{1,0:T(8,128)S(1)}, u32[]{:S(2)}, u32[]{:S(2)}) collective-permute-start(f32[32,512]{1,0:T(8,128)S(1)} %pad_maximum_fusion.11), channel_id=1, source_target_pairs={{0,8},{1,9},{2,10},{3,11},{4,12},{5,13},{6,14},{7,15},{8,0},{9,1},... | collective-permute-start | bytes 196616 | tf_op jit(solution)/shard_map/ppermute | solution.py:12
  97.3 8.2 %collective-permute-start.28 = (f32[32,512]{1,0:T(8,128)S(1)}, f32[32,512]{1,0:T(8,128)S(1)}, u32[]{:S(2)}, u32[]{:S(2)}) collective-permute-start(f32[32,512]{1,0:T(8,128)S(1)} %pad_maximum_fusion.11), channel_id=1, source_target_pairs={{0,4},{1,5},{2,6},{3,7},{4,8},{5,9},{6,10},{7,11},{8,12},{9,13},{1... | collective-permute-start | bytes 196616 | tf_op jit(solution)/shard_map/ppermute | solution.py:12
  99.5 6.4 %collective-permute-start.29 = (f32[32,512]{1,0:T(8,128)S(1)}, f32[32,512]{1,0:T(8,128)S(1)}, u32[]{:S(2)}, u32[]{:S(2)}) collective-permute-start(f32[32,512]{1,0:T(8,128)S(1)} %pad_maximum_fusion.11), channel_id=1, source_target_pairs={{0,12},{1,13},{2,14},{3,15},{4,0},{5,1},{6,2},{7,3},{8,4},{9,5},{1... | collective-permute-start | bytes 196616 | tf_op jit(solution)/shard_map/ppermute | solution.py:12
  107.2 2.0 %collective-permute-start.31 = (f32[17,32,128]{2,1,0:T(8,128)S(1)}, f32[17,32,128]{2,1,0:T(8,128)S(1)}, u32[]{:S(2)}, u32[]{:S(2)}) collective-permute-start(f32[17,32,128]{2,1,0:T(8,128)S(1)} %pad_maximum_fusion.1), channel_id=1, source_target_pairs={{0,16},{16,0},{32,48},{48,32},{64,80},{80,64},{96,112},{112,96},{1... | collective-permute-start | bytes 835592 | tf_op jit(solution)/shard_map/ppermute | solution.py:12
  109.4 5.1 %collective-permute-start.32 = (f32[9,32,128]{2,1,0:T(8,128)S(1)}, f32[9,32,128]{2,1,0:T(8,128)S(1)}, u32[]{:S(2)}, u32[]{:S(2)}) collective-permute-start(f32[9,32,128]{2,1,0:T(8,128)S(1)} %pad_maximum_fusion.4), channel_id=1, source_target_pairs={{0,128},{16,144},{32,160},{48,176},{64,192},{80,208},{96,224},{112... | collective-permute-start | bytes 442376 | tf_op jit(solution)/shard_map/ppermute | solution.py:12
  114.7 4.9 %collective-permute-start.35 = (f32[5,32,128]{2,1,0:T(8,128)S(1)}, f32[5,32,128]{2,1,0:T(8,128)S(1)}, u32[]{:S(2)}, u32[]{:S(2)}) collective-permute-start(f32[5,32,128]{2,1,0:T(8,128)S(1)} %get-tuple-element.49), channel_id=1, source_target_pairs={{0,64},{16,80},{32,96},{48,112},{64,0},{80,16},{96,32},{112,48},{1... | collective-permute-start | bytes 245768 | tf_op jit(solution)/shard_map/ppermute | solution.py:12
  115.8 3.7 %collective-permute-start.34 = (f32[5,32,128]{2,1,0:T(8,128)S(1)}, f32[5,32,128]{2,1,0:T(8,128)S(1)}, u32[]{:S(2)}, u32[]{:S(2)}) collective-permute-start(f32[5,32,128]{2,1,0:T(8,128)S(1)} %get-tuple-element.48), channel_id=1, source_target_pairs={{0,96},{16,112},{32,0},{48,16},{64,32},{80,48},{96,64},{112,80},{1... | collective-permute-start | bytes 245768 | tf_op jit(solution)/shard_map/ppermute | solution.py:12
  116.8 5.4 %collective-permute-start.33 = (f32[5,32,128]{2,1,0:T(8,128)S(1)}, f32[5,32,128]{2,1,0:T(8,128)S(1)}, u32[]{:S(2)}, u32[]{:S(2)}) collective-permute-start(f32[5,32,128]{2,1,0:T(8,128)S(1)} %get-tuple-element.47), channel_id=1, source_target_pairs={{0,32},{16,48},{32,64},{48,80},{64,96},{80,112},{96,0},{112,16},{1... | collective-permute-start | bytes 245768 | tf_op jit(solution)/shard_map/ppermute | solution.py:12
  122.6 2.8 %collective-permute-start.36 = (f32[64,32]{1,0:T(8,128)S(1)}, f32[64,32]{1,0:T(8,128)S(1)}, u32[]{:S(2)}, u32[]{:S(2)}) collective-permute-start(f32[64,32]{1,0:T(8,128)S(1)} %get-tuple-element.33), channel_id=1, source_target_pairs={{0,3},{1,0},{2,1},{3,2},{4,7},{5,4},{6,5},{7,6},{8,11},{9,8},{10,9... | collective-permute-start | bytes 24584 | tf_op jit(solution)/shard_map/ppermute | solution.py:12
  122.7 4.4 %collective-permute-start.37 = (f32[64,32]{1,0:T(8,128)S(1)}, f32[64,32]{1,0:T(8,128)S(1)}, u32[]{:S(2)}, u32[]{:S(2)}) collective-permute-start(f32[64,32]{1,0:T(8,128)S(1)} %get-tuple-element.32), channel_id=1, source_target_pairs={{0,2},{1,3},{2,0},{3,1},{4,6},{5,7},{6,4},{7,5},{8,10},{9,11},{10,... | collective-permute-start | bytes 24584 | tf_op jit(solution)/shard_map/ppermute | solution.py:12
  123.0 4.8 %collective-permute-start.38 = (f32[64,32]{1,0:T(8,128)S(1)}, f32[64,32]{1,0:T(8,128)S(1)}, u32[]{:S(2)}, u32[]{:S(2)}) collective-permute-start(f32[64,32]{1,0:T(8,128)S(1)} %get-tuple-element.30), channel_id=1, source_target_pairs={{0,1},{1,2},{2,3},{3,0},{4,5},{5,6},{6,7},{7,4},{8,9},{9,10},{10,1... | collective-permute-start | bytes 24584 | tf_op jit(solution)/shard_map/ppermute | solution.py:12

commit v3 on v2

--- a/solution.py
+++ b/solution.py
@@ -112,17 +112,16 @@
     for k in (1, 3, 2):
         mine = mine + x_move(pick(first, (x + k) % 4), k)
     turned = w.T.reshape(4, 32, width)
-    weights = [pick(turned, x)]
-    for k in (1, 2, 3):
-        weights.append(x_move(pick(turned, (x + k) % 4), k))
+    ws_far = x_move(pick(turned, (x + 2) % 4), 2)
+    far_left = x_move(jnp.concatenate([from_left[:half], pick(turned, (x + 1) % 4)]), 1)
+    far_right = x_move(jnp.concatenate([from_right[half:], pick(turned, (x + 3) % 4)]), 3)
     outputs = mine
     for k in (1, 3, 2):
         outputs = outputs + moved(mine, "rows", lambda r, k=k: (r + 4 * k) % 16)
-    far_left = x_move(from_left[:half], 1)
-    far_right = x_move(from_right[half:], 3)
 
-    xs = jnp.concatenate([own_x, from_left, jnp.concatenate([far_left, far_right]), from_right], axis=1)
-    ws = jnp.concatenate(weights, axis=1)
+    far = jnp.concatenate([far_left[:half], far_right[:half]])
+    xs = jnp.concatenate([own_x, from_left, far, from_right], axis=1)
+    ws = jnp.concatenate([pick(turned, x), far_left[half:], ws_far, far_right[half:]], axis=1)
     wide_x = xs.astype(jnp.float32)
     diag = diag_scale * jnp.sum(wide_x * wide_x, axis=0, keepdims=True)
 

time: 131 us -> 133 us (1.015)
  the two profiles are of different devices: /device:TPU:1 before, /device:TPU:6 now
where the time goes in v3:
time: 133 us
  waiting for transfers between devices  68.7 us (52%)
  starting transfers between devices  52 us (39%)
  matrix products  3.69 us (3%)
  other arithmetic  3.69 us (3%)
  local copies, waits for them, and re-layouts  3.52 us (3%)
    ppermute x37, waiting for transfers between devices, moved(): return lax.ppermute(value, axis, [(i, to(i)) for i in range(16)])  68.7 us
    ppermute x37, starting transfers between devices, moved(): return lax.ppermute(value, axis, [(i, to(i)) for i in range(16)])  52 us
  transfers between devices with their start and end apart: 37, of which 28 were waited for; matrix products, arithmetic and copies ran while one was open for 3% of the time, Pallas kernels for 0%

profile of v3, /device:TPU:6, one launch (start us, length us, event | category | flops | bytes accessed | tf_op | source)
XLA Modules:
  0.0 132.8 jit_solution(4233329103407183258)
XLA Ops:
  0.6 0.9 collective-permute-start.8
  1.5 2.4 %collective-permute-start.6 = (bf16[384,512]{1,0:T(8,128)(2,1)}, bf16[384,512]{1,0:T(8,128)(2,1)S(1)}, u32[]{:S(2)}, u32[]{:S(2)}) collective-permute-start(bf16[384,512]{1,0:T(8,128)(2,1)} %bitcast.165), channel_id=1, source_target_pairs={{0,1},{1,2},{2,3},{3,0},{4,5},{5,6},{6,7},{7,4},{8,9},{9,10},{10,1... | collective-permute-start | bytes 1179656 | tf_op jit(solution)/shard_map/ppermute | solution.py:12
  3.9 1.0 copy.32
  5.0 1.3 fusion
  6.3 1.1 collective-permute-start
  8.4 5.9 %collective-permute-done = f32[32,384]{1,0:T(8,128)S(1)} collective-permute-done((f32[32,384]{1,0:T(8,128)S(1)}, f32[32,384]{1,0:T(8,128)S(1)}, u32[]{:S(2)}, u32[]{:S(2)}) %collective-permute-start) | collective-permute-done | bytes 49184 | tf_op jit(solution)/shard_map/ppermute | solution.py:12
  14.4 1.7 %collective-permute-start.10 = (bf16[32,512]{1,0:T(8,128)(2,1)S(1)}, bf16[32,512]{1,0:T(8,128)(2,1)S(1)}, u32[]{:S(2)}, u32[]{:S(2)}) collective-permute-start(bf16[32,512]{1,0:T(8,128)(2,1)S(1)} %get-tuple-element.39), channel_id=1, source_target_pairs={{0,2},{1,3},{2,0},{3,1},{4,6},{5,7},{6,4},{7,5},{8,10},{9,11},{10,... | collective-permute-start | bytes 98312 | tf_op jit(solution)/shard_map/ppermute | solution.py:12
  16.1 7.3 %collective-permute-start.5 = (f32[32,384]{1,0:T(8,128)S(1)}, f32[32,384]{1,0:T(8,128)S(1)}, u32[]{:S(2)}, u32[]{:S(2)}) collective-permute-start(f32[32,384]{1,0:T(8,128)S(1)} %fusion.50), channel_id=1, source_target_pairs={{0,8},{1,9},{2,10},{3,11},{4,12},{5,13},{6,14},{7,15},{8,0},{9,1},... | collective-permute-start | bytes 147464 | tf_op jit(solution)/shard_map/ppermute | solution.py:12
  23.4 2.9 %collective-permute-start.3 = (f32[32,384]{1,0:T(8,128)S(1)}, f32[32,384]{1,0:T(8,128)S(1)}, u32[]{:S(2)}, u32[]{:S(2)}) collective-permute-start(f32[32,384]{1,0:T(8,128)S(1)} %fusion.50), channel_id=1, source_target_pairs={{0,4},{1,5},{2,6},{3,7},{4,8},{5,9},{6,10},{7,11},{8,12},{9,13},{1... | collective-permute-start | bytes 147464 | tf_op jit(solution)/shard_map/ppermute | solution.py:12
  26.3 2.9 %collective-permute-start.9 = (bf16[224,512]{1,0:T(8,128)(2,1)S(1)}, bf16[224,512]{1,0:T(8,128)(2,1)S(1)}, u32[]{:S(2)}, u32[]{:S(2)}) collective-permute-start(bf16[224,512]{1,0:T(8,128)(2,1)S(1)} %pad_maximum_fusion.3), channel_id=1, source_target_pairs={{0,3},{1,0},{2,1},{3,2},{4,7},{5,4},{6,5},{7,6},{8,11},{9,8},{10,9... | collective-permute-start | bytes 688136 | tf_op jit(solution)/shard_map/ppermute | solution.py:12
  29.8 3.8 %collective-permute-done.9 = bf16[224,512]{1,0:T(8,128)(2,1)S(1)} collective-permute-done((bf16[224,512]{1,0:T(8,128)(2,1)S(1)}, bf16[224,512]{1,0:T(8,128)(2,1)S(1)}, u32[]{:S(2)}, u32[]{:S(2)}) %collective-permute-start.9) | collective-permute-done | bytes 229408 | tf_op jit(solution)/shard_map/ppermute | solution.py:12
  33.7 1.7 %collective-permute-done.7 = bf16[224,512]{1,0:T(8,128)(2,1)S(1)} collective-permute-done((bf16[224,512]{1,0:T(8,128)(2,1)S(1)}, bf16[224,512]{1,0:T(8,128)(2,1)S(1)}, u32[]{:S(2)}, u32[]{:S(2)}) %collective-permute-start.7) | collective-permute-done | bytes 229408 | tf_op jit(solution)/shard_map/ppermute | solution.py:12
  36.5 1.3 %collective-permute-done.11 = f32[8,32,128]{2,1,0:T(8,128)S(1)} collective-permute-done((f32[8,32,128]{2,1,0:T(8,128)S(1)}, f32[8,32,128]{2,1,0:T(8,128)S(1)}, u32[]{:S(2)}, u32[]{:S(2)}) %collective-permute-start.11) | collective-permute-done | bytes 131104 | tf_op jit(solution)/shard_map/ppermute | solution.py:12
  37.9 1.1 collective-permute-start.12
  39.0 4.5 %collective-permute-done.12 = f32[8,32,128]{2,1,0:T(8,128)S(1)} collective-permute-done((f32[8,32,128]{2,1,0:T(8,128)S(1)}, f32[8,32,128]{2,1,0:T(8,128)S(1)}, u32[]{:S(2)}, u32[]{:S(2)}) %collective-permute-start.12) | collective-permute-done | bytes 131104 | tf_op jit(solution)/shard_map/ppermute | solution.py:12
  43.5 3.3 %collective-permute-start.15 = (f32[8,32,128]{2,1,0:T(8,128)S(1)}, f32[8,32,128]{2,1,0:T(8,128)S(1)}, u32[]{:S(2)}, u32[]{:S(2)}) collective-permute-start(f32[8,32,128]{2,1,0:T(8,128)S(1)} %add.297), channel_id=1, source_target_pairs={{0,64},{16,80},{32,96},{48,112},{64,0},{80,16},{96,32},{112,48},{1... | collective-permute-start | bytes 393224 | tf_op jit(solution)/shard_map/ppermute | solution.py:12
  46.8 1.1 collective-permute-start.14
  47.9 1.0 collective-permute-start.13
  48.8 2.2 %collective-permute-done.15 = f32[8,32,128]{2,1,0:T(8,128)S(1)} collective-permute-done((f32[8,32,128]{2,1,0:T(8,128)S(1)}, f32[8,32,128]{2,1,0:T(8,128)S(1)}, u32[]{:S(2)}, u32[]{:S(2)}) %collective-permute-start.15) | collective-permute-done | bytes 131104 | tf_op jit(solution)/shard_map/ppermute | solution.py:12
  51.0 1.9 %collective-permute-done.14 = f32[8,32,128]{2,1,0:T(8,128)S(1)} collective-permute-done((f32[8,32,128]{2,1,0:T(8,128)S(1)}, f32[8,32,128]{2,1,0:T(8,128)S(1)}, u32[]{:S(2)}, u32[]{:S(2)}) %collective-permute-start.14) | collective-permute-done | bytes 131104 | tf_op jit(solution)/shard_map/ppermute | solution.py:12
  53.0 1.1 collective-permute-done.13
  54.2 1.3 collective-permute-done.16
  56.9 3.6 %collective-permute-start.19 = (f32[32,512]{1,0:T(8,128)S(1)}, f32[32,512]{1,0:T(8,128)S(1)}, u32[]{:S(2)}, u32[]{:S(2)}) collective-permute-start(f32[32,512]{1,0:T(8,128)S(1)} %pad_maximum_fusion.12), channel_id=1, source_target_pairs={{0,8},{1,9},{2,10},{3,11},{4,12},{5,13},{6,14},{7,15},{8,0},{9,1},... | collective-permute-start | bytes 196616 | tf_op jit(solution)/shard_map/ppermute | solution.py:12
  60.4 2.8 %collective-permute-start.18 = (f32[32,512]{1,0:T(8,128)S(1)}, f32[32,512]{1,0:T(8,128)S(1)}, u32[]{:S(2)}, u32[]{:S(2)}) collective-permute-start(f32[32,512]{1,0:T(8,128)S(1)} %pad_maximum_fusion.12), channel_id=1, source_target_pairs={{0,12},{1,13},{2,14},{3,15},{4,0},{5,1},{6,2},{7,3},{8,4},{9,5},{1... | collective-permute-start | bytes 196616 | tf_op jit(solution)/shard_map/ppermute | solution.py:12
  63.4 1.7 %collective-permute-done.19 = f32[32,512]{1,0:T(8,128)S(1)} collective-permute-done((f32[32,512]{1,0:T(8,128)S(1)}, f32[32,512]{1,0:T(8,128)S(1)}, u32[]{:S(2)}, u32[]{:S(2)}) %collective-permute-start.19) | collective-permute-done | bytes 65568 | tf_op jit(solution)/shard_map/ppermute | solution.py:12
  65.1 3.3 %collective-permute-done.18 = f32[32,512]{1,0:T(8,128)S(1)} collective-permute-done((f32[32,512]{1,0:T(8,128)S(1)}, f32[32,512]{1,0:T(8,128)S(1)}, u32[]{:S(2)}, u32[]{:S(2)}) %collective-permute-start.18) | collective-permute-done | bytes 65568 | tf_op jit(solution)/shard_map/ppermute | solution.py:12
  68.4 1.8 %collective-permute-done.17 = f32[32,512]{1,0:T(8,128)S(1)} collective-permute-done((f32[32,512]{1,0:T(8,128)S(1)}, f32[32,512]{1,0:T(8,128)S(1)}, u32[]{:S(2)}, u32[]{:S(2)}) %collective-permute-start.17) | collective-permute-done | bytes 65568 | tf_op jit(solution)/shard_map/ppermute | solution.py:12
  71.6 1.3 collective-permute-done.20
  73.4 5.5 %collective-permute-done.21 = f32[9,32,128]{2,1,0:T(8,128)S(1)} collective-permute-done((f32[9,32,128]{2,1,0:T(8,128)S(1)}, f32[9,32,128]{2,1,0:T(8,128)S(1)}, u32[]{:S(2)}, u32[]{:S(2)}) %collective-permute-start.21) | collective-permute-done | bytes 147488 | tf_op jit(solution)/shard_map/ppermute | solution.py:12
  78.9 1.9 %collective-permute-start.24 = (f32[9,32,128]{2,1,0:T(8,128)S(1)}, f32[9,32,128]{2,1,0:T(8,128)S(1)}, u32[]{:S(2)}, u32[]{:S(2)}) collective-permute-start(f32[9,32,128]{2,1,0:T(8,128)S(1)} %add.309), channel_id=1, source_target_pairs={{0,64},{16,80},{32,96},{48,112},{64,0},{80,16},{96,32},{112,48},{1... | collective-permute-start | bytes 442376 | tf_op jit(solution)/shard_map/ppermute | solution.py:12
  80.8 1.2 collective-permute-start.23
  82.0 0.8 collective-permute-start.22
  82.8 4.4 %collective-permute-done.24 = f32[9,32,128]{2,1,0:T(8,128)S(1)} collective-permute-done((f32[9,32,128]{2,1,0:T(8,128)S(1)}, f32[9,32,128]{2,1,0:T(8,128)S(1)}, u32[]{:S(2)}, u32[]{:S(2)}) %collective-permute-start.24) | collective-permute-done | bytes 147488 | tf_op jit(solution)/shard_map/ppermute | solution.py:12
  87.7 1.4 %collective-permute-done.22 = f32[9,32,128]{2,1,0:T(8,128)S(1)} collective-permute-done((f32[9,32,128]{2,1,0:T(8,128)S(1)}, f32[9,32,128]{2,1,0:T(8,128)S(1)}, u32[]{:S(2)}, u32[]{:S(2)}) %collective-permute-start.22) | collective-permute-done | bytes 147488 | tf_op jit(solution)/shard_map/ppermute | solution.py:12
  89.4 1.3 collective-permute-done.25
  92.1 1.4 %collective-permute-start.28 = (f32[32,512]{1,0:T(8,128)S(1)}, f32[32,512]{1,0:T(8,128)S(1)}, u32[]{:S(2)}, u32[]{:S(2)}) collective-permute-start(f32[32,512]{1,0:T(8,128)S(1)} %pad_maximum_fusion.13), channel_id=1, source_target_pairs={{0,8},{1,9},{2,10},{3,11},{4,12},{5,13},{6,14},{7,15},{8,0},{9,1},... | collective-permute-start | bytes 196616 | tf_op jit(solution)/shard_map/ppermute | solution.py:12
  93.5 2.4 %collective-permute-start.27 = (f32[32,512]{1,0:T(8,128)S(1)}, f32[32,512]{1,0:T(8,128)S(1)}, u32[]{:S(2)}, u32[]{:S(2)}) collective-permute-start(f32[32,512]{1,0:T(8,128)S(1)} %pad_maximum_fusion.13), channel_id=1, source_target_pairs={{0,12},{1,13},{2,14},{3,15},{4,0},{5,1},{6,2},{7,3},{8,4},{9,5},{1... | collective-permute-start | bytes 196616 | tf_op jit(solution)/shard_map/ppermute | solution.py:12
  96.5 4.8 %collective-permute-done.28 = f32[32,512]{1,0:T(8,128)S(1)} collective-permute-done((f32[32,512]{1,0:T(8,128)S(1)}, f32[32,512]{1,0:T(8,128)S(1)}, u32[]{:S(2)}, u32[]{:S(2)}) %collective-permute-start.28) | collective-permute-done | bytes 65568 | tf_op jit(solution)/shard_map/ppermute | solution.py:12
  101.3 1.9 %collective-permute-done.26 = f32[32,512]{1,0:T(8,128)S(1)} collective-permute-done((f32[32,512]{1,0:T(8,128)S(1)}, f32[32,512]{1,0:T(8,128)S(1)}, u32[]{:S(2)}, u32[]{:S(2)}) %collective-permute-start.26) | collective-permute-done | bytes 65568 | tf_op jit(solution)/shard_map/ppermute | solution.py:12
  105.0 1.5 %collective-permute-done.29 = f32[17,32,128]{2,1,0:T(8,128)S(1)} collective-permute-done((f32[17,32,128]{2,1,0:T(8,128)S(1)}, f32[17,32,128]{2,1,0:T(8,128)S(1)}, u32[]{:S(2)}, u32[]{:S(2)}) %collective-permute-start.29) | collective-permute-done | bytes 278560 | tf_op jit(solution)/shard_map/ppermute | solution.py:12
  106.6 2.1 %collective-permute-start.30 = (f32[9,32,128]{2,1,0:T(8,128)S(1)}, f32[9,32,128]{2,1,0:T(8,128)S(1)}, u32[]{:S(2)}, u32[]{:S(2)}) collective-permute-start(f32[9,32,128]{2,1,0:T(8,128)S(1)} %pad_maximum_fusion.6), channel_id=1, source_target_pairs={{0,128},{16,144},{32,160},{48,176},{64,192},{80,208},{96,224},{112... | collective-permute-start | bytes 442376 | tf_op jit(solution)/shard_map/ppermute | solution.py:12
  108.8 4.1 %collective-permute-done.30 = f32[9,32,128]{2,1,0:T(8,128)S(1)} collective-permute-done((f32[9,32,128]{2,1,0:T(8,128)S(1)}, f32[9,32,128]{2,1,0:T(8,128)S(1)}, u32[]{:S(2)}, u32[]{:S(2)}) %collective-permute-start.30) | collective-permute-done | bytes 147488 | tf_op jit(solution)/shard_map/ppermute | solution.py:12
  113.1 3.2 %collective-permute-start.32 = (f32[5,32,128]{2,1,0:T(8,128)S(1)}, f32[5,32,128]{2,1,0:T(8,128)S(1)}, u32[]{:S(2)}, u32[]{:S(2)}) collective-permute-start(f32[5,32,128]{2,1,0:T(8,128)S(1)} %get-tuple-element.48), channel_id=1, source_target_pairs={{0,96},{16,112},{32,0},{48,16},{64,32},{80,48},{96,64},{112,80},{1... | collective-permute-start | bytes 245768 | tf_op jit(solution)/shard_map/ppermute | solution.py:12
  116.6 2.1 %collective-permute-done.31 = f32[5,32,128]{2,1,0:T(8,128)S(1)} collective-permute-done((f32[5,32,128]{2,1,0:T(8,128)S(1)}, f32[5,32,128]{2,1,0:T(8,128)S(1)}, u32[]{:S(2)}, u32[]{:S(2)}) %collective-permute-start.31) | collective-permute-done | bytes 81952 | tf_op jit(solution)/shard_map/ppermute | solution.py:12
  119.3 3.0 %collective-permute-done.33 = f32[5,32,128]{2,1,0:T(8,128)S(1)} collective-permute-done((f32[5,32,128]{2,1,0:T(8,128)S(1)}, f32[5,32,128]{2,1,0:T(8,128)S(1)}, u32[]{:S(2)}, u32[]{:S(2)}) %collective-permute-start.33) | collective-permute-done | bytes 81952 | tf_op jit(solution)/shard_map/ppermute | solution.py:12
  123.2 2.8 %collective-permute-start.36 = (f32[64,32]{1,0:T(8,128)S(1)}, f32[64,32]{1,0:T(8,128)S(1)}, u32[]{:S(2)}, u32[]{:S(2)}) collective-permute-start(f32[64,32]{1,0:T(8,128)S(1)} %get-tuple-element.30), channel_id=1, source_target_pairs={{0,1},{1,2},{2,3},{3,0},{4,5},{5,6},{6,7},{7,4},{8,9},{9,10},{10,1... | collective-permute-start | bytes 24584 | tf_op jit(solution)/shard_map/ppermute | solution.py:12
  126.0 2.2 %collective-permute-done.34 = f32[64,32]{1,0:T(8,128)S(1)} collective-permute-done((f32[64,32]{1,0:T(8,128)S(1)}, f32[64,32]{1,0:T(8,128)S(1)}, u32[]{:S(2)}, u32[]{:S(2)}) %collective-permute-start.34) | collective-permute-done | bytes 8224 | tf_op jit(solution)/shard_map/ppermute | solution.py:12
  128.1 3.3 %collective-permute-done.35 = f32[64,32]{1,0:T(8,128)S(1)} collective-permute-done((f32[64,32]{1,0:T(8,128)S(1)}, f32[64,32]{1,0:T(8,128)S(1)}, u32[]{:S(2)}, u32[]{:S(2)}) %collective-permute-start.35) | collective-permute-done | bytes 8224 | tf_op jit(solution)/shard_map/ppermute | solution.py:12
  (128 shorter events, 13.9 us)
Async XLA Ops:
  0.6 22.7 %collective-permute-start.8 = (bf16[384,512]{1,0:T(8,128)(2,1)}, bf16[384,512]{1,0:T(8,128)(2,1)S(1)}, u32[]{:S(2)}, u32[]{:S(2)}) collective-permute-start(bf16[384,512]{1,0:T(8,128)(2,1)} %bitcast.164), channel_id=1, source_target_pairs={{0,3},{1,0},{2,1},{3,2},{4,7},{5,4},{6,5},{7,6},{8,11},{9,8},{10,9... | collective-permute-start | bytes 1179656 | tf_op jit(solution)/shard_map/ppermute | solution.py:12
  1.5 24.8 %collective-permute-start.6 = (bf16[384,512]{1,0:T(8,128)(2,1)}, bf16[384,512]{1,0:T(8,128)(2,1)S(1)}, u32[]{:S(2)}, u32[]{:S(2)}) collective-permute-start(bf16[384,512]{1,0:T(8,128)(2,1)} %bitcast.165), channel_id=1, source_target_pairs={{0,1},{1,2},{2,3},{3,0},{4,5},{5,6},{6,7},{7,4},{8,9},{9,10},{10,1... | collective-permute-start | bytes 1179656 | tf_op jit(solution)/shard_map/ppermute | solution.py:12
  6.3 8.1 %collective-permute-start = (f32[32,384]{1,0:T(8,128)S(1)}, f32[32,384]{1,0:T(8,128)S(1)}, u32[]{:S(2)}, u32[]{:S(2)}) collective-permute-start(f32[32,384]{1,0:T(8,128)S(1)} %get-tuple-element.27), channel_id=1, source_target_pairs={{0,1},{1,2},{2,3},{3,0},{4,5},{5,6},{6,7},{7,4},{8,9},{9,10},{10,1... | collective-permute-start | bytes 147464 | tf_op jit(solution)/shard_map/ppermute | solution.py:12
  7.3 8.7 %collective-permute-start.2 = (f32[32,384]{1,0:T(8,128)S(1)}, f32[32,384]{1,0:T(8,128)S(1)}, u32[]{:S(2)}, u32[]{:S(2)}) collective-permute-start(f32[32,384]{1,0:T(8,128)S(1)} %get-tuple-element.28), channel_id=1, source_target_pairs={{0,2},{1,3},{2,0},{3,1},{4,6},{5,7},{6,4},{7,5},{8,10},{9,11},{10,... | collective-permute-start | bytes 147464 | tf_op jit(solution)/shard_map/ppermute | solution.py:12
  8.1 8.0 %collective-permute-start.1 = (f32[32,384]{1,0:T(8,128)S(1)}, f32[32,384]{1,0:T(8,128)S(1)}, u32[]{:S(2)}, u32[]{:S(2)}) collective-permute-start(f32[32,384]{1,0:T(8,128)S(1)} %get-tuple-element.29), channel_id=1, source_target_pairs={{0,3},{1,0},{2,1},{3,2},{4,7},{5,4},{6,5},{7,6},{8,11},{9,8},{10,9... | collective-permute-start | bytes 147464 | tf_op jit(solution)/shard_map/ppermute | solution.py:12
  8.4 27.0 %copy-start = (bf16[1,384,512]{2,1,0:T(8,128)(2,1)S(1)}, bf16[1,384,512]{2,1,0:T(8,128)(2,1)}, u32[]{:S(2)}) copy-start(bf16[1,384,512]{2,1,0:T(8,128)(2,1)} %param.2) | copy-start | bytes 1179652
  14.4 21.9 %collective-permute-start.10 = (bf16[32,512]{1,0:T(8,128)(2,1)S(1)}, bf16[32,512]{1,0:T(8,128)(2,1)S(1)}, u32[]{:S(2)}, u32[]{:S(2)}) collective-permute-start(bf16[32,512]{1,0:T(8,128)(2,1)S(1)} %get-tuple-element.39), channel_id=1, source_target_pairs={{0,2},{1,3},{2,0},{3,1},{4,6},{5,7},{6,4},{7,5},{8,10},{9,11},{10,... | collective-permute-start | bytes 98312 | tf_op jit(solution)/shard_map/ppermute | solution.py:12
  16.1 13.2 %collective-permute-start.5 = (f32[32,384]{1,0:T(8,128)S(1)}, f32[32,384]{1,0:T(8,128)S(1)}, u32[]{:S(2)}, u32[]{:S(2)}) collective-permute-start(f32[32,384]{1,0:T(8,128)S(1)} %fusion.50), channel_id=1, source_target_pairs={{0,8},{1,9},{2,10},{3,11},{4,12},{5,13},{6,14},{7,15},{8,0},{9,1},... | collective-permute-start | bytes 147464 | tf_op jit(solution)/shard_map/ppermute | solution.py:12
  23.4 6.4 %collective-permute-start.4 = (f32[32,384]{1,0:T(8,128)S(1)}, f32[32,384]{1,0:T(8,128)S(1)}, u32[]{:S(2)}, u32[]{:S(2)}) collective-permute-start(f32[32,384]{1,0:T(8,128)S(1)} %fusion.50), channel_id=1, source_target_pairs={{0,12},{1,13},{2,14},{3,15},{4,0},{5,1},{6,2},{7,3},{8,4},{9,5},{1... | collective-permute-start | bytes 147464 | tf_op jit(solution)/shard_map/ppermute | solution.py:12
  23.4 6.4 %collective-permute-start.3 = (f32[32,384]{1,0:T(8,128)S(1)}, f32[32,384]{1,0:T(8,128)S(1)}, u32[]{:S(2)}, u32[]{:S(2)}) collective-permute-start(f32[32,384]{1,0:T(8,128)S(1)} %fusion.50), channel_id=1, source_target_pairs={{0,4},{1,5},{2,6},{3,7},{4,8},{5,9},{6,10},{7,11},{8,12},{9,13},{1... | collective-permute-start | bytes 147464 | tf_op jit(solution)/shard_map/ppermute | solution.py:12
  26.3 7.3 %collective-permute-start.9 = (bf16[224,512]{1,0:T(8,128)(2,1)S(1)}, bf16[224,512]{1,0:T(8,128)(2,1)S(1)}, u32[]{:S(2)}, u32[]{:S(2)}) collective-permute-start(bf16[224,512]{1,0:T(8,128)(2,1)S(1)} %pad_maximum_fusion.3), channel_id=1, source_target_pairs={{0,3},{1,0},{2,1},{3,2},{4,7},{5,4},{6,5},{7,6},{8,11},{9,8},{10,9... | collective-permute-start | bytes 688136 | tf_op jit(solution)/shard_map/ppermute | solution.py:12
  29.3 6.1 %collective-permute-start.7 = (bf16[224,512]{1,0:T(8,128)(2,1)S(1)}, bf16[224,512]{1,0:T(8,128)(2,1)S(1)}, u32[]{:S(2)}, u32[]{:S(2)}) collective-permute-start(bf16[224,512]{1,0:T(8,128)(2,1)S(1)} %pad_maximum_fusion.2), channel_id=1, source_target_pairs={{0,1},{1,2},{2,3},{3,0},{4,5},{5,6},{6,7},{7,4},{8,9},{9,10},{10,1... | collective-permute-start | bytes 688136 | tf_op jit(solution)/shard_map/ppermute | solution.py:12
  36.4 1.4 %collective-permute-start.11 = (f32[8,32,128]{2,1,0:T(8,128)S(1)}, f32[8,32,128]{2,1,0:T(8,128)S(1)}, u32[]{:S(2)}, u32[]{:S(2)}) collective-permute-start(f32[8,32,128]{2,1,0:T(8,128)S(1)} %bitcast.185), channel_id=1, source_target_pairs={{0,16},{16,0},{32,48},{48,32},{64,80},{80,64},{96,112},{112,96},{1... | collective-permute-start | bytes 393224 | tf_op jit(solution)/shard_map/ppermute | solution.py:12
  37.9 5.6 %collective-permute-start.12 = (f32[8,32,128]{2,1,0:T(8,128)S(1)}, f32[8,32,128]{2,1,0:T(8,128)S(1)}, u32[]{:S(2)}, u32[]{:S(2)}) collective-permute-start(f32[8,32,128]{2,1,0:T(8,128)S(1)} %bitcast_add_fusion.1), channel_id=1, source_target_pairs={{0,128},{16,144},{32,160},{48,176},{64,192},{80,208},{96,224},{112... | collective-permute-start | bytes 393224 | tf_op jit(solution)/shard_map/ppermute | solution.py:12
  43.5 7.5 %collective-permute-start.15 = (f32[8,32,128]{2,1,0:T(8,128)S(1)}, f32[8,32,128]{2,1,0:T(8,128)S(1)}, u32[]{:S(2)}, u32[]{:S(2)}) collective-permute-start(f32[8,32,128]{2,1,0:T(8,128)S(1)} %add.297), channel_id=1, source_target_pairs={{0,64},{16,80},{32,96},{48,112},{64,0},{80,16},{96,32},{112,48},{1... | collective-permute-start | bytes 393224 | tf_op jit(solution)/shard_map/ppermute | solution.py:12
  46.8 6.2 %collective-permute-start.14 = (f32[8,32,128]{2,1,0:T(8,128)S(1)}, f32[8,32,128]{2,1,0:T(8,128)S(1)}, u32[]{:S(2)}, u32[]{:S(2)}) collective-permute-start(f32[8,32,128]{2,1,0:T(8,128)S(1)} %add.297), channel_id=1, source_target_pairs={{0,96},{16,112},{32,0},{48,16},{64,32},{80,48},{96,64},{112,80},{1... | collective-permute-start | bytes 393224 | tf_op jit(solution)/shard_map/ppermute | solution.py:12
  47.9 6.2 %collective-permute-start.13 = (f32[8,32,128]{2,1,0:T(8,128)S(1)}, f32[8,32,128]{2,1,0:T(8,128)S(1)}, u32[]{:S(2)}, u32[]{:S(2)}) collective-permute-start(f32[8,32,128]{2,1,0:T(8,128)S(1)} %add.297), channel_id=1, source_target_pairs={{0,32},{16,48},{32,64},{48,80},{64,96},{80,112},{96,0},{112,16},{1... | collective-permute-start | bytes 393224 | tf_op jit(solution)/shard_map/ppermute | solution.py:12
  54.1 1.4 %collective-permute-start.16 = (f32[8,32,128]{2,1,0:T(8,128)S(1)}, f32[8,32,128]{2,1,0:T(8,128)S(1)}, u32[]{:S(2)}, u32[]{:S(2)}) collective-permute-start(f32[8,32,128]{2,1,0:T(8,128)S(1)} %add_add_fusion.1), channel_id=1, source_target_pairs={{0,16},{16,0},{32,48},{48,32},{64,80},{80,64},{96,112},{112,96},{1... | collective-permute-start | bytes 393224 | tf_op jit(solution)/shard_map/ppermute | solution.py:12
  56.9 8.3 %collective-permute-start.19 = (f32[32,512]{1,0:T(8,128)S(1)}, f32[32,512]{1,0:T(8,128)S(1)}, u32[]{:S(2)}, u32[]{:S(2)}) collective-permute-start(f32[32,512]{1,0:T(8,128)S(1)} %pad_maximum_fusion.12), channel_id=1, source_target_pairs={{0,8},{1,9},{2,10},{3,11},{4,12},{5,13},{6,14},{7,15},{8,0},{9,1},... | collective-permute-start | bytes 196616 | tf_op jit(solution)/shard_map/ppermute | solution.py:12
  60.4 7.9 %collective-permute-start.18 = (f32[32,512]{1,0:T(8,128)S(1)}, f32[32,512]{1,0:T(8,128)S(1)}, u32[]{:S(2)}, u32[]{:S(2)}) collective-permute-start(f32[32,512]{1,0:T(8,128)S(1)} %pad_maximum_fusion.12), channel_id=1, source_target_pairs={{0,12},{1,13},{2,14},{3,15},{4,0},{5,1},{6,2},{7,3},{8,4},{9,5},{1... | collective-permute-start | bytes 196616 | tf_op jit(solution)/shard_map/ppermute | solution.py:12
  63.2 7.0 %collective-permute-start.17 = (f32[32,512]{1,0:T(8,128)S(1)}, f32[32,512]{1,0:T(8,128)S(1)}, u32[]{:S(2)}, u32[]{:S(2)}) collective-permute-start(f32[32,512]{1,0:T(8,128)S(1)} %pad_maximum_fusion.12), channel_id=1, source_target_pairs={{0,4},{1,5},{2,6},{3,7},{4,8},{5,9},{6,10},{7,11},{8,12},{9,13},{1... | collective-permute-start | bytes 196616 | tf_op jit(solution)/shard_map/ppermute | solution.py:12
  71.4 1.5 %collective-permute-start.20 = (f32[9,32,128]{2,1,0:T(8,128)S(1)}, f32[9,32,128]{2,1,0:T(8,128)S(1)}, u32[]{:S(2)}, u32[]{:S(2)}) collective-permute-start(f32[9,32,128]{2,1,0:T(8,128)S(1)} %pad_maximum_fusion.4), channel_id=1, source_target_pairs={{0,16},{16,0},{32,48},{48,32},{64,80},{80,64},{96,112},{112,96},{1... | collective-permute-start | bytes 442376 | tf_op jit(solution)/shard_map/ppermute | solution.py:12
  72.9 6.0 %collective-permute-start.21 = (f32[9,32,128]{2,1,0:T(8,128)S(1)}, f32[9,32,128]{2,1,0:T(8,128)S(1)}, u32[]{:S(2)}, u32[]{:S(2)}) collective-permute-start(f32[9,32,128]{2,1,0:T(8,128)S(1)} %fusion.26), channel_id=1, source_target_pairs={{0,128},{16,144},{32,160},{48,176},{64,192},{80,208},{96,224},{112... | collective-permute-start | bytes 442376 | tf_op jit(solution)/shard_map/ppermute | solution.py:12
  78.9 8.3 %collective-permute-start.24 = (f32[9,32,128]{2,1,0:T(8,128)S(1)}, f32[9,32,128]{2,1,0:T(8,128)S(1)}, u32[]{:S(2)}, u32[]{:S(2)}) collective-permute-start(f32[9,32,128]{2,1,0:T(8,128)S(1)} %add.309), channel_id=1, source_target_pairs={{0,64},{16,80},{32,96},{48,112},{64,0},{80,16},{96,32},{112,48},{1... | collective-permute-start | bytes 442376 | tf_op jit(solution)/shard_map/ppermute | solution.py:12
  80.8 6.9 %collective-permute-start.23 = (f32[9,32,128]{2,1,0:T(8,128)S(1)}, f32[9,32,128]{2,1,0:T(8,128)S(1)}, u32[]{:S(2)}, u32[]{:S(2)}) collective-permute-start(f32[9,32,128]{2,1,0:T(8,128)S(1)} %add.309), channel_id=1, source_target_pairs={{0,96},{16,112},{32,0},{48,16},{64,32},{80,48},{96,64},{112,80},{1... | collective-permute-start | bytes 442376 | tf_op jit(solution)/shard_map/ppermute | solution.py:12
  82.0 7.0 %collective-permute-start.22 = (f32[9,32,128]{2,1,0:T(8,128)S(1)}, f32[9,32,128]{2,1,0:T(8,128)S(1)}, u32[]{:S(2)}, u32[]{:S(2)}) collective-permute-start(f32[9,32,128]{2,1,0:T(8,128)S(1)} %add.309), channel_id=1, source_target_pairs={{0,32},{16,48},{32,64},{48,80},{64,96},{80,112},{96,0},{112,16},{1... | collective-permute-start | bytes 442376 | tf_op jit(solution)/shard_map/ppermute | solution.py:12
  89.3 1.4 %collective-permute-start.25 = (f32[8,32,128]{2,1,0:T(8,128)S(1)}, f32[8,32,128]{2,1,0:T(8,128)S(1)}, u32[]{:S(2)}, u32[]{:S(2)}) collective-permute-start(f32[8,32,128]{2,1,0:T(8,128)S(1)} %fusion.27), channel_id=1, source_target_pairs={{0,16},{16,0},{32,48},{48,32},{64,80},{80,64},{96,112},{112,96},{1... | collective-permute-start | bytes 393224 | tf_op jit(solution)/shard_map/ppermute | solution.py:12
  92.1 9.1 %collective-permute-start.28 = (f32[32,512]{1,0:T(8,128)S(1)}, f32[32,512]{1,0:T(8,128)S(1)}, u32[]{:S(2)}, u32[]{:S(2)}) collective-permute-start(f32[32,512]{1,0:T(8,128)S(1)} %pad_maximum_fusion.13), channel_id=1, source_target_pairs={{0,8},{1,9},{2,10},{3,11},{4,12},{5,13},{6,14},{7,15},{8,0},{9,1},... | collective-permute-start | bytes 196616 | tf_op jit(solution)/shard_map/ppermute | solution.py:12
  93.5 7.8 %collective-permute-start.27 = (f32[32,512]{1,0:T(8,128)S(1)}, f32[32,512]{1,0:T(8,128)S(1)}, u32[]{:S(2)}, u32[]{:S(2)}) collective-permute-start(f32[32,512]{1,0:T(8,128)S(1)} %pad_maximum_fusion.13), channel_id=1, source_target_pairs={{0,12},{1,13},{2,14},{3,15},{4,0},{5,1},{6,2},{7,3},{8,4},{9,5},{1... | collective-permute-start | bytes 196616 | tf_op jit(solution)/shard_map/ppermute | solution.py:12
  95.9 7.3 %collective-permute-start.26 = (f32[32,512]{1,0:T(8,128)S(1)}, f32[32,512]{1,0:T(8,128)S(1)}, u32[]{:S(2)}, u32[]{:S(2)}) collective-permute-start(f32[32,512]{1,0:T(8,128)S(1)} %pad_maximum_fusion.13), channel_id=1, source_target_pairs={{0,4},{1,5},{2,6},{3,7},{4,8},{5,9},{6,10},{7,11},{8,12},{9,13},{1... | collective-permute-start | bytes 196616 | tf_op jit(solution)/shard_map/ppermute | solution.py:12
  104.6 1.9 %collective-permute-start.29 = (f32[17,32,128]{2,1,0:T(8,128)S(1)}, f32[17,32,128]{2,1,0:T(8,128)S(1)}, u32[]{:S(2)}, u32[]{:S(2)}) collective-permute-start(f32[17,32,128]{2,1,0:T(8,128)S(1)} %pad_maximum_fusion.1), channel_id=1, source_target_pairs={{0,16},{16,0},{32,48},{48,32},{64,80},{80,64},{96,112},{112,96},{1... | collective-permute-start | bytes 835592 | tf_op jit(solution)/shard_map/ppermute | solution.py:12
  106.6 6.3 %collective-permute-start.30 = (f32[9,32,128]{2,1,0:T(8,128)S(1)}, f32[9,32,128]{2,1,0:T(8,128)S(1)}, u32[]{:S(2)}, u32[]{:S(2)}) collective-permute-start(f32[9,32,128]{2,1,0:T(8,128)S(1)} %pad_maximum_fusion.6), channel_id=1, source_target_pairs={{0,128},{16,144},{32,160},{48,176},{64,192},{80,208},{96,224},{112... | collective-permute-start | bytes 442376 | tf_op jit(solution)/shard_map/ppermute | solution.py:12
  113.0 5.7 %collective-permute-start.31 = (f32[5,32,128]{2,1,0:T(8,128)S(1)}, f32[5,32,128]{2,1,0:T(8,128)S(1)}, u32[]{:S(2)}, u32[]{:S(2)}) collective-permute-start(f32[5,32,128]{2,1,0:T(8,128)S(1)} %get-tuple-element.47), channel_id=1, source_target_pairs={{0,32},{16,48},{32,64},{48,80},{64,96},{80,112},{96,0},{112,16},{1... | collective-permute-start | bytes 245768 | tf_op jit(solution)/shard_map/ppermute | solution.py:12
  113.1 6.2 %collective-permute-start.32 = (f32[5,32,128]{2,1,0:T(8,128)S(1)}, f32[5,32,128]{2,1,0:T(8,128)S(1)}, u32[]{:S(2)}, u32[]{:S(2)}) collective-permute-start(f32[5,32,128]{2,1,0:T(8,128)S(1)} %get-tuple-element.48), channel_id=1, source_target_pairs={{0,96},{16,112},{32,0},{48,16},{64,32},{80,48},{96,64},{112,80},{1... | collective-permute-start | bytes 245768 | tf_op jit(solution)/shard_map/ppermute | solution.py:12
  116.3 5.9 %collective-permute-start.33 = (f32[5,32,128]{2,1,0:T(8,128)S(1)}, f32[5,32,128]{2,1,0:T(8,128)S(1)}, u32[]{:S(2)}, u32[]{:S(2)}) collective-permute-start(f32[5,32,128]{2,1,0:T(8,128)S(1)} %get-tuple-element.49), channel_id=1, source_target_pairs={{0,64},{16,80},{32,96},{48,112},{64,0},{80,16},{96,32},{112,48},{1... | collective-permute-start | bytes 245768 | tf_op jit(solution)/shard_map/ppermute | solution.py:12
  122.7 5.5 %collective-permute-start.34 = (f32[64,32]{1,0:T(8,128)S(1)}, f32[64,32]{1,0:T(8,128)S(1)}, u32[]{:S(2)}, u32[]{:S(2)}) collective-permute-start(f32[64,32]{1,0:T(8,128)S(1)} %get-tuple-element.33), channel_id=1, source_target_pairs={{0,3},{1,0},{2,1},{3,2},{4,7},{5,4},{6,5},{7,6},{8,11},{9,8},{10,9... | collective-permute-start | bytes 24584 | tf_op jit(solution)/shard_map/ppermute | solution.py:12
  123.2 8.2 %collective-permute-start.36 = (f32[64,32]{1,0:T(8,128)S(1)}, f32[64,32]{1,0:T(8,128)S(1)}, u32[]{:S(2)}, u32[]{:S(2)}) collective-permute-start(f32[64,32]{1,0:T(8,128)S(1)} %get-tuple-element.30), channel_id=1, source_target_pairs={{0,1},{1,2},{2,3},{3,0},{4,5},{5,6},{6,7},{7,4},{8,9},{9,10},{10,1... | collective-permute-start | bytes 24584 | tf_op jit(solution)/shard_map/ppermute | solution.py:12
  126.0 5.4 %collective-permute-start.35 = (f32[64,32]{1,0:T(8,128)S(1)}, f32[64,32]{1,0:T(8,128)S(1)}, u32[]{:S(2)}, u32[]{:S(2)}) collective-permute-start(f32[64,32]{1,0:T(8,128)S(1)} %get-tuple-element.32), channel_id=1, source_target_pairs={{0,2},{1,3},{2,0},{3,1},{4,6},{5,7},{6,4},{7,5},{8,10},{9,11},{10,... | collective-permute-start | bytes 24584 | tf_op jit(solution)/shard_map/ppermute | solution.py:12

commit v4 on v3

--- a/solution.py
+++ b/solution.py
@@ -12,12 +12,19 @@
     return lax.ppermute(value, axis, [(i, to(i)) for i in range(16)])
 
 
+def staged(value_of, move):
+    arrived = []
+    for k in (2, 3, 1):
+        arrived.append(move(value_of(k), k))
+    return arrived
+
+
 def x_move(value, k):
     return moved(value, "rows", lambda r: r - r % 4 + (r + k) % 4)
 
 
-def zhi_sum(value):
-    return value + sum(moved(value, "rows", lambda r, k=k: (r + 4 * k) % 16) for k in (1, 3, 2))
+def zhi_move(value, k):
+    return moved(value, "rows", lambda r: (r + 4 * k) % 16)
 
 
 def core_move(value):
@@ -30,6 +37,11 @@
 
 def y_move(value, k):
     return moved(value, "task", lambda t: (t & 9) | ((((t >> 1) & 3) + k) % 4) << 1)
+
+
+def sum_over(value, move):
+    two, three, one = staged(lambda k: value, move)
+    return value + one + three + two
 
 
 def pick(value, index, dim=0):
@@ -76,7 +88,7 @@
         own, other = jnp.concatenate([own, extra[None]]), jnp.concatenate([other, extra[None]])
     own = own + core_move(other)
     own = own + zlo_move(own)
-    return own + y_move(own, 1) + y_move(own, 3) + y_move(own, 2)
+    return sum_over(own, y_move)
 
 
 def with_scalars(value, scalars):
@@ -102,22 +114,19 @@
     scale = 1.0 / (tokens * tasks)
     gram_scale, diag_scale = ALPHA * scale, (1.0 - ALPHA) * scale
 
+    first = lax.dot_general(w, own_x, (((0,), (1,)), ((), ())), preferred_element_type=jnp.float32)
+    first = first.reshape(4, 32, tokens)
+    two, three, one = staged(lambda k: pick(first, (x + k) % 4), x_move)
+    mine = pick(first, x) + one + three + two
+    turned = w.T.reshape(4, 32, width)
+    ws_far = x_move(pick(turned, (x + 2) % 4), 2)
+
     half = tokens // 2
     from_left = x_move(own_x, 1)
     from_right = x_move(own_x, 3)
-
-    first = lax.dot_general(w, own_x, (((0,), (1,)), ((), ())), preferred_element_type=jnp.float32)
-    first = first.reshape(4, 32, tokens)
-    mine = pick(first, x)
-    for k in (1, 3, 2):
-        mine = mine + x_move(pick(first, (x + k) % 4), k)
-    turned = w.T.reshape(4, 32, width)
-    ws_far = x_move(pick(turned, (x + 2) % 4), 2)
+    outputs = sum_over(mine, zhi_move)
     far_left = x_move(jnp.concatenate([from_left[:half], pick(turned, (x + 1) % 4)]), 1)
     far_right = x_move(jnp.concatenate([from_right[half:], pick(turned, (x + 3) % 4)]), 3)
-    outputs = mine
-    for k in (1, 3, 2):
-        outputs = outputs + moved(mine, "rows", lambda r, k=k: (r + 4 * k) % 16)
 
     far = jnp.concatenate([far_left[:half], far_right[:half]])
     xs = jnp.concatenate([own_x, from_left, far, from_right], axis=1)
@@ -133,7 +142,7 @@
     target = flat(target_blocks)
 
     scalars = [total(target * target), total(diag * target * target)]
-    rows = zhi_sum(with_scalars(product(target, xs, 1), scalars))
+    rows = sum_over(with_scalars(product(target, xs, 1), scalars), zhi_move)
     image0, norm0, weigh0 = rows[:, :tokens], rows[:, tokens : tokens + 1], rows[:, tokens + 1 : tokens + 2]
     curve = jnp.broadcast_to(gram_scale * total(image0 * image0) + weigh0, (32, 128))
     part = task_half_sum(image_part(image0, target), curve, core)
@@ -143,7 +152,7 @@
     residual = flat(residual_blocks)
 
     scalars = [total(residual * residual), total(diag * residual * residual), total(diag * residual * target)]
-    rows = zhi_sum(with_scalars(product(residual, xs, 1), scalars))
+    rows = sum_over(with_scalars(product(residual, xs, 1), scalars), zhi_move)
     norm1, weigh1, cross = (rows[:, tokens + i : tokens + i + 1] for i in range(3))
     beta = norm1 / (norm0 + EPS)
     image1 = rows[:, :tokens] + beta * image0
@@ -163,7 +172,8 @@
     def for_y(k):
         return jnp.concatenate([pick(grid, ((y + k) % 4) // 2, 1), curve])
 
-    own = for_y(0) + y_move(for_y(1), 1) + y_move(for_y(3), 3) + y_move(for_y(2), 2)
+    two, three, one = staged(for_y, y_move)
+    own = for_y(0) + one + three + two
     alpha1 = norm1 / own[4][:, :1]
 
     def mine_of(blocks):
@@ -174,7 +184,8 @@
     both = jnp.concatenate([merged, my_residual - alpha1 * own[:4]], axis=1)
     both = lax.dynamic_slice_in_dim(both, 32 * (2 * ylow + core), 32, 2)
 
-    groups = jnp.stack([both[0]] + [x_move(both[k], 4 - k) for k in (1, 2, 3)])
+    two, three, one = staged(lambda k: both[4 - k], x_move)
+    groups = jnp.stack([both[0], three, two, one])
     groups = lax.dynamic_slice_in_dim(jnp.concatenate([groups, groups]), (4 - x) % 4, 4, 0)
     return groups[:, :32].reshape(128, 32).T, groups[:, 32:].reshape(128, 32).T
 

time: 133 us -> 134 us (level)
  the two profiles are of different devices: /device:TPU:6 before, /device:TPU:32 now
where the time goes in v4:
time: 134 us
  waiting for transfers between devices  70.2 us (52%)
  starting transfers between devices  51.5 us (38%)
  other arithmetic  3.69 us (3%)
  matrix products  3.68 us (3%)
  local copies, waits for them, and re-layouts  3.52 us (3%)
  between operations  1.51 us (1%)
    ppermute x37, waiting for transfers between devices, moved(): return lax.ppermute(value, axis, [(i, to(i)) for i in range(16)])  70.2 us
    ppermute x37, starting transfers between devices, moved(): return lax.ppermute(value, axis, [(i, to(i)) for i in range(16)])  51.5 us
  transfers between devices with their start and end apart: 37, of which 26 were waited for; matrix products, arithmetic and copies ran while one was open for 3% of the time, Pallas kernels for 0%

profile of v4, /device:TPU:32, one launch (start us, length us, event | category | flops | bytes accessed | tf_op | source)
XLA Modules:
  0.0 134.1 jit_solution(12066107427267400238)
XLA Ops:
  0.6 2.8 %collective-permute-start.8 = (bf16[384,512]{1,0:T(8,128)(2,1)}, bf16[384,512]{1,0:T(8,128)(2,1)S(1)}, u32[]{:S(2)}, u32[]{:S(2)}) collective-permute-start(bf16[384,512]{1,0:T(8,128)(2,1)} %bitcast.164), channel_id=1, source_target_pairs={{0,3},{1,0},{2,1},{3,2},{4,7},{5,4},{6,5},{7,6},{8,11},{9,8},{10,9... | collective-permute-start | bytes 1179656 | tf_op jit(solution)/shard_map/ppermute | solution.py:12
  3.5 1.0 copy.32
  4.5 1.3 fusion
  5.8 0.8 collective-permute-start
  6.6 3.9 %collective-permute-start.2 = (f32[32,384]{1,0:T(8,128)S(1)}, f32[32,384]{1,0:T(8,128)S(1)}, u32[]{:S(2)}, u32[]{:S(2)}) collective-permute-start(f32[32,384]{1,0:T(8,128)S(1)} %get-tuple-element.28), channel_id=1, source_target_pairs={{0,2},{1,3},{2,0},{3,1},{4,6},{5,7},{6,4},{7,5},{8,10},{9,11},{10,... | collective-permute-start | bytes 147464 | tf_op jit(solution)/shard_map/ppermute | solution.py:12
  10.9 6.7 %collective-permute-done = f32[32,384]{1,0:T(8,128)S(1)} collective-permute-done((f32[32,384]{1,0:T(8,128)S(1)}, f32[32,384]{1,0:T(8,128)S(1)}, u32[]{:S(2)}, u32[]{:S(2)}) %collective-permute-start) | collective-permute-done | bytes 49184 | tf_op jit(solution)/shard_map/ppermute | solution.py:12
  17.6 6.4 %collective-permute-start.5 = (f32[32,384]{1,0:T(8,128)S(1)}, f32[32,384]{1,0:T(8,128)S(1)}, u32[]{:S(2)}, u32[]{:S(2)}) collective-permute-start(f32[32,384]{1,0:T(8,128)S(1)} %fusion.50), channel_id=1, source_target_pairs={{0,8},{1,9},{2,10},{3,11},{4,12},{5,13},{6,14},{7,15},{8,0},{9,1},... | collective-permute-start | bytes 147464 | tf_op jit(solution)/shard_map/ppermute | solution.py:12
  24.5 2.4 %collective-permute-start.3 = (f32[32,384]{1,0:T(8,128)S(1)}, f32[32,384]{1,0:T(8,128)S(1)}, u32[]{:S(2)}, u32[]{:S(2)}) collective-permute-start(f32[32,384]{1,0:T(8,128)S(1)} %fusion.50), channel_id=1, source_target_pairs={{0,4},{1,5},{2,6},{3,7},{4,8},{5,9},{6,10},{7,11},{8,12},{9,13},{1... | collective-permute-start | bytes 147464 | tf_op jit(solution)/shard_map/ppermute | solution.py:12
  27.0 1.3 collective-permute-start.9
  28.3 0.9 collective-permute-start.7
  29.2 2.0 %collective-permute-done.3 = f32[32,384]{1,0:T(8,128)S(1)} collective-permute-done((f32[32,384]{1,0:T(8,128)S(1)}, f32[32,384]{1,0:T(8,128)S(1)}, u32[]{:S(2)}, u32[]{:S(2)}) %collective-permute-start.3) | collective-permute-done | bytes 49184 | tf_op jit(solution)/shard_map/ppermute | solution.py:12
  31.2 1.9 %collective-permute-done.9 = bf16[224,512]{1,0:T(8,128)(2,1)S(1)} collective-permute-done((bf16[224,512]{1,0:T(8,128)(2,1)S(1)}, bf16[224,512]{1,0:T(8,128)(2,1)S(1)}, u32[]{:S(2)}, u32[]{:S(2)}) %collective-permute-start.9) | collective-permute-done | bytes 229408 | tf_op jit(solution)/shard_map/ppermute | solution.py:12
  33.1 2.6 %collective-permute-done.7 = bf16[224,512]{1,0:T(8,128)(2,1)S(1)} collective-permute-done((bf16[224,512]{1,0:T(8,128)(2,1)S(1)}, bf16[224,512]{1,0:T(8,128)(2,1)S(1)}, u32[]{:S(2)}, u32[]{:S(2)}) %collective-permute-start.7) | collective-permute-done | bytes 229408 | tf_op jit(solution)/shard_map/ppermute | solution.py:12
  36.7 1.3 collective-permute-done.11
  38.1 1.1 collective-permute-start.12
  39.2 4.5 %collective-permute-done.12 = f32[8,32,128]{2,1,0:T(8,128)S(1)} collective-permute-done((f32[8,32,128]{2,1,0:T(8,128)S(1)}, f32[8,32,128]{2,1,0:T(8,128)S(1)}, u32[]{:S(2)}, u32[]{:S(2)}) %collective-permute-start.12) | collective-permute-done | bytes 131104 | tf_op jit(solution)/shard_map/ppermute | solution.py:12
  43.8 3.3 %collective-permute-start.15 = (f32[8,32,128]{2,1,0:T(8,128)S(1)}, f32[8,32,128]{2,1,0:T(8,128)S(1)}, u32[]{:S(2)}, u32[]{:S(2)}) collective-permute-start(f32[8,32,128]{2,1,0:T(8,128)S(1)} %add.297), channel_id=1, source_target_pairs={{0,64},{16,80},{32,96},{48,112},{64,0},{80,16},{96,32},{112,48},{1... | collective-permute-start | bytes 393224 | tf_op jit(solution)/shard_map/ppermute | solution.py:12
  47.0 1.0 collective-permute-start.14
  48.1 1.0 collective-permute-start.13
  49.1 2.2 %collective-permute-done.15 = f32[8,32,128]{2,1,0:T(8,128)S(1)} collective-permute-done((f32[8,32,128]{2,1,0:T(8,128)S(1)}, f32[8,32,128]{2,1,0:T(8,128)S(1)}, u32[]{:S(2)}, u32[]{:S(2)}) %collective-permute-start.15) | collective-permute-done | bytes 131104 | tf_op jit(solution)/shard_map/ppermute | solution.py:12
  51.3 1.9 %collective-permute-done.14 = f32[8,32,128]{2,1,0:T(8,128)S(1)} collective-permute-done((f32[8,32,128]{2,1,0:T(8,128)S(1)}, f32[8,32,128]{2,1,0:T(8,128)S(1)}, u32[]{:S(2)}, u32[]{:S(2)}) %collective-permute-start.14) | collective-permute-done | bytes 131104 | tf_op jit(solution)/shard_map/ppermute | solution.py:12
  53.2 1.1 collective-permute-done.13
  54.4 1.3 collective-permute-done.16
  57.1 3.3 %collective-permute-start.18 = (f32[32,512]{1,0:T(8,128)S(1)}, f32[32,512]{1,0:T(8,128)S(1)}, u32[]{:S(2)}, u32[]{:S(2)}) collective-permute-start(f32[32,512]{1,0:T(8,128)S(1)} %pad_maximum_fusion.12), channel_id=1, source_target_pairs={{0,12},{1,13},{2,14},{3,15},{4,0},{5,1},{6,2},{7,3},{8,4},{9,5},{1... | collective-permute-start | bytes 196616 | tf_op jit(solution)/shard_map/ppermute | solution.py:12
  60.4 3.0 %collective-permute-start.19 = (f32[32,512]{1,0:T(8,128)S(1)}, f32[32,512]{1,0:T(8,128)S(1)}, u32[]{:S(2)}, u32[]{:S(2)}) collective-permute-start(f32[32,512]{1,0:T(8,128)S(1)} %pad_maximum_fusion.12), channel_id=1, source_target_pairs={{0,8},{1,9},{2,10},{3,11},{4,12},{5,13},{6,14},{7,15},{8,0},{9,1},... | collective-permute-start | bytes 196616 | tf_op jit(solution)/shard_map/ppermute | solution.py:12
  63.7 5.9 %collective-permute-done.19 = f32[32,512]{1,0:T(8,128)S(1)} collective-permute-done((f32[32,512]{1,0:T(8,128)S(1)}, f32[32,512]{1,0:T(8,128)S(1)}, u32[]{:S(2)}, u32[]{:S(2)}) %collective-permute-start.19) | collective-permute-done | bytes 65568 | tf_op jit(solution)/shard_map/ppermute | solution.py:12
  69.7 1.5 %collective-permute-done.17 = f32[32,512]{1,0:T(8,128)S(1)} collective-permute-done((f32[32,512]{1,0:T(8,128)S(1)}, f32[32,512]{1,0:T(8,128)S(1)}, u32[]{:S(2)}, u32[]{:S(2)}) %collective-permute-start.17) | collective-permute-done | bytes 65568 | tf_op jit(solution)/shard_map/ppermute | solution.py:12
  72.6 1.3 collective-permute-done.20
  74.0 5.9 %collective-permute-done.21 = f32[9,32,128]{2,1,0:T(8,128)S(1)} collective-permute-done((f32[9,32,128]{2,1,0:T(8,128)S(1)}, f32[9,32,128]{2,1,0:T(8,128)S(1)}, u32[]{:S(2)}, u32[]{:S(2)}) %collective-permute-start.21) | collective-permute-done | bytes 147488 | tf_op jit(solution)/shard_map/ppermute | solution.py:12
  79.9 1.9 %collective-permute-start.24 = (f32[9,32,128]{2,1,0:T(8,128)S(1)}, f32[9,32,128]{2,1,0:T(8,128)S(1)}, u32[]{:S(2)}, u32[]{:S(2)}) collective-permute-start(f32[9,32,128]{2,1,0:T(8,128)S(1)} %add.309), channel_id=1, source_target_pairs={{0,64},{16,80},{32,96},{48,112},{64,0},{80,16},{96,32},{112,48},{1... | collective-permute-start | bytes 442376 | tf_op jit(solution)/shard_map/ppermute | solution.py:12
  81.8 1.2 collective-permute-start.23
  83.0 0.8 collective-permute-start.22
  83.8 4.4 %collective-permute-done.24 = f32[9,32,128]{2,1,0:T(8,128)S(1)} collective-permute-done((f32[9,32,128]{2,1,0:T(8,128)S(1)}, f32[9,32,128]{2,1,0:T(8,128)S(1)}, u32[]{:S(2)}, u32[]{:S(2)}) %collective-permute-start.24) | collective-permute-done | bytes 147488 | tf_op jit(solution)/shard_map/ppermute | solution.py:12
  88.6 1.4 %collective-permute-done.22 = f32[9,32,128]{2,1,0:T(8,128)S(1)} collective-permute-done((f32[9,32,128]{2,1,0:T(8,128)S(1)}, f32[9,32,128]{2,1,0:T(8,128)S(1)}, u32[]{:S(2)}, u32[]{:S(2)}) %collective-permute-start.22) | collective-permute-done | bytes 147488 | tf_op jit(solution)/shard_map/ppermute | solution.py:12
  90.4 1.3 collective-permute-done.25
  93.1 1.7 %collective-permute-start.27 = (f32[32,512]{1,0:T(8,128)S(1)}, f32[32,512]{1,0:T(8,128)S(1)}, u32[]{:S(2)}, u32[]{:S(2)}) collective-permute-start(f32[32,512]{1,0:T(8,128)S(1)} %pad_maximum_fusion.13), channel_id=1, source_target_pairs={{0,12},{1,13},{2,14},{3,15},{4,0},{5,1},{6,2},{7,3},{8,4},{9,5},{1... | collective-permute-start | bytes 196616 | tf_op jit(solution)/shard_map/ppermute | solution.py:12
  94.9 3.1 %collective-permute-start.28 = (f32[32,512]{1,0:T(8,128)S(1)}, f32[32,512]{1,0:T(8,128)S(1)}, u32[]{:S(2)}, u32[]{:S(2)}) collective-permute-start(f32[32,512]{1,0:T(8,128)S(1)} %pad_maximum_fusion.13), channel_id=1, source_target_pairs={{0,8},{1,9},{2,10},{3,11},{4,12},{5,13},{6,14},{7,15},{8,0},{9,1},... | collective-permute-start | bytes 196616 | tf_op jit(solution)/shard_map/ppermute | solution.py:12
  98.0 1.8 %collective-permute-start.26 = (f32[32,512]{1,0:T(8,128)S(1)}, f32[32,512]{1,0:T(8,128)S(1)}, u32[]{:S(2)}, u32[]{:S(2)}) collective-permute-start(f32[32,512]{1,0:T(8,128)S(1)} %pad_maximum_fusion.13), channel_id=1, source_target_pairs={{0,4},{1,5},{2,6},{3,7},{4,8},{5,9},{6,10},{7,11},{8,12},{9,13},{1... | collective-permute-start | bytes 196616 | tf_op jit(solution)/shard_map/ppermute | solution.py:12
  99.8 4.4 %collective-permute-done.28 = f32[32,512]{1,0:T(8,128)S(1)} collective-permute-done((f32[32,512]{1,0:T(8,128)S(1)}, f32[32,512]{1,0:T(8,128)S(1)}, u32[]{:S(2)}, u32[]{:S(2)}) %collective-permute-start.28) | collective-permute-done | bytes 65568 | tf_op jit(solution)/shard_map/ppermute | solution.py:12
  104.2 1.8 %collective-permute-done.26 = f32[32,512]{1,0:T(8,128)S(1)} collective-permute-done((f32[32,512]{1,0:T(8,128)S(1)}, f32[32,512]{1,0:T(8,128)S(1)}, u32[]{:S(2)}, u32[]{:S(2)}) %collective-permute-start.26) | collective-permute-done | bytes 65568 | tf_op jit(solution)/shard_map/ppermute | solution.py:12
  107.7 1.5 %collective-permute-done.29 = f32[17,32,128]{2,1,0:T(8,128)S(1)} collective-permute-done((f32[17,32,128]{2,1,0:T(8,128)S(1)}, f32[17,32,128]{2,1,0:T(8,128)S(1)}, u32[]{:S(2)}, u32[]{:S(2)}) %collective-permute-start.29) | collective-permute-done | bytes 278560 | tf_op jit(solution)/shard_map/ppermute | solution.py:12
  109.7 5.7 %collective-permute-done.30 = f32[9,32,128]{2,1,0:T(8,128)S(1)} collective-permute-done((f32[9,32,128]{2,1,0:T(8,128)S(1)}, f32[9,32,128]{2,1,0:T(8,128)S(1)}, u32[]{:S(2)}, u32[]{:S(2)}) %collective-permute-start.30) | collective-permute-done | bytes 147488 | tf_op jit(solution)/shard_map/ppermute | solution.py:12
  115.8 3.0 %collective-permute-start.32 = (f32[5,32,128]{2,1,0:T(8,128)S(1)}, f32[5,32,128]{2,1,0:T(8,128)S(1)}, u32[]{:S(2)}, u32[]{:S(2)}) collective-permute-start(f32[5,32,128]{2,1,0:T(8,128)S(1)} %get-tuple-element.48), channel_id=1, source_target_pairs={{0,96},{16,112},{32,0},{48,16},{64,32},{80,48},{96,64},{112,80},{1... | collective-permute-start | bytes 245768 | tf_op jit(solution)/shard_map/ppermute | solution.py:12
  119.3 2.0 %collective-permute-done.31 = f32[5,32,128]{2,1,0:T(8,128)S(1)} collective-permute-done((f32[5,32,128]{2,1,0:T(8,128)S(1)}, f32[5,32,128]{2,1,0:T(8,128)S(1)}, u32[]{:S(2)}, u32[]{:S(2)}) %collective-permute-start.31) | collective-permute-done | bytes 81952 | tf_op jit(solution)/shard_map/ppermute | solution.py:12
  121.7 3.1 %collective-permute-done.33 = f32[5,32,128]{2,1,0:T(8,128)S(1)} collective-permute-done((f32[5,32,128]{2,1,0:T(8,128)S(1)}, f32[5,32,128]{2,1,0:T(8,128)S(1)}, u32[]{:S(2)}, u32[]{:S(2)}) %collective-permute-start.33) | collective-permute-done | bytes 81952 | tf_op jit(solution)/shard_map/ppermute | solution.py:12
  125.1 1.3 collective-permute-start.34
  127.2 1.8 %collective-permute-start.35 = (f32[64,32]{1,0:T(8,128)S(1)}, f32[64,32]{1,0:T(8,128)S(1)}, u32[]{:S(2)}, u32[]{:S(2)}) collective-permute-start(f32[64,32]{1,0:T(8,128)S(1)} %get-tuple-element.32), channel_id=1, source_target_pairs={{0,2},{1,3},{2,0},{3,1},{4,6},{5,7},{6,4},{7,5},{8,10},{9,11},{10,... | collective-permute-start | bytes 24584 | tf_op jit(solution)/shard_map/ppermute | solution.py:12
  129.1 3.5 %collective-permute-done.35 = f32[64,32]{1,0:T(8,128)S(1)} collective-permute-done((f32[64,32]{1,0:T(8,128)S(1)}, f32[64,32]{1,0:T(8,128)S(1)}, u32[]{:S(2)}, u32[]{:S(2)}) %collective-permute-start.35) | collective-permute-done | bytes 8224 | tf_op jit(solution)/shard_map/ppermute | solution.py:12
  (128 shorter events, 13.0 us)
Async XLA Ops:
  0.6 23.9 %collective-permute-start.8 = (bf16[384,512]{1,0:T(8,128)(2,1)}, bf16[384,512]{1,0:T(8,128)(2,1)S(1)}, u32[]{:S(2)}, u32[]{:S(2)}) collective-permute-start(bf16[384,512]{1,0:T(8,128)(2,1)} %bitcast.164), channel_id=1, source_target_pairs={{0,3},{1,0},{2,1},{3,2},{4,7},{5,4},{6,5},{7,6},{8,11},{9,8},{10,9... | collective-permute-start | bytes 1179656 | tf_op jit(solution)/shard_map/ppermute | solution.py:12
  3.5 23.5 %collective-permute-start.6 = (bf16[384,512]{1,0:T(8,128)(2,1)}, bf16[384,512]{1,0:T(8,128)(2,1)S(1)}, u32[]{:S(2)}, u32[]{:S(2)}) collective-permute-start(bf16[384,512]{1,0:T(8,128)(2,1)} %bitcast.165), channel_id=1, source_target_pairs={{0,1},{1,2},{2,3},{3,0},{4,5},{5,6},{6,7},{7,4},{8,9},{9,10},{10,1... | collective-permute-start | bytes 1179656 | tf_op jit(solution)/shard_map/ppermute | solution.py:12
  5.8 11.8 %collective-permute-start = (f32[32,384]{1,0:T(8,128)S(1)}, f32[32,384]{1,0:T(8,128)S(1)}, u32[]{:S(2)}, u32[]{:S(2)}) collective-permute-start(f32[32,384]{1,0:T(8,128)S(1)} %get-tuple-element.27), channel_id=1, source_target_pairs={{0,1},{1,2},{2,3},{3,0},{4,5},{5,6},{6,7},{7,4},{8,9},{9,10},{10,1... | collective-permute-start | bytes 147464 | tf_op jit(solution)/shard_map/ppermute | solution.py:12
  6.6 10.9 %collective-permute-start.2 = (f32[32,384]{1,0:T(8,128)S(1)}, f32[32,384]{1,0:T(8,128)S(1)}, u32[]{:S(2)}, u32[]{:S(2)}) collective-permute-start(f32[32,384]{1,0:T(8,128)S(1)} %get-tuple-element.28), channel_id=1, source_target_pairs={{0,2},{1,3},{2,0},{3,1},{4,6},{5,7},{6,4},{7,5},{8,10},{9,11},{10,... | collective-permute-start | bytes 147464 | tf_op jit(solution)/shard_map/ppermute | solution.py:12
  10.6 7.0 %collective-permute-start.1 = (f32[32,384]{1,0:T(8,128)S(1)}, f32[32,384]{1,0:T(8,128)S(1)}, u32[]{:S(2)}, u32[]{:S(2)}) collective-permute-start(f32[32,384]{1,0:T(8,128)S(1)} %get-tuple-element.29), channel_id=1, source_target_pairs={{0,3},{1,0},{2,1},{3,2},{4,7},{5,4},{6,5},{7,6},{8,11},{9,8},{10,9... | collective-permute-start | bytes 147464 | tf_op jit(solution)/shard_map/ppermute | solution.py:12
  10.8 24.8 %copy-start = (bf16[1,384,512]{2,1,0:T(8,128)(2,1)S(1)}, bf16[1,384,512]{2,1,0:T(8,128)(2,1)}, u32[]{:S(2)}) copy-start(bf16[1,384,512]{2,1,0:T(8,128)(2,1)} %param.2) | copy-start | bytes 1179652
  17.6 19.0 %collective-permute-start.10 = (bf16[32,512]{1,0:T(8,128)(2,1)S(1)}, bf16[32,512]{1,0:T(8,128)(2,1)S(1)}, u32[]{:S(2)}, u32[]{:S(2)}) collective-permute-start(bf16[32,512]{1,0:T(8,128)(2,1)S(1)} %get-tuple-element.39), channel_id=1, source_target_pairs={{0,2},{1,3},{2,0},{3,1},{4,6},{5,7},{6,4},{7,5},{8,10},{9,11},{10,... | collective-permute-start | bytes 98312 | tf_op jit(solution)/shard_map/ppermute | solution.py:12
  17.6 10.7 %collective-permute-start.5 = (f32[32,384]{1,0:T(8,128)S(1)}, f32[32,384]{1,0:T(8,128)S(1)}, u32[]{:S(2)}, u32[]{:S(2)}) collective-permute-start(f32[32,384]{1,0:T(8,128)S(1)} %fusion.50), channel_id=1, source_target_pairs={{0,8},{1,9},{2,10},{3,11},{4,12},{5,13},{6,14},{7,15},{8,0},{9,1},... | collective-permute-start | bytes 147464 | tf_op jit(solution)/shard_map/ppermute | solution.py:12
  24.0 5.2 %collective-permute-start.4 = (f32[32,384]{1,0:T(8,128)S(1)}, f32[32,384]{1,0:T(8,128)S(1)}, u32[]{:S(2)}, u32[]{:S(2)}) collective-permute-start(f32[32,384]{1,0:T(8,128)S(1)} %fusion.50), channel_id=1, source_target_pairs={{0,12},{1,13},{2,14},{3,15},{4,0},{5,1},{6,2},{7,3},{8,4},{9,5},{1... | collective-permute-start | bytes 147464 | tf_op jit(solution)/shard_map/ppermute | solution.py:12
  24.5 6.6 %collective-permute-start.3 = (f32[32,384]{1,0:T(8,128)S(1)}, f32[32,384]{1,0:T(8,128)S(1)}, u32[]{:S(2)}, u32[]{:S(2)}) collective-permute-start(f32[32,384]{1,0:T(8,128)S(1)} %fusion.50), channel_id=1, source_target_pairs={{0,4},{1,5},{2,6},{3,7},{4,8},{5,9},{6,10},{7,11},{8,12},{9,13},{1... | collective-permute-start | bytes 147464 | tf_op jit(solution)/shard_map/ppermute | solution.py:12
  27.0 6.1 %collective-permute-start.9 = (bf16[224,512]{1,0:T(8,128)(2,1)S(1)}, bf16[224,512]{1,0:T(8,128)(2,1)S(1)}, u32[]{:S(2)}, u32[]{:S(2)}) collective-permute-start(bf16[224,512]{1,0:T(8,128)(2,1)S(1)} %pad_maximum_fusion.3), channel_id=1, source_target_pairs={{0,3},{1,0},{2,1},{3,2},{4,7},{5,4},{6,5},{7,6},{8,11},{9,8},{10,9... | collective-permute-start | bytes 688136 | tf_op jit(solution)/shard_map/ppermute | solution.py:12
  28.3 7.3 %collective-permute-start.7 = (bf16[224,512]{1,0:T(8,128)(2,1)S(1)}, bf16[224,512]{1,0:T(8,128)(2,1)S(1)}, u32[]{:S(2)}, u32[]{:S(2)}) collective-permute-start(bf16[224,512]{1,0:T(8,128)(2,1)S(1)} %pad_maximum_fusion.2), channel_id=1, source_target_pairs={{0,1},{1,2},{2,3},{3,0},{4,5},{5,6},{6,7},{7,4},{8,9},{9,10},{10,1... | collective-permute-start | bytes 688136 | tf_op jit(solution)/shard_map/ppermute | solution.py:12
  36.6 1.4 %collective-permute-start.11 = (f32[8,32,128]{2,1,0:T(8,128)S(1)}, f32[8,32,128]{2,1,0:T(8,128)S(1)}, u32[]{:S(2)}, u32[]{:S(2)}) collective-permute-start(f32[8,32,128]{2,1,0:T(8,128)S(1)} %bitcast.185), channel_id=1, source_target_pairs={{0,16},{16,0},{32,48},{48,32},{64,80},{80,64},{96,112},{112,96},{1... | collective-permute-start | bytes 393224 | tf_op jit(solution)/shard_map/ppermute | solution.py:12
  38.1 5.6 %collective-permute-start.12 = (f32[8,32,128]{2,1,0:T(8,128)S(1)}, f32[8,32,128]{2,1,0:T(8,128)S(1)}, u32[]{:S(2)}, u32[]{:S(2)}) collective-permute-start(f32[8,32,128]{2,1,0:T(8,128)S(1)} %bitcast_add_fusion.1), channel_id=1, source_target_pairs={{0,128},{16,144},{32,160},{48,176},{64,192},{80,208},{96,224},{112... | collective-permute-start | bytes 393224 | tf_op jit(solution)/shard_map/ppermute | solution.py:12
  43.8 7.5 %collective-permute-start.15 = (f32[8,32,128]{2,1,0:T(8,128)S(1)}, f32[8,32,128]{2,1,0:T(8,128)S(1)}, u32[]{:S(2)}, u32[]{:S(2)}) collective-permute-start(f32[8,32,128]{2,1,0:T(8,128)S(1)} %add.297), channel_id=1, source_target_pairs={{0,64},{16,80},{32,96},{48,112},{64,0},{80,16},{96,32},{112,48},{1... | collective-permute-start | bytes 393224 | tf_op jit(solution)/shard_map/ppermute | solution.py:12
  47.0 6.2 %collective-permute-start.14 = (f32[8,32,128]{2,1,0:T(8,128)S(1)}, f32[8,32,128]{2,1,0:T(8,128)S(1)}, u32[]{:S(2)}, u32[]{:S(2)}) collective-permute-start(f32[8,32,128]{2,1,0:T(8,128)S(1)} %add.297), channel_id=1, source_target_pairs={{0,96},{16,112},{32,0},{48,16},{64,32},{80,48},{96,64},{112,80},{1... | collective-permute-start | bytes 393224 | tf_op jit(solution)/shard_map/ppermute | solution.py:12
  48.1 6.2 %collective-permute-start.13 = (f32[8,32,128]{2,1,0:T(8,128)S(1)}, f32[8,32,128]{2,1,0:T(8,128)S(1)}, u32[]{:S(2)}, u32[]{:S(2)}) collective-permute-start(f32[8,32,128]{2,1,0:T(8,128)S(1)} %add.297), channel_id=1, source_target_pairs={{0,32},{16,48},{32,64},{48,80},{64,96},{80,112},{96,0},{112,16},{1... | collective-permute-start | bytes 393224 | tf_op jit(solution)/shard_map/ppermute | solution.py:12
  54.3 1.4 %collective-permute-start.16 = (f32[8,32,128]{2,1,0:T(8,128)S(1)}, f32[8,32,128]{2,1,0:T(8,128)S(1)}, u32[]{:S(2)}, u32[]{:S(2)}) collective-permute-start(f32[8,32,128]{2,1,0:T(8,128)S(1)} %add_add_fusion.1), channel_id=1, source_target_pairs={{0,16},{16,0},{32,48},{48,32},{64,80},{80,64},{96,112},{112,96},{1... | collective-permute-start | bytes 393224 | tf_op jit(solution)/shard_map/ppermute | solution.py:12
  57.1 6.7 %collective-permute-start.18 = (f32[32,512]{1,0:T(8,128)S(1)}, f32[32,512]{1,0:T(8,128)S(1)}, u32[]{:S(2)}, u32[]{:S(2)}) collective-permute-start(f32[32,512]{1,0:T(8,128)S(1)} %pad_maximum_fusion.12), channel_id=1, source_target_pairs={{0,12},{1,13},{2,14},{3,15},{4,0},{5,1},{6,2},{7,3},{8,4},{9,5},{1... | collective-permute-start | bytes 196616 | tf_op jit(solution)/shard_map/ppermute | solution.py:12
  60.4 9.3 %collective-permute-start.19 = (f32[32,512]{1,0:T(8,128)S(1)}, f32[32,512]{1,0:T(8,128)S(1)}, u32[]{:S(2)}, u32[]{:S(2)}) collective-permute-start(f32[32,512]{1,0:T(8,128)S(1)} %pad_maximum_fusion.12), channel_id=1, source_target_pairs={{0,8},{1,9},{2,10},{3,11},{4,12},{5,13},{6,14},{7,15},{8,0},{9,1},... | collective-permute-start | bytes 196616 | tf_op jit(solution)/shard_map/ppermute | solution.py:12
  63.4 7.8 %collective-permute-start.17 = (f32[32,512]{1,0:T(8,128)S(1)}, f32[32,512]{1,0:T(8,128)S(1)}, u32[]{:S(2)}, u32[]{:S(2)}) collective-permute-start(f32[32,512]{1,0:T(8,128)S(1)} %pad_maximum_fusion.12), channel_id=1, source_target_pairs={{0,4},{1,5},{2,6},{3,7},{4,8},{5,9},{6,10},{7,11},{8,12},{9,13},{1... | collective-permute-start | bytes 196616 | tf_op jit(solution)/shard_map/ppermute | solution.py:12
  72.4 1.5 %collective-permute-start.20 = (f32[9,32,128]{2,1,0:T(8,128)S(1)}, f32[9,32,128]{2,1,0:T(8,128)S(1)}, u32[]{:S(2)}, u32[]{:S(2)}) collective-permute-start(f32[9,32,128]{2,1,0:T(8,128)S(1)} %pad_maximum_fusion.4), channel_id=1, source_target_pairs={{0,16},{16,0},{32,48},{48,32},{64,80},{80,64},{96,112},{112,96},{1... | collective-permute-start | bytes 442376 | tf_op jit(solution)/shard_map/ppermute | solution.py:12
  73.9 6.0 %collective-permute-start.21 = (f32[9,32,128]{2,1,0:T(8,128)S(1)}, f32[9,32,128]{2,1,0:T(8,128)S(1)}, u32[]{:S(2)}, u32[]{:S(2)}) collective-permute-start(f32[9,32,128]{2,1,0:T(8,128)S(1)} %fusion.26), channel_id=1, source_target_pairs={{0,128},{16,144},{32,160},{48,176},{64,192},{80,208},{96,224},{112... | collective-permute-start | bytes 442376 | tf_op jit(solution)/shard_map/ppermute | solution.py:12
  79.9 8.3 %collective-permute-start.24 = (f32[9,32,128]{2,1,0:T(8,128)S(1)}, f32[9,32,128]{2,1,0:T(8,128)S(1)}, u32[]{:S(2)}, u32[]{:S(2)}) collective-permute-start(f32[9,32,128]{2,1,0:T(8,128)S(1)} %add.309), channel_id=1, source_target_pairs={{0,64},{16,80},{32,96},{48,112},{64,0},{80,16},{96,32},{112,48},{1... | collective-permute-start | bytes 442376 | tf_op jit(solution)/shard_map/ppermute | solution.py:12
  81.8 6.9 %collective-permute-start.23 = (f32[9,32,128]{2,1,0:T(8,128)S(1)}, f32[9,32,128]{2,1,0:T(8,128)S(1)}, u32[]{:S(2)}, u32[]{:S(2)}) collective-permute-start(f32[9,32,128]{2,1,0:T(8,128)S(1)} %add.309), channel_id=1, source_target_pairs={{0,96},{16,112},{32,0},{48,16},{64,32},{80,48},{96,64},{112,80},{1... | collective-permute-start | bytes 442376 | tf_op jit(solution)/shard_map/ppermute | solution.py:12
  83.0 7.0 %collective-permute-start.22 = (f32[9,32,128]{2,1,0:T(8,128)S(1)}, f32[9,32,128]{2,1,0:T(8,128)S(1)}, u32[]{:S(2)}, u32[]{:S(2)}) collective-permute-start(f32[9,32,128]{2,1,0:T(8,128)S(1)} %add.309), channel_id=1, source_target_pairs={{0,32},{16,48},{32,64},{48,80},{64,96},{80,112},{96,0},{112,16},{1... | collective-permute-start | bytes 442376 | tf_op jit(solution)/shard_map/ppermute | solution.py:12
  90.3 1.4 %collective-permute-start.25 = (f32[8,32,128]{2,1,0:T(8,128)S(1)}, f32[8,32,128]{2,1,0:T(8,128)S(1)}, u32[]{:S(2)}, u32[]{:S(2)}) collective-permute-start(f32[8,32,128]{2,1,0:T(8,128)S(1)} %fusion.27), channel_id=1, source_target_pairs={{0,16},{16,0},{32,48},{48,32},{64,80},{80,64},{96,112},{112,96},{1... | collective-permute-start | bytes 393224 | tf_op jit(solution)/shard_map/ppermute | solution.py:12
  93.1 6.7 %collective-permute-start.27 = (f32[32,512]{1,0:T(8,128)S(1)}, f32[32,512]{1,0:T(8,128)S(1)}, u32[]{:S(2)}, u32[]{:S(2)}) collective-permute-start(f32[32,512]{1,0:T(8,128)S(1)} %pad_maximum_fusion.13), channel_id=1, source_target_pairs={{0,12},{1,13},{2,14},{3,15},{4,0},{5,1},{6,2},{7,3},{8,4},{9,5},{1... | collective-permute-start | bytes 196616 | tf_op jit(solution)/shard_map/ppermute | solution.py:12
  94.9 9.3 %collective-permute-start.28 = (f32[32,512]{1,0:T(8,128)S(1)}, f32[32,512]{1,0:T(8,128)S(1)}, u32[]{:S(2)}, u32[]{:S(2)}) collective-permute-start(f32[32,512]{1,0:T(8,128)S(1)} %pad_maximum_fusion.13), channel_id=1, source_target_pairs={{0,8},{1,9},{2,10},{3,11},{4,12},{5,13},{6,14},{7,15},{8,0},{9,1},... | collective-permute-start | bytes 196616 | tf_op jit(solution)/shard_map/ppermute | solution.py:12
  98.0 8.0 %collective-permute-start.26 = (f32[32,512]{1,0:T(8,128)S(1)}, f32[32,512]{1,0:T(8,128)S(1)}, u32[]{:S(2)}, u32[]{:S(2)}) collective-permute-start(f32[32,512]{1,0:T(8,128)S(1)} %pad_maximum_fusion.13), channel_id=1, source_target_pairs={{0,4},{1,5},{2,6},{3,7},{4,8},{5,9},{6,10},{7,11},{8,12},{9,13},{1... | collective-permute-start | bytes 196616 | tf_op jit(solution)/shard_map/ppermute | solution.py:12
  107.4 1.9 %collective-permute-start.29 = (f32[17,32,128]{2,1,0:T(8,128)S(1)}, f32[17,32,128]{2,1,0:T(8,128)S(1)}, u32[]{:S(2)}, u32[]{:S(2)}) collective-permute-start(f32[17,32,128]{2,1,0:T(8,128)S(1)} %pad_maximum_fusion.1), channel_id=1, source_target_pairs={{0,16},{16,0},{32,48},{48,32},{64,80},{80,64},{96,112},{112,96},{1... | collective-permute-start | bytes 835592 | tf_op jit(solution)/shard_map/ppermute | solution.py:12
  109.4 6.0 %collective-permute-start.30 = (f32[9,32,128]{2,1,0:T(8,128)S(1)}, f32[9,32,128]{2,1,0:T(8,128)S(1)}, u32[]{:S(2)}, u32[]{:S(2)}) collective-permute-start(f32[9,32,128]{2,1,0:T(8,128)S(1)} %pad_maximum_fusion.6), channel_id=1, source_target_pairs={{0,128},{16,144},{32,160},{48,176},{64,192},{80,208},{96,224},{112... | collective-permute-start | bytes 442376 | tf_op jit(solution)/shard_map/ppermute | solution.py:12
  115.5 5.7 %collective-permute-start.31 = (f32[5,32,128]{2,1,0:T(8,128)S(1)}, f32[5,32,128]{2,1,0:T(8,128)S(1)}, u32[]{:S(2)}, u32[]{:S(2)}) collective-permute-start(f32[5,32,128]{2,1,0:T(8,128)S(1)} %get-tuple-element.47), channel_id=1, source_target_pairs={{0,32},{16,48},{32,64},{48,80},{64,96},{80,112},{96,0},{112,16},{1... | collective-permute-start | bytes 245768 | tf_op jit(solution)/shard_map/ppermute | solution.py:12
  115.8 5.9 %collective-permute-start.32 = (f32[5,32,128]{2,1,0:T(8,128)S(1)}, f32[5,32,128]{2,1,0:T(8,128)S(1)}, u32[]{:S(2)}, u32[]{:S(2)}) collective-permute-start(f32[5,32,128]{2,1,0:T(8,128)S(1)} %get-tuple-element.48), channel_id=1, source_target_pairs={{0,96},{16,112},{32,0},{48,16},{64,32},{80,48},{96,64},{112,80},{1... | collective-permute-start | bytes 245768 | tf_op jit(solution)/shard_map/ppermute | solution.py:12
  118.8 5.9 %collective-permute-start.33 = (f32[5,32,128]{2,1,0:T(8,128)S(1)}, f32[5,32,128]{2,1,0:T(8,128)S(1)}, u32[]{:S(2)}, u32[]{:S(2)}) collective-permute-start(f32[5,32,128]{2,1,0:T(8,128)S(1)} %get-tuple-element.49), channel_id=1, source_target_pairs={{0,64},{16,80},{32,96},{48,112},{64,0},{80,16},{96,32},{112,48},{1... | collective-permute-start | bytes 245768 | tf_op jit(solution)/shard_map/ppermute | solution.py:12
  125.1 4.0 %collective-permute-start.34 = (f32[64,32]{1,0:T(8,128)S(1)}, f32[64,32]{1,0:T(8,128)S(1)}, u32[]{:S(2)}, u32[]{:S(2)}) collective-permute-start(f32[64,32]{1,0:T(8,128)S(1)} %get-tuple-element.33), channel_id=1, source_target_pairs={{0,3},{1,0},{2,1},{3,2},{4,7},{5,4},{6,5},{7,6},{8,11},{9,8},{10,9... | collective-permute-start | bytes 24584 | tf_op jit(solution)/shard_map/ppermute | solution.py:12
  126.5 6.2 %collective-permute-start.36 = (f32[64,32]{1,0:T(8,128)S(1)}, f32[64,32]{1,0:T(8,128)S(1)}, u32[]{:S(2)}, u32[]{:S(2)}) collective-permute-start(f32[64,32]{1,0:T(8,128)S(1)} %get-tuple-element.30), channel_id=1, source_target_pairs={{0,1},{1,2},{2,3},{3,0},{4,5},{5,6},{6,7},{7,4},{8,9},{9,10},{10,1... | collective-permute-start | bytes 24584 | tf_op jit(solution)/shard_map/ppermute | solution.py:12
  127.2 5.4 %collective-permute-start.35 = (f32[64,32]{1,0:T(8,128)S(1)}, f32[64,32]{1,0:T(8,128)S(1)}, u32[]{:S(2)}, u32[]{:S(2)}) collective-permute-start(f32[64,32]{1,0:T(8,128)S(1)} %get-tuple-element.32), channel_id=1, source_target_pairs={{0,2},{1,3},{2,0},{3,1},{4,6},{5,7},{6,4},{7,5},{8,10},{9,11},{10,... | collective-permute-start | bytes 24584 | tf_op jit(solution)/shard_map/ppermute | solution.py:12

commit v5 on v4

--- a/solution.py
+++ b/solution.py
@@ -110,7 +110,7 @@
     tasks = lax.axis_size("task")
     row = lax.axis_index("rows")
     task = lax.axis_index("task")
-    x, core, ylow, yhigh, zlo = row % 4, task % 2, (task // 2) % 2, (task // 4) % 2, task // 8
+    x, core = row % 4, task % 2
     scale = 1.0 / (tokens * tasks)
     gram_scale, diag_scale = ALPHA * scale, (1.0 - ALPHA) * scale
 
@@ -158,36 +158,32 @@
     image1 = rows[:, :tokens] + beta * image0
     direction = residual + beta * target
     curve = gram_scale * total(image1 * image1) + weigh1 + 2.0 * beta * cross + beta * beta * weigh0
-    curve = jnp.broadcast_to(curve, (1, 32, 128))
 
-    part = image_part(image1, direction)
-    own = jnp.concatenate([part, curve])
-    own = (own + core_move(own)).reshape(17, 32, 128)
-    grid, curve = own[:16].reshape(4, 2, 2, 32, 128), own[16:]
-    own, other = pick(grid, zlo, 1).reshape(8, 32, 128), pick(grid, 1 - zlo, 1).reshape(8, 32, 128)
-    own = jnp.concatenate([own, curve]) + zlo_move(jnp.concatenate([other, curve]))
-    grid, curve = own[:8].reshape(4, 2, 32, 128), own[8:]
-    y = 2 * yhigh + ylow
+    def side_by_side(blocks):
+        return blocks.transpose(2, 0, 1).reshape(-1, 128)
 
-    def for_y(k):
-        return jnp.concatenate([pick(grid, ((y + k) % 4) // 2, 1), curve])
+    def per_lane(column):
+        return jnp.tile(column[:, 0], 4)[None]
 
-    two, three, one = staged(for_y, y_move)
-    own = for_y(0) + one + three + two
-    alpha1 = norm1 / own[4][:, :1]
+    part = gram_scale * product(image1, xs, 0) + diag * direction
+    part = side_by_side(part.reshape(32, 4, width).transpose(1, 0, 2)).reshape(16, 32, 128)
+    curve = jnp.broadcast_to(per_lane(curve)[None], (16, 8, 128))
+    total_part = jnp.sum(lax.all_to_all(jnp.concatenate([part, curve], axis=1), "task", 0, 0), axis=0)
 
     def mine_of(blocks):
-        return pick(blocks.reshape(4, 4, 32, 128), 2 * zlo + yhigh, 1)
+        four = pick(blocks.reshape(4, 4, 32, 128), task // 4, 1)
+        return side_by_side(lax.dynamic_slice_in_dim(four, 32 * (task % 4), 32, 2))
 
     my_target, my_residual = mine_of(target_blocks), mine_of(residual_blocks)
-    merged = alpha0 * my_target + alpha1 * (my_residual + beta * my_target)
-    both = jnp.concatenate([merged, my_residual - alpha1 * own[:4]], axis=1)
-    both = lax.dynamic_slice_in_dim(both, 32 * (2 * ylow + core), 32, 2)
+    alpha1 = per_lane(norm1) / total_part[32:33]
+    merged = per_lane(alpha0) * my_target + alpha1 * (my_residual + per_lane(beta) * my_target)
+    both = jnp.concatenate([merged, my_residual - alpha1 * total_part[:32]])
 
-    two, three, one = staged(lambda k: both[4 - k], x_move)
-    groups = jnp.stack([both[0], three, two, one])
+    two, three, one = staged(lambda k: both[:, 128 - 32 * k : 160 - 32 * k], x_move)
+    groups = jnp.stack([both[:, :32], three, two, one])
     groups = lax.dynamic_slice_in_dim(jnp.concatenate([groups, groups]), (4 - x) % 4, 4, 0)
-    return groups[:, :32].reshape(128, 32).T, groups[:, 32:].reshape(128, 32).T
+    result = groups.transpose(1, 0, 2).reshape(64, 128)
+    return result[:32], result[32:]
 
 
 def solution(mesh):

time: 134 us -> 132 us (0.985)
  the two profiles are of different devices: /device:TPU:32 before, /device:TPU:1 now
where the time goes in v5:
time: 132 us; the launch traced here: 130 us
  starting transfers between devices  60.6 us (46%)
  waiting for transfers between devices  55.5 us (42%)
  local copies, waits for them, and re-layouts  4.8 us (4%)
  other arithmetic  4.66 us (4%)
  matrix products  3.69 us (3%)
    ppermute x32, starting transfers between devices, moved(): return lax.ppermute(value, axis, [(i, to(i)) for i in range(16)])  54.6 us
    ppermute x32, waiting for transfers between devices, moved(): return lax.ppermute(value, axis, [(i, to(i)) for i in range(16)])  48.3 us
    all_to_all x1, waiting for transfers between devices, on_device(): lax.all_to_all(jnp.concatenate([part, curve], axis=1), 'task', 0, 0)  7.19 us
    all_to_all x1, starting transfers between devices, on_device(): lax.all_to_all(jnp.concatenate([part, curve], axis=1), 'task', 0, 0)  5.96 us
  transfers between devices with their start and end apart: 33, of which 22 were waited for; matrix products, arithmetic and copies ran while one was open for 3% of the time, Pallas kernels for 0%

profile of v5, /device:TPU:1, one launch (start us, length us, event | category | flops | bytes accessed | tf_op | source)
XLA Modules:
  0.0 130.3 jit_solution(439319221106224151)
XLA Ops:
  0.6 3.4 %collective-permute-start.8 = (bf16[384,512]{1,0:T(8,128)(2,1)}, bf16[384,512]{1,0:T(8,128)(2,1)S(1)}, u32[]{:S(2)}, u32[]{:S(2)}) collective-permute-start(bf16[384,512]{1,0:T(8,128)(2,1)} %bitcast.180), channel_id=1, source_target_pairs={{0,3},{1,0},{2,1},{3,2},{4,7},{5,4},{6,5},{7,6},{8,11},{9,8},{10,9... | collective-permute-start | bytes 1179656 | tf_op jit(solution)/shard_map/ppermute | solution.py:12
  4.0 1.0 copy.77
  5.0 1.3 fusion
  6.6 3.7 %collective-permute-start.2 = (f32[32,384]{1,0:T(8,128)S(1)}, f32[32,384]{1,0:T(8,128)S(1)}, u32[]{:S(2)}, u32[]{:S(2)}) collective-permute-start(f32[32,384]{1,0:T(8,128)S(1)} %get-tuple-element.24), channel_id=1, source_target_pairs={{0,2},{1,3},{2,0},{3,1},{4,6},{5,7},{6,4},{7,5},{8,10},{9,11},{10,... | collective-permute-start | bytes 147464 | tf_op jit(solution)/shard_map/ppermute | solution.py:12
  10.3 6.4 %collective-permute-done = f32[32,384]{1,0:T(8,128)S(1)} collective-permute-done((f32[32,384]{1,0:T(8,128)S(1)}, f32[32,384]{1,0:T(8,128)S(1)}, u32[]{:S(2)}, u32[]{:S(2)}) %collective-permute-start) | collective-permute-done | bytes 49184 | tf_op jit(solution)/shard_map/ppermute | solution.py:12
  16.8 7.0 %collective-permute-start.5 = (f32[32,384]{1,0:T(8,128)S(1)}, f32[32,384]{1,0:T(8,128)S(1)}, u32[]{:S(2)}, u32[]{:S(2)}) collective-permute-start(f32[32,384]{1,0:T(8,128)S(1)} %fusion.46), channel_id=1, source_target_pairs={{0,8},{1,9},{2,10},{3,11},{4,12},{5,13},{6,14},{7,15},{8,0},{9,1},... | collective-permute-start | bytes 147464 | tf_op jit(solution)/shard_map/ppermute | solution.py:12
  23.8 2.4 %collective-permute-start.3 = (f32[32,384]{1,0:T(8,128)S(1)}, f32[32,384]{1,0:T(8,128)S(1)}, u32[]{:S(2)}, u32[]{:S(2)}) collective-permute-start(f32[32,384]{1,0:T(8,128)S(1)} %fusion.46), channel_id=1, source_target_pairs={{0,4},{1,5},{2,6},{3,7},{4,8},{5,9},{6,10},{7,11},{8,12},{9,13},{1... | collective-permute-start | bytes 147464 | tf_op jit(solution)/shard_map/ppermute | solution.py:12
  26.2 1.0 collective-permute-start.9
  27.9 1.0 collective-permute-done.3
  29.0 2.5 %collective-permute-done.9 = bf16[224,512]{1,0:T(8,128)(2,1)S(1)} collective-permute-done((bf16[224,512]{1,0:T(8,128)(2,1)S(1)}, bf16[224,512]{1,0:T(8,128)(2,1)S(1)}, u32[]{:S(2)}, u32[]{:S(2)}) %collective-permute-start.9) | collective-permute-done | bytes 229408 | tf_op jit(solution)/shard_map/ppermute | solution.py:12
  31.4 2.0 %collective-permute-done.7 = bf16[224,512]{1,0:T(8,128)(2,1)S(1)} collective-permute-done((bf16[224,512]{1,0:T(8,128)(2,1)S(1)}, bf16[224,512]{1,0:T(8,128)(2,1)S(1)}, u32[]{:S(2)}, u32[]{:S(2)}) %collective-permute-start.7) | collective-permute-done | bytes 229408 | tf_op jit(solution)/shard_map/ppermute | solution.py:12
  34.4 4.7 %collective-permute-start.11 = (f32[8,32,128]{2,1,0:T(8,128)S(1)}, f32[8,32,128]{2,1,0:T(8,128)S(1)}, u32[]{:S(2)}, u32[]{:S(2)}) collective-permute-start(f32[8,32,128]{2,1,0:T(8,128)S(1)} %bitcast.197), channel_id=1, source_target_pairs={{0,16},{16,0},{32,48},{48,32},{64,80},{80,64},{96,112},{112,96},{1... | collective-permute-start | bytes 393224 | tf_op jit(solution)/shard_map/ppermute | solution.py:12
  39.1 1.0 collective-permute-done.11
  40.1 0.8 collective-permute-start.12
  40.9 4.0 %collective-permute-done.12 = f32[8,32,128]{2,1,0:T(8,128)S(1)} collective-permute-done((f32[8,32,128]{2,1,0:T(8,128)S(1)}, f32[8,32,128]{2,1,0:T(8,128)S(1)}, u32[]{:S(2)}, u32[]{:S(2)}) %collective-permute-start.12) | collective-permute-done | bytes 131104 | tf_op jit(solution)/shard_map/ppermute | solution.py:12
  44.9 3.0 %collective-permute-start.15 = (f32[8,32,128]{2,1,0:T(8,128)S(1)}, f32[8,32,128]{2,1,0:T(8,128)S(1)}, u32[]{:S(2)}, u32[]{:S(2)}) collective-permute-start(f32[8,32,128]{2,1,0:T(8,128)S(1)} %add.231), channel_id=1, source_target_pairs={{0,64},{16,80},{32,96},{48,112},{64,0},{80,16},{96,32},{112,48},{1... | collective-permute-start | bytes 393224 | tf_op jit(solution)/shard_map/ppermute | solution.py:12
  47.9 0.8 collective-permute-start.14
  49.4 0.9 collective-permute-done.15
  50.3 2.9 %collective-permute-done.14 = f32[8,32,128]{2,1,0:T(8,128)S(1)} collective-permute-done((f32[8,32,128]{2,1,0:T(8,128)S(1)}, f32[8,32,128]{2,1,0:T(8,128)S(1)}, u32[]{:S(2)}, u32[]{:S(2)}) %collective-permute-start.14) | collective-permute-done | bytes 131104 | tf_op jit(solution)/shard_map/ppermute | solution.py:12
  53.3 0.8 collective-permute-done.13
  54.1 2.7 %collective-permute-start.16 = (f32[8,32,128]{2,1,0:T(8,128)S(1)}, f32[8,32,128]{2,1,0:T(8,128)S(1)}, u32[]{:S(2)}, u32[]{:S(2)}) collective-permute-start(f32[8,32,128]{2,1,0:T(8,128)S(1)} %add_add_fusion.1), channel_id=1, source_target_pairs={{0,16},{16,0},{32,48},{48,32},{64,80},{80,64},{96,112},{112,96},{1... | collective-permute-start | bytes 393224 | tf_op jit(solution)/shard_map/ppermute | solution.py:12
  56.8 1.0 collective-permute-done.16
  59.1 2.5 %collective-permute-start.18 = (f32[32,512]{1,0:T(8,128)S(1)}, f32[32,512]{1,0:T(8,128)S(1)}, u32[]{:S(2)}, u32[]{:S(2)}) collective-permute-start(f32[32,512]{1,0:T(8,128)S(1)} %pad_maximum_fusion.6), channel_id=1, source_target_pairs={{0,12},{1,13},{2,14},{3,15},{4,0},{5,1},{6,2},{7,3},{8,4},{9,5},{1... | collective-permute-start | bytes 196616 | tf_op jit(solution)/shard_map/ppermute | solution.py:12
  61.6 3.2 %collective-permute-start.19 = (f32[32,512]{1,0:T(8,128)S(1)}, f32[32,512]{1,0:T(8,128)S(1)}, u32[]{:S(2)}, u32[]{:S(2)}) collective-permute-start(f32[32,512]{1,0:T(8,128)S(1)} %pad_maximum_fusion.6), channel_id=1, source_target_pairs={{0,8},{1,9},{2,10},{3,11},{4,12},{5,13},{6,14},{7,15},{8,0},{9,1},... | collective-permute-start | bytes 196616 | tf_op jit(solution)/shard_map/ppermute | solution.py:12
  65.3 3.4 %collective-permute-done.19 = f32[32,512]{1,0:T(8,128)S(1)} collective-permute-done((f32[32,512]{1,0:T(8,128)S(1)}, f32[32,512]{1,0:T(8,128)S(1)}, u32[]{:S(2)}, u32[]{:S(2)}) %collective-permute-start.19) | collective-permute-done | bytes 65568 | tf_op jit(solution)/shard_map/ppermute | solution.py:12
  68.7 1.7 %collective-permute-done.17 = f32[32,512]{1,0:T(8,128)S(1)} collective-permute-done((f32[32,512]{1,0:T(8,128)S(1)}, f32[32,512]{1,0:T(8,128)S(1)}, u32[]{:S(2)}, u32[]{:S(2)}) %collective-permute-start.17) | collective-permute-done | bytes 65568 | tf_op jit(solution)/shard_map/ppermute | solution.py:12
  71.6 2.2 %collective-permute-start.20 = (f32[9,32,128]{2,1,0:T(8,128)S(1)}, f32[9,32,128]{2,1,0:T(8,128)S(1)}, u32[]{:S(2)}, u32[]{:S(2)}) collective-permute-start(f32[9,32,128]{2,1,0:T(8,128)S(1)} %pad_maximum_fusion.4), channel_id=1, source_target_pairs={{0,16},{16,0},{32,48},{48,32},{64,80},{80,64},{96,112},{112,96},{1... | collective-permute-start | bytes 442376 | tf_op jit(solution)/shard_map/ppermute | solution.py:12
  73.8 1.0 collective-permute-done.20
  74.8 1.9 %collective-permute-start.21 = (f32[9,32,128]{2,1,0:T(8,128)S(1)}, f32[9,32,128]{2,1,0:T(8,128)S(1)}, u32[]{:S(2)}, u32[]{:S(2)}) collective-permute-start(f32[9,32,128]{2,1,0:T(8,128)S(1)} %fusion.26), channel_id=1, source_target_pairs={{0,128},{16,144},{32,160},{48,176},{64,192},{80,208},{96,224},{112... | collective-permute-start | bytes 442376 | tf_op jit(solution)/shard_map/ppermute | solution.py:12
  76.8 3.9 %collective-permute-done.21 = f32[9,32,128]{2,1,0:T(8,128)S(1)} collective-permute-done((f32[9,32,128]{2,1,0:T(8,128)S(1)}, f32[9,32,128]{2,1,0:T(8,128)S(1)}, u32[]{:S(2)}, u32[]{:S(2)}) %collective-permute-start.21) | collective-permute-done | bytes 147488 | tf_op jit(solution)/shard_map/ppermute | solution.py:12
  80.6 1.6 %collective-permute-start.24 = (f32[9,32,128]{2,1,0:T(8,128)S(1)}, f32[9,32,128]{2,1,0:T(8,128)S(1)}, u32[]{:S(2)}, u32[]{:S(2)}) collective-permute-start(f32[9,32,128]{2,1,0:T(8,128)S(1)} %add.243), channel_id=1, source_target_pairs={{0,64},{16,80},{32,96},{48,112},{64,0},{80,16},{96,32},{112,48},{1... | collective-permute-start | bytes 442376 | tf_op jit(solution)/shard_map/ppermute | solution.py:12
  82.2 1.0 collective-permute-start.23
  83.7 3.0 %collective-permute-done.24 = f32[9,32,128]{2,1,0:T(8,128)S(1)} collective-permute-done((f32[9,32,128]{2,1,0:T(8,128)S(1)}, f32[9,32,128]{2,1,0:T(8,128)S(1)}, u32[]{:S(2)}, u32[]{:S(2)}) %collective-permute-start.24) | collective-permute-done | bytes 147488 | tf_op jit(solution)/shard_map/ppermute | solution.py:12
  86.7 2.1 %collective-permute-done.23 = f32[9,32,128]{2,1,0:T(8,128)S(1)} collective-permute-done((f32[9,32,128]{2,1,0:T(8,128)S(1)}, f32[9,32,128]{2,1,0:T(8,128)S(1)}, u32[]{:S(2)}, u32[]{:S(2)}) %collective-permute-start.23) | collective-permute-done | bytes 147488 | tf_op jit(solution)/shard_map/ppermute | solution.py:12
  88.8 1.7 %collective-permute-done.22 = f32[9,32,128]{2,1,0:T(8,128)S(1)} collective-permute-done((f32[9,32,128]{2,1,0:T(8,128)S(1)}, f32[9,32,128]{2,1,0:T(8,128)S(1)}, u32[]{:S(2)}, u32[]{:S(2)}) %collective-permute-start.22) | collective-permute-done | bytes 147488 | tf_op jit(solution)/shard_map/ppermute | solution.py:12
  90.8 1.5 %collective-permute-start.25 = (f32[8,32,128]{2,1,0:T(8,128)S(1)}, f32[8,32,128]{2,1,0:T(8,128)S(1)}, u32[]{:S(2)}, u32[]{:S(2)}) collective-permute-start(f32[8,32,128]{2,1,0:T(8,128)S(1)} %fusion.27), channel_id=1, source_target_pairs={{0,16},{16,0},{32,48},{48,32},{64,80},{80,64},{96,112},{112,96},{1... | collective-permute-start | bytes 393224 | tf_op jit(solution)/shard_map/ppermute | solution.py:12
  92.2 1.0 collective-permute-done.25
  94.7 1.5 %collective-permute-start.27 = (f32[32,512]{1,0:T(8,128)S(1)}, f32[32,512]{1,0:T(8,128)S(1)}, u32[]{:S(2)}, u32[]{:S(2)}) collective-permute-start(f32[32,512]{1,0:T(8,128)S(1)} %pad_maximum_fusion.7), channel_id=1, source_target_pairs={{0,12},{1,13},{2,14},{3,15},{4,0},{5,1},{6,2},{7,3},{8,4},{9,5},{1... | collective-permute-start | bytes 196616 | tf_op jit(solution)/shard_map/ppermute | solution.py:12
  96.1 2.7 %collective-permute-start.28 = (f32[32,512]{1,0:T(8,128)S(1)}, f32[32,512]{1,0:T(8,128)S(1)}, u32[]{:S(2)}, u32[]{:S(2)}) collective-permute-start(f32[32,512]{1,0:T(8,128)S(1)} %pad_maximum_fusion.7), channel_id=1, source_target_pairs={{0,8},{1,9},{2,10},{3,11},{4,12},{5,13},{6,14},{7,15},{8,0},{9,1},... | collective-permute-start | bytes 196616 | tf_op jit(solution)/shard_map/ppermute | solution.py:12
  98.9 1.6 %collective-permute-start.26 = (f32[32,512]{1,0:T(8,128)S(1)}, f32[32,512]{1,0:T(8,128)S(1)}, u32[]{:S(2)}, u32[]{:S(2)}) collective-permute-start(f32[32,512]{1,0:T(8,128)S(1)} %pad_maximum_fusion.7), channel_id=1, source_target_pairs={{0,4},{1,5},{2,6},{3,7},{4,8},{5,9},{6,10},{7,11},{8,12},{9,13},{1... | collective-permute-start | bytes 196616 | tf_op jit(solution)/shard_map/ppermute | solution.py:12
  100.5 2.7 %collective-permute-done.28 = f32[32,512]{1,0:T(8,128)S(1)} collective-permute-done((f32[32,512]{1,0:T(8,128)S(1)}, f32[32,512]{1,0:T(8,128)S(1)}, u32[]{:S(2)}, u32[]{:S(2)}) %collective-permute-start.28) | collective-permute-done | bytes 65568 | tf_op jit(solution)/shard_map/ppermute | solution.py:12
  103.3 2.6 %collective-permute-done.26 = f32[32,512]{1,0:T(8,128)S(1)} collective-permute-done((f32[32,512]{1,0:T(8,128)S(1)}, f32[32,512]{1,0:T(8,128)S(1)}, u32[]{:S(2)}, u32[]{:S(2)}) %collective-permute-start.26) | collective-permute-done | bytes 65568 | tf_op jit(solution)/shard_map/ppermute | solution.py:12
  108.0 0.7 pad_maximum_fusion.1
  108.8 6.0 %all-to-all-start = ((f32[16,40,128]{2,1,0:T(8,128)}), f32[16,40,128]{2,1,0:T(8,128)S(1)}, u32[]{:S(2)}, u32[]{:S(2)}) async-start(f32[16,40,128]{2,1,0:T(8,128)} %pad_maximum_fusion.1), calls=%async_computation | async-start | bytes 655360 | tf_op jit(solution)/shard_map/all_to_all | solution.py:171
  115.2 7.2 %all-to-all-done = f32[16,40,128]{2,1,0:T(8,128)S(1)} async-done(((f32[16,40,128]{2,1,0:T(8,128)}), f32[16,40,128]{2,1,0:T(8,128)S(1)}, u32[]{:S(2)}, u32[]{:S(2)}) %all-to-all-start) | async-done | bytes 327712 | tf_op jit(solution)/shard_map/all_to_all | solution.py:171
  123.0 1.0 collective-permute-start.29
  124.7 1.4 %collective-permute-start.30 = (f32[64,32]{0,1:T(8,128)S(1)}, f32[64,32]{0,1:T(8,128)S(1)}, u32[]{:S(2)}, u32[]{:S(2)}) collective-permute-start(f32[64,32]{0,1:T(8,128)S(1)} %get-tuple-element.28), channel_id=1, source_target_pairs={{0,2},{1,3},{2,0},{3,1},{4,6},{5,7},{6,4},{7,5},{8,10},{9,11},{10,... | collective-permute-start | bytes 24584 | tf_op jit(solution)/shard_map/ppermute | solution.py:12
  126.1 2.7 %collective-permute-done.30 = f32[64,32]{0,1:T(8,128)S(1)} collective-permute-done((f32[64,32]{0,1:T(8,128)S(1)}, f32[64,32]{0,1:T(8,128)S(1)}, u32[]{:S(2)}, u32[]{:S(2)}) %collective-permute-start.30) | collective-permute-done | bytes 8224 | tf_op jit(solution)/shard_map/ppermute | solution.py:12
  (125 shorter events, 13.3 us)
Async XLA Ops:
  0.6 23.1 %collective-permute-start.8 = (bf16[384,512]{1,0:T(8,128)(2,1)}, bf16[384,512]{1,0:T(8,128)(2,1)S(1)}, u32[]{:S(2)}, u32[]{:S(2)}) collective-permute-start(bf16[384,512]{1,0:T(8,128)(2,1)} %bitcast.180), channel_id=1, source_target_pairs={{0,3},{1,0},{2,1},{3,2},{4,7},{5,4},{6,5},{7,6},{8,11},{9,8},{10,9... | collective-permute-start | bytes 1179656 | tf_op jit(solution)/shard_map/ppermute | solution.py:12
  4.0 22.2 %collective-permute-start.6 = (bf16[384,512]{1,0:T(8,128)(2,1)}, bf16[384,512]{1,0:T(8,128)(2,1)S(1)}, u32[]{:S(2)}, u32[]{:S(2)}) collective-permute-start(bf16[384,512]{1,0:T(8,128)(2,1)} %bitcast.181), channel_id=1, source_target_pairs={{0,1},{1,2},{2,3},{3,0},{4,5},{5,6},{6,7},{7,4},{8,9},{9,10},{10,1... | collective-permute-start | bytes 1179656 | tf_op jit(solution)/shard_map/ppermute | solution.py:12
  6.3 10.4 %collective-permute-start = (f32[32,384]{1,0:T(8,128)S(1)}, f32[32,384]{1,0:T(8,128)S(1)}, u32[]{:S(2)}, u32[]{:S(2)}) collective-permute-start(f32[32,384]{1,0:T(8,128)S(1)} %get-tuple-element.23), channel_id=1, source_target_pairs={{0,1},{1,2},{2,3},{3,0},{4,5},{5,6},{6,7},{7,4},{8,9},{9,10},{10,1... | collective-permute-start | bytes 147464 | tf_op jit(solution)/shard_map/ppermute | solution.py:12
  6.6 10.1 %collective-permute-start.2 = (f32[32,384]{1,0:T(8,128)S(1)}, f32[32,384]{1,0:T(8,128)S(1)}, u32[]{:S(2)}, u32[]{:S(2)}) collective-permute-start(f32[32,384]{1,0:T(8,128)S(1)} %get-tuple-element.24), channel_id=1, source_target_pairs={{0,2},{1,3},{2,0},{3,1},{4,6},{5,7},{6,4},{7,5},{8,10},{9,11},{10,... | collective-permute-start | bytes 147464 | tf_op jit(solution)/shard_map/ppermute | solution.py:12
  10.3 6.5 %collective-permute-start.1 = (f32[32,384]{1,0:T(8,128)S(1)}, f32[32,384]{1,0:T(8,128)S(1)}, u32[]{:S(2)}, u32[]{:S(2)}) collective-permute-start(f32[32,384]{1,0:T(8,128)S(1)} %get-tuple-element.25), channel_id=1, source_target_pairs={{0,3},{1,0},{2,1},{3,2},{4,7},{5,4},{6,5},{7,6},{8,11},{9,8},{10,9... | collective-permute-start | bytes 147464 | tf_op jit(solution)/shard_map/ppermute | solution.py:12
  10.3 23.2 %copy-start = (bf16[1,384,512]{2,1,0:T(8,128)(2,1)S(1)}, bf16[1,384,512]{2,1,0:T(8,128)(2,1)}, u32[]{:S(2)}) copy-start(bf16[1,384,512]{2,1,0:T(8,128)(2,1)} %param.2) | copy-start | bytes 1179652
  16.7 17.6 %collective-permute-start.10 = (bf16[32,512]{1,0:T(8,128)(2,1)S(1)}, bf16[32,512]{1,0:T(8,128)(2,1)S(1)}, u32[]{:S(2)}, u32[]{:S(2)}) collective-permute-start(bf16[32,512]{1,0:T(8,128)(2,1)S(1)} %get-tuple-element.30), channel_id=1, source_target_pairs={{0,2},{1,3},{2,0},{3,1},{4,6},{5,7},{6,4},{7,5},{8,10},{9,11},{10,... | collective-permute-start | bytes 98312 | tf_op jit(solution)/shard_map/ppermute | solution.py:12
  16.8 10.5 %collective-permute-start.5 = (f32[32,384]{1,0:T(8,128)S(1)}, f32[32,384]{1,0:T(8,128)S(1)}, u32[]{:S(2)}, u32[]{:S(2)}) collective-permute-start(f32[32,384]{1,0:T(8,128)S(1)} %fusion.46), channel_id=1, source_target_pairs={{0,8},{1,9},{2,10},{3,11},{4,12},{5,13},{6,14},{7,15},{8,0},{9,1},... | collective-permute-start | bytes 147464 | tf_op jit(solution)/shard_map/ppermute | solution.py:12
  23.8 4.1 %collective-permute-start.4 = (f32[32,384]{1,0:T(8,128)S(1)}, f32[32,384]{1,0:T(8,128)S(1)}, u32[]{:S(2)}, u32[]{:S(2)}) collective-permute-start(f32[32,384]{1,0:T(8,128)S(1)} %fusion.46), channel_id=1, source_target_pairs={{0,12},{1,13},{2,14},{3,15},{4,0},{5,1},{6,2},{7,3},{8,4},{9,5},{1... | collective-permute-start | bytes 147464 | tf_op jit(solution)/shard_map/ppermute | solution.py:12
  23.8 5.2 %collective-permute-start.3 = (f32[32,384]{1,0:T(8,128)S(1)}, f32[32,384]{1,0:T(8,128)S(1)}, u32[]{:S(2)}, u32[]{:S(2)}) collective-permute-start(f32[32,384]{1,0:T(8,128)S(1)} %fusion.46), channel_id=1, source_target_pairs={{0,4},{1,5},{2,6},{3,7},{4,8},{5,9},{6,10},{7,11},{8,12},{9,13},{1... | collective-permute-start | bytes 147464 | tf_op jit(solution)/shard_map/ppermute | solution.py:12
  26.2 5.2 %collective-permute-start.9 = (bf16[224,512]{1,0:T(8,128)(2,1)S(1)}, bf16[224,512]{1,0:T(8,128)(2,1)S(1)}, u32[]{:S(2)}, u32[]{:S(2)}) collective-permute-start(bf16[224,512]{1,0:T(8,128)(2,1)S(1)} %pad_maximum_fusion.3), channel_id=1, source_target_pairs={{0,3},{1,0},{2,1},{3,2},{4,7},{5,4},{6,5},{7,6},{8,11},{9,8},{10,9... | collective-permute-start | bytes 688136 | tf_op jit(solution)/shard_map/ppermute | solution.py:12
  27.3 6.2 %collective-permute-start.7 = (bf16[224,512]{1,0:T(8,128)(2,1)S(1)}, bf16[224,512]{1,0:T(8,128)(2,1)S(1)}, u32[]{:S(2)}, u32[]{:S(2)}) collective-permute-start(bf16[224,512]{1,0:T(8,128)(2,1)S(1)} %pad_maximum_fusion.2), channel_id=1, source_target_pairs={{0,1},{1,2},{2,3},{3,0},{4,5},{5,6},{6,7},{7,4},{8,9},{9,10},{10,1... | collective-permute-start | bytes 688136 | tf_op jit(solution)/shard_map/ppermute | solution.py:12
  34.4 5.7 %collective-permute-start.11 = (f32[8,32,128]{2,1,0:T(8,128)S(1)}, f32[8,32,128]{2,1,0:T(8,128)S(1)}, u32[]{:S(2)}, u32[]{:S(2)}) collective-permute-start(f32[8,32,128]{2,1,0:T(8,128)S(1)} %bitcast.197), channel_id=1, source_target_pairs={{0,16},{16,0},{32,48},{48,32},{64,80},{80,64},{96,112},{112,96},{1... | collective-permute-start | bytes 393224 | tf_op jit(solution)/shard_map/ppermute | solution.py:12
  40.1 4.8 %collective-permute-start.12 = (f32[8,32,128]{2,1,0:T(8,128)S(1)}, f32[8,32,128]{2,1,0:T(8,128)S(1)}, u32[]{:S(2)}, u32[]{:S(2)}) collective-permute-start(f32[8,32,128]{2,1,0:T(8,128)S(1)} %bitcast_add_fusion.1), channel_id=1, source_target_pairs={{0,128},{16,144},{32,160},{48,176},{64,192},{80,208},{96,224},{112... | collective-permute-start | bytes 393224 | tf_op jit(solution)/shard_map/ppermute | solution.py:12
  44.9 5.4 %collective-permute-start.15 = (f32[8,32,128]{2,1,0:T(8,128)S(1)}, f32[8,32,128]{2,1,0:T(8,128)S(1)}, u32[]{:S(2)}, u32[]{:S(2)}) collective-permute-start(f32[8,32,128]{2,1,0:T(8,128)S(1)} %add.231), channel_id=1, source_target_pairs={{0,64},{16,80},{32,96},{48,112},{64,0},{80,16},{96,32},{112,48},{1... | collective-permute-start | bytes 393224 | tf_op jit(solution)/shard_map/ppermute | solution.py:12
  47.9 5.4 %collective-permute-start.14 = (f32[8,32,128]{2,1,0:T(8,128)S(1)}, f32[8,32,128]{2,1,0:T(8,128)S(1)}, u32[]{:S(2)}, u32[]{:S(2)}) collective-permute-start(f32[8,32,128]{2,1,0:T(8,128)S(1)} %add.231), channel_id=1, source_target_pairs={{0,96},{16,112},{32,0},{48,16},{64,32},{80,48},{96,64},{112,80},{1... | collective-permute-start | bytes 393224 | tf_op jit(solution)/shard_map/ppermute | solution.py:12
  48.7 5.3 %collective-permute-start.13 = (f32[8,32,128]{2,1,0:T(8,128)S(1)}, f32[8,32,128]{2,1,0:T(8,128)S(1)}, u32[]{:S(2)}, u32[]{:S(2)}) collective-permute-start(f32[8,32,128]{2,1,0:T(8,128)S(1)} %add.231), channel_id=1, source_target_pairs={{0,32},{16,48},{32,64},{48,80},{64,96},{80,112},{96,0},{112,16},{1... | collective-permute-start | bytes 393224 | tf_op jit(solution)/shard_map/ppermute | solution.py:12
  54.1 3.7 %collective-permute-start.16 = (f32[8,32,128]{2,1,0:T(8,128)S(1)}, f32[8,32,128]{2,1,0:T(8,128)S(1)}, u32[]{:S(2)}, u32[]{:S(2)}) collective-permute-start(f32[8,32,128]{2,1,0:T(8,128)S(1)} %add_add_fusion.1), channel_id=1, source_target_pairs={{0,16},{16,0},{32,48},{48,32},{64,80},{80,64},{96,112},{112,96},{1... | collective-permute-start | bytes 393224 | tf_op jit(solution)/shard_map/ppermute | solution.py:12
  59.1 6.2 %collective-permute-start.18 = (f32[32,512]{1,0:T(8,128)S(1)}, f32[32,512]{1,0:T(8,128)S(1)}, u32[]{:S(2)}, u32[]{:S(2)}) collective-permute-start(f32[32,512]{1,0:T(8,128)S(1)} %pad_maximum_fusion.6), channel_id=1, source_target_pairs={{0,12},{1,13},{2,14},{3,15},{4,0},{5,1},{6,2},{7,3},{8,4},{9,5},{1... | collective-permute-start | bytes 196616 | tf_op jit(solution)/shard_map/ppermute | solution.py:12
  61.6 7.1 %collective-permute-start.19 = (f32[32,512]{1,0:T(8,128)S(1)}, f32[32,512]{1,0:T(8,128)S(1)}, u32[]{:S(2)}, u32[]{:S(2)}) collective-permute-start(f32[32,512]{1,0:T(8,128)S(1)} %pad_maximum_fusion.6), channel_id=1, source_target_pairs={{0,8},{1,9},{2,10},{3,11},{4,12},{5,13},{6,14},{7,15},{8,0},{9,1},... | collective-permute-start | bytes 196616 | tf_op jit(solution)/shard_map/ppermute | solution.py:12
  64.9 5.6 %collective-permute-start.17 = (f32[32,512]{1,0:T(8,128)S(1)}, f32[32,512]{1,0:T(8,128)S(1)}, u32[]{:S(2)}, u32[]{:S(2)}) collective-permute-start(f32[32,512]{1,0:T(8,128)S(1)} %pad_maximum_fusion.6), channel_id=1, source_target_pairs={{0,4},{1,5},{2,6},{3,7},{4,8},{5,9},{6,10},{7,11},{8,12},{9,13},{1... | collective-permute-start | bytes 196616 | tf_op jit(solution)/shard_map/ppermute | solution.py:12
  71.6 3.2 %collective-permute-start.20 = (f32[9,32,128]{2,1,0:T(8,128)S(1)}, f32[9,32,128]{2,1,0:T(8,128)S(1)}, u32[]{:S(2)}, u32[]{:S(2)}) collective-permute-start(f32[9,32,128]{2,1,0:T(8,128)S(1)} %pad_maximum_fusion.4), channel_id=1, source_target_pairs={{0,16},{16,0},{32,48},{48,32},{64,80},{80,64},{96,112},{112,96},{1... | collective-permute-start | bytes 442376 | tf_op jit(solution)/shard_map/ppermute | solution.py:12
  74.8 5.8 %collective-permute-start.21 = (f32[9,32,128]{2,1,0:T(8,128)S(1)}, f32[9,32,128]{2,1,0:T(8,128)S(1)}, u32[]{:S(2)}, u32[]{:S(2)}) collective-permute-start(f32[9,32,128]{2,1,0:T(8,128)S(1)} %fusion.26), channel_id=1, source_target_pairs={{0,128},{16,144},{32,160},{48,176},{64,192},{80,208},{96,224},{112... | collective-permute-start | bytes 442376 | tf_op jit(solution)/shard_map/ppermute | solution.py:12
  80.6 6.1 %collective-permute-start.24 = (f32[9,32,128]{2,1,0:T(8,128)S(1)}, f32[9,32,128]{2,1,0:T(8,128)S(1)}, u32[]{:S(2)}, u32[]{:S(2)}) collective-permute-start(f32[9,32,128]{2,1,0:T(8,128)S(1)} %add.243), channel_id=1, source_target_pairs={{0,64},{16,80},{32,96},{48,112},{64,0},{80,16},{96,32},{112,48},{1... | collective-permute-start | bytes 442376 | tf_op jit(solution)/shard_map/ppermute | solution.py:12
  82.2 6.6 %collective-permute-start.23 = (f32[9,32,128]{2,1,0:T(8,128)S(1)}, f32[9,32,128]{2,1,0:T(8,128)S(1)}, u32[]{:S(2)}, u32[]{:S(2)}) collective-permute-start(f32[9,32,128]{2,1,0:T(8,128)S(1)} %add.243), channel_id=1, source_target_pairs={{0,96},{16,112},{32,0},{48,16},{64,32},{80,48},{96,64},{112,80},{1... | collective-permute-start | bytes 442376 | tf_op jit(solution)/shard_map/ppermute | solution.py:12
  83.2 7.3 %collective-permute-start.22 = (f32[9,32,128]{2,1,0:T(8,128)S(1)}, f32[9,32,128]{2,1,0:T(8,128)S(1)}, u32[]{:S(2)}, u32[]{:S(2)}) collective-permute-start(f32[9,32,128]{2,1,0:T(8,128)S(1)} %add.243), channel_id=1, source_target_pairs={{0,32},{16,48},{32,64},{48,80},{64,96},{80,112},{96,0},{112,16},{1... | collective-permute-start | bytes 442376 | tf_op jit(solution)/shard_map/ppermute | solution.py:12
  90.8 2.5 %collective-permute-start.25 = (f32[8,32,128]{2,1,0:T(8,128)S(1)}, f32[8,32,128]{2,1,0:T(8,128)S(1)}, u32[]{:S(2)}, u32[]{:S(2)}) collective-permute-start(f32[8,32,128]{2,1,0:T(8,128)S(1)} %fusion.27), channel_id=1, source_target_pairs={{0,16},{16,0},{32,48},{48,32},{64,80},{80,64},{96,112},{112,96},{1... | collective-permute-start | bytes 393224 | tf_op jit(solution)/shard_map/ppermute | solution.py:12
  94.7 5.9 %collective-permute-start.27 = (f32[32,512]{1,0:T(8,128)S(1)}, f32[32,512]{1,0:T(8,128)S(1)}, u32[]{:S(2)}, u32[]{:S(2)}) collective-permute-start(f32[32,512]{1,0:T(8,128)S(1)} %pad_maximum_fusion.7), channel_id=1, source_target_pairs={{0,12},{1,13},{2,14},{3,15},{4,0},{5,1},{6,2},{7,3},{8,4},{9,5},{1... | collective-permute-start | bytes 196616 | tf_op jit(solution)/shard_map/ppermute | solution.py:12
  96.1 7.1 %collective-permute-start.28 = (f32[32,512]{1,0:T(8,128)S(1)}, f32[32,512]{1,0:T(8,128)S(1)}, u32[]{:S(2)}, u32[]{:S(2)}) collective-permute-start(f32[32,512]{1,0:T(8,128)S(1)} %pad_maximum_fusion.7), channel_id=1, source_target_pairs={{0,8},{1,9},{2,10},{3,11},{4,12},{5,13},{6,14},{7,15},{8,0},{9,1},... | collective-permute-start | bytes 196616 | tf_op jit(solution)/shard_map/ppermute | solution.py:12
  98.9 7.0 %collective-permute-start.26 = (f32[32,512]{1,0:T(8,128)S(1)}, f32[32,512]{1,0:T(8,128)S(1)}, u32[]{:S(2)}, u32[]{:S(2)}) collective-permute-start(f32[32,512]{1,0:T(8,128)S(1)} %pad_maximum_fusion.7), channel_id=1, source_target_pairs={{0,4},{1,5},{2,6},{3,7},{4,8},{5,9},{6,10},{7,11},{8,12},{9,13},{1... | collective-permute-start | bytes 196616 | tf_op jit(solution)/shard_map/ppermute | solution.py:12
  108.8 13.6 %all-to-all-start = ((f32[16,40,128]{2,1,0:T(8,128)}), f32[16,40,128]{2,1,0:T(8,128)S(1)}, u32[]{:S(2)}, u32[]{:S(2)}) async-start(f32[16,40,128]{2,1,0:T(8,128)} %pad_maximum_fusion.1), calls=%async_computation | async-start | bytes 655360 | tf_op jit(solution)/shard_map/all_to_all | solution.py:171
  123.0 3.1 %collective-permute-start.29 = (f32[64,32]{0,1:T(8,128)S(1)}, f32[64,32]{0,1:T(8,128)S(1)}, u32[]{:S(2)}, u32[]{:S(2)}) collective-permute-start(f32[64,32]{0,1:T(8,128)S(1)} %get-tuple-element.27), channel_id=1, source_target_pairs={{0,3},{1,0},{2,1},{3,2},{4,7},{5,4},{6,5},{7,6},{8,11},{9,8},{10,9... | collective-permute-start | bytes 24584 | tf_op jit(solution)/shard_map/ppermute | solution.py:12
  124.0 4.7 %collective-permute-start.31 = (f32[64,32]{0,1:T(8,128)S(1)}, f32[64,32]{0,1:T(8,128)S(1)}, u32[]{:S(2)}, u32[]{:S(2)}) collective-permute-start(f32[64,32]{0,1:T(8,128)S(1)} %get-tuple-element.26), channel_id=1, source_target_pairs={{0,1},{1,2},{2,3},{3,0},{4,5},{5,6},{6,7},{7,4},{8,9},{9,10},{10,1... | collective-permute-start | bytes 24584 | tf_op jit(solution)/shard_map/ppermute | solution.py:12
  124.7 4.1 %collective-permute-start.30 = (f32[64,32]{0,1:T(8,128)S(1)}, f32[64,32]{0,1:T(8,128)S(1)}, u32[]{:S(2)}, u32[]{:S(2)}) collective-permute-start(f32[64,32]{0,1:T(8,128)S(1)} %get-tuple-element.28), channel_id=1, source_target_pairs={{0,2},{1,3},{2,0},{3,1},{4,6},{5,7},{6,4},{7,5},{8,10},{9,11},{10,... | collective-permute-start | bytes 24584 | tf_op jit(solution)/shard_map/ppermute | solution.py:12

commit v6 on v5

--- a/solution.py
+++ b/solution.py
@@ -68,27 +68,8 @@
     return blocks.transpose(1, 0, 2).reshape(blocks.shape[1], -1)
 
 
-def halves(blocks, core):
-    grid = blocks.reshape((2, 2, 4) + blocks.shape[1:])
-    own, other = pick(grid, core, 1), pick(grid, 1 - core, 1)
-    return own.reshape((8,) + blocks.shape[1:]), other.reshape((8,) + blocks.shape[1:])
-
-
-def whole(own, core):
-    other = core_move(own)
-    shape = own.shape[1:]
-    own, other = own.reshape((2, 1, 4) + shape), other.reshape((2, 1, 4) + shape)
-    pair = jnp.where(core == 0, jnp.concatenate([own, other], 1), jnp.concatenate([other, own], 1))
-    return pair.reshape((16,) + shape)
-
-
-def task_half_sum(blocks, extra, core):
-    own, other = halves(blocks, core)
-    if extra is not None:
-        own, other = jnp.concatenate([own, extra[None]]), jnp.concatenate([other, extra[None]])
-    own = own + core_move(other)
-    own = own + zlo_move(own)
-    return sum_over(own, y_move)
+def zlo_y_sum(blocks):
+    return sum_over(blocks + zlo_move(blocks), y_move)
 
 
 def with_scalars(value, scalars):
@@ -129,55 +110,82 @@
     far_right = x_move(jnp.concatenate([from_right[half:], pick(turned, (x + 3) % 4)]), 3)
 
     far = jnp.concatenate([far_left[:half], far_right[:half]])
-    xs = jnp.concatenate([own_x, from_left, far, from_right], axis=1)
+    xs = lax.optimization_barrier(jnp.concatenate([own_x, from_left, far, from_right], axis=1))
     ws = jnp.concatenate([pick(turned, x), far_left[half:], ws_far, far_right[half:]], axis=1)
     wide_x = xs.astype(jnp.float32)
     diag = diag_scale * jnp.sum(wide_x * wide_x, axis=0, keepdims=True)
 
-    def image_part(y, vector):
-        return blocks_of(gram_scale * product(y, xs, 0) + diag * vector)
-
-    part = task_half_sum(image_part(outputs, ws.astype(jnp.float32)), None, core)
-    target_blocks = whole(part, core)
+    part = blocks_of(gram_scale * product(outputs, xs, 0) + diag * ws.astype(jnp.float32))
+    part = part.reshape(16, 2, 16, 128)
+    other = core_move(pick(part, 1 - core, 1))
+    target_blocks = zlo_y_sum(pick(part, core, 1) + other)
     target = flat(target_blocks)
 
+    xs_other = core_move(xs)
+    xs_other, diag = lax.optimization_barrier((xs_other, diag))
+    wide_x = xs_other.astype(jnp.float32)
+    diag = diag + diag_scale * jnp.sum(wide_x * wide_x, axis=0, keepdims=True)
+
+    def outputs_of(vector):
+        return jnp.concatenate([product(vector, xs, 1), product(vector, xs_other, 1)], axis=1)
+
+    def image_of(y, vector):
+        both = product(y[:, :tokens], xs, 0) + product(y[:, tokens:], xs_other, 0)
+        return gram_scale * both + diag * vector
+
+    def columns_of(rows, n):
+        return rows[:, : 2 * tokens], *(rows[:, 2 * tokens + i : 2 * tokens + i + 1] for i in range(n))
+
     scalars = [total(target * target), total(diag * target * target)]
-    rows = sum_over(with_scalars(product(target, xs, 1), scalars), zhi_move)
-    image0, norm0, weigh0 = rows[:, :tokens], rows[:, tokens : tokens + 1], rows[:, tokens + 1 : tokens + 2]
-    curve = jnp.broadcast_to(gram_scale * total(image0 * image0) + weigh0, (32, 128))
-    part = task_half_sum(image_part(image0, target), curve, core)
-    alpha0 = norm0 / part[8][:, :1]
-    residual_half = halves(target_blocks, core)[0] - alpha0[None] * part[:8]
-    residual_blocks = whole(residual_half, core)
+    rows = sum_over(with_scalars(outputs_of(target), scalars), zhi_move)
+    image0, norm0, weigh0 = columns_of(rows, 2)
+    curve = jnp.broadcast_to(gram_scale * total(image0 * image0) + weigh0, (1, 16, 128))
+    part = blocks_of(image_of(image0, target))
+    part = zlo_y_sum(jnp.concatenate([part, curve]))
+    alpha0 = norm0 / part[16][:, :1]
+    residual_blocks = target_blocks - alpha0[None] * part[:16]
     residual = flat(residual_blocks)
 
     scalars = [total(residual * residual), total(diag * residual * residual), total(diag * residual * target)]
-    rows = sum_over(with_scalars(product(residual, xs, 1), scalars), zhi_move)
-    norm1, weigh1, cross = (rows[:, tokens + i : tokens + i + 1] for i in range(3))
+    rows = sum_over(with_scalars(outputs_of(residual), scalars), zhi_move)
+    image1, norm1, weigh1, cross = columns_of(rows, 3)
     beta = norm1 / (norm0 + EPS)
-    image1 = rows[:, :tokens] + beta * image0
+    image1 = image1 + beta * image0
     direction = residual + beta * target
     curve = gram_scale * total(image1 * image1) + weigh1 + 2.0 * beta * cross + beta * beta * weigh0
 
-    def side_by_side(blocks):
-        return blocks.transpose(2, 0, 1).reshape(-1, 128)
-
-    def per_lane(column):
-        return jnp.tile(column[:, 0], 4)[None]
-
-    part = gram_scale * product(image1, xs, 0) + diag * direction
-    part = side_by_side(part.reshape(32, 4, width).transpose(1, 0, 2)).reshape(16, 32, 128)
-    curve = jnp.broadcast_to(per_lane(curve)[None], (16, 8, 128))
-    total_part = jnp.sum(lax.all_to_all(jnp.concatenate([part, curve], axis=1), "task", 0, 0), axis=0)
-
-    def mine_of(blocks):
-        four = pick(blocks.reshape(4, 4, 32, 128), task // 4, 1)
-        return side_by_side(lax.dynamic_slice_in_dim(four, 32 * (task % 4), 32, 2))
-
-    my_target, my_residual = mine_of(target_blocks), mine_of(residual_blocks)
-    alpha1 = per_lane(norm1) / total_part[32:33]
+    part = image_of(image1, direction)
+    part = part.reshape(16, 4, width).transpose(1, 0, 2).reshape(64, width).T.reshape(16, 2, 16, 64)
+    part = part.transpose(0, 2, 1, 3).reshape(16, 16, 128)
+    curve = jnp.broadcast_to(jnp.tile(curve[:, 0], 8)[None, None], (16, 8, 128))
+    part = lax.all_to_all(jnp.concatenate([part, curve], axis=1), "task", 0, 0)
+    part = jnp.sum(part.reshape(8, 2, 24, 128), axis=0)
+    curve = part[:, 16, :16].reshape(32)
+    part = part[:, :16].reshape(2, 16, 2, 4, 16).transpose(2, 1, 3, 0, 4).reshape(32, 128)
+
+    def rows_of(device):
+        def four(blocks):
+            four = pick(blocks.reshape(4, 4, 16, 128), device // 4, 1)
+            return lax.dynamic_slice_in_dim(four, 32 * (device % 4), 32, 2).reshape(64, 32)
+
+        wide = [jnp.broadcast_to(column, (16, 32)) for column in (alpha0, beta, norm1)]
+        return jnp.concatenate([four(target_blocks), four(residual_blocks)] + wide)
+
+    other = core_move(rows_of(task ^ 1))
+    own = rows_of(task)
+    both = jnp.where(core == 0, jnp.stack([own, other]), jnp.stack([other, own]))
+
+    def side_by_side(value):
+        return value.reshape(2, 4, 16, 32).transpose(3, 1, 0, 2).reshape(32, 128)
+
+    def per_lane(vector):
+        return jnp.tile(vector, 4)[None]
+
+    my_target, my_residual = side_by_side(both[:, :64]), side_by_side(both[:, 64:128])
+    alpha0, beta, norm1 = (both[:, 128 + 16 * i : 144 + 16 * i, 0].reshape(32) for i in range(3))
+    alpha1 = per_lane(norm1 / curve)
     merged = per_lane(alpha0) * my_target + alpha1 * (my_residual + per_lane(beta) * my_target)
-    both = jnp.concatenate([merged, my_residual - alpha1 * total_part[:32]])
+    both = jnp.concatenate([merged, my_residual - alpha1 * part])
 
     two, three, one = staged(lambda k: both[:, 128 - 32 * k : 160 - 32 * k], x_move)
     groups = jnp.stack([both[:, :32], three, two, one])

time: 132 us -> 128 us (0.970); the launches traced: 130 us -> 128 us
  waiting for transfers between devices: 55.5 us -> 44.3 us
  local copies, waits for them, and re-layouts: 4.8 us -> 9.55 us
  other arithmetic: 4.66 us -> 7.77 us
  matrix products: 3.69 us -> 5.48 us
    ppermute x32 -> x31, waiting for transfers between devices: 48.3 us -> 38.7 us  [moved(): return lax.ppermute(value, axis, [(i, to(i)) for i in range(16)])]
    reshape x1 -> x9, local copies, waits for them, and re-layouts: 0.02 us -> 4.05 us  [the longest x4 3.46 us: four(): lax.dynamic_slice_in_dim(four, 32 * (device % 4), 32, 2).reshape(64, 32)]
    all_to_all x1, starting transfers between devices: 5.96 us -> 3.64 us  [on_device(): part = lax.all_to_all(jnp.concatenate([part, curve], axis=1), 'task', 0, 0)]
    add x4 -> x3, other arithmetic: 0.11 us -> 1.98 us  [sum_over(): return value + one + three + two]
    dot_general x5 -> x9, matrix products: 2.41 us -> 4.2 us  [product(): lax.dot_general(pieces(value), x, (((1,), (dim,)), ((), ())), preferred_e...]
    all_to_all x1, waiting for transfers between devices: 7.19 us -> 5.65 us  [on_device(): part = lax.all_to_all(jnp.concatenate([part, curve], axis=1), 'task', 0, 0)]
    unnamed x13 -> x38, local copies, waits for them, and re-layouts: 1.33 us -> 2.79 us
    slice x3 -> x1, local copies, waits for them, and re-layouts: 1.45 us -> 0.08 us  [on_device(): return (result[:32], result[32:])]
  transfers between devices with their start and end apart: 33 -> 32, of which waited for: 22 -> 16; matrix products, arithmetic and copies ran while one was open for 3% -> 8% of each run, Pallas kernels for 0% -> 0%
where the time goes in v6:
time: 128 us
  starting transfers between devices  59.4 us (46%)
  waiting for transfers between devices  44.3 us (35%)
  local copies, waits for them, and re-layouts  9.55 us (7%)
  other arithmetic  7.77 us (6%)
  matrix products  5.48 us (4%)
  between operations  1.34 us (1%)
    ppermute x31, starting transfers between devices, moved(): return lax.ppermute(value, axis, [(i, to(i)) for i in range(16)])  55.8 us
    ppermute x31, waiting for transfers between devices, moved(): return lax.ppermute(value, axis, [(i, to(i)) for i in range(16)])  38.7 us
    all_to_all x1, waiting for transfers between devices, on_device(): part = lax.all_to_all(jnp.concatenate([part, curve], axis=1), 'task', 0, 0)  5.65 us
    dot_general x9, matrix products, product(): lax.dot_general(pieces(value), x, (((1,), (dim,)), ((), ())), preferred_e...  4.2 us
    all_to_all x1, starting transfers between devices, on_device(): part = lax.all_to_all(jnp.concatenate([part, curve], axis=1), 'task', 0, 0)  3.64 us
    reshape x4, local copies, waits for them, and re-layouts, four(): lax.dynamic_slice_in_dim(four, 32 * (device % 4), 32, 2).reshape(64, 32)  3.46 us
    unnamed x38, local copies, waits for them, and re-layouts  2.79 us
  transfers between devices with their start and end apart: 32, of which 16 were waited for; matrix products, arithmetic and copies ran while one was open for 8% of the time, Pallas kernels for 0%

profile of v6, /device:TPU:1, one launch (start us, length us, event | category | flops | bytes accessed | tf_op | source)
XLA Modules:
  0.0 127.9 jit_solution(14009322212766940383)
XLA Ops:
  0.6 2.1 %collective-permute-start.6 = (bf16[384,512]{1,0:T(8,128)(2,1)}, bf16[384,512]{1,0:T(8,128)(2,1)S(1)}, u32[]{:S(2)}, u32[]{:S(2)}) collective-permute-start(bf16[384,512]{1,0:T(8,128)(2,1)} %bitcast.188), channel_id=1, source_target_pairs={{0,1},{1,2},{2,3},{3,0},{4,5},{5,6},{6,7},{7,4},{8,9},{9,10},{10,1... | collective-permute-start | bytes 1179656 | tf_op jit(solution)/shard_map/ppermute | solution.py:12
  2.7 1.4 %collective-permute-start.8 = (bf16[384,512]{1,0:T(8,128)(2,1)}, bf16[384,512]{1,0:T(8,128)(2,1)S(1)}, u32[]{:S(2)}, u32[]{:S(2)}) collective-permute-start(bf16[384,512]{1,0:T(8,128)(2,1)} %bitcast.189), channel_id=1, source_target_pairs={{0,3},{1,0},{2,1},{3,2},{4,7},{5,4},{6,5},{7,6},{8,11},{9,8},{10,9... | collective-permute-start | bytes 1179656 | tf_op jit(solution)/shard_map/ppermute | solution.py:12
  4.1 1.0 copy.87
  5.1 1.3 %fusion = f32[4,32,384]{2,1,0:T(8,128)S(1)} fusion(bf16[4,32,512]{2,1,0:T(8,128)(2,1)S(1)} %bitcast.191, bf16[1,384,512]{2,1,0:T(8,128)(2,1)} %param.2), kind=kOutput, calls=%fused_computation.3 | convolution fusion | flops 50331648 | bytes 720896 | tf_op jit(solution)/shard_map/dot_general | solution.py:98
  6.6 2.6 %collective-permute-start.1 = (f32[32,384]{1,0:T(8,128)S(1)}, f32[32,384]{1,0:T(8,128)S(1)}, u32[]{:S(2)}, u32[]{:S(2)}) collective-permute-start(f32[32,384]{1,0:T(8,128)S(1)} %get-tuple-element.34), channel_id=1, source_target_pairs={{0,3},{1,0},{2,1},{3,2},{4,7},{5,4},{6,5},{7,6},{8,11},{9,8},{10,9... | collective-permute-start | bytes 147464 | tf_op jit(solution)/shard_map/ppermute | solution.py:12
  9.7 2.2 %collective-permute-done = f32[32,384]{1,0:T(8,128)S(1)} collective-permute-done((f32[32,384]{1,0:T(8,128)S(1)}, f32[32,384]{1,0:T(8,128)S(1)}, u32[]{:S(2)}, u32[]{:S(2)}) %collective-permute-start) | collective-permute-done | bytes 49184 | tf_op jit(solution)/shard_map/ppermute | solution.py:12
  11.9 3.9 %collective-permute-start.10 = (bf16[32,512]{1,0:T(8,128)(2,1)S(1)}, bf16[32,512]{1,0:T(8,128)(2,1)S(1)}, u32[]{:S(2)}, u32[]{:S(2)}) collective-permute-start(bf16[32,512]{1,0:T(8,128)(2,1)S(1)} %get-tuple-element.49), channel_id=1, source_target_pairs={{0,2},{1,3},{2,0},{3,1},{4,6},{5,7},{6,4},{7,5},{8,10},{9,11},{10,... | collective-permute-start | bytes 98312 | tf_op jit(solution)/shard_map/ppermute | solution.py:12
  15.8 3.0 %collective-permute-start.3 = (f32[32,384]{1,0:T(8,128)S(1)}, f32[32,384]{1,0:T(8,128)S(1)}, u32[]{:S(2)}, u32[]{:S(2)}) collective-permute-start(f32[32,384]{1,0:T(8,128)S(1)} %fusion.34), channel_id=1, source_target_pairs={{0,4},{1,5},{2,6},{3,7},{4,8},{5,9},{6,10},{7,11},{8,12},{9,13},{1... | collective-permute-start | bytes 147464 | tf_op jit(solution)/shard_map/ppermute | solution.py:12
  18.8 3.1 %collective-permute-start.4 = (f32[32,384]{1,0:T(8,128)S(1)}, f32[32,384]{1,0:T(8,128)S(1)}, u32[]{:S(2)}, u32[]{:S(2)}) collective-permute-start(f32[32,384]{1,0:T(8,128)S(1)} %fusion.34), channel_id=1, source_target_pairs={{0,12},{1,13},{2,14},{3,15},{4,0},{5,1},{6,2},{7,3},{8,4},{9,5},{1... | collective-permute-start | bytes 147464 | tf_op jit(solution)/shard_map/ppermute | solution.py:12
  22.0 4.4 %collective-permute-start.5 = (f32[32,384]{1,0:T(8,128)S(1)}, f32[32,384]{1,0:T(8,128)S(1)}, u32[]{:S(2)}, u32[]{:S(2)}) collective-permute-start(f32[32,384]{1,0:T(8,128)S(1)} %fusion.34), channel_id=1, source_target_pairs={{0,8},{1,9},{2,10},{3,11},{4,12},{5,13},{6,14},{7,15},{8,0},{9,1},... | collective-permute-start | bytes 147464 | tf_op jit(solution)/shard_map/ppermute | solution.py:12
  27.1 2.2 %collective-permute-start.9 = (bf16[224,512]{1,0:T(8,128)(2,1)S(1)}, bf16[224,512]{1,0:T(8,128)(2,1)S(1)}, u32[]{:S(2)}, u32[]{:S(2)}) collective-permute-start(bf16[224,512]{1,0:T(8,128)(2,1)S(1)} %pad_maximum_fusion.2), channel_id=1, source_target_pairs={{0,3},{1,0},{2,1},{3,2},{4,7},{5,4},{6,5},{7,6},{8,11},{9,8},{10,9... | collective-permute-start | bytes 688136 | tf_op jit(solution)/shard_map/ppermute | solution.py:12
  29.3 3.2 %collective-permute-done.7 = bf16[224,512]{1,0:T(8,128)(2,1)S(1)} collective-permute-done((bf16[224,512]{1,0:T(8,128)(2,1)S(1)}, bf16[224,512]{1,0:T(8,128)(2,1)S(1)}, u32[]{:S(2)}, u32[]{:S(2)}) %collective-permute-start.7) | collective-permute-done | bytes 229408 | tf_op jit(solution)/shard_map/ppermute | solution.py:12
  32.8 4.2 %collective-permute-start.16 = (bf16[384,2048]{1,0:T(8,128)(2,1)S(1)}, bf16[384,2048]{1,0:T(8,128)(2,1)S(1)}, u32[]{:S(2)}, u32[]{:S(2)}) collective-permute-start(bf16[384,2048]{1,0:T(8,128)(2,1)S(1)} %pad_maximum_fusion), channel_id=1, source_target_pairs={{0,16},{16,0},{32,48},{48,32},{64,80},{80,64},{96,112},{112,96},{1... | collective-permute-start | bytes 4718600 | tf_op jit(solution)/shard_map/ppermute | solution.py:12
  38.2 2.1 %collective-permute-done.11 = f32[16,16,128]{2,1,0:T(8,128)S(1)} collective-permute-done((f32[16,16,128]{2,1,0:T(8,128)S(1)}, f32[16,16,128]{2,1,0:T(8,128)S(1)}, u32[]{:S(2)}, u32[]{:S(2)}) %collective-permute-start.11) | collective-permute-done | bytes 131104 | tf_op jit(solution)/shard_map/ppermute | solution.py:12
  40.3 0.8 collective-permute-start.12
  41.1 3.9 %collective-permute-done.12 = f32[16,16,128]{2,1,0:T(8,128)S(1)} collective-permute-done((f32[16,16,128]{2,1,0:T(8,128)S(1)}, f32[16,16,128]{2,1,0:T(8,128)S(1)}, u32[]{:S(2)}, u32[]{:S(2)}) %collective-permute-start.12) | collective-permute-done | bytes 131104 | tf_op jit(solution)/shard_map/ppermute | solution.py:12
  45.1 1.4 %collective-permute-start.13 = (f32[16,16,128]{2,1,0:T(8,128)S(1)}, f32[16,16,128]{2,1,0:T(8,128)S(1)}, u32[]{:S(2)}, u32[]{:S(2)}) collective-permute-start(f32[16,16,128]{2,1,0:T(8,128)S(1)} %add.264), channel_id=1, source_target_pairs={{0,32},{16,48},{32,64},{48,80},{64,96},{80,112},{96,0},{112,16},{1... | collective-permute-start | bytes 393224 | tf_op jit(solution)/shard_map/ppermute | solution.py:12
  46.5 1.7 %collective-permute-start.14 = (f32[16,16,128]{2,1,0:T(8,128)S(1)}, f32[16,16,128]{2,1,0:T(8,128)S(1)}, u32[]{:S(2)}, u32[]{:S(2)}) collective-permute-start(f32[16,16,128]{2,1,0:T(8,128)S(1)} %add.264), channel_id=1, source_target_pairs={{0,96},{16,112},{32,0},{48,16},{64,32},{80,48},{96,64},{112,80},{1... | collective-permute-start | bytes 393224 | tf_op jit(solution)/shard_map/ppermute | solution.py:12
  48.2 1.4 %collective-permute-start.15 = (f32[16,16,128]{2,1,0:T(8,128)S(1)}, f32[16,16,128]{2,1,0:T(8,128)S(1)}, u32[]{:S(2)}, u32[]{:S(2)}) collective-permute-start(f32[16,16,128]{2,1,0:T(8,128)S(1)} %add.264), channel_id=1, source_target_pairs={{0,64},{16,80},{32,96},{48,112},{64,0},{80,16},{96,32},{112,48},{1... | collective-permute-start | bytes 393224 | tf_op jit(solution)/shard_map/ppermute | solution.py:12
  50.3 4.9 %collective-permute-done.15 = f32[16,16,128]{2,1,0:T(8,128)S(1)} collective-permute-done((f32[16,16,128]{2,1,0:T(8,128)S(1)}, f32[16,16,128]{2,1,0:T(8,128)S(1)}, u32[]{:S(2)}, u32[]{:S(2)}) %collective-permute-start.15) | collective-permute-done | bytes 131104 | tf_op jit(solution)/shard_map/ppermute | solution.py:12
  56.7 3.6 %collective-permute-start.18 = (f32[16,896]{1,0:T(8,128)S(1)}, f32[16,896]{1,0:T(8,128)S(1)}, u32[]{:S(2)}, u32[]{:S(2)}) collective-permute-start(f32[16,896]{1,0:T(8,128)S(1)} %pad_maximum_fusion.13), channel_id=1, source_target_pairs={{0,12},{1,13},{2,14},{3,15},{4,0},{5,1},{6,2},{7,3},{8,4},{9,5},{1... | collective-permute-start | bytes 172040 | tf_op jit(solution)/shard_map/ppermute | solution.py:12
  60.3 0.7 collective-permute-start.19
  61.0 1.1 collective-permute-done.17
  62.2 5.4 %collective-permute-done.19 = f32[16,896]{1,0:T(8,128)S(1)} collective-permute-done((f32[16,896]{1,0:T(8,128)S(1)}, f32[16,896]{1,0:T(8,128)S(1)}, u32[]{:S(2)}, u32[]{:S(2)}) %collective-permute-start.19) | collective-permute-done | bytes 57376 | tf_op jit(solution)/shard_map/ppermute | solution.py:12
  69.5 3.4 %collective-permute-done.20 = f32[17,16,128]{2,1,0:T(8,128)S(1)} collective-permute-done((f32[17,16,128]{2,1,0:T(8,128)S(1)}, f32[17,16,128]{2,1,0:T(8,128)S(1)}, u32[]{:S(2)}, u32[]{:S(2)}) %collective-permute-start.20) | collective-permute-done | bytes 139296 | tf_op jit(solution)/shard_map/ppermute | solution.py:12
  72.9 0.7 fusion.73
  73.6 2.7 %collective-permute-start.22 = (f32[17,16,128]{2,1,0:T(8,128)}, f32[17,16,128]{2,1,0:T(8,128)}, u32[]{:S(2)}, u32[]{:S(2)}) collective-permute-start(f32[17,16,128]{2,1,0:T(8,128)} %fusion.73), channel_id=1, source_target_pairs={{0,96},{16,112},{32,0},{48,16},{64,32},{80,48},{96,64},{112,80},{1... | collective-permute-start | bytes 417800 | tf_op jit(solution)/shard_map/ppermute | solution.py:12
  76.9 0.7 copy.100
  77.6 0.7 copy.96
  78.2 0.7 collective-permute-done.21
  78.9 1.2 collective-permute-done.22
  80.1 1.9 %collective-permute-done.23 = f32[17,16,128]{2,1,0:T(8,128)} collective-permute-done((f32[17,16,128]{2,1,0:T(8,128)}, f32[17,16,128]{2,1,0:T(8,128)}, u32[]{:S(2)}, u32[]{:S(2)}) %collective-permute-start.23) | collective-permute-done | bytes 139296 | tf_op jit(solution)/shard_map/ppermute | solution.py:12
  82.0 1.1 add_add_fusion
  85.7 3.6 %collective-permute-start.25 = (f32[16,896]{1,0:T(8,128)}, f32[16,896]{1,0:T(8,128)}, u32[]{:S(2)}, u32[]{:S(2)}) collective-permute-start(f32[16,896]{1,0:T(8,128)} %pad_maximum_fusion.14), channel_id=1, source_target_pairs={{0,12},{1,13},{2,14},{3,15},{4,0},{5,1},{6,2},{7,3},{8,4},{9,5},{1... | collective-permute-start | bytes 172040 | tf_op jit(solution)/shard_map/ppermute | solution.py:12
  89.2 1.0 collective-permute-start.26
  90.3 0.7 constant_dynamic-slice_fusion.2
  91.0 1.4 %copy.101 = f32[64,32]{0,1:T(8,128)} copy(f32[64,32]{1,0:T(8,128)} %bitcast.210) | data formatting | bytes 16384 | tf_op jit(solution)/shard_map/reshape | solution.py:169
  92.4 0.7 copy.97
  93.1 4.7 %collective-permute-done.26 = f32[16,896]{1,0:T(8,128)} collective-permute-done((f32[16,896]{1,0:T(8,128)}, f32[16,896]{1,0:T(8,128)}, u32[]{:S(2)}, u32[]{:S(2)}) %collective-permute-start.26) | collective-permute-done | bytes 57376 | tf_op jit(solution)/shard_map/ppermute | solution.py:12
  97.7 0.9 add_add_fusion.2
  100.9 6.3 %collective-permute-start.27 = (f32[176,32]{0,1:T(8,128)S(1)}, f32[176,32]{0,1:T(8,128)S(1)}, u32[]{:S(2)}, u32[]{:S(2)}) collective-permute-start(f32[176,32]{0,1:T(8,128)S(1)} %concatenate.77), channel_id=1, source_target_pairs={{0,16},{16,0},{32,48},{48,32},{64,80},{80,64},{96,112},{112,96},{1... | collective-permute-start | bytes 67592 | tf_op jit(solution)/shard_map/ppermute | solution.py:12
  107.2 0.7 pad_maximum_fusion.3
  107.9 3.6 %all-to-all-start = ((f32[16,24,128]{2,1,0:T(8,128)}), f32[16,24,128]{2,1,0:T(8,128)S(1)}, u32[]{:S(2)}, u32[]{:S(2)}) async-start(f32[16,24,128]{2,1,0:T(8,128)} %pad_maximum_fusion.3), calls=%async_computation | async-start | bytes 393216 | tf_op jit(solution)/shard_map/all_to_all | solution.py:161
  112.5 5.7 %all-to-all-done = f32[16,24,128]{2,1,0:T(8,128)S(1)} async-done(((f32[16,24,128]{2,1,0:T(8,128)}), f32[16,24,128]{2,1,0:T(8,128)S(1)}, u32[]{:S(2)}, u32[]{:S(2)}) %all-to-all-start) | async-done | bytes 196640 | tf_op jit(solution)/shard_map/all_to_all | solution.py:161
  119.0 3.1 %collective-permute-start.28 = (f32[64,32]{0,1:T(8,128)S(1)}, f32[64,32]{0,1:T(8,128)S(1)}, u32[]{:S(2)}, u32[]{:S(2)}) collective-permute-start(f32[64,32]{0,1:T(8,128)S(1)} %get-tuple-element.38), channel_id=1, source_target_pairs={{0,3},{1,0},{2,1},{3,2},{4,7},{5,4},{6,5},{7,6},{8,11},{9,8},{10,9... | collective-permute-start | bytes 24584 | tf_op jit(solution)/shard_map/ppermute | solution.py:12
  123.0 3.3 %collective-permute-done.29 = f32[64,32]{0,1:T(8,128)S(1)} collective-permute-done((f32[64,32]{0,1:T(8,128)S(1)}, f32[64,32]{0,1:T(8,128)S(1)}, u32[]{:S(2)}, u32[]{:S(2)}) %collective-permute-start.29) | collective-permute-done | bytes 8224 | tf_op jit(solution)/shard_map/ppermute | solution.py:12
  126.6 0.7 copy.112
  127.2 0.7 copy.113
  (172 shorter events, 14.9 us)
Async XLA Ops:
  0.6 21.3 %collective-permute-start.6 = (bf16[384,512]{1,0:T(8,128)(2,1)}, bf16[384,512]{1,0:T(8,128)(2,1)S(1)}, u32[]{:S(2)}, u32[]{:S(2)}) collective-permute-start(bf16[384,512]{1,0:T(8,128)(2,1)} %bitcast.188), channel_id=1, source_target_pairs={{0,1},{1,2},{2,3},{3,0},{4,5},{5,6},{6,7},{7,4},{8,9},{9,10},{10,1... | collective-permute-start | bytes 1179656 | tf_op jit(solution)/shard_map/ppermute | solution.py:12
  2.7 23.6 %collective-permute-start.8 = (bf16[384,512]{1,0:T(8,128)(2,1)}, bf16[384,512]{1,0:T(8,128)(2,1)S(1)}, u32[]{:S(2)}, u32[]{:S(2)}) collective-permute-start(bf16[384,512]{1,0:T(8,128)(2,1)} %bitcast.189), channel_id=1, source_target_pairs={{0,3},{1,0},{2,1},{3,2},{4,7},{5,4},{6,5},{7,6},{8,11},{9,8},{10,9... | collective-permute-start | bytes 1179656 | tf_op jit(solution)/shard_map/ppermute | solution.py:12
  6.4 5.5 %collective-permute-start = (f32[32,384]{1,0:T(8,128)S(1)}, f32[32,384]{1,0:T(8,128)S(1)}, u32[]{:S(2)}, u32[]{:S(2)}) collective-permute-start(f32[32,384]{1,0:T(8,128)S(1)} %get-tuple-element.32), channel_id=1, source_target_pairs={{0,1},{1,2},{2,3},{3,0},{4,5},{5,6},{6,7},{7,4},{8,9},{9,10},{10,1... | collective-permute-start | bytes 147464 | tf_op jit(solution)/shard_map/ppermute | solution.py:12
  6.6 9.2 %collective-permute-start.1 = (f32[32,384]{1,0:T(8,128)S(1)}, f32[32,384]{1,0:T(8,128)S(1)}, u32[]{:S(2)}, u32[]{:S(2)}) collective-permute-start(f32[32,384]{1,0:T(8,128)S(1)} %get-tuple-element.34), channel_id=1, source_target_pairs={{0,3},{1,0},{2,1},{3,2},{4,7},{5,4},{6,5},{7,6},{8,11},{9,8},{10,9... | collective-permute-start | bytes 147464 | tf_op jit(solution)/shard_map/ppermute | solution.py:12
  9.2 6.6 %collective-permute-start.2 = (f32[32,384]{1,0:T(8,128)S(1)}, f32[32,384]{1,0:T(8,128)S(1)}, u32[]{:S(2)}, u32[]{:S(2)}) collective-permute-start(f32[32,384]{1,0:T(8,128)S(1)} %get-tuple-element.33), channel_id=1, source_target_pairs={{0,2},{1,3},{2,0},{3,1},{4,6},{5,7},{6,4},{7,5},{8,10},{9,11},{10,... | collective-permute-start | bytes 147464 | tf_op jit(solution)/shard_map/ppermute | solution.py:12
  9.6 23.0 %copy-start = (bf16[1,384,512]{2,1,0:T(8,128)(2,1)S(1)}, bf16[1,384,512]{2,1,0:T(8,128)(2,1)}, u32[]{:S(2)}) copy-start(bf16[1,384,512]{2,1,0:T(8,128)(2,1)} %param.2) | copy-start | bytes 1179652
  11.9 25.9 %collective-permute-start.10 = (bf16[32,512]{1,0:T(8,128)(2,1)S(1)}, bf16[32,512]{1,0:T(8,128)(2,1)S(1)}, u32[]{:S(2)}, u32[]{:S(2)}) collective-permute-start(bf16[32,512]{1,0:T(8,128)(2,1)S(1)} %get-tuple-element.49), channel_id=1, source_target_pairs={{0,2},{1,3},{2,0},{3,1},{4,6},{5,7},{6,4},{7,5},{8,10},{9,11},{10,... | collective-permute-start | bytes 98312 | tf_op jit(solution)/shard_map/ppermute | solution.py:12
  15.8 11.3 %collective-permute-start.3 = (f32[32,384]{1,0:T(8,128)S(1)}, f32[32,384]{1,0:T(8,128)S(1)}, u32[]{:S(2)}, u32[]{:S(2)}) collective-permute-start(f32[32,384]{1,0:T(8,128)S(1)} %fusion.34), channel_id=1, source_target_pairs={{0,4},{1,5},{2,6},{3,7},{4,8},{5,9},{6,10},{7,11},{8,12},{9,13},{1... | collective-permute-start | bytes 147464 | tf_op jit(solution)/shard_map/ppermute | solution.py:12
  18.8 10.4 %collective-permute-start.4 = (f32[32,384]{1,0:T(8,128)S(1)}, f32[32,384]{1,0:T(8,128)S(1)}, u32[]{:S(2)}, u32[]{:S(2)}) collective-permute-start(f32[32,384]{1,0:T(8,128)S(1)} %fusion.34), channel_id=1, source_target_pairs={{0,12},{1,13},{2,14},{3,15},{4,0},{5,1},{6,2},{7,3},{8,4},{9,5},{1... | collective-permute-start | bytes 147464 | tf_op jit(solution)/shard_map/ppermute | solution.py:12
  22.0 7.3 %collective-permute-start.5 = (f32[32,384]{1,0:T(8,128)S(1)}, f32[32,384]{1,0:T(8,128)S(1)}, u32[]{:S(2)}, u32[]{:S(2)}) collective-permute-start(f32[32,384]{1,0:T(8,128)S(1)} %fusion.34), channel_id=1, source_target_pairs={{0,8},{1,9},{2,10},{3,11},{4,12},{5,13},{6,14},{7,15},{8,0},{9,1},... | collective-permute-start | bytes 147464 | tf_op jit(solution)/shard_map/ppermute | solution.py:12
  26.4 6.2 %collective-permute-start.7 = (bf16[224,512]{1,0:T(8,128)(2,1)S(1)}, bf16[224,512]{1,0:T(8,128)(2,1)S(1)}, u32[]{:S(2)}, u32[]{:S(2)}) collective-permute-start(bf16[224,512]{1,0:T(8,128)(2,1)S(1)} %pad_maximum_fusion.1), channel_id=1, source_target_pairs={{0,1},{1,2},{2,3},{3,0},{4,5},{5,6},{6,7},{7,4},{8,9},{9,10},{10,1... | collective-permute-start | bytes 688136 | tf_op jit(solution)/shard_map/ppermute | solution.py:12
  27.1 5.5 %collective-permute-start.9 = (bf16[224,512]{1,0:T(8,128)(2,1)S(1)}, bf16[224,512]{1,0:T(8,128)(2,1)S(1)}, u32[]{:S(2)}, u32[]{:S(2)}) collective-permute-start(bf16[224,512]{1,0:T(8,128)(2,1)S(1)} %pad_maximum_fusion.2), channel_id=1, source_target_pairs={{0,3},{1,0},{2,1},{3,2},{4,7},{5,4},{6,5},{7,6},{8,11},{9,8},{10,9... | collective-permute-start | bytes 688136 | tf_op jit(solution)/shard_map/ppermute | solution.py:12
  32.8 16.8 %collective-permute-start.16 = (bf16[384,2048]{1,0:T(8,128)(2,1)S(1)}, bf16[384,2048]{1,0:T(8,128)(2,1)S(1)}, u32[]{:S(2)}, u32[]{:S(2)}) collective-permute-start(bf16[384,2048]{1,0:T(8,128)(2,1)S(1)} %pad_maximum_fusion), channel_id=1, source_target_pairs={{0,16},{16,0},{32,48},{48,32},{64,80},{80,64},{96,112},{112,96},{1... | collective-permute-start | bytes 4718600 | tf_op jit(solution)/shard_map/ppermute | solution.py:12
  38.0 2.2 %collective-permute-start.11 = (f32[16,16,128]{2,1,0:T(8,128)S(1)}, f32[16,16,128]{2,1,0:T(8,128)S(1)}, u32[]{:S(2)}, u32[]{:S(2)}) collective-permute-start(f32[16,16,128]{2,1,0:T(8,128)S(1)} %bitcast.207), channel_id=1, source_target_pairs={{0,16},{16,0},{32,48},{48,32},{64,80},{80,64},{96,112},{112,96},{1... | collective-permute-start | bytes 393224 | tf_op jit(solution)/shard_map/ppermute | solution.py:12
  40.3 4.8 %collective-permute-start.12 = (f32[16,16,128]{2,1,0:T(8,128)S(1)}, f32[16,16,128]{2,1,0:T(8,128)S(1)}, u32[]{:S(2)}, u32[]{:S(2)}) collective-permute-start(f32[16,16,128]{2,1,0:T(8,128)S(1)} %fusion.19), channel_id=1, source_target_pairs={{0,128},{16,144},{32,160},{48,176},{64,192},{80,208},{96,224},{112... | collective-permute-start | bytes 393224 | tf_op jit(solution)/shard_map/ppermute | solution.py:12
  41.1 15.4 %copy-start.9 = (pred[128]{0:T(512)(128)(4,1)}, pred[128]{0:T(512)(128)(4,1)S(1)}, u32[]{:S(2)}) copy-start(pred[128]{0:T(512)(128)(4,1)S(1)} %get-tuple-element.66) | copy-start | bytes 388
  41.1 15.4 %copy-start.11 = (pred[128]{0:T(512)(128)(4,1)}, pred[128]{0:T(512)(128)(4,1)S(1)}, u32[]{:S(2)}) copy-start(pred[128]{0:T(512)(128)(4,1)S(1)} %get-tuple-element.67) | copy-start | bytes 388
  45.1 5.2 %collective-permute-start.13 = (f32[16,16,128]{2,1,0:T(8,128)S(1)}, f32[16,16,128]{2,1,0:T(8,128)S(1)}, u32[]{:S(2)}, u32[]{:S(2)}) collective-permute-start(f32[16,16,128]{2,1,0:T(8,128)S(1)} %add.264), channel_id=1, source_target_pairs={{0,32},{16,48},{32,64},{48,80},{64,96},{80,112},{96,0},{112,16},{1... | collective-permute-start | bytes 393224 | tf_op jit(solution)/shard_map/ppermute | solution.py:12
  46.5 3.8 %collective-permute-start.14 = (f32[16,16,128]{2,1,0:T(8,128)S(1)}, f32[16,16,128]{2,1,0:T(8,128)S(1)}, u32[]{:S(2)}, u32[]{:S(2)}) collective-permute-start(f32[16,16,128]{2,1,0:T(8,128)S(1)} %add.264), channel_id=1, source_target_pairs={{0,96},{16,112},{32,0},{48,16},{64,32},{80,48},{96,64},{112,80},{1... | collective-permute-start | bytes 393224 | tf_op jit(solution)/shard_map/ppermute | solution.py:12
  48.2 7.0 %collective-permute-start.15 = (f32[16,16,128]{2,1,0:T(8,128)S(1)}, f32[16,16,128]{2,1,0:T(8,128)S(1)}, u32[]{:S(2)}, u32[]{:S(2)}) collective-permute-start(f32[16,16,128]{2,1,0:T(8,128)S(1)} %add.264), channel_id=1, source_target_pairs={{0,64},{16,80},{32,96},{48,112},{64,0},{80,16},{96,32},{112,48},{1... | collective-permute-start | bytes 393224 | tf_op jit(solution)/shard_map/ppermute | solution.py:12
  56.7 5.5 %collective-permute-start.17 = (f32[16,896]{1,0:T(8,128)S(1)}, f32[16,896]{1,0:T(8,128)S(1)}, u32[]{:S(2)}, u32[]{:S(2)}) collective-permute-start(f32[16,896]{1,0:T(8,128)S(1)} %pad_maximum_fusion.13), channel_id=1, source_target_pairs={{0,4},{1,5},{2,6},{3,7},{4,8},{5,9},{6,10},{7,11},{8,12},{9,13},{1... | collective-permute-start | bytes 172040 | tf_op jit(solution)/shard_map/ppermute | solution.py:12
  56.7 5.4 %collective-permute-start.18 = (f32[16,896]{1,0:T(8,128)S(1)}, f32[16,896]{1,0:T(8,128)S(1)}, u32[]{:S(2)}, u32[]{:S(2)}) collective-permute-start(f32[16,896]{1,0:T(8,128)S(1)} %pad_maximum_fusion.13), channel_id=1, source_target_pairs={{0,12},{1,13},{2,14},{3,15},{4,0},{5,1},{6,2},{7,3},{8,4},{9,5},{1... | collective-permute-start | bytes 172040 | tf_op jit(solution)/shard_map/ppermute | solution.py:12
  60.3 7.3 %collective-permute-start.19 = (f32[16,896]{1,0:T(8,128)S(1)}, f32[16,896]{1,0:T(8,128)S(1)}, u32[]{:S(2)}, u32[]{:S(2)}) collective-permute-start(f32[16,896]{1,0:T(8,128)S(1)} %pad_maximum_fusion.13), channel_id=1, source_target_pairs={{0,8},{1,9},{2,10},{3,11},{4,12},{5,13},{6,14},{7,15},{8,0},{9,1},... | collective-permute-start | bytes 172040 | tf_op jit(solution)/shard_map/ppermute | solution.py:12
  68.9 4.0 %collective-permute-start.20 = (f32[17,16,128]{2,1,0:T(8,128)S(1)}, f32[17,16,128]{2,1,0:T(8,128)S(1)}, u32[]{:S(2)}, u32[]{:S(2)}) collective-permute-start(f32[17,16,128]{2,1,0:T(8,128)S(1)} %pad_maximum_fusion.4), channel_id=1, source_target_pairs={{0,128},{16,144},{32,160},{48,176},{64,192},{80,208},{96,224},{112... | collective-permute-start | bytes 417800 | tf_op jit(solution)/shard_map/ppermute | solution.py:12
  73.6 5.3 %collective-permute-start.21 = (f32[17,16,128]{2,1,0:T(8,128)}, f32[17,16,128]{2,1,0:T(8,128)S(1)}, u32[]{:S(2)}, u32[]{:S(2)}) collective-permute-start(f32[17,16,128]{2,1,0:T(8,128)} %fusion.73), channel_id=1, source_target_pairs={{0,32},{16,48},{32,64},{48,80},{64,96},{80,112},{96,0},{112,16},{1... | collective-permute-start | bytes 417800 | tf_op jit(solution)/shard_map/ppermute | solution.py:12
  73.6 6.5 %collective-permute-start.22 = (f32[17,16,128]{2,1,0:T(8,128)}, f32[17,16,128]{2,1,0:T(8,128)}, u32[]{:S(2)}, u32[]{:S(2)}) collective-permute-start(f32[17,16,128]{2,1,0:T(8,128)} %fusion.73), channel_id=1, source_target_pairs={{0,96},{16,112},{32,0},{48,16},{64,32},{80,48},{96,64},{112,80},{1... | collective-permute-start | bytes 417800 | tf_op jit(solution)/shard_map/ppermute | solution.py:12
  76.3 5.7 %collective-permute-start.23 = (f32[17,16,128]{2,1,0:T(8,128)}, f32[17,16,128]{2,1,0:T(8,128)}, u32[]{:S(2)}, u32[]{:S(2)}) collective-permute-start(f32[17,16,128]{2,1,0:T(8,128)} %fusion.73), channel_id=1, source_target_pairs={{0,64},{16,80},{32,96},{48,112},{64,0},{80,16},{96,32},{112,48},{1... | collective-permute-start | bytes 417800 | tf_op jit(solution)/shard_map/ppermute | solution.py:12
  83.2 0.5 copy-start.7
  83.8 1.2 copy-start.10
  83.8 1.2 copy-start.12
  83.8 1.2 copy-start.13
  84.9 8.2 %copy-start.1 = (f32[16,384]{1,0:T(8,128)}, f32[16,384]{1,0:T(8,128)S(1)}, u32[]{:S(2)}) copy-start(f32[16,384]{1,0:T(8,128)S(1)} %slice_add_fusion.6) | copy-start | bytes 73732
  85.0 5.2 %copy-start.2 = (f32[16,128]{1,0:T(8,128)}, f32[16,128]{1,0:T(8,128)S(1)}, u32[]{:S(2)}) copy-start(f32[16,128]{1,0:T(8,128)S(1)} %select_select_fusion) | copy-start | bytes 24580
  85.7 7.4 %collective-permute-start.24 = (f32[16,896]{1,0:T(8,128)}, f32[16,896]{1,0:T(8,128)}, u32[]{:S(2)}, u32[]{:S(2)}) collective-permute-start(f32[16,896]{1,0:T(8,128)} %pad_maximum_fusion.14), channel_id=1, source_target_pairs={{0,4},{1,5},{2,6},{3,7},{4,8},{5,9},{6,10},{7,11},{8,12},{9,13},{1... | collective-permute-start | bytes 172040 | tf_op jit(solution)/shard_map/ppermute | solution.py:12
  85.7 7.4 %collective-permute-start.25 = (f32[16,896]{1,0:T(8,128)}, f32[16,896]{1,0:T(8,128)}, u32[]{:S(2)}, u32[]{:S(2)}) collective-permute-start(f32[16,896]{1,0:T(8,128)} %pad_maximum_fusion.14), channel_id=1, source_target_pairs={{0,12},{1,13},{2,14},{3,15},{4,0},{5,1},{6,2},{7,3},{8,4},{9,5},{1... | collective-permute-start | bytes 172040 | tf_op jit(solution)/shard_map/ppermute | solution.py:12
  89.2 8.5 %collective-permute-start.26 = (f32[16,896]{1,0:T(8,128)}, f32[16,896]{1,0:T(8,128)}, u32[]{:S(2)}, u32[]{:S(2)}) collective-permute-start(f32[16,896]{1,0:T(8,128)} %pad_maximum_fusion.14), channel_id=1, source_target_pairs={{0,8},{1,9},{2,10},{3,11},{4,12},{5,13},{6,14},{7,15},{8,0},{9,1},... | collective-permute-start | bytes 172040 | tf_op jit(solution)/shard_map/ppermute | solution.py:12
  99.7 1.0 copy-start.8
  99.7 1.0 copy-start.4
  99.7 1.0 copy-start.6
  99.8 11.8 %copy-start.3 = (f32[64,32]{0,1:T(8,128)S(1)}, f32[64,32]{0,1:T(8,128)}, u32[]{:S(2)}) copy-start(f32[64,32]{0,1:T(8,128)} %copy.96) | copy-start | bytes 24580
  99.8 11.8 %copy-start.5 = (f32[64,32]{0,1:T(8,128)S(1)}, f32[64,32]{0,1:T(8,128)}, u32[]{:S(2)}) copy-start(f32[64,32]{0,1:T(8,128)} %copy.97) | copy-start | bytes 24580
  100.9 10.8 %collective-permute-start.27 = (f32[176,32]{0,1:T(8,128)S(1)}, f32[176,32]{0,1:T(8,128)S(1)}, u32[]{:S(2)}, u32[]{:S(2)}) collective-permute-start(f32[176,32]{0,1:T(8,128)S(1)} %concatenate.77), channel_id=1, source_target_pairs={{0,16},{16,0},{32,48},{48,32},{64,80},{80,64},{96,112},{112,96},{1... | collective-permute-start | bytes 67592 | tf_op jit(solution)/shard_map/ppermute | solution.py:12
  107.9 10.3 %all-to-all-start = ((f32[16,24,128]{2,1,0:T(8,128)}), f32[16,24,128]{2,1,0:T(8,128)S(1)}, u32[]{:S(2)}, u32[]{:S(2)}) async-start(f32[16,24,128]{2,1,0:T(8,128)} %pad_maximum_fusion.3), calls=%async_computation | async-start | bytes 393216 | tf_op jit(solution)/shard_map/all_to_all | solution.py:161
  119.0 4.0 %collective-permute-start.28 = (f32[64,32]{0,1:T(8,128)S(1)}, f32[64,32]{0,1:T(8,128)S(1)}, u32[]{:S(2)}, u32[]{:S(2)}) collective-permute-start(f32[64,32]{0,1:T(8,128)S(1)} %get-tuple-element.38), channel_id=1, source_target_pairs={{0,3},{1,0},{2,1},{3,2},{4,7},{5,4},{6,5},{7,6},{8,11},{9,8},{10,9... | collective-permute-start | bytes 24584 | tf_op jit(solution)/shard_map/ppermute | solution.py:12
  122.2 4.1 %collective-permute-start.29 = (f32[64,32]{0,1:T(8,128)S(1)}, f32[64,32]{0,1:T(8,128)S(1)}, u32[]{:S(2)}, u32[]{:S(2)}) collective-permute-start(f32[64,32]{0,1:T(8,128)S(1)} %get-tuple-element.39), channel_id=1, source_target_pairs={{0,2},{1,3},{2,0},{3,1},{4,6},{5,7},{6,4},{7,5},{8,10},{9,11},{10,... | collective-permute-start | bytes 24584 | tf_op jit(solution)/shard_map/ppermute | solution.py:12
  122.3 4.1 %collective-permute-start.30 = (f32[64,32]{0,1:T(8,128)S(1)}, f32[64,32]{0,1:T(8,128)S(1)}, u32[]{:S(2)}, u32[]{:S(2)}) collective-permute-start(f32[64,32]{0,1:T(8,128)S(1)} %get-tuple-element.37), channel_id=1, source_target_pairs={{0,1},{1,2},{2,3},{3,0},{4,5},{5,6},{6,7},{7,4},{8,9},{9,10},{10,1... | collective-permute-start | bytes 24584 | tf_op jit(solution)/shard_map/ppermute | solution.py:12

commit v7 on v6

--- a/solution.py
+++ b/solution.py
@@ -100,20 +100,24 @@
     two, three, one = staged(lambda k: pick(first, (x + k) % 4), x_move)
     mine = pick(first, x) + one + three + two
     turned = w.T.reshape(4, 32, width)
-    ws_far = x_move(pick(turned, (x + 2) % 4), 2)
 
     half = tokens // 2
-    from_left = x_move(own_x, 1)
+    from_left = x_move(jnp.concatenate([own_x, pick(turned, (x + 2) % 4)]), 1)
     from_right = x_move(own_x, 3)
     outputs = sum_over(mine, zhi_move)
-    far_left = x_move(jnp.concatenate([from_left[:half], pick(turned, (x + 1) % 4)]), 1)
+    far_left = jnp.concatenate([from_left[:half], from_left[tokens:], pick(turned, (x + 1) % 4)])
+    far_left = x_move(far_left, 1)
     far_right = x_move(jnp.concatenate([from_right[half:], pick(turned, (x + 3) % 4)]), 3)
 
+    def squares(value):
+        wide = value.astype(jnp.float32)
+        return diag_scale * jnp.sum(wide * wide, axis=0, keepdims=True)
+
     far = jnp.concatenate([far_left[:half], far_right[:half]])
-    xs = lax.optimization_barrier(jnp.concatenate([own_x, from_left, far, from_right], axis=1))
-    ws = jnp.concatenate([pick(turned, x), far_left[half:], ws_far, far_right[half:]], axis=1)
-    wide_x = xs.astype(jnp.float32)
-    diag = diag_scale * jnp.sum(wide_x * wide_x, axis=0, keepdims=True)
+    xs = lax.optimization_barrier(jnp.concatenate([own_x, from_left[:tokens], far, from_right], axis=1))
+    ws = [pick(turned, x), far_left[half + 32 :], far_left[half : half + 32], far_right[half:]]
+    ws = jnp.concatenate(ws, axis=1)
+    diag = squares(xs)
 
     part = blocks_of(gram_scale * product(outputs, xs, 0) + diag * ws.astype(jnp.float32))
     part = part.reshape(16, 2, 16, 128)
@@ -123,8 +127,7 @@
 
     xs_other = core_move(xs)
     xs_other, diag = lax.optimization_barrier((xs_other, diag))
-    wide_x = xs_other.astype(jnp.float32)
-    diag = diag + diag_scale * jnp.sum(wide_x * wide_x, axis=0, keepdims=True)
+    diag = diag + squares(xs_other)
 
     def outputs_of(vector):
         return jnp.concatenate([product(vector, xs, 1), product(vector, xs_other, 1)], axis=1)
@@ -163,26 +166,24 @@
     curve = part[:, 16, :16].reshape(32)
     part = part[:, :16].reshape(2, 16, 2, 4, 16).transpose(2, 1, 3, 0, 4).reshape(32, 128)
 
-    def rows_of(device):
-        def four(blocks):
-            four = pick(blocks.reshape(4, 4, 16, 128), device // 4, 1)
-            return lax.dynamic_slice_in_dim(four, 32 * (device % 4), 32, 2).reshape(64, 32)
-
-        wide = [jnp.broadcast_to(column, (16, 32)) for column in (alpha0, beta, norm1)]
-        return jnp.concatenate([four(target_blocks), four(residual_blocks)] + wide)
-
-    other = core_move(rows_of(task ^ 1))
-    own = rows_of(task)
+    def piece_of(blocks):
+        return pick(blocks.reshape(4, 4, 16, 128), task // 4, 1)
+
+    lane = lax.broadcasted_iota(jnp.int32, (16, 128), 1)
+    scalars = jnp.where(lane < 32, alpha0, jnp.where(lane < 64, beta, norm1))
+    own = jnp.concatenate([piece_of(target_blocks), piece_of(residual_blocks), scalars[None]])
+    other = core_move(own)
     both = jnp.where(core == 0, jnp.stack([own, other]), jnp.stack([other, own]))
+    alpha0, beta, norm1 = (both[:, 8, :, 32 * i].reshape(32) for i in range(3))
+    both = lax.dynamic_slice_in_dim(both, 32 * (task % 4), 32, 3)
 
     def side_by_side(value):
-        return value.reshape(2, 4, 16, 32).transpose(3, 1, 0, 2).reshape(32, 128)
+        return value.transpose(3, 1, 0, 2).reshape(32, 128)
 
     def per_lane(vector):
         return jnp.tile(vector, 4)[None]
 
-    my_target, my_residual = side_by_side(both[:, :64]), side_by_side(both[:, 64:128])
-    alpha0, beta, norm1 = (both[:, 128 + 16 * i : 144 + 16 * i, 0].reshape(32) for i in range(3))
+    my_target, my_residual = side_by_side(both[:, :4]), side_by_side(both[:, 4:8])
     alpha1 = per_lane(norm1 / curve)
     merged = per_lane(alpha0) * my_target + alpha1 * (my_residual + per_lane(beta) * my_target)
     both = jnp.concatenate([merged, my_residual - alpha1 * part])

time: 128 us -> 129 us (level)
  waiting for transfers between devices: 44.3 us -> 57.4 us
  starting transfers between devices: 59.4 us -> 54.2 us
  local copies, waits for them, and re-layouts: 9.55 us -> 4.81 us
  other arithmetic: 7.77 us -> 6.21 us
    ppermute x31 -> x30, waiting for transfers between devices: 38.7 us -> 51.8 us  [moved(): return lax.ppermute(value, axis, [(i, to(i)) for i in range(16)])]
    ppermute x31 -> x30, starting transfers between devices: 55.8 us -> 50.5 us  [moved(): return lax.ppermute(value, axis, [(i, to(i)) for i in range(16)])]
    reshape x4 -> x0, local copies, waits for them, and re-layouts: 3.46 us -> none  [four(): lax.dynamic_slice_in_dim(four, 32 * (device % 4), 32, 2).reshape(64, 32)]
    unnamed x38 -> x14, local copies, waits for them, and re-layouts: 2.79 us -> 2.49 us
  transfers between devices with their start and end apart: 32 -> 31, of which waited for: 16 -> 20; matrix products, arithmetic and copies ran while one was open for 8% -> 4% of each run, Pallas kernels for 0% -> 0%
where the time goes in v7:
time: 129 us; the launch traced here: 128 us
  waiting for transfers between devices  57.4 us (44%)
  starting transfers between devices  54.2 us (42%)
  other arithmetic  6.21 us (5%)
  local copies, waits for them, and re-layouts  4.81 us (4%)
  matrix products  4.49 us (3%)
    ppermute x30, waiting for transfers between devices, moved(): return lax.ppermute(value, axis, [(i, to(i)) for i in range(16)])  51.8 us
    ppermute x30, starting transfers between devices, moved(): return lax.ppermute(value, axis, [(i, to(i)) for i in range(16)])  50.5 us
    all_to_all x1, waiting for transfers between devices, on_device(): part = lax.all_to_all(jnp.concatenate([part, curve], axis=1), 'task', 0, 0)  5.6 us
    dot_general x9, matrix products, product(): lax.dot_general(pieces(value), x, (((1,), (dim,)), ((), ())), preferred_e...  4.21 us
    all_to_all x1, starting transfers between devices, on_device(): part = lax.all_to_all(jnp.concatenate([part, curve], axis=1), 'task', 0, 0)  3.64 us
  transfers between devices with their start and end apart: 31, of which 20 were waited for; matrix products, arithmetic and copies ran while one was open for 4% of the time, Pallas kernels for 0%

profile of v7, /device:TPU:1, one launch (start us, length us, event | category | flops | bytes accessed | tf_op | source)
XLA Modules:
  0.0 128.4 jit_solution(14546738311081025203)
XLA Ops:
  0.6 3.4 %collective-permute-start.8 = (bf16[384,512]{1,0:T(8,128)(2,1)}, bf16[384,512]{1,0:T(8,128)(2,1)S(1)}, u32[]{:S(2)}, u32[]{:S(2)}) collective-permute-start(bf16[384,512]{1,0:T(8,128)(2,1)} %bitcast.178), channel_id=1, source_target_pairs={{0,3},{1,0},{2,1},{3,2},{4,7},{5,4},{6,5},{7,6},{8,11},{9,8},{10,9... | collective-permute-start | bytes 1179656 | tf_op jit(solution)/shard_map/ppermute | solution.py:12
  4.0 1.0 copy.94
  5.1 1.0 pad_maximum_fusion.1
  6.8 2.6 %collective-permute-start.1 = (f32[32,384]{1,0:T(8,128)S(1)}, f32[32,384]{1,0:T(8,128)S(1)}, u32[]{:S(2)}, u32[]{:S(2)}) collective-permute-start(f32[32,384]{1,0:T(8,128)S(1)} %get-tuple-element.38), channel_id=1, source_target_pairs={{0,3},{1,0},{2,1},{3,2},{4,7},{5,4},{6,5},{7,6},{8,11},{9,8},{10,9... | collective-permute-start | bytes 147464 | tf_op jit(solution)/shard_map/ppermute | solution.py:12
  9.4 1.1 collective-permute-start.2
  10.4 9.0 %collective-permute-done = f32[32,384]{1,0:T(8,128)S(1)} collective-permute-done((f32[32,384]{1,0:T(8,128)S(1)}, f32[32,384]{1,0:T(8,128)S(1)}, u32[]{:S(2)}, u32[]{:S(2)}) %collective-permute-start) | collective-permute-done | bytes 49184 | tf_op jit(solution)/shard_map/ppermute | solution.py:12
  19.4 3.1 %collective-permute-start.3 = (f32[32,384]{1,0:T(8,128)S(1)}, f32[32,384]{1,0:T(8,128)S(1)}, u32[]{:S(2)}, u32[]{:S(2)}) collective-permute-start(f32[32,384]{1,0:T(8,128)S(1)} %fusion.34), channel_id=1, source_target_pairs={{0,4},{1,5},{2,6},{3,7},{4,8},{5,9},{6,10},{7,11},{8,12},{9,13},{1... | collective-permute-start | bytes 147464 | tf_op jit(solution)/shard_map/ppermute | solution.py:12
  22.5 3.1 %collective-permute-start.4 = (f32[32,384]{1,0:T(8,128)S(1)}, f32[32,384]{1,0:T(8,128)S(1)}, u32[]{:S(2)}, u32[]{:S(2)}) collective-permute-start(f32[32,384]{1,0:T(8,128)S(1)} %fusion.34), channel_id=1, source_target_pairs={{0,12},{1,13},{2,14},{3,15},{4,0},{5,1},{6,2},{7,3},{8,4},{9,5},{1... | collective-permute-start | bytes 147464 | tf_op jit(solution)/shard_map/ppermute | solution.py:12
  25.6 4.4 %collective-permute-start.5 = (f32[32,384]{1,0:T(8,128)S(1)}, f32[32,384]{1,0:T(8,128)S(1)}, u32[]{:S(2)}, u32[]{:S(2)}) collective-permute-start(f32[32,384]{1,0:T(8,128)S(1)} %fusion.34), channel_id=1, source_target_pairs={{0,8},{1,9},{2,10},{3,11},{4,12},{5,13},{6,14},{7,15},{8,0},{9,1},... | collective-permute-start | bytes 147464 | tf_op jit(solution)/shard_map/ppermute | solution.py:12
  30.2 1.5 %collective-permute-start.7 = (bf16[256,512]{1,0:T(8,128)(2,1)S(1)}, bf16[256,512]{1,0:T(8,128)(2,1)S(1)}, u32[]{:S(2)}, u32[]{:S(2)}) collective-permute-start(bf16[256,512]{1,0:T(8,128)(2,1)S(1)} %pad_maximum_fusion.2), channel_id=1, source_target_pairs={{0,1},{1,2},{2,3},{3,0},{4,5},{5,6},{6,7},{7,4},{8,9},{9,10},{10,1... | collective-permute-start | bytes 786440 | tf_op jit(solution)/shard_map/ppermute | solution.py:12
  31.7 0.8 collective-permute-done.5
  32.6 2.7 %collective-permute-done.9 = bf16[224,512]{1,0:T(8,128)(2,1)S(1)} collective-permute-done((bf16[224,512]{1,0:T(8,128)(2,1)S(1)}, bf16[224,512]{1,0:T(8,128)(2,1)S(1)}, u32[]{:S(2)}, u32[]{:S(2)}) %collective-permute-start.9) | collective-permute-done | bytes 229408 | tf_op jit(solution)/shard_map/ppermute | solution.py:12
  35.3 1.4 %collective-permute-done.7 = bf16[256,512]{1,0:T(8,128)(2,1)S(1)} collective-permute-done((bf16[256,512]{1,0:T(8,128)(2,1)S(1)}, bf16[256,512]{1,0:T(8,128)(2,1)S(1)}, u32[]{:S(2)}, u32[]{:S(2)}) %collective-permute-start.7) | collective-permute-done | bytes 262176 | tf_op jit(solution)/shard_map/ppermute | solution.py:12
  37.3 4.4 %collective-permute-start.15 = (bf16[384,2048]{1,0:T(8,128)(2,1)S(1)}, bf16[384,2048]{1,0:T(8,128)(2,1)S(1)}, u32[]{:S(2)}, u32[]{:S(2)}) collective-permute-start(bf16[384,2048]{1,0:T(8,128)(2,1)S(1)} %pad_maximum_fusion), channel_id=1, source_target_pairs={{0,16},{16,0},{32,48},{48,32},{64,80},{80,64},{96,112},{112,96},{1... | collective-permute-start | bytes 4718600 | tf_op jit(solution)/shard_map/ppermute | solution.py:12
  42.6 2.3 %collective-permute-done.10 = f32[16,16,128]{2,1,0:T(8,128)S(1)} collective-permute-done((f32[16,16,128]{2,1,0:T(8,128)S(1)}, f32[16,16,128]{2,1,0:T(8,128)S(1)}, u32[]{:S(2)}, u32[]{:S(2)}) %collective-permute-start.10) | collective-permute-done | bytes 131104 | tf_op jit(solution)/shard_map/ppermute | solution.py:12
  45.0 0.8 collective-permute-start.11
  45.8 3.9 %collective-permute-done.11 = f32[16,16,128]{2,1,0:T(8,128)S(1)} collective-permute-done((f32[16,16,128]{2,1,0:T(8,128)S(1)}, f32[16,16,128]{2,1,0:T(8,128)S(1)}, u32[]{:S(2)}, u32[]{:S(2)}) %collective-permute-start.11) | collective-permute-done | bytes 131104 | tf_op jit(solution)/shard_map/ppermute | solution.py:12
  49.8 1.4 %collective-permute-start.12 = (f32[16,16,128]{2,1,0:T(8,128)S(1)}, f32[16,16,128]{2,1,0:T(8,128)S(1)}, u32[]{:S(2)}, u32[]{:S(2)}) collective-permute-start(f32[16,16,128]{2,1,0:T(8,128)S(1)} %add.233), channel_id=1, source_target_pairs={{0,32},{16,48},{32,64},{48,80},{64,96},{80,112},{96,0},{112,16},{1... | collective-permute-start | bytes 393224 | tf_op jit(solution)/shard_map/ppermute | solution.py:12
  51.1 1.5 %collective-permute-start.13 = (f32[16,16,128]{2,1,0:T(8,128)S(1)}, f32[16,16,128]{2,1,0:T(8,128)S(1)}, u32[]{:S(2)}, u32[]{:S(2)}) collective-permute-start(f32[16,16,128]{2,1,0:T(8,128)S(1)} %add.233), channel_id=1, source_target_pairs={{0,96},{16,112},{32,0},{48,16},{64,32},{80,48},{96,64},{112,80},{1... | collective-permute-start | bytes 393224 | tf_op jit(solution)/shard_map/ppermute | solution.py:12
  52.7 1.6 %collective-permute-start.14 = (f32[16,16,128]{2,1,0:T(8,128)S(1)}, f32[16,16,128]{2,1,0:T(8,128)S(1)}, u32[]{:S(2)}, u32[]{:S(2)}) collective-permute-start(f32[16,16,128]{2,1,0:T(8,128)S(1)} %add.233), channel_id=1, source_target_pairs={{0,64},{16,80},{32,96},{48,112},{64,0},{80,16},{96,32},{112,48},{1... | collective-permute-start | bytes 393224 | tf_op jit(solution)/shard_map/ppermute | solution.py:12
  55.0 4.7 %collective-permute-done.14 = f32[16,16,128]{2,1,0:T(8,128)S(1)} collective-permute-done((f32[16,16,128]{2,1,0:T(8,128)S(1)}, f32[16,16,128]{2,1,0:T(8,128)S(1)}, u32[]{:S(2)}, u32[]{:S(2)}) %collective-permute-start.14) | collective-permute-done | bytes 131104 | tf_op jit(solution)/shard_map/ppermute | solution.py:12
  59.9 0.6 fusion.25
  60.4 0.6 fusion.24
  61.2 3.6 %collective-permute-start.17 = (f32[16,896]{1,0:T(8,128)S(1)}, f32[16,896]{1,0:T(8,128)S(1)}, u32[]{:S(2)}, u32[]{:S(2)}) collective-permute-start(f32[16,896]{1,0:T(8,128)S(1)} %pad_maximum_fusion.13), channel_id=1, source_target_pairs={{0,12},{1,13},{2,14},{3,15},{4,0},{5,1},{6,2},{7,3},{8,4},{9,5},{1... | collective-permute-start | bytes 172040 | tf_op jit(solution)/shard_map/ppermute | solution.py:12
  64.8 0.7 collective-permute-start.18
  65.5 1.3 %collective-permute-done.16 = f32[16,896]{1,0:T(8,128)S(1)} collective-permute-done((f32[16,896]{1,0:T(8,128)S(1)}, f32[16,896]{1,0:T(8,128)S(1)}, u32[]{:S(2)}, u32[]{:S(2)}) %collective-permute-start.16) | collective-permute-done | bytes 57376 | tf_op jit(solution)/shard_map/ppermute | solution.py:12
  66.8 5.2 %collective-permute-done.18 = f32[16,896]{1,0:T(8,128)S(1)} collective-permute-done((f32[16,896]{1,0:T(8,128)S(1)}, f32[16,896]{1,0:T(8,128)S(1)}, u32[]{:S(2)}, u32[]{:S(2)}) %collective-permute-start.18) | collective-permute-done | bytes 57376 | tf_op jit(solution)/shard_map/ppermute | solution.py:12
  73.4 0.7 collective-permute-start.19
  74.1 3.3 %collective-permute-done.19 = f32[17,16,128]{2,1,0:T(8,128)S(1)} collective-permute-done((f32[17,16,128]{2,1,0:T(8,128)S(1)}, f32[17,16,128]{2,1,0:T(8,128)S(1)}, u32[]{:S(2)}, u32[]{:S(2)}) %collective-permute-start.19) | collective-permute-done | bytes 139296 | tf_op jit(solution)/shard_map/ppermute | solution.py:12
  77.5 2.7 %collective-permute-start.21 = (f32[17,16,128]{2,1,0:T(8,128)S(1)}, f32[17,16,128]{2,1,0:T(8,128)}, u32[]{:S(2)}, u32[]{:S(2)}) collective-permute-start(f32[17,16,128]{2,1,0:T(8,128)S(1)} %fusion.73), channel_id=1, source_target_pairs={{0,96},{16,112},{32,0},{48,16},{64,32},{80,48},{96,64},{112,80},{1... | collective-permute-start | bytes 417800 | tf_op jit(solution)/shard_map/ppermute | solution.py:12
  80.2 2.5 %collective-permute-done.20 = f32[17,16,128]{2,1,0:T(8,128)} collective-permute-done((f32[17,16,128]{2,1,0:T(8,128)S(1)}, f32[17,16,128]{2,1,0:T(8,128)}, u32[]{:S(2)}, u32[]{:S(2)}) %collective-permute-start.20) | collective-permute-done | bytes 139296 | tf_op jit(solution)/shard_map/ppermute | solution.py:12
  82.7 0.9 collective-permute-done.21
  83.7 2.0 %collective-permute-done.22 = f32[17,16,128]{2,1,0:T(8,128)} collective-permute-done((f32[17,16,128]{2,1,0:T(8,128)S(1)}, f32[17,16,128]{2,1,0:T(8,128)}, u32[]{:S(2)}, u32[]{:S(2)}) %collective-permute-start.22) | collective-permute-done | bytes 139296 | tf_op jit(solution)/shard_map/ppermute | solution.py:12
  85.7 1.1 add_add_fusion
  87.7 0.6 fusion.22
  88.5 3.6 %collective-permute-start.24 = (f32[16,896]{1,0:T(8,128)S(1)}, f32[16,896]{1,0:T(8,128)S(1)}, u32[]{:S(2)}, u32[]{:S(2)}) collective-permute-start(f32[16,896]{1,0:T(8,128)S(1)} %pad_maximum_fusion.14), channel_id=1, source_target_pairs={{0,12},{1,13},{2,14},{3,15},{4,0},{5,1},{6,2},{7,3},{8,4},{9,5},{1... | collective-permute-start | bytes 172040 | tf_op jit(solution)/shard_map/ppermute | solution.py:12
  92.1 0.8 collective-permute-start.25
  92.9 0.8 collective-permute-done.23
  93.7 6.7 %collective-permute-done.25 = f32[16,896]{1,0:T(8,128)S(1)} collective-permute-done((f32[16,896]{1,0:T(8,128)S(1)}, f32[16,896]{1,0:T(8,128)S(1)}, u32[]{:S(2)}, u32[]{:S(2)}) %collective-permute-start.25) | collective-permute-done | bytes 57376 | tf_op jit(solution)/shard_map/ppermute | solution.py:12
  102.6 6.4 %collective-permute-start.26 = (f32[9,16,128]{2,1,0:T(8,128)S(1)}, f32[9,16,128]{2,1,0:T(8,128)S(1)}, u32[]{:S(2)}, u32[]{:S(2)}) collective-permute-start(f32[9,16,128]{2,1,0:T(8,128)S(1)} %get-tuple-element.53), channel_id=1, source_target_pairs={{0,16},{16,0},{32,48},{48,32},{64,80},{80,64},{96,112},{112,96},{1... | collective-permute-start | bytes 221192 | tf_op jit(solution)/shard_map/ppermute | solution.py:12
  108.9 0.7 pad_maximum_fusion.4
  109.6 3.6 %all-to-all-start = ((f32[16,24,128]{2,1,0:T(8,128)}), f32[16,24,128]{2,1,0:T(8,128)S(1)}, u32[]{:S(2)}, u32[]{:S(2)}) async-start(f32[16,24,128]{2,1,0:T(8,128)} %pad_maximum_fusion.4), calls=%async_computation | async-start | bytes 393216 | tf_op jit(solution)/shard_map/all_to_all | solution.py:164
  114.1 5.6 %all-to-all-done = f32[16,24,128]{2,1,0:T(8,128)S(1)} async-done(((f32[16,24,128]{2,1,0:T(8,128)}), f32[16,24,128]{2,1,0:T(8,128)S(1)}, u32[]{:S(2)}, u32[]{:S(2)}) %all-to-all-start) | async-done | bytes 196640 | tf_op jit(solution)/shard_map/all_to_all | solution.py:164
  120.7 2.3 %collective-permute-start.28 = (f32[64,32]{0,1:T(8,128)S(1)}, f32[64,32]{0,1:T(8,128)S(1)}, u32[]{:S(2)}, u32[]{:S(2)}) collective-permute-start(f32[64,32]{0,1:T(8,128)S(1)} %get-tuple-element.43), channel_id=1, source_target_pairs={{0,2},{1,3},{2,0},{3,1},{4,6},{5,7},{6,4},{7,5},{8,10},{9,11},{10,... | collective-permute-start | bytes 24584 | tf_op jit(solution)/shard_map/ppermute | solution.py:12
  123.2 1.6 %collective-permute-done.28 = f32[64,32]{0,1:T(8,128)S(1)} collective-permute-done((f32[64,32]{0,1:T(8,128)S(1)}, f32[64,32]{0,1:T(8,128)S(1)}, u32[]{:S(2)}, u32[]{:S(2)}) %collective-permute-start.28) | collective-permute-done | bytes 8224 | tf_op jit(solution)/shard_map/ppermute | solution.py:12
  124.8 2.0 %collective-permute-done.29 = f32[64,32]{0,1:T(8,128)S(1)} collective-permute-done((f32[64,32]{0,1:T(8,128)S(1)}, f32[64,32]{0,1:T(8,128)S(1)}, u32[]{:S(2)}, u32[]{:S(2)}) %collective-permute-start.29) | collective-permute-done | bytes 8224 | tf_op jit(solution)/shard_map/ppermute | solution.py:12
  127.0 0.7 copy.109
  127.7 0.7 copy.110
  (141 shorter events, 10.3 us)
Async XLA Ops:
  0.6 5.6 %copy-start = (bf16[1,384,512]{2,1,0:T(8,128)(2,1)S(1)}, bf16[1,384,512]{2,1,0:T(8,128)(2,1)}, u32[]{:S(2)}) copy-start(bf16[1,384,512]{2,1,0:T(8,128)(2,1)} %param.2) | copy-start | bytes 1179652
  0.6 29.4 %collective-permute-start.8 = (bf16[384,512]{1,0:T(8,128)(2,1)}, bf16[384,512]{1,0:T(8,128)(2,1)S(1)}, u32[]{:S(2)}, u32[]{:S(2)}) collective-permute-start(bf16[384,512]{1,0:T(8,128)(2,1)} %bitcast.178), channel_id=1, source_target_pairs={{0,3},{1,0},{2,1},{3,2},{4,7},{5,4},{6,5},{7,6},{8,11},{9,8},{10,9... | collective-permute-start | bytes 1179656 | tf_op jit(solution)/shard_map/ppermute | solution.py:12
  6.1 24.0 %collective-permute-start.6 = (bf16[416,512]{1,0:T(8,128)(2,1)S(1)}, bf16[416,512]{1,0:T(8,128)(2,1)S(1)}, u32[]{:S(2)}, u32[]{:S(2)}) collective-permute-start(bf16[416,512]{1,0:T(8,128)(2,1)S(1)} %pad_maximum_fusion.1), channel_id=1, source_target_pairs={{0,1},{1,2},{2,3},{3,0},{4,5},{5,6},{6,7},{7,4},{8,9},{9,10},{10,1... | collective-permute-start | bytes 1277960 | tf_op jit(solution)/shard_map/ppermute | solution.py:12
  6.5 12.9 %collective-permute-start = (f32[32,384]{1,0:T(8,128)S(1)}, f32[32,384]{1,0:T(8,128)S(1)}, u32[]{:S(2)}, u32[]{:S(2)}) collective-permute-start(f32[32,384]{1,0:T(8,128)S(1)} %get-tuple-element.36), channel_id=1, source_target_pairs={{0,1},{1,2},{2,3},{3,0},{4,5},{5,6},{6,7},{7,4},{8,9},{9,10},{10,1... | collective-permute-start | bytes 147464 | tf_op jit(solution)/shard_map/ppermute | solution.py:12
  6.8 12.6 %collective-permute-start.1 = (f32[32,384]{1,0:T(8,128)S(1)}, f32[32,384]{1,0:T(8,128)S(1)}, u32[]{:S(2)}, u32[]{:S(2)}) collective-permute-start(f32[32,384]{1,0:T(8,128)S(1)} %get-tuple-element.38), channel_id=1, source_target_pairs={{0,3},{1,0},{2,1},{3,2},{4,7},{5,4},{6,5},{7,6},{8,11},{9,8},{10,9... | collective-permute-start | bytes 147464 | tf_op jit(solution)/shard_map/ppermute | solution.py:12
  9.4 10.1 %collective-permute-start.2 = (f32[32,384]{1,0:T(8,128)S(1)}, f32[32,384]{1,0:T(8,128)S(1)}, u32[]{:S(2)}, u32[]{:S(2)}) collective-permute-start(f32[32,384]{1,0:T(8,128)S(1)} %get-tuple-element.37), channel_id=1, source_target_pairs={{0,2},{1,3},{2,0},{3,1},{4,6},{5,7},{6,4},{7,5},{8,10},{9,11},{10,... | collective-permute-start | bytes 147464 | tf_op jit(solution)/shard_map/ppermute | solution.py:12
  19.4 12.3 %collective-permute-start.3 = (f32[32,384]{1,0:T(8,128)S(1)}, f32[32,384]{1,0:T(8,128)S(1)}, u32[]{:S(2)}, u32[]{:S(2)}) collective-permute-start(f32[32,384]{1,0:T(8,128)S(1)} %fusion.34), channel_id=1, source_target_pairs={{0,4},{1,5},{2,6},{3,7},{4,8},{5,9},{6,10},{7,11},{8,12},{9,13},{1... | collective-permute-start | bytes 147464 | tf_op jit(solution)/shard_map/ppermute | solution.py:12
  22.5 9.2 %collective-permute-start.4 = (f32[32,384]{1,0:T(8,128)S(1)}, f32[32,384]{1,0:T(8,128)S(1)}, u32[]{:S(2)}, u32[]{:S(2)}) collective-permute-start(f32[32,384]{1,0:T(8,128)S(1)} %fusion.34), channel_id=1, source_target_pairs={{0,12},{1,13},{2,14},{3,15},{4,0},{5,1},{6,2},{7,3},{8,4},{9,5},{1... | collective-permute-start | bytes 147464 | tf_op jit(solution)/shard_map/ppermute | solution.py:12
  25.6 6.9 %collective-permute-start.5 = (f32[32,384]{1,0:T(8,128)S(1)}, f32[32,384]{1,0:T(8,128)S(1)}, u32[]{:S(2)}, u32[]{:S(2)}) collective-permute-start(f32[32,384]{1,0:T(8,128)S(1)} %fusion.34), channel_id=1, source_target_pairs={{0,8},{1,9},{2,10},{3,11},{4,12},{5,13},{6,14},{7,15},{8,0},{9,1},... | collective-permute-start | bytes 147464 | tf_op jit(solution)/shard_map/ppermute | solution.py:12
  30.0 5.2 %collective-permute-start.9 = (bf16[224,512]{1,0:T(8,128)(2,1)S(1)}, bf16[224,512]{1,0:T(8,128)(2,1)S(1)}, u32[]{:S(2)}, u32[]{:S(2)}) collective-permute-start(bf16[224,512]{1,0:T(8,128)(2,1)S(1)} %pad_maximum_fusion.3), channel_id=1, source_target_pairs={{0,3},{1,0},{2,1},{3,2},{4,7},{5,4},{6,5},{7,6},{8,11},{9,8},{10,9... | collective-permute-start | bytes 688136 | tf_op jit(solution)/shard_map/ppermute | solution.py:12
  30.2 6.5 %collective-permute-start.7 = (bf16[256,512]{1,0:T(8,128)(2,1)S(1)}, bf16[256,512]{1,0:T(8,128)(2,1)S(1)}, u32[]{:S(2)}, u32[]{:S(2)}) collective-permute-start(bf16[256,512]{1,0:T(8,128)(2,1)S(1)} %pad_maximum_fusion.2), channel_id=1, source_target_pairs={{0,1},{1,2},{2,3},{3,0},{4,5},{5,6},{6,7},{7,4},{8,9},{9,10},{10,1... | collective-permute-start | bytes 786440 | tf_op jit(solution)/shard_map/ppermute | solution.py:12
  35.3 1.6 %copy-start.1 = (bf16[224,512]{1,0:T(8,128)(2,1)}, bf16[224,512]{1,0:T(8,128)(2,1)S(1)}, u32[]{:S(2)}) copy-start(bf16[224,512]{1,0:T(8,128)(2,1)S(1)} %collective-permute-done.9) | copy-start | bytes 688132
  37.3 4.8 %slice-start = ((bf16[224,512]{1,0:T(8,128)(2,1)}), bf16[32,512]{1,0:T(8,128)(2,1)S(1)}, s32[]{:S(2)}) async-start(bf16[224,512]{1,0:T(8,128)(2,1)} %copy-done.1), calls=%async_computation.1 | async-start | bytes 65536 | tf_op jit(solution)/shard_map/slice | solution.py:118
  37.3 16.9 %collective-permute-start.15 = (bf16[384,2048]{1,0:T(8,128)(2,1)S(1)}, bf16[384,2048]{1,0:T(8,128)(2,1)S(1)}, u32[]{:S(2)}, u32[]{:S(2)}) collective-permute-start(bf16[384,2048]{1,0:T(8,128)(2,1)S(1)} %pad_maximum_fusion), channel_id=1, source_target_pairs={{0,16},{16,0},{32,48},{48,32},{64,80},{80,64},{96,112},{112,96},{1... | collective-permute-start | bytes 4718600 | tf_op jit(solution)/shard_map/ppermute | solution.py:12
  42.3 2.6 %collective-permute-start.10 = (f32[16,16,128]{2,1,0:T(8,128)S(1)}, f32[16,16,128]{2,1,0:T(8,128)S(1)}, u32[]{:S(2)}, u32[]{:S(2)}) collective-permute-start(f32[16,16,128]{2,1,0:T(8,128)S(1)} %bitcast.196), channel_id=1, source_target_pairs={{0,16},{16,0},{32,48},{48,32},{64,80},{80,64},{96,112},{112,96},{1... | collective-permute-start | bytes 393224 | tf_op jit(solution)/shard_map/ppermute | solution.py:12
  45.0 4.8 %collective-permute-start.11 = (f32[16,16,128]{2,1,0:T(8,128)S(1)}, f32[16,16,128]{2,1,0:T(8,128)S(1)}, u32[]{:S(2)}, u32[]{:S(2)}) collective-permute-start(f32[16,16,128]{2,1,0:T(8,128)S(1)} %fusion.19), channel_id=1, source_target_pairs={{0,128},{16,144},{32,160},{48,176},{64,192},{80,208},{96,224},{112... | collective-permute-start | bytes 393224 | tf_op jit(solution)/shard_map/ppermute | solution.py:12
  49.8 5.2 %collective-permute-start.12 = (f32[16,16,128]{2,1,0:T(8,128)S(1)}, f32[16,16,128]{2,1,0:T(8,128)S(1)}, u32[]{:S(2)}, u32[]{:S(2)}) collective-permute-start(f32[16,16,128]{2,1,0:T(8,128)S(1)} %add.233), channel_id=1, source_target_pairs={{0,32},{16,48},{32,64},{48,80},{64,96},{80,112},{96,0},{112,16},{1... | collective-permute-start | bytes 393224 | tf_op jit(solution)/shard_map/ppermute | solution.py:12
  51.1 3.8 %collective-permute-start.13 = (f32[16,16,128]{2,1,0:T(8,128)S(1)}, f32[16,16,128]{2,1,0:T(8,128)S(1)}, u32[]{:S(2)}, u32[]{:S(2)}) collective-permute-start(f32[16,16,128]{2,1,0:T(8,128)S(1)} %add.233), channel_id=1, source_target_pairs={{0,96},{16,112},{32,0},{48,16},{64,32},{80,48},{96,64},{112,80},{1... | collective-permute-start | bytes 393224 | tf_op jit(solution)/shard_map/ppermute | solution.py:12
  52.7 7.0 %collective-permute-start.14 = (f32[16,16,128]{2,1,0:T(8,128)S(1)}, f32[16,16,128]{2,1,0:T(8,128)S(1)}, u32[]{:S(2)}, u32[]{:S(2)}) collective-permute-start(f32[16,16,128]{2,1,0:T(8,128)S(1)} %add.233), channel_id=1, source_target_pairs={{0,64},{16,80},{32,96},{48,112},{64,0},{80,16},{96,32},{112,48},{1... | collective-permute-start | bytes 393224 | tf_op jit(solution)/shard_map/ppermute | solution.py:12
  61.1 5.7 %collective-permute-start.16 = (f32[16,896]{1,0:T(8,128)S(1)}, f32[16,896]{1,0:T(8,128)S(1)}, u32[]{:S(2)}, u32[]{:S(2)}) collective-permute-start(f32[16,896]{1,0:T(8,128)S(1)} %pad_maximum_fusion.13), channel_id=1, source_target_pairs={{0,4},{1,5},{2,6},{3,7},{4,8},{5,9},{6,10},{7,11},{8,12},{9,13},{1... | collective-permute-start | bytes 172040 | tf_op jit(solution)/shard_map/ppermute | solution.py:12
  61.2 5.6 %collective-permute-start.17 = (f32[16,896]{1,0:T(8,128)S(1)}, f32[16,896]{1,0:T(8,128)S(1)}, u32[]{:S(2)}, u32[]{:S(2)}) collective-permute-start(f32[16,896]{1,0:T(8,128)S(1)} %pad_maximum_fusion.13), channel_id=1, source_target_pairs={{0,12},{1,13},{2,14},{3,15},{4,0},{5,1},{6,2},{7,3},{8,4},{9,5},{1... | collective-permute-start | bytes 172040 | tf_op jit(solution)/shard_map/ppermute | solution.py:12
  64.8 7.3 %collective-permute-start.18 = (f32[16,896]{1,0:T(8,128)S(1)}, f32[16,896]{1,0:T(8,128)S(1)}, u32[]{:S(2)}, u32[]{:S(2)}) collective-permute-start(f32[16,896]{1,0:T(8,128)S(1)} %pad_maximum_fusion.13), channel_id=1, source_target_pairs={{0,8},{1,9},{2,10},{3,11},{4,12},{5,13},{6,14},{7,15},{8,0},{9,1},... | collective-permute-start | bytes 172040 | tf_op jit(solution)/shard_map/ppermute | solution.py:12
  73.4 4.0 %collective-permute-start.19 = (f32[17,16,128]{2,1,0:T(8,128)S(1)}, f32[17,16,128]{2,1,0:T(8,128)S(1)}, u32[]{:S(2)}, u32[]{:S(2)}) collective-permute-start(f32[17,16,128]{2,1,0:T(8,128)S(1)} %pad_maximum_fusion.5), channel_id=1, source_target_pairs={{0,128},{16,144},{32,160},{48,176},{64,192},{80,208},{96,224},{112... | collective-permute-start | bytes 417800 | tf_op jit(solution)/shard_map/ppermute | solution.py:12
  77.4 5.3 %collective-permute-start.20 = (f32[17,16,128]{2,1,0:T(8,128)S(1)}, f32[17,16,128]{2,1,0:T(8,128)}, u32[]{:S(2)}, u32[]{:S(2)}) collective-permute-start(f32[17,16,128]{2,1,0:T(8,128)S(1)} %fusion.73), channel_id=1, source_target_pairs={{0,32},{16,48},{32,64},{48,80},{64,96},{80,112},{96,0},{112,16},{1... | collective-permute-start | bytes 417800 | tf_op jit(solution)/shard_map/ppermute | solution.py:12
  77.5 6.2 %collective-permute-start.21 = (f32[17,16,128]{2,1,0:T(8,128)S(1)}, f32[17,16,128]{2,1,0:T(8,128)}, u32[]{:S(2)}, u32[]{:S(2)}) collective-permute-start(f32[17,16,128]{2,1,0:T(8,128)S(1)} %fusion.73), channel_id=1, source_target_pairs={{0,96},{16,112},{32,0},{48,16},{64,32},{80,48},{96,64},{112,80},{1... | collective-permute-start | bytes 417800 | tf_op jit(solution)/shard_map/ppermute | solution.py:12
  80.2 5.5 %collective-permute-start.22 = (f32[17,16,128]{2,1,0:T(8,128)S(1)}, f32[17,16,128]{2,1,0:T(8,128)}, u32[]{:S(2)}, u32[]{:S(2)}) collective-permute-start(f32[17,16,128]{2,1,0:T(8,128)S(1)} %fusion.73), channel_id=1, source_target_pairs={{0,64},{16,80},{32,96},{48,112},{64,0},{80,16},{96,32},{112,48},{1... | collective-permute-start | bytes 417800 | tf_op jit(solution)/shard_map/ppermute | solution.py:12
  88.4 5.2 %collective-permute-start.23 = (f32[16,896]{1,0:T(8,128)S(1)}, f32[16,896]{1,0:T(8,128)S(1)}, u32[]{:S(2)}, u32[]{:S(2)}) collective-permute-start(f32[16,896]{1,0:T(8,128)S(1)} %pad_maximum_fusion.14), channel_id=1, source_target_pairs={{0,4},{1,5},{2,6},{3,7},{4,8},{5,9},{6,10},{7,11},{8,12},{9,13},{1... | collective-permute-start | bytes 172040 | tf_op jit(solution)/shard_map/ppermute | solution.py:12
  88.5 5.1 %collective-permute-start.24 = (f32[16,896]{1,0:T(8,128)S(1)}, f32[16,896]{1,0:T(8,128)S(1)}, u32[]{:S(2)}, u32[]{:S(2)}) collective-permute-start(f32[16,896]{1,0:T(8,128)S(1)} %pad_maximum_fusion.14), channel_id=1, source_target_pairs={{0,12},{1,13},{2,14},{3,15},{4,0},{5,1},{6,2},{7,3},{8,4},{9,5},{1... | collective-permute-start | bytes 172040 | tf_op jit(solution)/shard_map/ppermute | solution.py:12
  92.1 8.3 %collective-permute-start.25 = (f32[16,896]{1,0:T(8,128)S(1)}, f32[16,896]{1,0:T(8,128)S(1)}, u32[]{:S(2)}, u32[]{:S(2)}) collective-permute-start(f32[16,896]{1,0:T(8,128)S(1)} %pad_maximum_fusion.14), channel_id=1, source_target_pairs={{0,8},{1,9},{2,10},{3,11},{4,12},{5,13},{6,14},{7,15},{8,0},{9,1},... | collective-permute-start | bytes 172040 | tf_op jit(solution)/shard_map/ppermute | solution.py:12
  102.6 10.7 %collective-permute-start.26 = (f32[9,16,128]{2,1,0:T(8,128)S(1)}, f32[9,16,128]{2,1,0:T(8,128)S(1)}, u32[]{:S(2)}, u32[]{:S(2)}) collective-permute-start(f32[9,16,128]{2,1,0:T(8,128)S(1)} %get-tuple-element.53), channel_id=1, source_target_pairs={{0,16},{16,0},{32,48},{48,32},{64,80},{80,64},{96,112},{112,96},{1... | collective-permute-start | bytes 221192 | tf_op jit(solution)/shard_map/ppermute | solution.py:12
  109.6 10.0 %all-to-all-start = ((f32[16,24,128]{2,1,0:T(8,128)}), f32[16,24,128]{2,1,0:T(8,128)S(1)}, u32[]{:S(2)}, u32[]{:S(2)}) async-start(f32[16,24,128]{2,1,0:T(8,128)} %pad_maximum_fusion.4), calls=%async_computation | async-start | bytes 393216 | tf_op jit(solution)/shard_map/all_to_all | solution.py:164
  120.5 2.7 %collective-permute-start.27 = (f32[64,32]{0,1:T(8,128)S(1)}, f32[64,32]{0,1:T(8,128)S(1)}, u32[]{:S(2)}, u32[]{:S(2)}) collective-permute-start(f32[64,32]{0,1:T(8,128)S(1)} %get-tuple-element.42), channel_id=1, source_target_pairs={{0,3},{1,0},{2,1},{3,2},{4,7},{5,4},{6,5},{7,6},{8,11},{9,8},{10,9... | collective-permute-start | bytes 24584 | tf_op jit(solution)/shard_map/ppermute | solution.py:12
  120.7 4.1 %collective-permute-start.28 = (f32[64,32]{0,1:T(8,128)S(1)}, f32[64,32]{0,1:T(8,128)S(1)}, u32[]{:S(2)}, u32[]{:S(2)}) collective-permute-start(f32[64,32]{0,1:T(8,128)S(1)} %get-tuple-element.43), channel_id=1, source_target_pairs={{0,2},{1,3},{2,0},{3,1},{4,6},{5,7},{6,4},{7,5},{8,10},{9,11},{10,... | collective-permute-start | bytes 24584 | tf_op jit(solution)/shard_map/ppermute | solution.py:12
  123.0 3.8 %collective-permute-start.29 = (f32[64,32]{0,1:T(8,128)S(1)}, f32[64,32]{0,1:T(8,128)S(1)}, u32[]{:S(2)}, u32[]{:S(2)}) collective-permute-start(f32[64,32]{0,1:T(8,128)S(1)} %get-tuple-element.41), channel_id=1, source_target_pairs={{0,1},{1,2},{2,3},{3,0},{4,5},{5,6},{6,7},{7,4},{8,9},{9,10},{10,1... | collective-permute-start | bytes 24584 | tf_op jit(solution)/shard_map/ppermute | solution.py:12

commit v8 on v7

--- a/solution.py
+++ b/solution.py
@@ -1,6 +1,7 @@
 import jax
 import jax.numpy as jnp
 from jax import lax
+from jax.experimental.layout import Layout, with_layout_constraint
 from jax.sharding import PartitionSpec as P
 
 
@@ -188,10 +189,16 @@
     merged = per_lane(alpha0) * my_target + alpha1 * (my_residual + per_lane(beta) * my_target)
     both = jnp.concatenate([merged, my_residual - alpha1 * part])
 
-    two, three, one = staged(lambda k: both[:, 128 - 32 * k : 160 - 32 * k], x_move)
-    groups = jnp.stack([both[:, :32], three, two, one])
-    groups = lax.dynamic_slice_in_dim(jnp.concatenate([groups, groups]), (4 - x) % 4, 4, 0)
-    result = groups.transpose(1, 0, 2).reshape(64, 128)
+    mine = lax.broadcasted_iota(jnp.int32, (64, 128), 1) // 32 == x
+
+    turns = jnp.stack([jnp.roll(both, 32 * k, axis=1) for k in range(4)])
+
+    def placed(k):
+        piece = jnp.where(mine, pick(turns, (x - k) % 4), 0.0)
+        return with_layout_constraint(piece, Layout(major_to_minor=(0, 1)))
+
+    two, three, one = staged(lambda k: placed(4 - k), x_move)
+    result = placed(0) + three + two + one
     return result[:32], result[32:]
 
 

time: 129 us -> 128 us (level)
    all_to_all x1, starting transfers between devices: 3.64 us -> 9.6 us  [on_device(): part = lax.all_to_all(jnp.concatenate([part, curve], axis=1), 'task', 0, 0)]
    ppermute x30, starting transfers between devices: 50.5 us -> 44.7 us  [moved(): return lax.ppermute(value, axis, [(i, to(i)) for i in range(16)])]
    unnamed x14 -> x7, local copies, waits for them, and re-layouts: 2.49 us -> 1.11 us
    all_to_all x1, waiting for transfers between devices: 5.6 us -> 4.31 us  [on_device(): part = lax.all_to_all(jnp.concatenate([part, curve], axis=1), 'task', 0, 0)]
  transfers between devices with their start and end apart: 31 -> 31, of which waited for: 20 -> 21; matrix products, arithmetic and copies ran while one was open for 4% -> 3% of each run, Pallas kernels for 0% -> 0%
where the time goes in v8:
time: 128 us
  waiting for transfers between devices  57.3 us (45%)
  starting transfers between devices  54.3 us (42%)
  other arithmetic  6.41 us (5%)
  matrix products  4.49 us (4%)
  local copies, waits for them, and re-layouts  4.28 us (3%)
    ppermute x30, waiting for transfers between devices, moved(): return lax.ppermute(value, axis, [(i, to(i)) for i in range(16)])  53 us
    ppermute x30, starting transfers between devices, moved(): return lax.ppermute(value, axis, [(i, to(i)) for i in range(16)])  44.7 us
    all_to_all x1, starting transfers between devices, on_device(): part = lax.all_to_all(jnp.concatenate([part, curve], axis=1), 'task', 0, 0)  9.6 us
    all_to_all x1, waiting for transfers between devices, on_device(): part = lax.all_to_all(jnp.concatenate([part, curve], axis=1), 'task', 0, 0)  4.31 us
    dot_general x9, matrix products, product(): lax.dot_general(pieces(value), x, (((1,), (dim,)), ((), ())), preferred_e...  4.21 us
  transfers between devices with their start and end apart: 31, of which 21 were waited for; matrix products, arithmetic and copies ran while one was open for 3% of the time, Pallas kernels for 0%

profile of v8, /device:TPU:1, one launch (start us, length us, event | category | flops | bytes accessed | tf_op | source)
XLA Modules:
  0.0 128.0 jit_solution(16845157324966922503)
XLA Ops:
  0.6 3.4 %collective-permute-start.8 = (bf16[384,512]{1,0:T(8,128)(2,1)}, bf16[384,512]{1,0:T(8,128)(2,1)S(1)}, u32[]{:S(2)}, u32[]{:S(2)}) collective-permute-start(bf16[384,512]{1,0:T(8,128)(2,1)} %bitcast.181), channel_id=1, source_target_pairs={{0,3},{1,0},{2,1},{3,2},{4,7},{5,4},{6,5},{7,6},{8,11},{9,8},{10,9... | collective-permute-start | bytes 1179656 | tf_op jit(solution)/shard_map/ppermute | solution.py:13
  4.0 1.0 copy.96
  5.1 1.0 pad_maximum_fusion.1
  6.8 2.6 %collective-permute-start.1 = (f32[32,384]{1,0:T(8,128)S(1)}, f32[32,384]{1,0:T(8,128)S(1)}, u32[]{:S(2)}, u32[]{:S(2)}) collective-permute-start(f32[32,384]{1,0:T(8,128)S(1)} %get-tuple-element.32), channel_id=1, source_target_pairs={{0,3},{1,0},{2,1},{3,2},{4,7},{5,4},{6,5},{7,6},{8,11},{9,8},{10,9... | collective-permute-start | bytes 147464 | tf_op jit(solution)/shard_map/ppermute | solution.py:13
  9.3 1.1 collective-permute-start.2
  10.4 9.0 %collective-permute-done = f32[32,384]{1,0:T(8,128)S(1)} collective-permute-done((f32[32,384]{1,0:T(8,128)S(1)}, f32[32,384]{1,0:T(8,128)S(1)}, u32[]{:S(2)}, u32[]{:S(2)}) %collective-permute-start) | collective-permute-done | bytes 49184 | tf_op jit(solution)/shard_map/ppermute | solution.py:13
  19.4 3.1 %collective-permute-start.3 = (f32[32,384]{1,0:T(8,128)S(1)}, f32[32,384]{1,0:T(8,128)S(1)}, u32[]{:S(2)}, u32[]{:S(2)}) collective-permute-start(f32[32,384]{1,0:T(8,128)S(1)} %fusion.34), channel_id=1, source_target_pairs={{0,4},{1,5},{2,6},{3,7},{4,8},{5,9},{6,10},{7,11},{8,12},{9,13},{1... | collective-permute-start | bytes 147464 | tf_op jit(solution)/shard_map/ppermute | solution.py:13
  22.5 3.1 %collective-permute-start.4 = (f32[32,384]{1,0:T(8,128)S(1)}, f32[32,384]{1,0:T(8,128)S(1)}, u32[]{:S(2)}, u32[]{:S(2)}) collective-permute-start(f32[32,384]{1,0:T(8,128)S(1)} %fusion.34), channel_id=1, source_target_pairs={{0,12},{1,13},{2,14},{3,15},{4,0},{5,1},{6,2},{7,3},{8,4},{9,5},{1... | collective-permute-start | bytes 147464 | tf_op jit(solution)/shard_map/ppermute | solution.py:13
  25.6 4.4 %collective-permute-start.5 = (f32[32,384]{1,0:T(8,128)S(1)}, f32[32,384]{1,0:T(8,128)S(1)}, u32[]{:S(2)}, u32[]{:S(2)}) collective-permute-start(f32[32,384]{1,0:T(8,128)S(1)} %fusion.34), channel_id=1, source_target_pairs={{0,8},{1,9},{2,10},{3,11},{4,12},{5,13},{6,14},{7,15},{8,0},{9,1},... | collective-permute-start | bytes 147464 | tf_op jit(solution)/shard_map/ppermute | solution.py:13
  30.2 1.5 %collective-permute-start.7 = (bf16[256,512]{1,0:T(8,128)(2,1)S(1)}, bf16[256,512]{1,0:T(8,128)(2,1)S(1)}, u32[]{:S(2)}, u32[]{:S(2)}) collective-permute-start(bf16[256,512]{1,0:T(8,128)(2,1)S(1)} %pad_maximum_fusion.2), channel_id=1, source_target_pairs={{0,1},{1,2},{2,3},{3,0},{4,5},{5,6},{6,7},{7,4},{8,9},{9,10},{10,1... | collective-permute-start | bytes 786440 | tf_op jit(solution)/shard_map/ppermute | solution.py:13
  31.7 0.8 collective-permute-done.5
  32.6 2.7 %collective-permute-done.9 = bf16[224,512]{1,0:T(8,128)(2,1)S(1)} collective-permute-done((bf16[224,512]{1,0:T(8,128)(2,1)S(1)}, bf16[224,512]{1,0:T(8,128)(2,1)S(1)}, u32[]{:S(2)}, u32[]{:S(2)}) %collective-permute-start.9) | collective-permute-done | bytes 229408 | tf_op jit(solution)/shard_map/ppermute | solution.py:13
  35.3 1.4 %collective-permute-done.7 = bf16[256,512]{1,0:T(8,128)(2,1)S(1)} collective-permute-done((bf16[256,512]{1,0:T(8,128)(2,1)S(1)}, bf16[256,512]{1,0:T(8,128)(2,1)S(1)}, u32[]{:S(2)}, u32[]{:S(2)}) %collective-permute-start.7) | collective-permute-done | bytes 262176 | tf_op jit(solution)/shard_map/ppermute | solution.py:13
  37.3 4.4 %collective-permute-start.15 = (bf16[384,2048]{1,0:T(8,128)(2,1)S(1)}, bf16[384,2048]{1,0:T(8,128)(2,1)S(1)}, u32[]{:S(2)}, u32[]{:S(2)}) collective-permute-start(bf16[384,2048]{1,0:T(8,128)(2,1)S(1)} %pad_maximum_fusion), channel_id=1, source_target_pairs={{0,16},{16,0},{32,48},{48,32},{64,80},{80,64},{96,112},{112,96},{1... | collective-permute-start | bytes 4718600 | tf_op jit(solution)/shard_map/ppermute | solution.py:13
  42.6 2.3 %collective-permute-done.10 = f32[16,16,128]{2,1,0:T(8,128)S(1)} collective-permute-done((f32[16,16,128]{2,1,0:T(8,128)S(1)}, f32[16,16,128]{2,1,0:T(8,128)S(1)}, u32[]{:S(2)}, u32[]{:S(2)}) %collective-permute-start.10) | collective-permute-done | bytes 131104 | tf_op jit(solution)/shard_map/ppermute | solution.py:13
  45.0 0.8 collective-permute-start.11
  45.8 3.9 %collective-permute-done.11 = f32[16,16,128]{2,1,0:T(8,128)S(1)} collective-permute-done((f32[16,16,128]{2,1,0:T(8,128)S(1)}, f32[16,16,128]{2,1,0:T(8,128)S(1)}, u32[]{:S(2)}, u32[]{:S(2)}) %collective-permute-start.11) | collective-permute-done | bytes 131104 | tf_op jit(solution)/shard_map/ppermute | solution.py:13
  49.8 1.4 %collective-permute-start.12 = (f32[16,16,128]{2,1,0:T(8,128)S(1)}, f32[16,16,128]{2,1,0:T(8,128)S(1)}, u32[]{:S(2)}, u32[]{:S(2)}) collective-permute-start(f32[16,16,128]{2,1,0:T(8,128)S(1)} %add.266), channel_id=1, source_target_pairs={{0,32},{16,48},{32,64},{48,80},{64,96},{80,112},{96,0},{112,16},{1... | collective-permute-start | bytes 393224 | tf_op jit(solution)/shard_map/ppermute | solution.py:13
  51.1 1.5 %collective-permute-start.13 = (f32[16,16,128]{2,1,0:T(8,128)S(1)}, f32[16,16,128]{2,1,0:T(8,128)S(1)}, u32[]{:S(2)}, u32[]{:S(2)}) collective-permute-start(f32[16,16,128]{2,1,0:T(8,128)S(1)} %add.266), channel_id=1, source_target_pairs={{0,96},{16,112},{32,0},{48,16},{64,32},{80,48},{96,64},{112,80},{1... | collective-permute-start | bytes 393224 | tf_op jit(solution)/shard_map/ppermute | solution.py:13
  52.7 1.6 %collective-permute-start.14 = (f32[16,16,128]{2,1,0:T(8,128)S(1)}, f32[16,16,128]{2,1,0:T(8,128)S(1)}, u32[]{:S(2)}, u32[]{:S(2)}) collective-permute-start(f32[16,16,128]{2,1,0:T(8,128)S(1)} %add.266), channel_id=1, source_target_pairs={{0,64},{16,80},{32,96},{48,112},{64,0},{80,16},{96,32},{112,48},{1... | collective-permute-start | bytes 393224 | tf_op jit(solution)/shard_map/ppermute | solution.py:13
  55.0 4.7 %collective-permute-done.14 = f32[16,16,128]{2,1,0:T(8,128)S(1)} collective-permute-done((f32[16,16,128]{2,1,0:T(8,128)S(1)}, f32[16,16,128]{2,1,0:T(8,128)S(1)}, u32[]{:S(2)}, u32[]{:S(2)}) %collective-permute-start.14) | collective-permute-done | bytes 131104 | tf_op jit(solution)/shard_map/ppermute | solution.py:13
  59.9 0.6 fusion.25
  60.4 0.6 fusion.24
  61.2 3.6 %collective-permute-start.17 = (f32[16,896]{1,0:T(8,128)S(1)}, f32[16,896]{1,0:T(8,128)S(1)}, u32[]{:S(2)}, u32[]{:S(2)}) collective-permute-start(f32[16,896]{1,0:T(8,128)S(1)} %pad_maximum_fusion.14), channel_id=1, source_target_pairs={{0,12},{1,13},{2,14},{3,15},{4,0},{5,1},{6,2},{7,3},{8,4},{9,5},{1... | collective-permute-start | bytes 172040 | tf_op jit(solution)/shard_map/ppermute | solution.py:13
  64.8 0.7 collective-permute-start.18
  65.5 1.3 %collective-permute-done.16 = f32[16,896]{1,0:T(8,128)S(1)} collective-permute-done((f32[16,896]{1,0:T(8,128)S(1)}, f32[16,896]{1,0:T(8,128)S(1)}, u32[]{:S(2)}, u32[]{:S(2)}) %collective-permute-start.16) | collective-permute-done | bytes 57376 | tf_op jit(solution)/shard_map/ppermute | solution.py:13
  66.8 5.2 %collective-permute-done.18 = f32[16,896]{1,0:T(8,128)S(1)} collective-permute-done((f32[16,896]{1,0:T(8,128)S(1)}, f32[16,896]{1,0:T(8,128)S(1)}, u32[]{:S(2)}, u32[]{:S(2)}) %collective-permute-start.18) | collective-permute-done | bytes 57376 | tf_op jit(solution)/shard_map/ppermute | solution.py:13
  73.4 0.7 collective-permute-start.19
  74.1 3.3 %collective-permute-done.19 = f32[17,16,128]{2,1,0:T(8,128)S(1)} collective-permute-done((f32[17,16,128]{2,1,0:T(8,128)S(1)}, f32[17,16,128]{2,1,0:T(8,128)S(1)}, u32[]{:S(2)}, u32[]{:S(2)}) %collective-permute-start.19) | collective-permute-done | bytes 139296 | tf_op jit(solution)/shard_map/ppermute | solution.py:13
  77.5 2.7 %collective-permute-start.21 = (f32[17,16,128]{2,1,0:T(8,128)S(1)}, f32[17,16,128]{2,1,0:T(8,128)}, u32[]{:S(2)}, u32[]{:S(2)}) collective-permute-start(f32[17,16,128]{2,1,0:T(8,128)S(1)} %fusion.76), channel_id=1, source_target_pairs={{0,96},{16,112},{32,0},{48,16},{64,32},{80,48},{96,64},{112,80},{1... | collective-permute-start | bytes 417800 | tf_op jit(solution)/shard_map/ppermute | solution.py:13
  80.2 2.5 %collective-permute-done.20 = f32[17,16,128]{2,1,0:T(8,128)} collective-permute-done((f32[17,16,128]{2,1,0:T(8,128)S(1)}, f32[17,16,128]{2,1,0:T(8,128)}, u32[]{:S(2)}, u32[]{:S(2)}) %collective-permute-start.20) | collective-permute-done | bytes 139296 | tf_op jit(solution)/shard_map/ppermute | solution.py:13
  82.7 0.9 collective-permute-done.21
  83.7 2.0 %collective-permute-done.22 = f32[17,16,128]{2,1,0:T(8,128)} collective-permute-done((f32[17,16,128]{2,1,0:T(8,128)S(1)}, f32[17,16,128]{2,1,0:T(8,128)}, u32[]{:S(2)}, u32[]{:S(2)}) %collective-permute-start.22) | collective-permute-done | bytes 139296 | tf_op jit(solution)/shard_map/ppermute | solution.py:13
  85.7 1.1 add_add_fusion
  87.2 0.6 fusion.23
  87.7 0.6 fusion.22
  88.5 3.6 %collective-permute-start.24 = (f32[16,896]{1,0:T(8,128)S(1)}, f32[16,896]{1,0:T(8,128)S(1)}, u32[]{:S(2)}, u32[]{:S(2)}) collective-permute-start(f32[16,896]{1,0:T(8,128)S(1)} %pad_maximum_fusion.15), channel_id=1, source_target_pairs={{0,12},{1,13},{2,14},{3,15},{4,0},{5,1},{6,2},{7,3},{8,4},{9,5},{1... | collective-permute-start | bytes 172040 | tf_op jit(solution)/shard_map/ppermute | solution.py:13
  92.1 0.8 collective-permute-start.25
  92.9 0.8 collective-permute-done.23
  93.7 6.7 %collective-permute-done.25 = f32[16,896]{1,0:T(8,128)S(1)} collective-permute-done((f32[16,896]{1,0:T(8,128)S(1)}, f32[16,896]{1,0:T(8,128)S(1)}, u32[]{:S(2)}, u32[]{:S(2)}) %collective-permute-start.25) | collective-permute-done | bytes 57376 | tf_op jit(solution)/shard_map/ppermute | solution.py:13
  102.5 0.7 pad_maximum_fusion.5
  103.2 9.6 %all-to-all-start = ((f32[16,24,128]{2,1,0:T(8,128)}), f32[16,24,128]{2,1,0:T(8,128)S(1)}, u32[]{:S(2)}, u32[]{:S(2)}) async-start(f32[16,24,128]{2,1,0:T(8,128)} %pad_maximum_fusion.5), calls=%async_computation | async-start | bytes 393216 | tf_op jit(solution)/shard_map/all_to_all | solution.py:165
  113.4 1.0 collective-permute-done.26
  115.2 4.3 %all-to-all-done = f32[16,24,128]{2,1,0:T(8,128)S(1)} async-done(((f32[16,24,128]{2,1,0:T(8,128)}), f32[16,24,128]{2,1,0:T(8,128)S(1)}, u32[]{:S(2)}, u32[]{:S(2)}) %all-to-all-start) | async-done | bytes 196640 | tf_op jit(solution)/shard_map/all_to_all | solution.py:165
  121.1 2.3 %collective-permute-start.28 = (f32[64,128]{1,0:T(8,128)S(1)}, f32[64,128]{1,0:T(8,128)S(1)}, u32[]{:S(2)}, u32[]{:S(2)}) collective-permute-start(f32[64,128]{1,0:T(8,128)S(1)} %get-tuple-element.65), channel_id=1, source_target_pairs={{0,2},{1,3},{2,0},{3,1},{4,6},{5,7},{6,4},{7,5},{8,10},{9,11},{10,... | collective-permute-start | bytes 98312 | tf_op jit(solution)/shard_map/ppermute | solution.py:13
  123.8 1.6 %collective-permute-done.28 = f32[64,128]{1,0:T(8,128)S(1)} collective-permute-done((f32[64,128]{1,0:T(8,128)S(1)}, f32[64,128]{1,0:T(8,128)S(1)}, u32[]{:S(2)}, u32[]{:S(2)}) %collective-permute-start.28) | collective-permute-done | bytes 32800 | tf_op jit(solution)/shard_map/ppermute | solution.py:13
  125.4 1.9 %collective-permute-done.29 = f32[64,128]{1,0:T(8,128)S(1)} collective-permute-done((f32[64,128]{1,0:T(8,128)S(1)}, f32[64,128]{1,0:T(8,128)S(1)}, u32[]{:S(2)}, u32[]{:S(2)}) %collective-permute-start.29) | collective-permute-done | bytes 32800 | tf_op jit(solution)/shard_map/ppermute | solution.py:13
  127.4 0.6 fusion.80
  (146 shorter events, 10.9 us)
Async XLA Ops:
  0.6 5.6 %copy-start = (bf16[1,384,512]{2,1,0:T(8,128)(2,1)S(1)}, bf16[1,384,512]{2,1,0:T(8,128)(2,1)}, u32[]{:S(2)}) copy-start(bf16[1,384,512]{2,1,0:T(8,128)(2,1)} %param.2) | copy-start | bytes 1179652
  0.6 29.3 %collective-permute-start.8 = (bf16[384,512]{1,0:T(8,128)(2,1)}, bf16[384,512]{1,0:T(8,128)(2,1)S(1)}, u32[]{:S(2)}, u32[]{:S(2)}) collective-permute-start(bf16[384,512]{1,0:T(8,128)(2,1)} %bitcast.181), channel_id=1, source_target_pairs={{0,3},{1,0},{2,1},{3,2},{4,7},{5,4},{6,5},{7,6},{8,11},{9,8},{10,9... | collective-permute-start | bytes 1179656 | tf_op jit(solution)/shard_map/ppermute | solution.py:13
  6.1 24.0 %collective-permute-start.6 = (bf16[416,512]{1,0:T(8,128)(2,1)S(1)}, bf16[416,512]{1,0:T(8,128)(2,1)S(1)}, u32[]{:S(2)}, u32[]{:S(2)}) collective-permute-start(bf16[416,512]{1,0:T(8,128)(2,1)S(1)} %pad_maximum_fusion.1), channel_id=1, source_target_pairs={{0,1},{1,2},{2,3},{3,0},{4,5},{5,6},{6,7},{7,4},{8,9},{9,10},{10,1... | collective-permute-start | bytes 1277960 | tf_op jit(solution)/shard_map/ppermute | solution.py:13
  6.5 12.9 %collective-permute-start = (f32[32,384]{1,0:T(8,128)S(1)}, f32[32,384]{1,0:T(8,128)S(1)}, u32[]{:S(2)}, u32[]{:S(2)}) collective-permute-start(f32[32,384]{1,0:T(8,128)S(1)} %get-tuple-element.30), channel_id=1, source_target_pairs={{0,1},{1,2},{2,3},{3,0},{4,5},{5,6},{6,7},{7,4},{8,9},{9,10},{10,1... | collective-permute-start | bytes 147464 | tf_op jit(solution)/shard_map/ppermute | solution.py:13
  6.8 12.6 %collective-permute-start.1 = (f32[32,384]{1,0:T(8,128)S(1)}, f32[32,384]{1,0:T(8,128)S(1)}, u32[]{:S(2)}, u32[]{:S(2)}) collective-permute-start(f32[32,384]{1,0:T(8,128)S(1)} %get-tuple-element.32), channel_id=1, source_target_pairs={{0,3},{1,0},{2,1},{3,2},{4,7},{5,4},{6,5},{7,6},{8,11},{9,8},{10,9... | collective-permute-start | bytes 147464 | tf_op jit(solution)/shard_map/ppermute | solution.py:13
  9.3 10.1 %collective-permute-start.2 = (f32[32,384]{1,0:T(8,128)S(1)}, f32[32,384]{1,0:T(8,128)S(1)}, u32[]{:S(2)}, u32[]{:S(2)}) collective-permute-start(f32[32,384]{1,0:T(8,128)S(1)} %get-tuple-element.31), channel_id=1, source_target_pairs={{0,2},{1,3},{2,0},{3,1},{4,6},{5,7},{6,4},{7,5},{8,10},{9,11},{10,... | collective-permute-start | bytes 147464 | tf_op jit(solution)/shard_map/ppermute | solution.py:13
  19.4 12.3 %collective-permute-start.3 = (f32[32,384]{1,0:T(8,128)S(1)}, f32[32,384]{1,0:T(8,128)S(1)}, u32[]{:S(2)}, u32[]{:S(2)}) collective-permute-start(f32[32,384]{1,0:T(8,128)S(1)} %fusion.34), channel_id=1, source_target_pairs={{0,4},{1,5},{2,6},{3,7},{4,8},{5,9},{6,10},{7,11},{8,12},{9,13},{1... | collective-permute-start | bytes 147464 | tf_op jit(solution)/shard_map/ppermute | solution.py:13
  22.5 9.2 %collective-permute-start.4 = (f32[32,384]{1,0:T(8,128)S(1)}, f32[32,384]{1,0:T(8,128)S(1)}, u32[]{:S(2)}, u32[]{:S(2)}) collective-permute-start(f32[32,384]{1,0:T(8,128)S(1)} %fusion.34), channel_id=1, source_target_pairs={{0,12},{1,13},{2,14},{3,15},{4,0},{5,1},{6,2},{7,3},{8,4},{9,5},{1... | collective-permute-start | bytes 147464 | tf_op jit(solution)/shard_map/ppermute | solution.py:13
  25.6 6.9 %collective-permute-start.5 = (f32[32,384]{1,0:T(8,128)S(1)}, f32[32,384]{1,0:T(8,128)S(1)}, u32[]{:S(2)}, u32[]{:S(2)}) collective-permute-start(f32[32,384]{1,0:T(8,128)S(1)} %fusion.34), channel_id=1, source_target_pairs={{0,8},{1,9},{2,10},{3,11},{4,12},{5,13},{6,14},{7,15},{8,0},{9,1},... | collective-permute-start | bytes 147464 | tf_op jit(solution)/shard_map/ppermute | solution.py:13
  30.0 5.2 %collective-permute-start.9 = (bf16[224,512]{1,0:T(8,128)(2,1)S(1)}, bf16[224,512]{1,0:T(8,128)(2,1)S(1)}, u32[]{:S(2)}, u32[]{:S(2)}) collective-permute-start(bf16[224,512]{1,0:T(8,128)(2,1)S(1)} %pad_maximum_fusion.4), channel_id=1, source_target_pairs={{0,3},{1,0},{2,1},{3,2},{4,7},{5,4},{6,5},{7,6},{8,11},{9,8},{10,9... | collective-permute-start | bytes 688136 | tf_op jit(solution)/shard_map/ppermute | solution.py:13
  30.2 6.5 %collective-permute-start.7 = (bf16[256,512]{1,0:T(8,128)(2,1)S(1)}, bf16[256,512]{1,0:T(8,128)(2,1)S(1)}, u32[]{:S(2)}, u32[]{:S(2)}) collective-permute-start(bf16[256,512]{1,0:T(8,128)(2,1)S(1)} %pad_maximum_fusion.2), channel_id=1, source_target_pairs={{0,1},{1,2},{2,3},{3,0},{4,5},{5,6},{6,7},{7,4},{8,9},{9,10},{10,1... | collective-permute-start | bytes 786440 | tf_op jit(solution)/shard_map/ppermute | solution.py:13
  35.3 1.6 %copy-start.1 = (bf16[224,512]{1,0:T(8,128)(2,1)}, bf16[224,512]{1,0:T(8,128)(2,1)S(1)}, u32[]{:S(2)}) copy-start(bf16[224,512]{1,0:T(8,128)(2,1)S(1)} %collective-permute-done.9) | copy-start | bytes 688132
  37.3 4.8 %slice-start = ((bf16[224,512]{1,0:T(8,128)(2,1)}), bf16[32,512]{1,0:T(8,128)(2,1)S(1)}, s32[]{:S(2)}) async-start(bf16[224,512]{1,0:T(8,128)(2,1)} %copy-done.1), calls=%async_computation.1 | async-start | bytes 65536 | tf_op jit(solution)/shard_map/slice | solution.py:119
  37.3 16.9 %collective-permute-start.15 = (bf16[384,2048]{1,0:T(8,128)(2,1)S(1)}, bf16[384,2048]{1,0:T(8,128)(2,1)S(1)}, u32[]{:S(2)}, u32[]{:S(2)}) collective-permute-start(bf16[384,2048]{1,0:T(8,128)(2,1)S(1)} %pad_maximum_fusion), channel_id=1, source_target_pairs={{0,16},{16,0},{32,48},{48,32},{64,80},{80,64},{96,112},{112,96},{1... | collective-permute-start | bytes 4718600 | tf_op jit(solution)/shard_map/ppermute | solution.py:13
  42.3 2.6 %collective-permute-start.10 = (f32[16,16,128]{2,1,0:T(8,128)S(1)}, f32[16,16,128]{2,1,0:T(8,128)S(1)}, u32[]{:S(2)}, u32[]{:S(2)}) collective-permute-start(f32[16,16,128]{2,1,0:T(8,128)S(1)} %bitcast.197), channel_id=1, source_target_pairs={{0,16},{16,0},{32,48},{48,32},{64,80},{80,64},{96,112},{112,96},{1... | collective-permute-start | bytes 393224 | tf_op jit(solution)/shard_map/ppermute | solution.py:13
  45.0 4.8 %collective-permute-start.11 = (f32[16,16,128]{2,1,0:T(8,128)S(1)}, f32[16,16,128]{2,1,0:T(8,128)S(1)}, u32[]{:S(2)}, u32[]{:S(2)}) collective-permute-start(f32[16,16,128]{2,1,0:T(8,128)S(1)} %fusion.19), channel_id=1, source_target_pairs={{0,128},{16,144},{32,160},{48,176},{64,192},{80,208},{96,224},{112... | collective-permute-start | bytes 393224 | tf_op jit(solution)/shard_map/ppermute | solution.py:13
  49.8 5.2 %collective-permute-start.12 = (f32[16,16,128]{2,1,0:T(8,128)S(1)}, f32[16,16,128]{2,1,0:T(8,128)S(1)}, u32[]{:S(2)}, u32[]{:S(2)}) collective-permute-start(f32[16,16,128]{2,1,0:T(8,128)S(1)} %add.266), channel_id=1, source_target_pairs={{0,32},{16,48},{32,64},{48,80},{64,96},{80,112},{96,0},{112,16},{1... | collective-permute-start | bytes 393224 | tf_op jit(solution)/shard_map/ppermute | solution.py:13
  51.1 3.8 %collective-permute-start.13 = (f32[16,16,128]{2,1,0:T(8,128)S(1)}, f32[16,16,128]{2,1,0:T(8,128)S(1)}, u32[]{:S(2)}, u32[]{:S(2)}) collective-permute-start(f32[16,16,128]{2,1,0:T(8,128)S(1)} %add.266), channel_id=1, source_target_pairs={{0,96},{16,112},{32,0},{48,16},{64,32},{80,48},{96,64},{112,80},{1... | collective-permute-start | bytes 393224 | tf_op jit(solution)/shard_map/ppermute | solution.py:13
  52.7 7.0 %collective-permute-start.14 = (f32[16,16,128]{2,1,0:T(8,128)S(1)}, f32[16,16,128]{2,1,0:T(8,128)S(1)}, u32[]{:S(2)}, u32[]{:S(2)}) collective-permute-start(f32[16,16,128]{2,1,0:T(8,128)S(1)} %add.266), channel_id=1, source_target_pairs={{0,64},{16,80},{32,96},{48,112},{64,0},{80,16},{96,32},{112,48},{1... | collective-permute-start | bytes 393224 | tf_op jit(solution)/shard_map/ppermute | solution.py:13
  61.1 5.7 %collective-permute-start.16 = (f32[16,896]{1,0:T(8,128)S(1)}, f32[16,896]{1,0:T(8,128)S(1)}, u32[]{:S(2)}, u32[]{:S(2)}) collective-permute-start(f32[16,896]{1,0:T(8,128)S(1)} %pad_maximum_fusion.14), channel_id=1, source_target_pairs={{0,4},{1,5},{2,6},{3,7},{4,8},{5,9},{6,10},{7,11},{8,12},{9,13},{1... | collective-permute-start | bytes 172040 | tf_op jit(solution)/shard_map/ppermute | solution.py:13
  61.2 5.6 %collective-permute-start.17 = (f32[16,896]{1,0:T(8,128)S(1)}, f32[16,896]{1,0:T(8,128)S(1)}, u32[]{:S(2)}, u32[]{:S(2)}) collective-permute-start(f32[16,896]{1,0:T(8,128)S(1)} %pad_maximum_fusion.14), channel_id=1, source_target_pairs={{0,12},{1,13},{2,14},{3,15},{4,0},{5,1},{6,2},{7,3},{8,4},{9,5},{1... | collective-permute-start | bytes 172040 | tf_op jit(solution)/shard_map/ppermute | solution.py:13
  64.8 7.3 %collective-permute-start.18 = (f32[16,896]{1,0:T(8,128)S(1)}, f32[16,896]{1,0:T(8,128)S(1)}, u32[]{:S(2)}, u32[]{:S(2)}) collective-permute-start(f32[16,896]{1,0:T(8,128)S(1)} %pad_maximum_fusion.14), channel_id=1, source_target_pairs={{0,8},{1,9},{2,10},{3,11},{4,12},{5,13},{6,14},{7,15},{8,0},{9,1},... | collective-permute-start | bytes 172040 | tf_op jit(solution)/shard_map/ppermute | solution.py:13
  73.4 4.0 %collective-permute-start.19 = (f32[17,16,128]{2,1,0:T(8,128)S(1)}, f32[17,16,128]{2,1,0:T(8,128)S(1)}, u32[]{:S(2)}, u32[]{:S(2)}) collective-permute-start(f32[17,16,128]{2,1,0:T(8,128)S(1)} %pad_maximum_fusion.6), channel_id=1, source_target_pairs={{0,128},{16,144},{32,160},{48,176},{64,192},{80,208},{96,224},{112... | collective-permute-start | bytes 417800 | tf_op jit(solution)/shard_map/ppermute | solution.py:13
  77.4 5.3 %collective-permute-start.20 = (f32[17,16,128]{2,1,0:T(8,128)S(1)}, f32[17,16,128]{2,1,0:T(8,128)}, u32[]{:S(2)}, u32[]{:S(2)}) collective-permute-start(f32[17,16,128]{2,1,0:T(8,128)S(1)} %fusion.76), channel_id=1, source_target_pairs={{0,32},{16,48},{32,64},{48,80},{64,96},{80,112},{96,0},{112,16},{1... | collective-permute-start | bytes 417800 | tf_op jit(solution)/shard_map/ppermute | solution.py:13
  77.5 6.2 %collective-permute-start.21 = (f32[17,16,128]{2,1,0:T(8,128)S(1)}, f32[17,16,128]{2,1,0:T(8,128)}, u32[]{:S(2)}, u32[]{:S(2)}) collective-permute-start(f32[17,16,128]{2,1,0:T(8,128)S(1)} %fusion.76), channel_id=1, source_target_pairs={{0,96},{16,112},{32,0},{48,16},{64,32},{80,48},{96,64},{112,80},{1... | collective-permute-start | bytes 417800 | tf_op jit(solution)/shard_map/ppermute | solution.py:13
  80.2 5.5 %collective-permute-start.22 = (f32[17,16,128]{2,1,0:T(8,128)S(1)}, f32[17,16,128]{2,1,0:T(8,128)}, u32[]{:S(2)}, u32[]{:S(2)}) collective-permute-start(f32[17,16,128]{2,1,0:T(8,128)S(1)} %fusion.76), channel_id=1, source_target_pairs={{0,64},{16,80},{32,96},{48,112},{64,0},{80,16},{96,32},{112,48},{1... | collective-permute-start | bytes 417800 | tf_op jit(solution)/shard_map/ppermute | solution.py:13
  88.4 5.2 %collective-permute-start.23 = (f32[16,896]{1,0:T(8,128)S(1)}, f32[16,896]{1,0:T(8,128)S(1)}, u32[]{:S(2)}, u32[]{:S(2)}) collective-permute-start(f32[16,896]{1,0:T(8,128)S(1)} %pad_maximum_fusion.15), channel_id=1, source_target_pairs={{0,4},{1,5},{2,6},{3,7},{4,8},{5,9},{6,10},{7,11},{8,12},{9,13},{1... | collective-permute-start | bytes 172040 | tf_op jit(solution)/shard_map/ppermute | solution.py:13
  88.5 5.1 %collective-permute-start.24 = (f32[16,896]{1,0:T(8,128)S(1)}, f32[16,896]{1,0:T(8,128)S(1)}, u32[]{:S(2)}, u32[]{:S(2)}) collective-permute-start(f32[16,896]{1,0:T(8,128)S(1)} %pad_maximum_fusion.15), channel_id=1, source_target_pairs={{0,12},{1,13},{2,14},{3,15},{4,0},{5,1},{6,2},{7,3},{8,4},{9,5},{1... | collective-permute-start | bytes 172040 | tf_op jit(solution)/shard_map/ppermute | solution.py:13
  92.1 8.3 %collective-permute-start.25 = (f32[16,896]{1,0:T(8,128)S(1)}, f32[16,896]{1,0:T(8,128)S(1)}, u32[]{:S(2)}, u32[]{:S(2)}) collective-permute-start(f32[16,896]{1,0:T(8,128)S(1)} %pad_maximum_fusion.15), channel_id=1, source_target_pairs={{0,8},{1,9},{2,10},{3,11},{4,12},{5,13},{6,14},{7,15},{8,0},{9,1},... | collective-permute-start | bytes 172040 | tf_op jit(solution)/shard_map/ppermute | solution.py:13
  103.2 16.3 %all-to-all-start = ((f32[16,24,128]{2,1,0:T(8,128)}), f32[16,24,128]{2,1,0:T(8,128)S(1)}, u32[]{:S(2)}, u32[]{:S(2)}) async-start(f32[16,24,128]{2,1,0:T(8,128)} %pad_maximum_fusion.5), calls=%async_computation | async-start | bytes 393216 | tf_op jit(solution)/shard_map/all_to_all | solution.py:165
  112.9 1.6 %collective-permute-start.26 = (f32[9,16,128]{2,1,0:T(8,128)S(1)}, f32[9,16,128]{2,1,0:T(8,128)S(1)}, u32[]{:S(2)}, u32[]{:S(2)}) collective-permute-start(f32[9,16,128]{2,1,0:T(8,128)S(1)} %get-tuple-element.50), channel_id=1, source_target_pairs={{0,16},{16,0},{32,48},{48,32},{64,80},{80,64},{96,112},{112,96},{1... | collective-permute-start | bytes 221192 | tf_op jit(solution)/shard_map/ppermute | solution.py:13
  121.0 2.8 %collective-permute-start.27 = (f32[64,128]{1,0:T(8,128)S(1)}, f32[64,128]{1,0:T(8,128)S(1)}, u32[]{:S(2)}, u32[]{:S(2)}) collective-permute-start(f32[64,128]{1,0:T(8,128)S(1)} %get-tuple-element.63), channel_id=1, source_target_pairs={{0,3},{1,0},{2,1},{3,2},{4,7},{5,4},{6,5},{7,6},{8,11},{9,8},{10,9... | collective-permute-start | bytes 98312 | tf_op jit(solution)/shard_map/ppermute | solution.py:13
  121.1 4.4 %collective-permute-start.28 = (f32[64,128]{1,0:T(8,128)S(1)}, f32[64,128]{1,0:T(8,128)S(1)}, u32[]{:S(2)}, u32[]{:S(2)}) collective-permute-start(f32[64,128]{1,0:T(8,128)S(1)} %get-tuple-element.65), channel_id=1, source_target_pairs={{0,2},{1,3},{2,0},{3,1},{4,6},{5,7},{6,4},{7,5},{8,10},{9,11},{10,... | collective-permute-start | bytes 98312 | tf_op jit(solution)/shard_map/ppermute | solution.py:13
  123.4 4.0 %collective-permute-start.29 = (f32[64,128]{1,0:T(8,128)S(1)}, f32[64,128]{1,0:T(8,128)S(1)}, u32[]{:S(2)}, u32[]{:S(2)}) collective-permute-start(f32[64,128]{1,0:T(8,128)S(1)} %get-tuple-element.64), channel_id=1, source_target_pairs={{0,1},{1,2},{2,3},{3,0},{4,5},{5,6},{6,7},{7,4},{8,9},{9,10},{10,1... | collective-permute-start | bytes 98312 | tf_op jit(solution)/shard_map/ppermute | solution.py:13

commit v9 on v7

--- a/solution.py
+++ b/solution.py
@@ -95,8 +95,8 @@
     scale = 1.0 / (tokens * tasks)
     gram_scale, diag_scale = ALPHA * scale, (1.0 - ALPHA) * scale
 
-    first = lax.dot_general(w, own_x, (((0,), (1,)), ((), ())), preferred_element_type=jnp.float32)
-    first = first.reshape(4, 32, tokens)
+    first = lax.optimization_barrier(jnp.dot(own_x, w, preferred_element_type=jnp.float32))
+    first = first.T.reshape(4, 32, tokens)
     two, three, one = staged(lambda k: pick(first, (x + k) % 4), x_move)
     mine = pick(first, x) + one + three + two
     turned = w.T.reshape(4, 32, width)
@@ -114,12 +114,17 @@
         return diag_scale * jnp.sum(wide * wide, axis=0, keepdims=True)
 
     far = jnp.concatenate([far_left[:half], far_right[:half]])
-    xs = lax.optimization_barrier(jnp.concatenate([own_x, from_left[:tokens], far, from_right], axis=1))
+    blocks = [own_x, from_left[:tokens], far, from_right]
     ws = [pick(turned, x), far_left[half + 32 :], far_left[half : half + 32], far_right[half:]]
-    ws = jnp.concatenate(ws, axis=1)
-    diag = squares(xs)
-
-    part = blocks_of(gram_scale * product(outputs, xs, 0) + diag * ws.astype(jnp.float32))
+    diags = [squares(block) for block in blocks]
+    part = [
+        gram_scale * product(outputs, block, 0) + d * piece.astype(jnp.float32)
+        for block, d, piece in zip(blocks, diags, ws)
+    ]
+    part = jnp.concatenate([blocks_of(block) for block in part])
+    xs = lax.optimization_barrier(jnp.concatenate(blocks, axis=1))
+    diag = jnp.concatenate(diags, axis=1)
+
     part = part.reshape(16, 2, 16, 128)
     other = core_move(pick(part, 1 - core, 1))
     target_blocks = zlo_y_sum(pick(part, core, 1) + other)

time: 129 us -> 129 us (level)
  waiting for transfers between devices: 57.4 us -> 41.8 us
  starting transfers between devices: 54.2 us -> 63.4 us
  matrix products: 4.49 us -> 7.28 us
  local copies, waits for them, and re-layouts: 4.81 us -> 6.83 us
  other arithmetic: 6.21 us -> 7.82 us
    ppermute x30, waiting for transfers between devices: 51.8 us -> 36.2 us  [moved(): return lax.ppermute(value, axis, [(i, to(i)) for i in range(16)])]
    ppermute x30, starting transfers between devices: 50.5 us -> 59.7 us  [moved(): return lax.ppermute(value, axis, [(i, to(i)) for i in range(16)])]
    reshape x0 -> x4, local copies, waits for them, and re-layouts: none -> 2.17 us  [blocks_of(): return value.reshape(value.shape[0], -1, 128).transpose(1, 0, 2)]
    dot_general x9 -> x12, matrix products: 4.21 us -> 5.96 us  [product(): lax.dot_general(pieces(value), x, (((1,), (dim,)), ((), ())), preferred_e...]
    add x0 -> x3, other arithmetic: none -> 1.57 us  [on_device(): gram_scale * product(outputs, block, 0) + d * piece.astype(jnp.float32)]
  transfers between devices with their start and end apart: 31 -> 31, of which waited for: 20 -> 19; matrix products, arithmetic and copies ran while one was open for 4% -> 7% of each run, Pallas kernels for 0% -> 0%
where the time goes in v9:
time: 129 us; the launch traced here: 128 us
  starting transfers between devices  63.4 us (49%)
  waiting for transfers between devices  41.8 us (32%)
  other arithmetic  7.82 us (6%)
  matrix products  7.28 us (6%)
  local copies, waits for them, and re-layouts  6.83 us (5%)
  between operations  1.35 us (1%)
    ppermute x30, starting transfers between devices, moved(): return lax.ppermute(value, axis, [(i, to(i)) for i in range(16)])  59.7 us
    ppermute x30, waiting for transfers between devices, moved(): return lax.ppermute(value, axis, [(i, to(i)) for i in range(16)])  36.2 us
    dot_general x12, matrix products, product(): lax.dot_general(pieces(value), x, (((1,), (dim,)), ((), ())), preferred_e...  5.96 us
    all_to_all x1, waiting for transfers between devices, on_device(): part = lax.all_to_all(jnp.concatenate([part, curve], axis=1), 'task', 0, 0)  5.6 us
    all_to_all x1, starting transfers between devices, on_device(): part = lax.all_to_all(jnp.concatenate([part, curve], axis=1), 'task', 0, 0)  3.64 us
  transfers between devices with their start and end apart: 31, of which 19 were waited for; matrix products, arithmetic and copies ran while one was open for 7% of the time, Pallas kernels for 0%

profile of v9, /device:TPU:1, one launch (start us, length us, event | category | flops | bytes accessed | tf_op | source)
XLA Modules:
  0.0 128.5 jit_solution(12499247978425599739)
XLA Ops:
  0.7 1.3 %fusion.18 = f32[384,128]{1,0:T(8,128)S(1)} fusion(bf16[1,512,128]{2,1,0:T(8,128)(2,1)} %param.3, bf16[1,384,512]{2,1,0:T(8,128)(2,1)} %param.2), kind=kOutput, calls=%fused_computation.56 | convolution fusion | flops 50331648 | bytes 720896 | tf_op jit(solution)/shard_map/dot_general | solution.py:98
  2.2 2.1 %collective-permute-start = (f32[32,384]{1,0:T(8,128)S(1)}, f32[32,384]{1,0:T(8,128)S(1)}, u32[]{:S(2)}, u32[]{:S(2)}) collective-permute-start(f32[32,384]{1,0:T(8,128)S(1)} %get-tuple-element.36), channel_id=1, source_target_pairs={{0,1},{1,2},{2,3},{3,0},{4,5},{5,6},{6,7},{7,4},{8,9},{9,10},{10,1... | collective-permute-start | bytes 147464 | tf_op jit(solution)/shard_map/ppermute | solution.py:12
  4.3 1.4 %collective-permute-start.1 = (f32[32,384]{1,0:T(8,128)S(1)}, f32[32,384]{1,0:T(8,128)S(1)}, u32[]{:S(2)}, u32[]{:S(2)}) collective-permute-start(f32[32,384]{1,0:T(8,128)S(1)} %get-tuple-element.38), channel_id=1, source_target_pairs={{0,3},{1,0},{2,1},{3,2},{4,7},{5,4},{6,5},{7,6},{8,11},{9,8},{10,9... | collective-permute-start | bytes 147464 | tf_op jit(solution)/shard_map/ppermute | solution.py:12
  5.7 1.6 %collective-permute-start.2 = (f32[32,384]{1,0:T(8,128)S(1)}, f32[32,384]{1,0:T(8,128)S(1)}, u32[]{:S(2)}, u32[]{:S(2)}) collective-permute-start(f32[32,384]{1,0:T(8,128)S(1)} %get-tuple-element.37), channel_id=1, source_target_pairs={{0,2},{1,3},{2,0},{3,1},{4,6},{5,7},{6,4},{7,5},{8,10},{9,11},{10,... | collective-permute-start | bytes 147464 | tf_op jit(solution)/shard_map/ppermute | solution.py:12
  7.3 0.9 collective-permute-start.8
  9.2 1.0 collective-permute-done.2
  10.2 3.1 %collective-permute-start.3 = (f32[32,384]{1,0:T(8,128)S(1)}, f32[32,384]{1,0:T(8,128)S(1)}, u32[]{:S(2)}, u32[]{:S(2)}) collective-permute-start(f32[32,384]{1,0:T(8,128)S(1)} %fusion.36), channel_id=1, source_target_pairs={{0,4},{1,5},{2,6},{3,7},{4,8},{5,9},{6,10},{7,11},{8,12},{9,13},{1... | collective-permute-start | bytes 147464 | tf_op jit(solution)/shard_map/ppermute | solution.py:12
  13.3 3.1 %collective-permute-start.4 = (f32[32,384]{1,0:T(8,128)S(1)}, f32[32,384]{1,0:T(8,128)S(1)}, u32[]{:S(2)}, u32[]{:S(2)}) collective-permute-start(f32[32,384]{1,0:T(8,128)S(1)} %fusion.36), channel_id=1, source_target_pairs={{0,12},{1,13},{2,14},{3,15},{4,0},{5,1},{6,2},{7,3},{8,4},{9,5},{1... | collective-permute-start | bytes 147464 | tf_op jit(solution)/shard_map/ppermute | solution.py:12
  16.4 4.4 %collective-permute-start.5 = (f32[32,384]{1,0:T(8,128)S(1)}, f32[32,384]{1,0:T(8,128)S(1)}, u32[]{:S(2)}, u32[]{:S(2)}) collective-permute-start(f32[32,384]{1,0:T(8,128)S(1)} %fusion.36), channel_id=1, source_target_pairs={{0,8},{1,9},{2,10},{3,11},{4,12},{5,13},{6,14},{7,15},{8,0},{9,1},... | collective-permute-start | bytes 147464 | tf_op jit(solution)/shard_map/ppermute | solution.py:12
  20.8 3.0 %collective-permute-done.5 = f32[32,384]{1,0:T(8,128)S(1)} collective-permute-done((f32[32,384]{1,0:T(8,128)S(1)}, f32[32,384]{1,0:T(8,128)S(1)}, u32[]{:S(2)}, u32[]{:S(2)}) %collective-permute-start.5) | collective-permute-done | bytes 49184 | tf_op jit(solution)/shard_map/ppermute | solution.py:12
  24.8 1.4 %collective-permute-start.9 = (bf16[224,512]{1,0:T(8,128)(2,1)S(1)}, bf16[224,512]{1,0:T(8,128)(2,1)S(1)}, u32[]{:S(2)}, u32[]{:S(2)}) collective-permute-start(bf16[224,512]{1,0:T(8,128)(2,1)S(1)} %pad_maximum_fusion.6), channel_id=1, source_target_pairs={{0,3},{1,0},{2,1},{3,2},{4,7},{5,4},{6,5},{7,6},{8,11},{9,8},{10,9... | collective-permute-start | bytes 688136 | tf_op jit(solution)/shard_map/ppermute | solution.py:12
  26.8 0.8 fusion.79
  27.8 1.9 %collective-permute-done.9 = bf16[224,512]{1,0:T(8,128)(2,1)S(1)} collective-permute-done((bf16[224,512]{1,0:T(8,128)(2,1)S(1)}, bf16[224,512]{1,0:T(8,128)(2,1)S(1)}, u32[]{:S(2)}, u32[]{:S(2)}) %collective-permute-start.9) | collective-permute-done | bytes 229408 | tf_op jit(solution)/shard_map/ppermute | solution.py:12
  29.8 3.3 %collective-permute-done.7 = bf16[256,512]{1,0:T(8,128)(2,1)S(1)} collective-permute-done((bf16[256,512]{1,0:T(8,128)(2,1)S(1)}, bf16[256,512]{1,0:T(8,128)(2,1)S(1)}, u32[]{:S(2)}, u32[]{:S(2)}) %collective-permute-start.7) | collective-permute-done | bytes 262176 | tf_op jit(solution)/shard_map/ppermute | solution.py:12
  34.0 5.3 %collective-permute-start.15 = (bf16[384,2048]{1,0:T(8,128)(2,1)S(1)}, bf16[384,2048]{1,0:T(8,128)(2,1)S(1)}, u32[]{:S(2)}, u32[]{:S(2)}) collective-permute-start(bf16[384,2048]{1,0:T(8,128)(2,1)S(1)} %pad_maximum_fusion), channel_id=1, source_target_pairs={{0,16},{16,0},{32,48},{48,32},{64,80},{80,64},{96,112},{112,96},{1... | collective-permute-start | bytes 4718600 | tf_op jit(solution)/shard_map/ppermute | solution.py:12
  39.9 1.5 %reshape.318 = f32[32,4,128]{2,1,0:T(4,128)} reshape(f32[32,512]{1,0:T(8,128)} %fusion.25) | data formatting | bytes 131072 | tf_op jit(solution)/shard_map/reshape | solution.py:64
  41.5 0.9 fusion
  42.4 0.9 fusion.29
  43.4 0.9 pad_maximum_fusion.4
  44.5 1.3 %collective-permute-done.10 = f32[16,16,128]{2,1,0:T(8,128)S(1)} collective-permute-done((f32[16,16,128]{2,1,0:T(8,128)S(1)}, f32[16,16,128]{2,1,0:T(8,128)S(1)}, u32[]{:S(2)}, u32[]{:S(2)}) %collective-permute-start.10) | collective-permute-done | bytes 131104 | tf_op jit(solution)/shard_map/ppermute | solution.py:12
  45.9 0.8 collective-permute-start.11
  46.8 4.2 %collective-permute-done.11 = f32[16,16,128]{2,1,0:T(8,128)S(1)} collective-permute-done((f32[16,16,128]{2,1,0:T(8,128)S(1)}, f32[16,16,128]{2,1,0:T(8,128)S(1)}, u32[]{:S(2)}, u32[]{:S(2)}) %collective-permute-start.11) | collective-permute-done | bytes 131104 | tf_op jit(solution)/shard_map/ppermute | solution.py:12
  50.9 1.4 %collective-permute-start.12 = (f32[16,16,128]{2,1,0:T(8,128)S(1)}, f32[16,16,128]{2,1,0:T(8,128)S(1)}, u32[]{:S(2)}, u32[]{:S(2)}) collective-permute-start(f32[16,16,128]{2,1,0:T(8,128)S(1)} %add.257), channel_id=1, source_target_pairs={{0,32},{16,48},{32,64},{48,80},{64,96},{80,112},{96,0},{112,16},{1... | collective-permute-start | bytes 393224 | tf_op jit(solution)/shard_map/ppermute | solution.py:12
  52.3 1.7 %collective-permute-start.13 = (f32[16,16,128]{2,1,0:T(8,128)S(1)}, f32[16,16,128]{2,1,0:T(8,128)S(1)}, u32[]{:S(2)}, u32[]{:S(2)}) collective-permute-start(f32[16,16,128]{2,1,0:T(8,128)S(1)} %add.257), channel_id=1, source_target_pairs={{0,96},{16,112},{32,0},{48,16},{64,32},{80,48},{96,64},{112,80},{1... | collective-permute-start | bytes 393224 | tf_op jit(solution)/shard_map/ppermute | solution.py:12
  54.0 1.4 %collective-permute-start.14 = (f32[16,16,128]{2,1,0:T(8,128)S(1)}, f32[16,16,128]{2,1,0:T(8,128)S(1)}, u32[]{:S(2)}, u32[]{:S(2)}) collective-permute-start(f32[16,16,128]{2,1,0:T(8,128)S(1)} %add.257), channel_id=1, source_target_pairs={{0,64},{16,80},{32,96},{48,112},{64,0},{80,16},{96,32},{112,48},{1... | collective-permute-start | bytes 393224 | tf_op jit(solution)/shard_map/ppermute | solution.py:12
  56.4 4.5 %collective-permute-done.14 = f32[16,16,128]{2,1,0:T(8,128)S(1)} collective-permute-done((f32[16,16,128]{2,1,0:T(8,128)S(1)}, f32[16,16,128]{2,1,0:T(8,128)S(1)}, u32[]{:S(2)}, u32[]{:S(2)}) %collective-permute-start.14) | collective-permute-done | bytes 131104 | tf_op jit(solution)/shard_map/ppermute | solution.py:12
  62.3 1.2 collective-permute-start.16
  63.5 2.5 %collective-permute-start.17 = (f32[16,896]{1,0:T(8,128)S(1)}, f32[16,896]{1,0:T(8,128)S(1)}, u32[]{:S(2)}, u32[]{:S(2)}) collective-permute-start(f32[16,896]{1,0:T(8,128)S(1)} %pad_maximum_fusion.16), channel_id=1, source_target_pairs={{0,12},{1,13},{2,14},{3,15},{4,0},{5,1},{6,2},{7,3},{8,4},{9,5},{1... | collective-permute-start | bytes 172040 | tf_op jit(solution)/shard_map/ppermute | solution.py:12
  66.0 4.7 %collective-permute-start.18 = (f32[16,896]{1,0:T(8,128)S(1)}, f32[16,896]{1,0:T(8,128)S(1)}, u32[]{:S(2)}, u32[]{:S(2)}) collective-permute-start(f32[16,896]{1,0:T(8,128)S(1)} %pad_maximum_fusion.16), channel_id=1, source_target_pairs={{0,8},{1,9},{2,10},{3,11},{4,12},{5,13},{6,14},{7,15},{8,0},{9,1},... | collective-permute-start | bytes 172040 | tf_op jit(solution)/shard_map/ppermute | solution.py:12
  70.7 2.3 %collective-permute-done.18 = f32[16,896]{1,0:T(8,128)S(1)} collective-permute-done((f32[16,896]{1,0:T(8,128)S(1)}, f32[16,896]{1,0:T(8,128)S(1)}, u32[]{:S(2)}, u32[]{:S(2)}) %collective-permute-start.18) | collective-permute-done | bytes 57376 | tf_op jit(solution)/shard_map/ppermute | solution.py:12
  74.3 1.6 %collective-permute-start.19 = (f32[17,16,128]{2,1,0:T(8,128)S(1)}, f32[17,16,128]{2,1,0:T(8,128)S(1)}, u32[]{:S(2)}, u32[]{:S(2)}) collective-permute-start(f32[17,16,128]{2,1,0:T(8,128)S(1)} %pad_maximum_fusion.8), channel_id=1, source_target_pairs={{0,128},{16,144},{32,160},{48,176},{64,192},{80,208},{96,224},{112... | collective-permute-start | bytes 417800 | tf_op jit(solution)/shard_map/ppermute | solution.py:12
  75.9 2.4 %collective-permute-done.19 = f32[17,16,128]{2,1,0:T(8,128)S(1)} collective-permute-done((f32[17,16,128]{2,1,0:T(8,128)S(1)}, f32[17,16,128]{2,1,0:T(8,128)S(1)}, u32[]{:S(2)}, u32[]{:S(2)}) %collective-permute-start.19) | collective-permute-done | bytes 139296 | tf_op jit(solution)/shard_map/ppermute | solution.py:12
  78.4 2.7 %collective-permute-start.21 = (f32[17,16,128]{2,1,0:T(8,128)S(1)}, f32[17,16,128]{2,1,0:T(8,128)}, u32[]{:S(2)}, u32[]{:S(2)}) collective-permute-start(f32[17,16,128]{2,1,0:T(8,128)S(1)} %fusion.80), channel_id=1, source_target_pairs={{0,96},{16,112},{32,0},{48,16},{64,32},{80,48},{96,64},{112,80},{1... | collective-permute-start | bytes 417800 | tf_op jit(solution)/shard_map/ppermute | solution.py:12
  81.1 2.5 %collective-permute-done.20 = f32[17,16,128]{2,1,0:T(8,128)} collective-permute-done((f32[17,16,128]{2,1,0:T(8,128)S(1)}, f32[17,16,128]{2,1,0:T(8,128)}, u32[]{:S(2)}, u32[]{:S(2)}) %collective-permute-start.20) | collective-permute-done | bytes 139296 | tf_op jit(solution)/shard_map/ppermute | solution.py:12
  83.6 0.9 collective-permute-done.21
  84.6 2.0 %collective-permute-done.22 = f32[17,16,128]{2,1,0:T(8,128)} collective-permute-done((f32[17,16,128]{2,1,0:T(8,128)S(1)}, f32[17,16,128]{2,1,0:T(8,128)}, u32[]{:S(2)}, u32[]{:S(2)}) %collective-permute-start.22) | collective-permute-done | bytes 139296 | tf_op jit(solution)/shard_map/ppermute | solution.py:12
  86.6 1.1 add_add_fusion
  89.4 1.6 %collective-permute-start.23 = (f32[16,896]{1,0:T(8,128)S(1)}, f32[16,896]{1,0:T(8,128)S(1)}, u32[]{:S(2)}, u32[]{:S(2)}) collective-permute-start(f32[16,896]{1,0:T(8,128)S(1)} %pad_maximum_fusion.17), channel_id=1, source_target_pairs={{0,4},{1,5},{2,6},{3,7},{4,8},{5,9},{6,10},{7,11},{8,12},{9,13},{1... | collective-permute-start | bytes 172040 | tf_op jit(solution)/shard_map/ppermute | solution.py:12
  91.0 2.0 %collective-permute-start.24 = (f32[16,896]{1,0:T(8,128)S(1)}, f32[16,896]{1,0:T(8,128)S(1)}, u32[]{:S(2)}, u32[]{:S(2)}) collective-permute-start(f32[16,896]{1,0:T(8,128)S(1)} %pad_maximum_fusion.17), channel_id=1, source_target_pairs={{0,12},{1,13},{2,14},{3,15},{4,0},{5,1},{6,2},{7,3},{8,4},{9,5},{1... | collective-permute-start | bytes 172040 | tf_op jit(solution)/shard_map/ppermute | solution.py:12
  93.0 5.0 %collective-permute-start.25 = (f32[16,896]{1,0:T(8,128)S(1)}, f32[16,896]{1,0:T(8,128)S(1)}, u32[]{:S(2)}, u32[]{:S(2)}) collective-permute-start(f32[16,896]{1,0:T(8,128)S(1)} %pad_maximum_fusion.17), channel_id=1, source_target_pairs={{0,8},{1,9},{2,10},{3,11},{4,12},{5,13},{6,14},{7,15},{8,0},{9,1},... | collective-permute-start | bytes 172040 | tf_op jit(solution)/shard_map/ppermute | solution.py:12
  98.0 2.3 %collective-permute-done.25 = f32[16,896]{1,0:T(8,128)S(1)} collective-permute-done((f32[16,896]{1,0:T(8,128)S(1)}, f32[16,896]{1,0:T(8,128)S(1)}, u32[]{:S(2)}, u32[]{:S(2)}) %collective-permute-start.25) | collective-permute-done | bytes 57376 | tf_op jit(solution)/shard_map/ppermute | solution.py:12
  102.5 7.4 %collective-permute-start.26 = (f32[9,16,128]{2,1,0:T(8,128)S(1)}, f32[9,16,128]{2,1,0:T(8,128)S(1)}, u32[]{:S(2)}, u32[]{:S(2)}) collective-permute-start(f32[9,16,128]{2,1,0:T(8,128)S(1)} %get-tuple-element.52), channel_id=1, source_target_pairs={{0,16},{16,0},{32,48},{48,32},{64,80},{80,64},{96,112},{112,96},{1... | collective-permute-start | bytes 221192 | tf_op jit(solution)/shard_map/ppermute | solution.py:12
  110.6 3.6 %all-to-all-start = ((f32[16,24,128]{2,1,0:T(8,128)}), f32[16,24,128]{2,1,0:T(8,128)S(1)}, u32[]{:S(2)}, u32[]{:S(2)}) async-start(f32[16,24,128]{2,1,0:T(8,128)} %pad_maximum_fusion.7), calls=%async_computation | async-start | bytes 393216 | tf_op jit(solution)/shard_map/all_to_all | solution.py:169
  115.0 5.6 %all-to-all-done = f32[16,24,128]{2,1,0:T(8,128)S(1)} async-done(((f32[16,24,128]{2,1,0:T(8,128)}), f32[16,24,128]{2,1,0:T(8,128)S(1)}, u32[]{:S(2)}, u32[]{:S(2)}) %all-to-all-start) | async-done | bytes 196640 | tf_op jit(solution)/shard_map/all_to_all | solution.py:169
  122.3 0.8 collective-permute-start.29
  123.2 0.9 collective-permute-done.27
  124.1 1.6 %collective-permute-done.28 = f32[64,32]{0,1:T(8,128)S(1)} collective-permute-done((f32[64,32]{0,1:T(8,128)S(1)}, f32[64,32]{0,1:T(8,128)S(1)}, u32[]{:S(2)}, u32[]{:S(2)}) %collective-permute-start.28) | collective-permute-done | bytes 8224 | tf_op jit(solution)/shard_map/ppermute | solution.py:12
  125.7 1.2 collective-permute-done.29
  (161 shorter events, 17.0 us)
Async XLA Ops:
  0.6 7.7 %copy-start = (bf16[1,384,512]{2,1,0:T(8,128)(2,1)S(1)}, bf16[1,384,512]{2,1,0:T(8,128)(2,1)}, u32[]{:S(2)}) copy-start(bf16[1,384,512]{2,1,0:T(8,128)(2,1)} %param.2) | copy-start | bytes 1179652
  0.6 7.5 %copy-start.1 = (bf16[1,512,128]{2,1,0:T(8,128)(2,1)S(1)}, bf16[1,512,128]{2,1,0:T(8,128)(2,1)}, u32[]{:S(2)}) copy-start(bf16[1,512,128]{2,1,0:T(8,128)(2,1)} %param.3) | copy-start | bytes 393220
  2.2 7.0 %collective-permute-start = (f32[32,384]{1,0:T(8,128)S(1)}, f32[32,384]{1,0:T(8,128)S(1)}, u32[]{:S(2)}, u32[]{:S(2)}) collective-permute-start(f32[32,384]{1,0:T(8,128)S(1)} %get-tuple-element.36), channel_id=1, source_target_pairs={{0,1},{1,2},{2,3},{3,0},{4,5},{5,6},{6,7},{7,4},{8,9},{9,10},{10,1... | collective-permute-start | bytes 147464 | tf_op jit(solution)/shard_map/ppermute | solution.py:12
  4.3 4.9 %collective-permute-start.1 = (f32[32,384]{1,0:T(8,128)S(1)}, f32[32,384]{1,0:T(8,128)S(1)}, u32[]{:S(2)}, u32[]{:S(2)}) collective-permute-start(f32[32,384]{1,0:T(8,128)S(1)} %get-tuple-element.38), channel_id=1, source_target_pairs={{0,3},{1,0},{2,1},{3,2},{4,7},{5,4},{6,5},{7,6},{8,11},{9,8},{10,9... | collective-permute-start | bytes 147464 | tf_op jit(solution)/shard_map/ppermute | solution.py:12
  5.7 4.5 %collective-permute-start.2 = (f32[32,384]{1,0:T(8,128)S(1)}, f32[32,384]{1,0:T(8,128)S(1)}, u32[]{:S(2)}, u32[]{:S(2)}) collective-permute-start(f32[32,384]{1,0:T(8,128)S(1)} %get-tuple-element.37), channel_id=1, source_target_pairs={{0,2},{1,3},{2,0},{3,1},{4,6},{5,7},{6,4},{7,5},{8,10},{9,11},{10,... | collective-permute-start | bytes 147464 | tf_op jit(solution)/shard_map/ppermute | solution.py:12
  7.3 17.4 %collective-permute-start.8 = (bf16[384,512]{1,0:T(8,128)(2,1)}, bf16[384,512]{1,0:T(8,128)(2,1)S(1)}, u32[]{:S(2)}, u32[]{:S(2)}) collective-permute-start(bf16[384,512]{1,0:T(8,128)(2,1)} %bitcast.183), channel_id=1, source_target_pairs={{0,3},{1,0},{2,1},{3,2},{4,7},{5,4},{6,5},{7,6},{8,11},{9,8},{10,9... | collective-permute-start | bytes 1179656 | tf_op jit(solution)/shard_map/ppermute | solution.py:12
  8.4 18.1 %collective-permute-start.6 = (bf16[416,512]{1,0:T(8,128)(2,1)S(1)}, bf16[416,512]{1,0:T(8,128)(2,1)S(1)}, u32[]{:S(2)}, u32[]{:S(2)}) collective-permute-start(bf16[416,512]{1,0:T(8,128)(2,1)S(1)} %pad_maximum_fusion.1), channel_id=1, source_target_pairs={{0,1},{1,2},{2,3},{3,0},{4,5},{5,6},{6,7},{7,4},{8,9},{9,10},{10,1... | collective-permute-start | bytes 1277960 | tf_op jit(solution)/shard_map/ppermute | solution.py:12
  10.2 10.6 %collective-permute-start.3 = (f32[32,384]{1,0:T(8,128)S(1)}, f32[32,384]{1,0:T(8,128)S(1)}, u32[]{:S(2)}, u32[]{:S(2)}) collective-permute-start(f32[32,384]{1,0:T(8,128)S(1)} %fusion.36), channel_id=1, source_target_pairs={{0,4},{1,5},{2,6},{3,7},{4,8},{5,9},{6,10},{7,11},{8,12},{9,13},{1... | collective-permute-start | bytes 147464 | tf_op jit(solution)/shard_map/ppermute | solution.py:12
  13.3 7.5 %collective-permute-start.4 = (f32[32,384]{1,0:T(8,128)S(1)}, f32[32,384]{1,0:T(8,128)S(1)}, u32[]{:S(2)}, u32[]{:S(2)}) collective-permute-start(f32[32,384]{1,0:T(8,128)S(1)} %fusion.36), channel_id=1, source_target_pairs={{0,12},{1,13},{2,14},{3,15},{4,0},{5,1},{6,2},{7,3},{8,4},{9,5},{1... | collective-permute-start | bytes 147464 | tf_op jit(solution)/shard_map/ppermute | solution.py:12
  16.4 7.4 %collective-permute-start.5 = (f32[32,384]{1,0:T(8,128)S(1)}, f32[32,384]{1,0:T(8,128)S(1)}, u32[]{:S(2)}, u32[]{:S(2)}) collective-permute-start(f32[32,384]{1,0:T(8,128)S(1)} %fusion.36), channel_id=1, source_target_pairs={{0,8},{1,9},{2,10},{3,11},{4,12},{5,13},{6,14},{7,15},{8,0},{9,1},... | collective-permute-start | bytes 147464 | tf_op jit(solution)/shard_map/ppermute | solution.py:12
  23.8 2.9 %copy-start.2 = (bf16[32,384]{1,0:T(8,128)(2,1)}, bf16[32,384]{1,0:T(8,128)(2,1)S(1)}, u32[]{:S(2)}) copy-start(bf16[32,384]{1,0:T(8,128)(2,1)S(1)} %get-tuple-element.30) | copy-start | bytes 73732
  23.9 2.9 %copy-start.3 = (bf16[32,384]{1,0:T(8,128)(2,1)}, bf16[32,384]{1,0:T(8,128)(2,1)S(1)}, u32[]{:S(2)}) copy-start(bf16[32,384]{1,0:T(8,128)(2,1)S(1)} %fusion.34) | copy-start | bytes 73732
  24.8 4.9 %collective-permute-start.9 = (bf16[224,512]{1,0:T(8,128)(2,1)S(1)}, bf16[224,512]{1,0:T(8,128)(2,1)S(1)}, u32[]{:S(2)}, u32[]{:S(2)}) collective-permute-start(bf16[224,512]{1,0:T(8,128)(2,1)S(1)} %pad_maximum_fusion.6), channel_id=1, source_target_pairs={{0,3},{1,0},{2,1},{3,2},{4,7},{5,4},{6,5},{7,6},{8,11},{9,8},{10,9... | collective-permute-start | bytes 688136 | tf_op jit(solution)/shard_map/ppermute | solution.py:12
  26.6 6.5 %collective-permute-start.7 = (bf16[256,512]{1,0:T(8,128)(2,1)S(1)}, bf16[256,512]{1,0:T(8,128)(2,1)S(1)}, u32[]{:S(2)}, u32[]{:S(2)}) collective-permute-start(bf16[256,512]{1,0:T(8,128)(2,1)S(1)} %pad_maximum_fusion.3), channel_id=1, source_target_pairs={{0,1},{1,2},{2,3},{3,0},{4,5},{5,6},{6,7},{7,4},{8,9},{9,10},{10,1... | collective-permute-start | bytes 786440 | tf_op jit(solution)/shard_map/ppermute | solution.py:12
  33.1 0.7 copy-start.4
  34.0 21.4 %collective-permute-start.15 = (bf16[384,2048]{1,0:T(8,128)(2,1)S(1)}, bf16[384,2048]{1,0:T(8,128)(2,1)S(1)}, u32[]{:S(2)}, u32[]{:S(2)}) collective-permute-start(bf16[384,2048]{1,0:T(8,128)(2,1)S(1)} %pad_maximum_fusion), channel_id=1, source_target_pairs={{0,16},{16,0},{32,48},{48,32},{64,80},{80,64},{96,112},{112,96},{1... | collective-permute-start | bytes 4718600 | tf_op jit(solution)/shard_map/ppermute | solution.py:12
  44.4 1.4 %collective-permute-start.10 = (f32[16,16,128]{2,1,0:T(8,128)S(1)}, f32[16,16,128]{2,1,0:T(8,128)S(1)}, u32[]{:S(2)}, u32[]{:S(2)}) collective-permute-start(f32[16,16,128]{2,1,0:T(8,128)S(1)} %bitcast.210), channel_id=1, source_target_pairs={{0,16},{16,0},{32,48},{48,32},{64,80},{80,64},{96,112},{112,96},{1... | collective-permute-start | bytes 393224 | tf_op jit(solution)/shard_map/ppermute | solution.py:12
  45.9 5.0 %collective-permute-start.11 = (f32[16,16,128]{2,1,0:T(8,128)S(1)}, f32[16,16,128]{2,1,0:T(8,128)S(1)}, u32[]{:S(2)}, u32[]{:S(2)}) collective-permute-start(f32[16,16,128]{2,1,0:T(8,128)S(1)} %fusion.15), channel_id=1, source_target_pairs={{0,128},{16,144},{32,160},{48,176},{64,192},{80,208},{96,224},{112... | collective-permute-start | bytes 393224 | tf_op jit(solution)/shard_map/ppermute | solution.py:12
  50.9 5.2 %collective-permute-start.12 = (f32[16,16,128]{2,1,0:T(8,128)S(1)}, f32[16,16,128]{2,1,0:T(8,128)S(1)}, u32[]{:S(2)}, u32[]{:S(2)}) collective-permute-start(f32[16,16,128]{2,1,0:T(8,128)S(1)} %add.257), channel_id=1, source_target_pairs={{0,32},{16,48},{32,64},{48,80},{64,96},{80,112},{96,0},{112,16},{1... | collective-permute-start | bytes 393224 | tf_op jit(solution)/shard_map/ppermute | solution.py:12
  52.3 4.1 %collective-permute-start.13 = (f32[16,16,128]{2,1,0:T(8,128)S(1)}, f32[16,16,128]{2,1,0:T(8,128)S(1)}, u32[]{:S(2)}, u32[]{:S(2)}) collective-permute-start(f32[16,16,128]{2,1,0:T(8,128)S(1)} %add.257), channel_id=1, source_target_pairs={{0,96},{16,112},{32,0},{48,16},{64,32},{80,48},{96,64},{112,80},{1... | collective-permute-start | bytes 393224 | tf_op jit(solution)/shard_map/ppermute | solution.py:12
  54.0 6.9 %collective-permute-start.14 = (f32[16,16,128]{2,1,0:T(8,128)S(1)}, f32[16,16,128]{2,1,0:T(8,128)S(1)}, u32[]{:S(2)}, u32[]{:S(2)}) collective-permute-start(f32[16,16,128]{2,1,0:T(8,128)S(1)} %add.257), channel_id=1, source_target_pairs={{0,64},{16,80},{32,96},{48,112},{64,0},{80,16},{96,32},{112,48},{1... | collective-permute-start | bytes 393224 | tf_op jit(solution)/shard_map/ppermute | solution.py:12
  62.3 8.3 %collective-permute-start.16 = (f32[16,896]{1,0:T(8,128)S(1)}, f32[16,896]{1,0:T(8,128)S(1)}, u32[]{:S(2)}, u32[]{:S(2)}) collective-permute-start(f32[16,896]{1,0:T(8,128)S(1)} %pad_maximum_fusion.16), channel_id=1, source_target_pairs={{0,4},{1,5},{2,6},{3,7},{4,8},{5,9},{6,10},{7,11},{8,12},{9,13},{1... | collective-permute-start | bytes 172040 | tf_op jit(solution)/shard_map/ppermute | solution.py:12
  63.5 7.2 %collective-permute-start.17 = (f32[16,896]{1,0:T(8,128)S(1)}, f32[16,896]{1,0:T(8,128)S(1)}, u32[]{:S(2)}, u32[]{:S(2)}) collective-permute-start(f32[16,896]{1,0:T(8,128)S(1)} %pad_maximum_fusion.16), channel_id=1, source_target_pairs={{0,12},{1,13},{2,14},{3,15},{4,0},{5,1},{6,2},{7,3},{8,4},{9,5},{1... | collective-permute-start | bytes 172040 | tf_op jit(solution)/shard_map/ppermute | solution.py:12
  66.0 6.9 %collective-permute-start.18 = (f32[16,896]{1,0:T(8,128)S(1)}, f32[16,896]{1,0:T(8,128)S(1)}, u32[]{:S(2)}, u32[]{:S(2)}) collective-permute-start(f32[16,896]{1,0:T(8,128)S(1)} %pad_maximum_fusion.16), channel_id=1, source_target_pairs={{0,8},{1,9},{2,10},{3,11},{4,12},{5,13},{6,14},{7,15},{8,0},{9,1},... | collective-permute-start | bytes 172040 | tf_op jit(solution)/shard_map/ppermute | solution.py:12
  74.3 4.0 %collective-permute-start.19 = (f32[17,16,128]{2,1,0:T(8,128)S(1)}, f32[17,16,128]{2,1,0:T(8,128)S(1)}, u32[]{:S(2)}, u32[]{:S(2)}) collective-permute-start(f32[17,16,128]{2,1,0:T(8,128)S(1)} %pad_maximum_fusion.8), channel_id=1, source_target_pairs={{0,128},{16,144},{32,160},{48,176},{64,192},{80,208},{96,224},{112... | collective-permute-start | bytes 417800 | tf_op jit(solution)/shard_map/ppermute | solution.py:12
  78.3 5.3 %collective-permute-start.20 = (f32[17,16,128]{2,1,0:T(8,128)S(1)}, f32[17,16,128]{2,1,0:T(8,128)}, u32[]{:S(2)}, u32[]{:S(2)}) collective-permute-start(f32[17,16,128]{2,1,0:T(8,128)S(1)} %fusion.80), channel_id=1, source_target_pairs={{0,32},{16,48},{32,64},{48,80},{64,96},{80,112},{96,0},{112,16},{1... | collective-permute-start | bytes 417800 | tf_op jit(solution)/shard_map/ppermute | solution.py:12
  78.4 6.2 %collective-permute-start.21 = (f32[17,16,128]{2,1,0:T(8,128)S(1)}, f32[17,16,128]{2,1,0:T(8,128)}, u32[]{:S(2)}, u32[]{:S(2)}) collective-permute-start(f32[17,16,128]{2,1,0:T(8,128)S(1)} %fusion.80), channel_id=1, source_target_pairs={{0,96},{16,112},{32,0},{48,16},{64,32},{80,48},{96,64},{112,80},{1... | collective-permute-start | bytes 417800 | tf_op jit(solution)/shard_map/ppermute | solution.py:12
  81.1 5.5 %collective-permute-start.22 = (f32[17,16,128]{2,1,0:T(8,128)S(1)}, f32[17,16,128]{2,1,0:T(8,128)}, u32[]{:S(2)}, u32[]{:S(2)}) collective-permute-start(f32[17,16,128]{2,1,0:T(8,128)S(1)} %fusion.80), channel_id=1, source_target_pairs={{0,64},{16,80},{32,96},{48,112},{64,0},{80,16},{96,32},{112,48},{1... | collective-permute-start | bytes 417800 | tf_op jit(solution)/shard_map/ppermute | solution.py:12
  89.4 8.6 %collective-permute-start.23 = (f32[16,896]{1,0:T(8,128)S(1)}, f32[16,896]{1,0:T(8,128)S(1)}, u32[]{:S(2)}, u32[]{:S(2)}) collective-permute-start(f32[16,896]{1,0:T(8,128)S(1)} %pad_maximum_fusion.17), channel_id=1, source_target_pairs={{0,4},{1,5},{2,6},{3,7},{4,8},{5,9},{6,10},{7,11},{8,12},{9,13},{1... | collective-permute-start | bytes 172040 | tf_op jit(solution)/shard_map/ppermute | solution.py:12
  91.0 7.0 %collective-permute-start.24 = (f32[16,896]{1,0:T(8,128)S(1)}, f32[16,896]{1,0:T(8,128)S(1)}, u32[]{:S(2)}, u32[]{:S(2)}) collective-permute-start(f32[16,896]{1,0:T(8,128)S(1)} %pad_maximum_fusion.17), channel_id=1, source_target_pairs={{0,12},{1,13},{2,14},{3,15},{4,0},{5,1},{6,2},{7,3},{8,4},{9,5},{1... | collective-permute-start | bytes 172040 | tf_op jit(solution)/shard_map/ppermute | solution.py:12
  93.0 7.3 %collective-permute-start.25 = (f32[16,896]{1,0:T(8,128)S(1)}, f32[16,896]{1,0:T(8,128)S(1)}, u32[]{:S(2)}, u32[]{:S(2)}) collective-permute-start(f32[16,896]{1,0:T(8,128)S(1)} %pad_maximum_fusion.17), channel_id=1, source_target_pairs={{0,8},{1,9},{2,10},{3,11},{4,12},{5,13},{6,14},{7,15},{8,0},{9,1},... | collective-permute-start | bytes 172040 | tf_op jit(solution)/shard_map/ppermute | solution.py:12
  102.5 11.7 %collective-permute-start.26 = (f32[9,16,128]{2,1,0:T(8,128)S(1)}, f32[9,16,128]{2,1,0:T(8,128)S(1)}, u32[]{:S(2)}, u32[]{:S(2)}) collective-permute-start(f32[9,16,128]{2,1,0:T(8,128)S(1)} %get-tuple-element.52), channel_id=1, source_target_pairs={{0,16},{16,0},{32,48},{48,32},{64,80},{80,64},{96,112},{112,96},{1... | collective-permute-start | bytes 221192 | tf_op jit(solution)/shard_map/ppermute | solution.py:12
  110.6 10.0 %all-to-all-start = ((f32[16,24,128]{2,1,0:T(8,128)}), f32[16,24,128]{2,1,0:T(8,128)S(1)}, u32[]{:S(2)}, u32[]{:S(2)}) async-start(f32[16,24,128]{2,1,0:T(8,128)} %pad_maximum_fusion.7), calls=%async_computation | async-start | bytes 393216 | tf_op jit(solution)/shard_map/all_to_all | solution.py:169
  121.4 2.7 %collective-permute-start.27 = (f32[64,32]{0,1:T(8,128)S(1)}, f32[64,32]{0,1:T(8,128)S(1)}, u32[]{:S(2)}, u32[]{:S(2)}) collective-permute-start(f32[64,32]{0,1:T(8,128)S(1)} %get-tuple-element.42), channel_id=1, source_target_pairs={{0,3},{1,0},{2,1},{3,2},{4,7},{5,4},{6,5},{7,6},{8,11},{9,8},{10,9... | collective-permute-start | bytes 24584 | tf_op jit(solution)/shard_map/ppermute | solution.py:12
  121.6 4.1 %collective-permute-start.28 = (f32[64,32]{0,1:T(8,128)S(1)}, f32[64,32]{0,1:T(8,128)S(1)}, u32[]{:S(2)}, u32[]{:S(2)}) collective-permute-start(f32[64,32]{0,1:T(8,128)S(1)} %get-tuple-element.43), channel_id=1, source_target_pairs={{0,2},{1,3},{2,0},{3,1},{4,6},{5,7},{6,4},{7,5},{8,10},{9,11},{10,... | collective-permute-start | bytes 24584 | tf_op jit(solution)/shard_map/ppermute | solution.py:12
  122.3 4.6 %collective-permute-start.29 = (f32[64,32]{0,1:T(8,128)S(1)}, f32[64,32]{0,1:T(8,128)S(1)}, u32[]{:S(2)}, u32[]{:S(2)}) collective-permute-start(f32[64,32]{0,1:T(8,128)S(1)} %get-tuple-element.41), channel_id=1, source_target_pairs={{0,1},{1,2},{2,3},{3,0},{4,5},{5,6},{6,7},{7,4},{8,9},{9,10},{10,1... | collective-permute-start | bytes 24584 | tf_op jit(solution)/shard_map/ppermute | solution.py:12

commit v10 on v9

--- a/solution.py
+++ b/solution.py
@@ -154,8 +154,18 @@
     residual_blocks = target_blocks - alpha0[None] * part[:16]
     residual = flat(residual_blocks)
 
+    def piece_of(blocks):
+        return pick(blocks.reshape(4, 4, 16, 128), task // 4, 1)
+
+    own = jnp.concatenate([piece_of(target_blocks), piece_of(residual_blocks)])
+    other = core_move(own)
+    both = jnp.where(core == 0, jnp.stack([own, other]), jnp.stack([other, own]))
+    both = lax.dynamic_slice_in_dim(both, 32 * (task % 4), 32, 3)
+    my_target, my_residual = (both[:, i : i + 4].transpose(3, 1, 0, 2).reshape(32, 128) for i in (0, 4))
+
     scalars = [total(residual * residual), total(diag * residual * residual), total(diag * residual * target)]
     rows = sum_over(with_scalars(outputs_of(residual), scalars), zhi_move)
+    rows, my_target, my_residual = lax.optimization_barrier((rows, my_target, my_residual))
     image1, norm1, weigh1, cross = columns_of(rows, 3)
     beta = norm1 / (norm0 + EPS)
     image1 = image1 + beta * image0
@@ -165,30 +175,18 @@
     part = image_of(image1, direction)
     part = part.reshape(16, 4, width).transpose(1, 0, 2).reshape(64, width).T.reshape(16, 2, 16, 64)
     part = part.transpose(0, 2, 1, 3).reshape(16, 16, 128)
-    curve = jnp.broadcast_to(jnp.tile(curve[:, 0], 8)[None, None], (16, 8, 128))
-    part = lax.all_to_all(jnp.concatenate([part, curve], axis=1), "task", 0, 0)
-    part = jnp.sum(part.reshape(8, 2, 24, 128), axis=0)
+    scalars = [jnp.tile(column[:, 0], 8)[None] for column in (curve, alpha0, beta, norm1)]
+    scalars = jnp.concatenate(scalars + [jnp.zeros((4, 128), jnp.float32)])
+    scalars = jnp.broadcast_to(scalars[None], (16, 8, 128))
+    part = lax.all_to_all(jnp.concatenate([part, scalars], axis=1), "task", 0, 0).reshape(8, 2, 24, 128)
+    alpha0, beta, norm1 = (part[0, :, i, :16].reshape(32) for i in (17, 18, 19))
+    part = jnp.sum(part, axis=0)
     curve = part[:, 16, :16].reshape(32)
     part = part[:, :16].reshape(2, 16, 2, 4, 16).transpose(2, 1, 3, 0, 4).reshape(32, 128)
 
-    def piece_of(blocks):
-        return pick(blocks.reshape(4, 4, 16, 128), task // 4, 1)
-
-    lane = lax.broadcasted_iota(jnp.int32, (16, 128), 1)
-    scalars = jnp.where(lane < 32, alpha0, jnp.where(lane < 64, beta, norm1))
-    own = jnp.concatenate([piece_of(target_blocks), piece_of(residual_blocks), scalars[None]])
-    other = core_move(own)
-    both = jnp.where(core == 0, jnp.stack([own, other]), jnp.stack([other, own]))
-    alpha0, beta, norm1 = (both[:, 8, :, 32 * i].reshape(32) for i in range(3))
-    both = lax.dynamic_slice_in_dim(both, 32 * (task % 4), 32, 3)
-
-    def side_by_side(value):
-        return value.transpose(3, 1, 0, 2).reshape(32, 128)
-
     def per_lane(vector):
         return jnp.tile(vector, 4)[None]
 
-    my_target, my_residual = side_by_side(both[:, :4]), side_by_side(both[:, 4:8])
     alpha1 = per_lane(norm1 / curve)
     merged = per_lane(alpha0) * my_target + alpha1 * (my_residual + per_lane(beta) * my_target)
     both = jnp.concatenate([merged, my_residual - alpha1 * part])

time: 129 us -> 135 us (1.047)
  other arithmetic: 7.82 us -> 12.6 us
  local copies, waits for them, and re-layouts: 6.83 us -> 8.77 us
  waiting for transfers between devices: 41.8 us -> 40.3 us
    ppermute x30, waiting for transfers between devices: 36.2 us -> 33.6 us  [moved(): return lax.ppermute(value, axis, [(i, to(i)) for i in range(16)])]
    all_to_all x1, starting transfers between devices: 3.64 us -> 5.5 us  [on_device(): lax.all_to_all(jnp.concatenate([part, scalars], axis=1), 'task', 0, 0)]
  transfers between devices with their start and end apart: 31 -> 31, of which waited for: 19 -> 18; matrix products, arithmetic and copies ran while one was open for 7% -> 8% of each run, Pallas kernels for 0% -> 0%
where the time goes in v10:
time: 135 us
  starting transfers between devices  64.2 us (48%)
  waiting for transfers between devices  40.3 us (30%)
  other arithmetic  12.6 us (9%)
  local copies, waits for them, and re-layouts  8.77 us (6%)
  matrix products  7.27 us (5%)
  between operations  1.43 us (1%)
    ppermute x30, starting transfers between devices, moved(): return lax.ppermute(value, axis, [(i, to(i)) for i in range(16)])  58.7 us
    ppermute x30, waiting for transfers between devices, moved(): return lax.ppermute(value, axis, [(i, to(i)) for i in range(16)])  33.6 us
    all_to_all x1, waiting for transfers between devices, on_device(): lax.all_to_all(jnp.concatenate([part, scalars], axis=1), 'task', 0, 0)  6.72 us
    dot_general x12, matrix products, product(): lax.dot_general(pieces(value), x, (((1,), (dim,)), ((), ())), preferred_e...  5.94 us
    all_to_all x1, starting transfers between devices, on_device(): lax.all_to_all(jnp.concatenate([part, scalars], axis=1), 'task', 0, 0)  5.5 us
  transfers between devices with their start and end apart: 31, of which 18 were waited for; matrix products, arithmetic and copies ran while one was open for 8% of the time, Pallas kernels for 0%

profile of v10, /device:TPU:1, one launch (start us, length us, event | category | flops | bytes accessed | tf_op | source)
XLA Modules:
  0.0 134.5 jit_solution(15824628035691603829)
XLA Ops:
  0.7 1.3 fusion.19
  2.2 2.1 %collective-permute-start = (f32[32,384]{1,0:T(8,128)S(1)}, f32[32,384]{1,0:T(8,128)S(1)}, u32[]{:S(2)}, u32[]{:S(2)}) collective-permute-start(f32[32,384]{1,0:T(8,128)S(1)} %get-tuple-element.38), channel_id=1, source_target_pairs={{0,1},{1,2},{2,3},{3,0},{4,5},{5,6},{6,7},{7,4},{8,9},{9,10},{10,1... | collective-permute-start | bytes 147464 | tf_op jit(solution)/shard_map/ppermute | solution.py:12
  4.3 1.4 %collective-permute-start.1 = (f32[32,384]{1,0:T(8,128)S(1)}, f32[32,384]{1,0:T(8,128)S(1)}, u32[]{:S(2)}, u32[]{:S(2)}) collective-permute-start(f32[32,384]{1,0:T(8,128)S(1)} %get-tuple-element.40), channel_id=1, source_target_pairs={{0,3},{1,0},{2,1},{3,2},{4,7},{5,4},{6,5},{7,6},{8,11},{9,8},{10,9... | collective-permute-start | bytes 147464 | tf_op jit(solution)/shard_map/ppermute | solution.py:12
  5.7 1.6 %collective-permute-start.2 = (f32[32,384]{1,0:T(8,128)S(1)}, f32[32,384]{1,0:T(8,128)S(1)}, u32[]{:S(2)}, u32[]{:S(2)}) collective-permute-start(f32[32,384]{1,0:T(8,128)S(1)} %get-tuple-element.39), channel_id=1, source_target_pairs={{0,2},{1,3},{2,0},{3,1},{4,6},{5,7},{6,4},{7,5},{8,10},{9,11},{10,... | collective-permute-start | bytes 147464 | tf_op jit(solution)/shard_map/ppermute | solution.py:12
  7.3 0.9 collective-permute-start.8
  9.2 1.0 collective-permute-done.2
  10.2 3.1 %collective-permute-start.3 = (f32[32,384]{1,0:T(8,128)S(1)}, f32[32,384]{1,0:T(8,128)S(1)}, u32[]{:S(2)}, u32[]{:S(2)}) collective-permute-start(f32[32,384]{1,0:T(8,128)S(1)} %fusion.35), channel_id=1, source_target_pairs={{0,4},{1,5},{2,6},{3,7},{4,8},{5,9},{6,10},{7,11},{8,12},{9,13},{1... | collective-permute-start | bytes 147464 | tf_op jit(solution)/shard_map/ppermute | solution.py:12
  13.3 3.1 %collective-permute-start.4 = (f32[32,384]{1,0:T(8,128)S(1)}, f32[32,384]{1,0:T(8,128)S(1)}, u32[]{:S(2)}, u32[]{:S(2)}) collective-permute-start(f32[32,384]{1,0:T(8,128)S(1)} %fusion.35), channel_id=1, source_target_pairs={{0,12},{1,13},{2,14},{3,15},{4,0},{5,1},{6,2},{7,3},{8,4},{9,5},{1... | collective-permute-start | bytes 147464 | tf_op jit(solution)/shard_map/ppermute | solution.py:12
  16.4 4.4 %collective-permute-start.5 = (f32[32,384]{1,0:T(8,128)S(1)}, f32[32,384]{1,0:T(8,128)S(1)}, u32[]{:S(2)}, u32[]{:S(2)}) collective-permute-start(f32[32,384]{1,0:T(8,128)S(1)} %fusion.35), channel_id=1, source_target_pairs={{0,8},{1,9},{2,10},{3,11},{4,12},{5,13},{6,14},{7,15},{8,0},{9,1},... | collective-permute-start | bytes 147464 | tf_op jit(solution)/shard_map/ppermute | solution.py:12
  20.8 3.0 %collective-permute-done.5 = f32[32,384]{1,0:T(8,128)S(1)} collective-permute-done((f32[32,384]{1,0:T(8,128)S(1)}, f32[32,384]{1,0:T(8,128)S(1)}, u32[]{:S(2)}, u32[]{:S(2)}) %collective-permute-start.5) | collective-permute-done | bytes 49184 | tf_op jit(solution)/shard_map/ppermute | solution.py:12
  24.8 1.4 %collective-permute-start.9 = (bf16[224,512]{1,0:T(8,128)(2,1)S(1)}, bf16[224,512]{1,0:T(8,128)(2,1)S(1)}, u32[]{:S(2)}, u32[]{:S(2)}) collective-permute-start(bf16[224,512]{1,0:T(8,128)(2,1)S(1)} %pad_maximum_fusion.6), channel_id=1, source_target_pairs={{0,3},{1,0},{2,1},{3,2},{4,7},{5,4},{6,5},{7,6},{8,11},{9,8},{10,9... | collective-permute-start | bytes 688136 | tf_op jit(solution)/shard_map/ppermute | solution.py:12
  26.8 0.8 fusion.75
  27.8 1.9 %collective-permute-done.9 = bf16[224,512]{1,0:T(8,128)(2,1)S(1)} collective-permute-done((bf16[224,512]{1,0:T(8,128)(2,1)S(1)}, bf16[224,512]{1,0:T(8,128)(2,1)S(1)}, u32[]{:S(2)}, u32[]{:S(2)}) %collective-permute-start.9) | collective-permute-done | bytes 229408 | tf_op jit(solution)/shard_map/ppermute | solution.py:12
  29.8 3.3 %collective-permute-done.7 = bf16[256,512]{1,0:T(8,128)(2,1)S(1)} collective-permute-done((bf16[256,512]{1,0:T(8,128)(2,1)S(1)}, bf16[256,512]{1,0:T(8,128)(2,1)S(1)}, u32[]{:S(2)}, u32[]{:S(2)}) %collective-permute-start.7) | collective-permute-done | bytes 262176 | tf_op jit(solution)/shard_map/ppermute | solution.py:12
  34.0 5.3 %collective-permute-start.15 = (bf16[384,2048]{1,0:T(8,128)(2,1)S(1)}, bf16[384,2048]{1,0:T(8,128)(2,1)S(1)}, u32[]{:S(2)}, u32[]{:S(2)}) collective-permute-start(bf16[384,2048]{1,0:T(8,128)(2,1)S(1)} %pad_maximum_fusion), channel_id=1, source_target_pairs={{0,16},{16,0},{32,48},{48,32},{64,80},{80,64},{96,112},{112,96},{1... | collective-permute-start | bytes 4718600 | tf_op jit(solution)/shard_map/ppermute | solution.py:12
  39.9 1.5 %reshape.191 = f32[32,4,128]{2,1,0:T(4,128)} reshape(f32[32,512]{1,0:T(8,128)} %fusion.26) | data formatting | bytes 131072 | tf_op jit(solution)/shard_map/reshape | solution.py:64
  41.5 0.9 fusion
  42.4 0.9 fusion.30
  43.4 0.9 pad_maximum_fusion.4
  44.6 1.3 collective-permute-done.10
  46.8 4.2 %collective-permute-done.11 = f32[16,16,128]{2,1,0:T(8,128)S(1)} collective-permute-done((f32[16,16,128]{2,1,0:T(8,128)S(1)}, f32[16,16,128]{2,1,0:T(8,128)S(1)}, u32[]{:S(2)}, u32[]{:S(2)}) %collective-permute-start.11) | collective-permute-done | bytes 131104 | tf_op jit(solution)/shard_map/ppermute | solution.py:12
  51.0 1.4 %collective-permute-start.12 = (f32[16,16,128]{2,1,0:T(8,128)S(1)}, f32[16,16,128]{2,1,0:T(8,128)S(1)}, u32[]{:S(2)}, u32[]{:S(2)}) collective-permute-start(f32[16,16,128]{2,1,0:T(8,128)S(1)} %add.257), channel_id=1, source_target_pairs={{0,32},{16,48},{32,64},{48,80},{64,96},{80,112},{96,0},{112,16},{1... | collective-permute-start | bytes 393224 | tf_op jit(solution)/shard_map/ppermute | solution.py:12
  52.3 1.7 %collective-permute-start.13 = (f32[16,16,128]{2,1,0:T(8,128)S(1)}, f32[16,16,128]{2,1,0:T(8,128)S(1)}, u32[]{:S(2)}, u32[]{:S(2)}) collective-permute-start(f32[16,16,128]{2,1,0:T(8,128)S(1)} %add.257), channel_id=1, source_target_pairs={{0,96},{16,112},{32,0},{48,16},{64,32},{80,48},{96,64},{112,80},{1... | collective-permute-start | bytes 393224 | tf_op jit(solution)/shard_map/ppermute | solution.py:12
  54.0 1.4 %collective-permute-start.14 = (f32[16,16,128]{2,1,0:T(8,128)S(1)}, f32[16,16,128]{2,1,0:T(8,128)S(1)}, u32[]{:S(2)}, u32[]{:S(2)}) collective-permute-start(f32[16,16,128]{2,1,0:T(8,128)S(1)} %add.257), channel_id=1, source_target_pairs={{0,64},{16,80},{32,96},{48,112},{64,0},{80,16},{96,32},{112,48},{1... | collective-permute-start | bytes 393224 | tf_op jit(solution)/shard_map/ppermute | solution.py:12
  56.5 4.5 %collective-permute-done.14 = f32[16,16,128]{2,1,0:T(8,128)S(1)} collective-permute-done((f32[16,16,128]{2,1,0:T(8,128)S(1)}, f32[16,16,128]{2,1,0:T(8,128)S(1)}, u32[]{:S(2)}, u32[]{:S(2)}) %collective-permute-start.14) | collective-permute-done | bytes 131104 | tf_op jit(solution)/shard_map/ppermute | solution.py:12
  62.4 1.2 collective-permute-start.16
  63.5 2.5 %collective-permute-start.17 = (f32[16,896]{1,0:T(8,128)S(1)}, f32[16,896]{1,0:T(8,128)S(1)}, u32[]{:S(2)}, u32[]{:S(2)}) collective-permute-start(f32[16,896]{1,0:T(8,128)S(1)} %pad_maximum_fusion.16), channel_id=1, source_target_pairs={{0,12},{1,13},{2,14},{3,15},{4,0},{5,1},{6,2},{7,3},{8,4},{9,5},{1... | collective-permute-start | bytes 172040 | tf_op jit(solution)/shard_map/ppermute | solution.py:12
  66.0 4.7 %collective-permute-start.18 = (f32[16,896]{1,0:T(8,128)S(1)}, f32[16,896]{1,0:T(8,128)S(1)}, u32[]{:S(2)}, u32[]{:S(2)}) collective-permute-start(f32[16,896]{1,0:T(8,128)S(1)} %pad_maximum_fusion.16), channel_id=1, source_target_pairs={{0,8},{1,9},{2,10},{3,11},{4,12},{5,13},{6,14},{7,15},{8,0},{9,1},... | collective-permute-start | bytes 172040 | tf_op jit(solution)/shard_map/ppermute | solution.py:12
  70.7 2.3 %collective-permute-done.18 = f32[16,896]{1,0:T(8,128)S(1)} collective-permute-done((f32[16,896]{1,0:T(8,128)S(1)}, f32[16,896]{1,0:T(8,128)S(1)}, u32[]{:S(2)}, u32[]{:S(2)}) %collective-permute-start.18) | collective-permute-done | bytes 57376 | tf_op jit(solution)/shard_map/ppermute | solution.py:12
  74.3 1.6 %collective-permute-start.19 = (f32[17,16,128]{2,1,0:T(8,128)S(1)}, f32[17,16,128]{2,1,0:T(8,128)S(1)}, u32[]{:S(2)}, u32[]{:S(2)}) collective-permute-start(f32[17,16,128]{2,1,0:T(8,128)S(1)} %pad_maximum_fusion.8), channel_id=1, source_target_pairs={{0,128},{16,144},{32,160},{48,176},{64,192},{80,208},{96,224},{112... | collective-permute-start | bytes 417800 | tf_op jit(solution)/shard_map/ppermute | solution.py:12
  75.9 2.4 %collective-permute-done.19 = f32[17,16,128]{2,1,0:T(8,128)S(1)} collective-permute-done((f32[17,16,128]{2,1,0:T(8,128)S(1)}, f32[17,16,128]{2,1,0:T(8,128)S(1)}, u32[]{:S(2)}, u32[]{:S(2)}) %collective-permute-start.19) | collective-permute-done | bytes 139296 | tf_op jit(solution)/shard_map/ppermute | solution.py:12
  79.0 2.7 %collective-permute-start.21 = (f32[17,16,128]{2,1,0:T(8,128)}, f32[17,16,128]{2,1,0:T(8,128)}, u32[]{:S(2)}, u32[]{:S(2)}) collective-permute-start(f32[17,16,128]{2,1,0:T(8,128)} %fusion.77), channel_id=1, source_target_pairs={{0,96},{16,112},{32,0},{48,16},{64,32},{80,48},{96,64},{112,80},{1... | collective-permute-start | bytes 417800 | tf_op jit(solution)/shard_map/ppermute | solution.py:12
  82.2 2.1 %collective-permute-done.20 = f32[17,16,128]{2,1,0:T(8,128)S(1)} collective-permute-done((f32[17,16,128]{2,1,0:T(8,128)}, f32[17,16,128]{2,1,0:T(8,128)S(1)}, u32[]{:S(2)}, u32[]{:S(2)}) %collective-permute-start.20) | collective-permute-done | bytes 139296 | tf_op jit(solution)/shard_map/ppermute | solution.py:12
  84.3 1.2 collective-permute-done.21
  85.5 1.9 %collective-permute-done.22 = f32[17,16,128]{2,1,0:T(8,128)} collective-permute-done((f32[17,16,128]{2,1,0:T(8,128)}, f32[17,16,128]{2,1,0:T(8,128)}, u32[]{:S(2)}, u32[]{:S(2)}) %collective-permute-start.22) | collective-permute-done | bytes 139296 | tf_op jit(solution)/shard_map/ppermute | solution.py:12
  87.4 1.1 add_add_fusion
  90.9 1.5 %collective-permute-start.23 = (f32[16,896]{1,0:T(8,128)}, f32[16,896]{1,0:T(8,128)}, u32[]{:S(2)}, u32[]{:S(2)}) collective-permute-start(f32[16,896]{1,0:T(8,128)} %pad_maximum_fusion.17), channel_id=1, source_target_pairs={{0,4},{1,5},{2,6},{3,7},{4,8},{5,9},{6,10},{7,11},{8,12},{9,13},{1... | collective-permute-start | bytes 172040 | tf_op jit(solution)/shard_map/ppermute | solution.py:12
  92.4 2.0 %collective-permute-start.24 = (f32[16,896]{1,0:T(8,128)}, f32[16,896]{1,0:T(8,128)}, u32[]{:S(2)}, u32[]{:S(2)}) collective-permute-start(f32[16,896]{1,0:T(8,128)} %pad_maximum_fusion.17), channel_id=1, source_target_pairs={{0,12},{1,13},{2,14},{3,15},{4,0},{5,1},{6,2},{7,3},{8,4},{9,5},{1... | collective-permute-start | bytes 172040 | tf_op jit(solution)/shard_map/ppermute | solution.py:12
  94.4 5.0 %collective-permute-start.25 = (f32[16,896]{1,0:T(8,128)}, f32[16,896]{1,0:T(8,128)}, u32[]{:S(2)}, u32[]{:S(2)}) collective-permute-start(f32[16,896]{1,0:T(8,128)} %pad_maximum_fusion.17), channel_id=1, source_target_pairs={{0,8},{1,9},{2,10},{3,11},{4,12},{5,13},{6,14},{7,15},{8,0},{9,1},... | collective-permute-start | bytes 172040 | tf_op jit(solution)/shard_map/ppermute | solution.py:12
  100.1 6.5 %collective-permute-start.26 = (f32[8,16,128]{2,1,0:T(8,128)}, f32[8,16,128]{2,1,0:T(8,128)}, u32[]{:S(2)}, u32[]{:S(2)}) collective-permute-start(f32[8,16,128]{2,1,0:T(8,128)} %get-tuple-element.58), channel_id=1, source_target_pairs={{0,16},{16,0},{32,48},{48,32},{64,80},{80,64},{96,112},{112,96},{1... | collective-permute-start | bytes 196616 | tf_op jit(solution)/shard_map/ppermute | solution.py:12
  107.2 0.9 add_add_fusion.2
  108.1 1.1 fusion.12
  114.0 5.5 %all-to-all-start = ((f32[16,24,128]{2,1,0:T(8,128)}), f32[16,24,128]{2,1,0:T(8,128)S(1)}, u32[]{:S(2)}, u32[]{:S(2)}) async-start(f32[16,24,128]{2,1,0:T(8,128)} %pad_maximum_fusion.7), calls=%async_computation | async-start | bytes 393216 | tf_op jit(solution)/shard_map/all_to_all | solution.py:181
  119.5 6.7 %all-to-all-done = f32[16,24,128]{2,1,0:T(8,128)S(1)} async-done(((f32[16,24,128]{2,1,0:T(8,128)}), f32[16,24,128]{2,1,0:T(8,128)S(1)}, u32[]{:S(2)}, u32[]{:S(2)}) %all-to-all-start) | async-done | bytes 196640 | tf_op jit(solution)/shard_map/all_to_all | solution.py:181
  128.4 0.8 collective-permute-start.29
  129.2 0.9 collective-permute-done.27
  130.2 1.6 %collective-permute-done.28 = f32[64,32]{0,1:T(8,128)S(1)} collective-permute-done((f32[64,32]{0,1:T(8,128)S(1)}, f32[64,32]{0,1:T(8,128)S(1)}, u32[]{:S(2)}, u32[]{:S(2)}) %collective-permute-start.28) | collective-permute-done | bytes 8224 | tf_op jit(solution)/shard_map/ppermute | solution.py:12
  131.8 1.2 collective-permute-done.29
  (197 shorter events, 22.5 us)
Async XLA Ops:
  0.6 7.7 %copy-start = (bf16[1,384,512]{2,1,0:T(8,128)(2,1)S(1)}, bf16[1,384,512]{2,1,0:T(8,128)(2,1)}, u32[]{:S(2)}) copy-start(bf16[1,384,512]{2,1,0:T(8,128)(2,1)} %param.2) | copy-start | bytes 1179652
  0.6 7.5 %copy-start.1 = (bf16[1,512,128]{2,1,0:T(8,128)(2,1)S(1)}, bf16[1,512,128]{2,1,0:T(8,128)(2,1)}, u32[]{:S(2)}) copy-start(bf16[1,512,128]{2,1,0:T(8,128)(2,1)} %param.3) | copy-start | bytes 393220
  2.2 7.0 %collective-permute-start = (f32[32,384]{1,0:T(8,128)S(1)}, f32[32,384]{1,0:T(8,128)S(1)}, u32[]{:S(2)}, u32[]{:S(2)}) collective-permute-start(f32[32,384]{1,0:T(8,128)S(1)} %get-tuple-element.38), channel_id=1, source_target_pairs={{0,1},{1,2},{2,3},{3,0},{4,5},{5,6},{6,7},{7,4},{8,9},{9,10},{10,1... | collective-permute-start | bytes 147464 | tf_op jit(solution)/shard_map/ppermute | solution.py:12
  4.3 4.9 %collective-permute-start.1 = (f32[32,384]{1,0:T(8,128)S(1)}, f32[32,384]{1,0:T(8,128)S(1)}, u32[]{:S(2)}, u32[]{:S(2)}) collective-permute-start(f32[32,384]{1,0:T(8,128)S(1)} %get-tuple-element.40), channel_id=1, source_target_pairs={{0,3},{1,0},{2,1},{3,2},{4,7},{5,4},{6,5},{7,6},{8,11},{9,8},{10,9... | collective-permute-start | bytes 147464 | tf_op jit(solution)/shard_map/ppermute | solution.py:12
  5.7 4.5 %collective-permute-start.2 = (f32[32,384]{1,0:T(8,128)S(1)}, f32[32,384]{1,0:T(8,128)S(1)}, u32[]{:S(2)}, u32[]{:S(2)}) collective-permute-start(f32[32,384]{1,0:T(8,128)S(1)} %get-tuple-element.39), channel_id=1, source_target_pairs={{0,2},{1,3},{2,0},{3,1},{4,6},{5,7},{6,4},{7,5},{8,10},{9,11},{10,... | collective-permute-start | bytes 147464 | tf_op jit(solution)/shard_map/ppermute | solution.py:12
  7.3 17.4 %collective-permute-start.8 = (bf16[384,512]{1,0:T(8,128)(2,1)}, bf16[384,512]{1,0:T(8,128)(2,1)S(1)}, u32[]{:S(2)}, u32[]{:S(2)}) collective-permute-start(bf16[384,512]{1,0:T(8,128)(2,1)} %bitcast.171), channel_id=1, source_target_pairs={{0,3},{1,0},{2,1},{3,2},{4,7},{5,4},{6,5},{7,6},{8,11},{9,8},{10,9... | collective-permute-start | bytes 1179656 | tf_op jit(solution)/shard_map/ppermute | solution.py:12
  8.4 18.1 %collective-permute-start.6 = (bf16[416,512]{1,0:T(8,128)(2,1)S(1)}, bf16[416,512]{1,0:T(8,128)(2,1)S(1)}, u32[]{:S(2)}, u32[]{:S(2)}) collective-permute-start(bf16[416,512]{1,0:T(8,128)(2,1)S(1)} %pad_maximum_fusion.1), channel_id=1, source_target_pairs={{0,1},{1,2},{2,3},{3,0},{4,5},{5,6},{6,7},{7,4},{8,9},{9,10},{10,1... | collective-permute-start | bytes 1277960 | tf_op jit(solution)/shard_map/ppermute | solution.py:12
  10.2 10.6 %collective-permute-start.3 = (f32[32,384]{1,0:T(8,128)S(1)}, f32[32,384]{1,0:T(8,128)S(1)}, u32[]{:S(2)}, u32[]{:S(2)}) collective-permute-start(f32[32,384]{1,0:T(8,128)S(1)} %fusion.35), channel_id=1, source_target_pairs={{0,4},{1,5},{2,6},{3,7},{4,8},{5,9},{6,10},{7,11},{8,12},{9,13},{1... | collective-permute-start | bytes 147464 | tf_op jit(solution)/shard_map/ppermute | solution.py:12
  13.3 7.5 %collective-permute-start.4 = (f32[32,384]{1,0:T(8,128)S(1)}, f32[32,384]{1,0:T(8,128)S(1)}, u32[]{:S(2)}, u32[]{:S(2)}) collective-permute-start(f32[32,384]{1,0:T(8,128)S(1)} %fusion.35), channel_id=1, source_target_pairs={{0,12},{1,13},{2,14},{3,15},{4,0},{5,1},{6,2},{7,3},{8,4},{9,5},{1... | collective-permute-start | bytes 147464 | tf_op jit(solution)/shard_map/ppermute | solution.py:12
  16.4 7.4 %collective-permute-start.5 = (f32[32,384]{1,0:T(8,128)S(1)}, f32[32,384]{1,0:T(8,128)S(1)}, u32[]{:S(2)}, u32[]{:S(2)}) collective-permute-start(f32[32,384]{1,0:T(8,128)S(1)} %fusion.35), channel_id=1, source_target_pairs={{0,8},{1,9},{2,10},{3,11},{4,12},{5,13},{6,14},{7,15},{8,0},{9,1},... | collective-permute-start | bytes 147464 | tf_op jit(solution)/shard_map/ppermute | solution.py:12
  23.8 3.0 %copy-start.2 = (bf16[32,384]{1,0:T(8,128)(2,1)}, bf16[32,384]{1,0:T(8,128)(2,1)S(1)}, u32[]{:S(2)}) copy-start(bf16[32,384]{1,0:T(8,128)(2,1)S(1)} %get-tuple-element.32) | copy-start | bytes 73732
  23.9 2.9 %copy-start.3 = (bf16[32,384]{1,0:T(8,128)(2,1)}, bf16[32,384]{1,0:T(8,128)(2,1)S(1)}, u32[]{:S(2)}) copy-start(bf16[32,384]{1,0:T(8,128)(2,1)S(1)} %fusion.33) | copy-start | bytes 73732
  24.8 4.9 %collective-permute-start.9 = (bf16[224,512]{1,0:T(8,128)(2,1)S(1)}, bf16[224,512]{1,0:T(8,128)(2,1)S(1)}, u32[]{:S(2)}, u32[]{:S(2)}) collective-permute-start(bf16[224,512]{1,0:T(8,128)(2,1)S(1)} %pad_maximum_fusion.6), channel_id=1, source_target_pairs={{0,3},{1,0},{2,1},{3,2},{4,7},{5,4},{6,5},{7,6},{8,11},{9,8},{10,9... | collective-permute-start | bytes 688136 | tf_op jit(solution)/shard_map/ppermute | solution.py:12
  26.6 6.5 %collective-permute-start.7 = (bf16[256,512]{1,0:T(8,128)(2,1)S(1)}, bf16[256,512]{1,0:T(8,128)(2,1)S(1)}, u32[]{:S(2)}, u32[]{:S(2)}) collective-permute-start(bf16[256,512]{1,0:T(8,128)(2,1)S(1)} %pad_maximum_fusion.3), channel_id=1, source_target_pairs={{0,1},{1,2},{2,3},{3,0},{4,5},{5,6},{6,7},{7,4},{8,9},{9,10},{10,1... | collective-permute-start | bytes 786440 | tf_op jit(solution)/shard_map/ppermute | solution.py:12
  27.8 14.6 %copy-start.9 = (f32[512]{0:T(512)}, f32[512]{0:T(512)S(1)}, u32[]{:S(2)}) copy-start(f32[512]{0:T(512)S(1)} %broadcast_multiply_fusion.3) | copy-start | bytes 6148
  34.0 21.4 %collective-permute-start.15 = (bf16[384,2048]{1,0:T(8,128)(2,1)S(1)}, bf16[384,2048]{1,0:T(8,128)(2,1)S(1)}, u32[]{:S(2)}, u32[]{:S(2)}) collective-permute-start(bf16[384,2048]{1,0:T(8,128)(2,1)S(1)} %pad_maximum_fusion), channel_id=1, source_target_pairs={{0,16},{16,0},{32,48},{48,32},{64,80},{80,64},{96,112},{112,96},{1... | collective-permute-start | bytes 4718600 | tf_op jit(solution)/shard_map/ppermute | solution.py:12
  43.4 3.4 %copy-start.10 = (f32[512]{0:T(512)S(1)}, f32[512]{0:T(512)}, u32[]{:S(2)}) copy-start(f32[512]{0:T(512)} %copy-done.9) | copy-start | bytes 6148
  44.5 1.4 %collective-permute-start.10 = (f32[16,16,128]{2,1,0:T(8,128)S(1)}, f32[16,16,128]{2,1,0:T(8,128)S(1)}, u32[]{:S(2)}, u32[]{:S(2)}) collective-permute-start(f32[16,16,128]{2,1,0:T(8,128)S(1)} %bitcast.201), channel_id=1, source_target_pairs={{0,16},{16,0},{32,48},{48,32},{64,80},{80,64},{96,112},{112,96},{1... | collective-permute-start | bytes 393224 | tf_op jit(solution)/shard_map/ppermute | solution.py:12
  44.6 17.7 %copy-start.13 = (pred[128]{0:T(512)(128)(4,1)}, pred[128]{0:T(512)(128)(4,1)S(1)}, u32[]{:S(2)}) copy-start(pred[128]{0:T(512)(128)(4,1)S(1)} %get-tuple-element.67) | copy-start | bytes 388
  44.6 17.7 %copy-start.15 = (pred[128]{0:T(512)(128)(4,1)}, pred[128]{0:T(512)(128)(4,1)S(1)}, u32[]{:S(2)}) copy-start(pred[128]{0:T(512)(128)(4,1)S(1)} %get-tuple-element.68) | copy-start | bytes 388
  46.0 5.0 %collective-permute-start.11 = (f32[16,16,128]{2,1,0:T(8,128)S(1)}, f32[16,16,128]{2,1,0:T(8,128)S(1)}, u32[]{:S(2)}, u32[]{:S(2)}) collective-permute-start(f32[16,16,128]{2,1,0:T(8,128)S(1)} %fusion.16), channel_id=1, source_target_pairs={{0,128},{16,144},{32,160},{48,176},{64,192},{80,208},{96,224},{112... | collective-permute-start | bytes 393224 | tf_op jit(solution)/shard_map/ppermute | solution.py:12
  51.0 5.2 %collective-permute-start.12 = (f32[16,16,128]{2,1,0:T(8,128)S(1)}, f32[16,16,128]{2,1,0:T(8,128)S(1)}, u32[]{:S(2)}, u32[]{:S(2)}) collective-permute-start(f32[16,16,128]{2,1,0:T(8,128)S(1)} %add.257), channel_id=1, source_target_pairs={{0,32},{16,48},{32,64},{48,80},{64,96},{80,112},{96,0},{112,16},{1... | collective-permute-start | bytes 393224 | tf_op jit(solution)/shard_map/ppermute | solution.py:12
  52.3 4.1 %collective-permute-start.13 = (f32[16,16,128]{2,1,0:T(8,128)S(1)}, f32[16,16,128]{2,1,0:T(8,128)S(1)}, u32[]{:S(2)}, u32[]{:S(2)}) collective-permute-start(f32[16,16,128]{2,1,0:T(8,128)S(1)} %add.257), channel_id=1, source_target_pairs={{0,96},{16,112},{32,0},{48,16},{64,32},{80,48},{96,64},{112,80},{1... | collective-permute-start | bytes 393224 | tf_op jit(solution)/shard_map/ppermute | solution.py:12
  54.0 6.9 %collective-permute-start.14 = (f32[16,16,128]{2,1,0:T(8,128)S(1)}, f32[16,16,128]{2,1,0:T(8,128)S(1)}, u32[]{:S(2)}, u32[]{:S(2)}) collective-permute-start(f32[16,16,128]{2,1,0:T(8,128)S(1)} %add.257), channel_id=1, source_target_pairs={{0,64},{16,80},{32,96},{48,112},{64,0},{80,16},{96,32},{112,48},{1... | collective-permute-start | bytes 393224 | tf_op jit(solution)/shard_map/ppermute | solution.py:12
  62.4 8.3 %collective-permute-start.16 = (f32[16,896]{1,0:T(8,128)S(1)}, f32[16,896]{1,0:T(8,128)S(1)}, u32[]{:S(2)}, u32[]{:S(2)}) collective-permute-start(f32[16,896]{1,0:T(8,128)S(1)} %pad_maximum_fusion.16), channel_id=1, source_target_pairs={{0,4},{1,5},{2,6},{3,7},{4,8},{5,9},{6,10},{7,11},{8,12},{9,13},{1... | collective-permute-start | bytes 172040 | tf_op jit(solution)/shard_map/ppermute | solution.py:12
  63.5 7.2 %collective-permute-start.17 = (f32[16,896]{1,0:T(8,128)S(1)}, f32[16,896]{1,0:T(8,128)S(1)}, u32[]{:S(2)}, u32[]{:S(2)}) collective-permute-start(f32[16,896]{1,0:T(8,128)S(1)} %pad_maximum_fusion.16), channel_id=1, source_target_pairs={{0,12},{1,13},{2,14},{3,15},{4,0},{5,1},{6,2},{7,3},{8,4},{9,5},{1... | collective-permute-start | bytes 172040 | tf_op jit(solution)/shard_map/ppermute | solution.py:12
  66.0 6.9 %collective-permute-start.18 = (f32[16,896]{1,0:T(8,128)S(1)}, f32[16,896]{1,0:T(8,128)S(1)}, u32[]{:S(2)}, u32[]{:S(2)}) collective-permute-start(f32[16,896]{1,0:T(8,128)S(1)} %pad_maximum_fusion.16), channel_id=1, source_target_pairs={{0,8},{1,9},{2,10},{3,11},{4,12},{5,13},{6,14},{7,15},{8,0},{9,1},... | collective-permute-start | bytes 172040 | tf_op jit(solution)/shard_map/ppermute | solution.py:12
  74.3 4.0 %collective-permute-start.19 = (f32[17,16,128]{2,1,0:T(8,128)S(1)}, f32[17,16,128]{2,1,0:T(8,128)S(1)}, u32[]{:S(2)}, u32[]{:S(2)}) collective-permute-start(f32[17,16,128]{2,1,0:T(8,128)S(1)} %pad_maximum_fusion.8), channel_id=1, source_target_pairs={{0,128},{16,144},{32,160},{48,176},{64,192},{80,208},{96,224},{112... | collective-permute-start | bytes 417800 | tf_op jit(solution)/shard_map/ppermute | solution.py:12
  79.0 5.3 %collective-permute-start.20 = (f32[17,16,128]{2,1,0:T(8,128)}, f32[17,16,128]{2,1,0:T(8,128)S(1)}, u32[]{:S(2)}, u32[]{:S(2)}) collective-permute-start(f32[17,16,128]{2,1,0:T(8,128)} %fusion.77), channel_id=1, source_target_pairs={{0,32},{16,48},{32,64},{48,80},{64,96},{80,112},{96,0},{112,16},{1... | collective-permute-start | bytes 417800 | tf_op jit(solution)/shard_map/ppermute | solution.py:12
  79.0 6.5 %collective-permute-start.21 = (f32[17,16,128]{2,1,0:T(8,128)}, f32[17,16,128]{2,1,0:T(8,128)}, u32[]{:S(2)}, u32[]{:S(2)}) collective-permute-start(f32[17,16,128]{2,1,0:T(8,128)} %fusion.77), channel_id=1, source_target_pairs={{0,96},{16,112},{32,0},{48,16},{64,32},{80,48},{96,64},{112,80},{1... | collective-permute-start | bytes 417800 | tf_op jit(solution)/shard_map/ppermute | solution.py:12
  81.7 5.7 %collective-permute-start.22 = (f32[17,16,128]{2,1,0:T(8,128)}, f32[17,16,128]{2,1,0:T(8,128)}, u32[]{:S(2)}, u32[]{:S(2)}) collective-permute-start(f32[17,16,128]{2,1,0:T(8,128)} %fusion.77), channel_id=1, source_target_pairs={{0,64},{16,80},{32,96},{48,112},{64,0},{80,16},{96,32},{112,48},{1... | collective-permute-start | bytes 417800 | tf_op jit(solution)/shard_map/ppermute | solution.py:12
  88.9 1.2 copy-start.14
  88.9 1.2 copy-start.16
  89.0 1.2 copy-start.19
  90.1 17.0 %copy-start.7 = (f32[16,384]{1,0:T(8,128)}, f32[16,384]{1,0:T(8,128)S(1)}, u32[]{:S(2)}) copy-start(f32[16,384]{1,0:T(8,128)S(1)} %slice_add_fusion.8) | copy-start | bytes 73732
  90.2 9.2 %copy-start.8 = (f32[16,128]{1,0:T(8,128)}, f32[16,128]{1,0:T(8,128)S(1)}, u32[]{:S(2)}) copy-start(f32[16,128]{1,0:T(8,128)S(1)} %select_select_fusion) | copy-start | bytes 24580
  90.9 16.3 %collective-permute-start.23 = (f32[16,896]{1,0:T(8,128)}, f32[16,896]{1,0:T(8,128)}, u32[]{:S(2)}, u32[]{:S(2)}) collective-permute-start(f32[16,896]{1,0:T(8,128)} %pad_maximum_fusion.17), channel_id=1, source_target_pairs={{0,4},{1,5},{2,6},{3,7},{4,8},{5,9},{6,10},{7,11},{8,12},{9,13},{1... | collective-permute-start | bytes 172040 | tf_op jit(solution)/shard_map/ppermute | solution.py:12
  92.4 14.8 %collective-permute-start.24 = (f32[16,896]{1,0:T(8,128)}, f32[16,896]{1,0:T(8,128)}, u32[]{:S(2)}, u32[]{:S(2)}) collective-permute-start(f32[16,896]{1,0:T(8,128)} %pad_maximum_fusion.17), channel_id=1, source_target_pairs={{0,12},{1,13},{2,14},{3,15},{4,0},{5,1},{6,2},{7,3},{8,4},{9,5},{1... | collective-permute-start | bytes 172040 | tf_op jit(solution)/shard_map/ppermute | solution.py:12
  94.4 12.7 %collective-permute-start.25 = (f32[16,896]{1,0:T(8,128)}, f32[16,896]{1,0:T(8,128)}, u32[]{:S(2)}, u32[]{:S(2)}) collective-permute-start(f32[16,896]{1,0:T(8,128)} %pad_maximum_fusion.17), channel_id=1, source_target_pairs={{0,8},{1,9},{2,10},{3,11},{4,12},{5,13},{6,14},{7,15},{8,0},{9,1},... | collective-permute-start | bytes 172040 | tf_op jit(solution)/shard_map/ppermute | solution.py:12
  100.1 8.0 %collective-permute-start.26 = (f32[8,16,128]{2,1,0:T(8,128)}, f32[8,16,128]{2,1,0:T(8,128)}, u32[]{:S(2)}, u32[]{:S(2)}) collective-permute-start(f32[8,16,128]{2,1,0:T(8,128)} %get-tuple-element.58), channel_id=1, source_target_pairs={{0,16},{16,0},{32,48},{48,32},{64,80},{80,64},{96,112},{112,96},{1... | collective-permute-start | bytes 196616 | tf_op jit(solution)/shard_map/ppermute | solution.py:12
  110.6 1.5 %copy-start.11 = (f32[16]{0:T(128)}, f32[16]{0:T(128)S(1)}, u32[]{:S(2)}) copy-start(f32[16]{0:T(128)S(1)} %fusion.73) | copy-start | bytes 196
  112.1 1.2 copy-start.17
  112.2 15.1 %copy-start.5 = (f32[32,4,2,16]{0,3,2,1:T(8,128)S(1)}, f32[32,4,2,16]{0,3,2,1:T(8,128)}, u32[]{:S(2)}) copy-start(f32[32,4,2,16]{0,3,2,1:T(8,128)} %copy.61) | copy-start | bytes 49156
  112.2 15.1 %copy-start.6 = (f32[32,4,2,16]{0,3,2,1:T(8,128)S(1)}, f32[32,4,2,16]{0,3,2,1:T(8,128)}, u32[]{:S(2)}) copy-start(f32[32,4,2,16]{0,3,2,1:T(8,128)} %copy.62) | copy-start | bytes 49156
  114.0 12.2 %all-to-all-start = ((f32[16,24,128]{2,1,0:T(8,128)}), f32[16,24,128]{2,1,0:T(8,128)S(1)}, u32[]{:S(2)}, u32[]{:S(2)}) async-start(f32[16,24,128]{2,1,0:T(8,128)} %pad_maximum_fusion.7), calls=%async_computation | async-start | bytes 393216 | tf_op jit(solution)/shard_map/all_to_all | solution.py:181
  127.5 2.7 %collective-permute-start.27 = (f32[64,32]{0,1:T(8,128)S(1)}, f32[64,32]{0,1:T(8,128)S(1)}, u32[]{:S(2)}, u32[]{:S(2)}) collective-permute-start(f32[64,32]{0,1:T(8,128)S(1)} %get-tuple-element.42), channel_id=1, source_target_pairs={{0,3},{1,0},{2,1},{3,2},{4,7},{5,4},{6,5},{7,6},{8,11},{9,8},{10,9... | collective-permute-start | bytes 24584 | tf_op jit(solution)/shard_map/ppermute | solution.py:12
  127.7 4.1 %collective-permute-start.28 = (f32[64,32]{0,1:T(8,128)S(1)}, f32[64,32]{0,1:T(8,128)S(1)}, u32[]{:S(2)}, u32[]{:S(2)}) collective-permute-start(f32[64,32]{0,1:T(8,128)S(1)} %get-tuple-element.43), channel_id=1, source_target_pairs={{0,2},{1,3},{2,0},{3,1},{4,6},{5,7},{6,4},{7,5},{8,10},{9,11},{10,... | collective-permute-start | bytes 24584 | tf_op jit(solution)/shard_map/ppermute | solution.py:12
  128.4 4.6 %collective-permute-start.29 = (f32[64,32]{0,1:T(8,128)S(1)}, f32[64,32]{0,1:T(8,128)S(1)}, u32[]{:S(2)}, u32[]{:S(2)}) collective-permute-start(f32[64,32]{0,1:T(8,128)S(1)} %get-tuple-element.41), channel_id=1, source_target_pairs={{0,1},{1,2},{2,3},{3,0},{4,5},{5,6},{6,7},{7,4},{8,9},{9,10},{10,1... | collective-permute-start | bytes 24584 | tf_op jit(solution)/shard_map/ppermute | solution.py:12
  (3 other events, 2.3 us)

commit v11 on v9

--- a/solution.py
+++ b/solution.py
@@ -1,6 +1,7 @@
 import jax
 import jax.numpy as jnp
 from jax import lax
+from jax.experimental.layout import Layout, with_layout_constraint
 from jax.sharding import PartitionSpec as P
 
 
@@ -193,10 +194,16 @@
     merged = per_lane(alpha0) * my_target + alpha1 * (my_residual + per_lane(beta) * my_target)
     both = jnp.concatenate([merged, my_residual - alpha1 * part])
 
-    two, three, one = staged(lambda k: both[:, 128 - 32 * k : 160 - 32 * k], x_move)
-    groups = jnp.stack([both[:, :32], three, two, one])
-    groups = lax.dynamic_slice_in_dim(jnp.concatenate([groups, groups]), (4 - x) % 4, 4, 0)
-    result = groups.transpose(1, 0, 2).reshape(64, 128)
+    mine = lax.broadcasted_iota(jnp.int32, (64, 128), 1) // 32 == x
+
+    turns = jnp.stack([jnp.roll(both, 32 * k, axis=1) for k in range(4)])
+
+    def placed(k):
+        piece = jnp.where(mine, pick(turns, (x - k) % 4), 0.0)
+        return with_layout_constraint(piece, Layout(major_to_minor=(0, 1)))
+
+    two, three, one = staged(lambda k: placed(4 - k), x_move)
+    result = placed(0) + three + two + one
     return result[:32], result[32:]
 
 

time: 129 us -> 128 us (level)
    all_to_all x1, starting transfers between devices: 3.64 us -> 10.6 us  [on_device(): part = lax.all_to_all(jnp.concatenate([part, curve], axis=1), 'task', 0, 0)]
    ppermute x30, starting transfers between devices: 59.7 us -> 52.8 us  [moved(): return lax.ppermute(value, axis, [(i, to(i)) for i in range(16)])]
    unnamed x18 -> x11, local copies, waits for them, and re-layouts: 2.12 us -> 0.74 us
    all_to_all x1, waiting for transfers between devices: 5.6 us -> 4.31 us  [on_device(): part = lax.all_to_all(jnp.concatenate([part, curve], axis=1), 'task', 0, 0)]
  transfers between devices with their start and end apart: 31 -> 31, of which waited for: 19 -> 20; matrix products, arithmetic and copies ran while one was open for 7% -> 7% of each run, Pallas kernels for 0% -> 0%
where the time goes in v11:
time: 128 us
  starting transfers between devices  63.4 us (50%)
  waiting for transfers between devices  41.5 us (32%)
  other arithmetic  8.02 us (6%)
  matrix products  7.28 us (6%)
  local copies, waits for them, and re-layouts  6.3 us (5%)
  between operations  1.34 us (1%)
    ppermute x30, starting transfers between devices, moved(): return lax.ppermute(value, axis, [(i, to(i)) for i in range(16)])  52.8 us
    ppermute x30, waiting for transfers between devices, moved(): return lax.ppermute(value, axis, [(i, to(i)) for i in range(16)])  37.2 us
    all_to_all x1, starting transfers between devices, on_device(): part = lax.all_to_all(jnp.concatenate([part, curve], axis=1), 'task', 0, 0)  10.6 us
    dot_general x12, matrix products, product(): lax.dot_general(pieces(value), x, (((1,), (dim,)), ((), ())), preferred_e...  5.96 us
    all_to_all x1, waiting for transfers between devices, on_device(): part = lax.all_to_all(jnp.concatenate([part, curve], axis=1), 'task', 0, 0)  4.31 us
  transfers between devices with their start and end apart: 31, of which 20 were waited for; matrix products, arithmetic and copies ran while one was open for 7% of the time, Pallas kernels for 0%

profile of v11, /device:TPU:1, one launch (start us, length us, event | category | flops | bytes accessed | tf_op | source)
XLA Modules:
  0.0 127.8 jit_solution(3260833907971376579)
XLA Ops:
  0.7 1.3 %fusion.18 = f32[384,128]{1,0:T(8,128)S(1)} fusion(bf16[1,512,128]{2,1,0:T(8,128)(2,1)} %param.3, bf16[1,384,512]{2,1,0:T(8,128)(2,1)} %param.2), kind=kOutput, calls=%fused_computation.57 | convolution fusion | flops 50331648 | bytes 720896 | tf_op jit(solution)/shard_map/dot_general | solution.py:99
  2.2 2.1 %collective-permute-start = (f32[32,384]{1,0:T(8,128)S(1)}, f32[32,384]{1,0:T(8,128)S(1)}, u32[]{:S(2)}, u32[]{:S(2)}) collective-permute-start(f32[32,384]{1,0:T(8,128)S(1)} %get-tuple-element.30), channel_id=1, source_target_pairs={{0,1},{1,2},{2,3},{3,0},{4,5},{5,6},{6,7},{7,4},{8,9},{9,10},{10,1... | collective-permute-start | bytes 147464 | tf_op jit(solution)/shard_map/ppermute | solution.py:13
  4.3 1.4 %collective-permute-start.1 = (f32[32,384]{1,0:T(8,128)S(1)}, f32[32,384]{1,0:T(8,128)S(1)}, u32[]{:S(2)}, u32[]{:S(2)}) collective-permute-start(f32[32,384]{1,0:T(8,128)S(1)} %get-tuple-element.32), channel_id=1, source_target_pairs={{0,3},{1,0},{2,1},{3,2},{4,7},{5,4},{6,5},{7,6},{8,11},{9,8},{10,9... | collective-permute-start | bytes 147464 | tf_op jit(solution)/shard_map/ppermute | solution.py:13
  5.7 1.6 %collective-permute-start.2 = (f32[32,384]{1,0:T(8,128)S(1)}, f32[32,384]{1,0:T(8,128)S(1)}, u32[]{:S(2)}, u32[]{:S(2)}) collective-permute-start(f32[32,384]{1,0:T(8,128)S(1)} %get-tuple-element.31), channel_id=1, source_target_pairs={{0,2},{1,3},{2,0},{3,1},{4,6},{5,7},{6,4},{7,5},{8,10},{9,11},{10,... | collective-permute-start | bytes 147464 | tf_op jit(solution)/shard_map/ppermute | solution.py:13
  7.3 0.9 collective-permute-start.8
  9.2 1.0 collective-permute-done.2
  10.2 3.1 %collective-permute-start.3 = (f32[32,384]{1,0:T(8,128)S(1)}, f32[32,384]{1,0:T(8,128)S(1)}, u32[]{:S(2)}, u32[]{:S(2)}) collective-permute-start(f32[32,384]{1,0:T(8,128)S(1)} %fusion.36), channel_id=1, source_target_pairs={{0,4},{1,5},{2,6},{3,7},{4,8},{5,9},{6,10},{7,11},{8,12},{9,13},{1... | collective-permute-start | bytes 147464 | tf_op jit(solution)/shard_map/ppermute | solution.py:13
  13.3 3.1 %collective-permute-start.4 = (f32[32,384]{1,0:T(8,128)S(1)}, f32[32,384]{1,0:T(8,128)S(1)}, u32[]{:S(2)}, u32[]{:S(2)}) collective-permute-start(f32[32,384]{1,0:T(8,128)S(1)} %fusion.36), channel_id=1, source_target_pairs={{0,12},{1,13},{2,14},{3,15},{4,0},{5,1},{6,2},{7,3},{8,4},{9,5},{1... | collective-permute-start | bytes 147464 | tf_op jit(solution)/shard_map/ppermute | solution.py:13
  16.4 4.4 %collective-permute-start.5 = (f32[32,384]{1,0:T(8,128)S(1)}, f32[32,384]{1,0:T(8,128)S(1)}, u32[]{:S(2)}, u32[]{:S(2)}) collective-permute-start(f32[32,384]{1,0:T(8,128)S(1)} %fusion.36), channel_id=1, source_target_pairs={{0,8},{1,9},{2,10},{3,11},{4,12},{5,13},{6,14},{7,15},{8,0},{9,1},... | collective-permute-start | bytes 147464 | tf_op jit(solution)/shard_map/ppermute | solution.py:13
  20.8 3.0 %collective-permute-done.5 = f32[32,384]{1,0:T(8,128)S(1)} collective-permute-done((f32[32,384]{1,0:T(8,128)S(1)}, f32[32,384]{1,0:T(8,128)S(1)}, u32[]{:S(2)}, u32[]{:S(2)}) %collective-permute-start.5) | collective-permute-done | bytes 49184 | tf_op jit(solution)/shard_map/ppermute | solution.py:13
  24.8 1.4 %collective-permute-start.9 = (bf16[224,512]{1,0:T(8,128)(2,1)S(1)}, bf16[224,512]{1,0:T(8,128)(2,1)S(1)}, u32[]{:S(2)}, u32[]{:S(2)}) collective-permute-start(bf16[224,512]{1,0:T(8,128)(2,1)S(1)} %pad_maximum_fusion.7), channel_id=1, source_target_pairs={{0,3},{1,0},{2,1},{3,2},{4,7},{5,4},{6,5},{7,6},{8,11},{9,8},{10,9... | collective-permute-start | bytes 688136 | tf_op jit(solution)/shard_map/ppermute | solution.py:13
  26.8 0.8 fusion.82
  27.8 1.9 %collective-permute-done.9 = bf16[224,512]{1,0:T(8,128)(2,1)S(1)} collective-permute-done((bf16[224,512]{1,0:T(8,128)(2,1)S(1)}, bf16[224,512]{1,0:T(8,128)(2,1)S(1)}, u32[]{:S(2)}, u32[]{:S(2)}) %collective-permute-start.9) | collective-permute-done | bytes 229408 | tf_op jit(solution)/shard_map/ppermute | solution.py:13
  29.8 3.3 %collective-permute-done.7 = bf16[256,512]{1,0:T(8,128)(2,1)S(1)} collective-permute-done((bf16[256,512]{1,0:T(8,128)(2,1)S(1)}, bf16[256,512]{1,0:T(8,128)(2,1)S(1)}, u32[]{:S(2)}, u32[]{:S(2)}) %collective-permute-start.7) | collective-permute-done | bytes 262176 | tf_op jit(solution)/shard_map/ppermute | solution.py:13
  34.0 5.3 %collective-permute-start.15 = (bf16[384,2048]{1,0:T(8,128)(2,1)S(1)}, bf16[384,2048]{1,0:T(8,128)(2,1)S(1)}, u32[]{:S(2)}, u32[]{:S(2)}) collective-permute-start(bf16[384,2048]{1,0:T(8,128)(2,1)S(1)} %pad_maximum_fusion), channel_id=1, source_target_pairs={{0,16},{16,0},{32,48},{48,32},{64,80},{80,64},{96,112},{112,96},{1... | collective-permute-start | bytes 4718600 | tf_op jit(solution)/shard_map/ppermute | solution.py:13
  39.9 1.5 %reshape.315 = f32[32,4,128]{2,1,0:T(4,128)} reshape(f32[32,512]{1,0:T(8,128)} %fusion.25) | data formatting | bytes 131072 | tf_op jit(solution)/shard_map/reshape | solution.py:65
  41.5 0.9 fusion
  42.4 0.9 fusion.29
  43.4 0.9 pad_maximum_fusion.4
  44.5 1.3 %collective-permute-done.10 = f32[16,16,128]{2,1,0:T(8,128)S(1)} collective-permute-done((f32[16,16,128]{2,1,0:T(8,128)S(1)}, f32[16,16,128]{2,1,0:T(8,128)S(1)}, u32[]{:S(2)}, u32[]{:S(2)}) %collective-permute-start.10) | collective-permute-done | bytes 131104 | tf_op jit(solution)/shard_map/ppermute | solution.py:13
  45.9 0.8 collective-permute-start.11
  46.8 4.2 %collective-permute-done.11 = f32[16,16,128]{2,1,0:T(8,128)S(1)} collective-permute-done((f32[16,16,128]{2,1,0:T(8,128)S(1)}, f32[16,16,128]{2,1,0:T(8,128)S(1)}, u32[]{:S(2)}, u32[]{:S(2)}) %collective-permute-start.11) | collective-permute-done | bytes 131104 | tf_op jit(solution)/shard_map/ppermute | solution.py:13
  50.9 1.4 %collective-permute-start.12 = (f32[16,16,128]{2,1,0:T(8,128)S(1)}, f32[16,16,128]{2,1,0:T(8,128)S(1)}, u32[]{:S(2)}, u32[]{:S(2)}) collective-permute-start(f32[16,16,128]{2,1,0:T(8,128)S(1)} %add.290), channel_id=1, source_target_pairs={{0,32},{16,48},{32,64},{48,80},{64,96},{80,112},{96,0},{112,16},{1... | collective-permute-start | bytes 393224 | tf_op jit(solution)/shard_map/ppermute | solution.py:13
  52.3 1.7 %collective-permute-start.13 = (f32[16,16,128]{2,1,0:T(8,128)S(1)}, f32[16,16,128]{2,1,0:T(8,128)S(1)}, u32[]{:S(2)}, u32[]{:S(2)}) collective-permute-start(f32[16,16,128]{2,1,0:T(8,128)S(1)} %add.290), channel_id=1, source_target_pairs={{0,96},{16,112},{32,0},{48,16},{64,32},{80,48},{96,64},{112,80},{1... | collective-permute-start | bytes 393224 | tf_op jit(solution)/shard_map/ppermute | solution.py:13
  54.0 1.4 %collective-permute-start.14 = (f32[16,16,128]{2,1,0:T(8,128)S(1)}, f32[16,16,128]{2,1,0:T(8,128)S(1)}, u32[]{:S(2)}, u32[]{:S(2)}) collective-permute-start(f32[16,16,128]{2,1,0:T(8,128)S(1)} %add.290), channel_id=1, source_target_pairs={{0,64},{16,80},{32,96},{48,112},{64,0},{80,16},{96,32},{112,48},{1... | collective-permute-start | bytes 393224 | tf_op jit(solution)/shard_map/ppermute | solution.py:13
  56.4 4.5 %collective-permute-done.14 = f32[16,16,128]{2,1,0:T(8,128)S(1)} collective-permute-done((f32[16,16,128]{2,1,0:T(8,128)S(1)}, f32[16,16,128]{2,1,0:T(8,128)S(1)}, u32[]{:S(2)}, u32[]{:S(2)}) %collective-permute-start.14) | collective-permute-done | bytes 131104 | tf_op jit(solution)/shard_map/ppermute | solution.py:13
  62.3 1.1 collective-permute-start.16
  63.5 2.5 %collective-permute-start.17 = (f32[16,896]{1,0:T(8,128)S(1)}, f32[16,896]{1,0:T(8,128)S(1)}, u32[]{:S(2)}, u32[]{:S(2)}) collective-permute-start(f32[16,896]{1,0:T(8,128)S(1)} %pad_maximum_fusion.17), channel_id=1, source_target_pairs={{0,12},{1,13},{2,14},{3,15},{4,0},{5,1},{6,2},{7,3},{8,4},{9,5},{1... | collective-permute-start | bytes 172040 | tf_op jit(solution)/shard_map/ppermute | solution.py:13
  66.0 4.7 %collective-permute-start.18 = (f32[16,896]{1,0:T(8,128)S(1)}, f32[16,896]{1,0:T(8,128)S(1)}, u32[]{:S(2)}, u32[]{:S(2)}) collective-permute-start(f32[16,896]{1,0:T(8,128)S(1)} %pad_maximum_fusion.17), channel_id=1, source_target_pairs={{0,8},{1,9},{2,10},{3,11},{4,12},{5,13},{6,14},{7,15},{8,0},{9,1},... | collective-permute-start | bytes 172040 | tf_op jit(solution)/shard_map/ppermute | solution.py:13
  70.7 2.3 %collective-permute-done.18 = f32[16,896]{1,0:T(8,128)S(1)} collective-permute-done((f32[16,896]{1,0:T(8,128)S(1)}, f32[16,896]{1,0:T(8,128)S(1)}, u32[]{:S(2)}, u32[]{:S(2)}) %collective-permute-start.18) | collective-permute-done | bytes 57376 | tf_op jit(solution)/shard_map/ppermute | solution.py:13
  74.3 1.6 %collective-permute-start.19 = (f32[17,16,128]{2,1,0:T(8,128)S(1)}, f32[17,16,128]{2,1,0:T(8,128)S(1)}, u32[]{:S(2)}, u32[]{:S(2)}) collective-permute-start(f32[17,16,128]{2,1,0:T(8,128)S(1)} %pad_maximum_fusion.9), channel_id=1, source_target_pairs={{0,128},{16,144},{32,160},{48,176},{64,192},{80,208},{96,224},{112... | collective-permute-start | bytes 417800 | tf_op jit(solution)/shard_map/ppermute | solution.py:13
  75.9 2.4 %collective-permute-done.19 = f32[17,16,128]{2,1,0:T(8,128)S(1)} collective-permute-done((f32[17,16,128]{2,1,0:T(8,128)S(1)}, f32[17,16,128]{2,1,0:T(8,128)S(1)}, u32[]{:S(2)}, u32[]{:S(2)}) %collective-permute-start.19) | collective-permute-done | bytes 139296 | tf_op jit(solution)/shard_map/ppermute | solution.py:13
  78.4 2.7 %collective-permute-start.21 = (f32[17,16,128]{2,1,0:T(8,128)S(1)}, f32[17,16,128]{2,1,0:T(8,128)}, u32[]{:S(2)}, u32[]{:S(2)}) collective-permute-start(f32[17,16,128]{2,1,0:T(8,128)S(1)} %fusion.83), channel_id=1, source_target_pairs={{0,96},{16,112},{32,0},{48,16},{64,32},{80,48},{96,64},{112,80},{1... | collective-permute-start | bytes 417800 | tf_op jit(solution)/shard_map/ppermute | solution.py:13
  81.1 2.5 %collective-permute-done.20 = f32[17,16,128]{2,1,0:T(8,128)} collective-permute-done((f32[17,16,128]{2,1,0:T(8,128)S(1)}, f32[17,16,128]{2,1,0:T(8,128)}, u32[]{:S(2)}, u32[]{:S(2)}) %collective-permute-start.20) | collective-permute-done | bytes 139296 | tf_op jit(solution)/shard_map/ppermute | solution.py:13
  83.6 0.9 collective-permute-done.21
  84.6 2.0 %collective-permute-done.22 = f32[17,16,128]{2,1,0:T(8,128)} collective-permute-done((f32[17,16,128]{2,1,0:T(8,128)S(1)}, f32[17,16,128]{2,1,0:T(8,128)}, u32[]{:S(2)}, u32[]{:S(2)}) %collective-permute-start.22) | collective-permute-done | bytes 139296 | tf_op jit(solution)/shard_map/ppermute | solution.py:13
  86.6 1.1 add_add_fusion
  89.4 1.6 %collective-permute-start.23 = (f32[16,896]{1,0:T(8,128)S(1)}, f32[16,896]{1,0:T(8,128)S(1)}, u32[]{:S(2)}, u32[]{:S(2)}) collective-permute-start(f32[16,896]{1,0:T(8,128)S(1)} %pad_maximum_fusion.18), channel_id=1, source_target_pairs={{0,4},{1,5},{2,6},{3,7},{4,8},{5,9},{6,10},{7,11},{8,12},{9,13},{1... | collective-permute-start | bytes 172040 | tf_op jit(solution)/shard_map/ppermute | solution.py:13
  91.0 2.0 %collective-permute-start.24 = (f32[16,896]{1,0:T(8,128)S(1)}, f32[16,896]{1,0:T(8,128)S(1)}, u32[]{:S(2)}, u32[]{:S(2)}) collective-permute-start(f32[16,896]{1,0:T(8,128)S(1)} %pad_maximum_fusion.18), channel_id=1, source_target_pairs={{0,12},{1,13},{2,14},{3,15},{4,0},{5,1},{6,2},{7,3},{8,4},{9,5},{1... | collective-permute-start | bytes 172040 | tf_op jit(solution)/shard_map/ppermute | solution.py:13
  93.0 5.0 %collective-permute-start.25 = (f32[16,896]{1,0:T(8,128)S(1)}, f32[16,896]{1,0:T(8,128)S(1)}, u32[]{:S(2)}, u32[]{:S(2)}) collective-permute-start(f32[16,896]{1,0:T(8,128)S(1)} %pad_maximum_fusion.18), channel_id=1, source_target_pairs={{0,8},{1,9},{2,10},{3,11},{4,12},{5,13},{6,14},{7,15},{8,0},{9,1},... | collective-permute-start | bytes 172040 | tf_op jit(solution)/shard_map/ppermute | solution.py:13
  98.0 2.3 %collective-permute-done.25 = f32[16,896]{1,0:T(8,128)S(1)} collective-permute-done((f32[16,896]{1,0:T(8,128)S(1)}, f32[16,896]{1,0:T(8,128)S(1)}, u32[]{:S(2)}, u32[]{:S(2)}) %collective-permute-start.25) | collective-permute-done | bytes 57376 | tf_op jit(solution)/shard_map/ppermute | solution.py:13
  103.1 10.6 %all-to-all-start = ((f32[16,24,128]{2,1,0:T(8,128)}), f32[16,24,128]{2,1,0:T(8,128)S(1)}, u32[]{:S(2)}, u32[]{:S(2)}) async-start(f32[16,24,128]{2,1,0:T(8,128)} %pad_maximum_fusion.8), calls=%async_computation | async-start | bytes 393216 | tf_op jit(solution)/shard_map/all_to_all | solution.py:170
  114.3 1.0 collective-permute-done.26
  116.1 4.3 %all-to-all-done = f32[16,24,128]{2,1,0:T(8,128)S(1)} async-done(((f32[16,24,128]{2,1,0:T(8,128)}), f32[16,24,128]{2,1,0:T(8,128)S(1)}, u32[]{:S(2)}, u32[]{:S(2)}) %all-to-all-start) | async-done | bytes 196640 | tf_op jit(solution)/shard_map/all_to_all | solution.py:170
  122.7 0.7 collective-permute-start.29
  123.5 1.2 collective-permute-done.27
  124.8 1.6 %collective-permute-done.28 = f32[64,128]{1,0:T(8,128)S(1)} collective-permute-done((f32[64,128]{1,0:T(8,128)S(1)}, f32[64,128]{1,0:T(8,128)S(1)}, u32[]{:S(2)}, u32[]{:S(2)}) %collective-permute-start.28) | collective-permute-done | bytes 32800 | tf_op jit(solution)/shard_map/ppermute | solution.py:13
  126.4 0.8 collective-permute-done.29
  (166 shorter events, 17.2 us)
Async XLA Ops:
  0.6 7.7 %copy-start = (bf16[1,384,512]{2,1,0:T(8,128)(2,1)S(1)}, bf16[1,384,512]{2,1,0:T(8,128)(2,1)}, u32[]{:S(2)}) copy-start(bf16[1,384,512]{2,1,0:T(8,128)(2,1)} %param.2) | copy-start | bytes 1179652
  0.6 7.5 %copy-start.1 = (bf16[1,512,128]{2,1,0:T(8,128)(2,1)S(1)}, bf16[1,512,128]{2,1,0:T(8,128)(2,1)}, u32[]{:S(2)}) copy-start(bf16[1,512,128]{2,1,0:T(8,128)(2,1)} %param.3) | copy-start | bytes 393220
  2.2 7.0 %collective-permute-start = (f32[32,384]{1,0:T(8,128)S(1)}, f32[32,384]{1,0:T(8,128)S(1)}, u32[]{:S(2)}, u32[]{:S(2)}) collective-permute-start(f32[32,384]{1,0:T(8,128)S(1)} %get-tuple-element.30), channel_id=1, source_target_pairs={{0,1},{1,2},{2,3},{3,0},{4,5},{5,6},{6,7},{7,4},{8,9},{9,10},{10,1... | collective-permute-start | bytes 147464 | tf_op jit(solution)/shard_map/ppermute | solution.py:13
  4.3 4.9 %collective-permute-start.1 = (f32[32,384]{1,0:T(8,128)S(1)}, f32[32,384]{1,0:T(8,128)S(1)}, u32[]{:S(2)}, u32[]{:S(2)}) collective-permute-start(f32[32,384]{1,0:T(8,128)S(1)} %get-tuple-element.32), channel_id=1, source_target_pairs={{0,3},{1,0},{2,1},{3,2},{4,7},{5,4},{6,5},{7,6},{8,11},{9,8},{10,9... | collective-permute-start | bytes 147464 | tf_op jit(solution)/shard_map/ppermute | solution.py:13
  5.7 4.5 %collective-permute-start.2 = (f32[32,384]{1,0:T(8,128)S(1)}, f32[32,384]{1,0:T(8,128)S(1)}, u32[]{:S(2)}, u32[]{:S(2)}) collective-permute-start(f32[32,384]{1,0:T(8,128)S(1)} %get-tuple-element.31), channel_id=1, source_target_pairs={{0,2},{1,3},{2,0},{3,1},{4,6},{5,7},{6,4},{7,5},{8,10},{9,11},{10,... | collective-permute-start | bytes 147464 | tf_op jit(solution)/shard_map/ppermute | solution.py:13
  7.3 17.4 %collective-permute-start.8 = (bf16[384,512]{1,0:T(8,128)(2,1)}, bf16[384,512]{1,0:T(8,128)(2,1)S(1)}, u32[]{:S(2)}, u32[]{:S(2)}) collective-permute-start(bf16[384,512]{1,0:T(8,128)(2,1)} %bitcast.186), channel_id=1, source_target_pairs={{0,3},{1,0},{2,1},{3,2},{4,7},{5,4},{6,5},{7,6},{8,11},{9,8},{10,9... | collective-permute-start | bytes 1179656 | tf_op jit(solution)/shard_map/ppermute | solution.py:13
  8.4 18.1 %collective-permute-start.6 = (bf16[416,512]{1,0:T(8,128)(2,1)S(1)}, bf16[416,512]{1,0:T(8,128)(2,1)S(1)}, u32[]{:S(2)}, u32[]{:S(2)}) collective-permute-start(bf16[416,512]{1,0:T(8,128)(2,1)S(1)} %pad_maximum_fusion.1), channel_id=1, source_target_pairs={{0,1},{1,2},{2,3},{3,0},{4,5},{5,6},{6,7},{7,4},{8,9},{9,10},{10,1... | collective-permute-start | bytes 1277960 | tf_op jit(solution)/shard_map/ppermute | solution.py:13
  10.2 10.6 %collective-permute-start.3 = (f32[32,384]{1,0:T(8,128)S(1)}, f32[32,384]{1,0:T(8,128)S(1)}, u32[]{:S(2)}, u32[]{:S(2)}) collective-permute-start(f32[32,384]{1,0:T(8,128)S(1)} %fusion.36), channel_id=1, source_target_pairs={{0,4},{1,5},{2,6},{3,7},{4,8},{5,9},{6,10},{7,11},{8,12},{9,13},{1... | collective-permute-start | bytes 147464 | tf_op jit(solution)/shard_map/ppermute | solution.py:13
  13.3 7.5 %collective-permute-start.4 = (f32[32,384]{1,0:T(8,128)S(1)}, f32[32,384]{1,0:T(8,128)S(1)}, u32[]{:S(2)}, u32[]{:S(2)}) collective-permute-start(f32[32,384]{1,0:T(8,128)S(1)} %fusion.36), channel_id=1, source_target_pairs={{0,12},{1,13},{2,14},{3,15},{4,0},{5,1},{6,2},{7,3},{8,4},{9,5},{1... | collective-permute-start | bytes 147464 | tf_op jit(solution)/shard_map/ppermute | solution.py:13
  16.4 7.4 %collective-permute-start.5 = (f32[32,384]{1,0:T(8,128)S(1)}, f32[32,384]{1,0:T(8,128)S(1)}, u32[]{:S(2)}, u32[]{:S(2)}) collective-permute-start(f32[32,384]{1,0:T(8,128)S(1)} %fusion.36), channel_id=1, source_target_pairs={{0,8},{1,9},{2,10},{3,11},{4,12},{5,13},{6,14},{7,15},{8,0},{9,1},... | collective-permute-start | bytes 147464 | tf_op jit(solution)/shard_map/ppermute | solution.py:13
  23.8 2.9 %copy-start.2 = (bf16[32,384]{1,0:T(8,128)(2,1)}, bf16[32,384]{1,0:T(8,128)(2,1)S(1)}, u32[]{:S(2)}) copy-start(bf16[32,384]{1,0:T(8,128)(2,1)S(1)} %get-tuple-element.20) | copy-start | bytes 73732
  23.9 2.9 %copy-start.3 = (bf16[32,384]{1,0:T(8,128)(2,1)}, bf16[32,384]{1,0:T(8,128)(2,1)S(1)}, u32[]{:S(2)}) copy-start(bf16[32,384]{1,0:T(8,128)(2,1)S(1)} %fusion.34) | copy-start | bytes 73732
  24.8 4.9 %collective-permute-start.9 = (bf16[224,512]{1,0:T(8,128)(2,1)S(1)}, bf16[224,512]{1,0:T(8,128)(2,1)S(1)}, u32[]{:S(2)}, u32[]{:S(2)}) collective-permute-start(bf16[224,512]{1,0:T(8,128)(2,1)S(1)} %pad_maximum_fusion.7), channel_id=1, source_target_pairs={{0,3},{1,0},{2,1},{3,2},{4,7},{5,4},{6,5},{7,6},{8,11},{9,8},{10,9... | collective-permute-start | bytes 688136 | tf_op jit(solution)/shard_map/ppermute | solution.py:13
  26.6 6.5 %collective-permute-start.7 = (bf16[256,512]{1,0:T(8,128)(2,1)S(1)}, bf16[256,512]{1,0:T(8,128)(2,1)S(1)}, u32[]{:S(2)}, u32[]{:S(2)}) collective-permute-start(bf16[256,512]{1,0:T(8,128)(2,1)S(1)} %pad_maximum_fusion.3), channel_id=1, source_target_pairs={{0,1},{1,2},{2,3},{3,0},{4,5},{5,6},{6,7},{7,4},{8,9},{9,10},{10,1... | collective-permute-start | bytes 786440 | tf_op jit(solution)/shard_map/ppermute | solution.py:13
  33.1 0.7 copy-start.4
  34.0 21.4 %collective-permute-start.15 = (bf16[384,2048]{1,0:T(8,128)(2,1)S(1)}, bf16[384,2048]{1,0:T(8,128)(2,1)S(1)}, u32[]{:S(2)}, u32[]{:S(2)}) collective-permute-start(bf16[384,2048]{1,0:T(8,128)(2,1)S(1)} %pad_maximum_fusion), channel_id=1, source_target_pairs={{0,16},{16,0},{32,48},{48,32},{64,80},{80,64},{96,112},{112,96},{1... | collective-permute-start | bytes 4718600 | tf_op jit(solution)/shard_map/ppermute | solution.py:13
  44.4 1.4 %collective-permute-start.10 = (f32[16,16,128]{2,1,0:T(8,128)S(1)}, f32[16,16,128]{2,1,0:T(8,128)S(1)}, u32[]{:S(2)}, u32[]{:S(2)}) collective-permute-start(f32[16,16,128]{2,1,0:T(8,128)S(1)} %bitcast.211), channel_id=1, source_target_pairs={{0,16},{16,0},{32,48},{48,32},{64,80},{80,64},{96,112},{112,96},{1... | collective-permute-start | bytes 393224 | tf_op jit(solution)/shard_map/ppermute | solution.py:13
  45.9 5.0 %collective-permute-start.11 = (f32[16,16,128]{2,1,0:T(8,128)S(1)}, f32[16,16,128]{2,1,0:T(8,128)S(1)}, u32[]{:S(2)}, u32[]{:S(2)}) collective-permute-start(f32[16,16,128]{2,1,0:T(8,128)S(1)} %fusion.15), channel_id=1, source_target_pairs={{0,128},{16,144},{32,160},{48,176},{64,192},{80,208},{96,224},{112... | collective-permute-start | bytes 393224 | tf_op jit(solution)/shard_map/ppermute | solution.py:13
  50.9 5.2 %collective-permute-start.12 = (f32[16,16,128]{2,1,0:T(8,128)S(1)}, f32[16,16,128]{2,1,0:T(8,128)S(1)}, u32[]{:S(2)}, u32[]{:S(2)}) collective-permute-start(f32[16,16,128]{2,1,0:T(8,128)S(1)} %add.290), channel_id=1, source_target_pairs={{0,32},{16,48},{32,64},{48,80},{64,96},{80,112},{96,0},{112,16},{1... | collective-permute-start | bytes 393224 | tf_op jit(solution)/shard_map/ppermute | solution.py:13
  52.3 4.1 %collective-permute-start.13 = (f32[16,16,128]{2,1,0:T(8,128)S(1)}, f32[16,16,128]{2,1,0:T(8,128)S(1)}, u32[]{:S(2)}, u32[]{:S(2)}) collective-permute-start(f32[16,16,128]{2,1,0:T(8,128)S(1)} %add.290), channel_id=1, source_target_pairs={{0,96},{16,112},{32,0},{48,16},{64,32},{80,48},{96,64},{112,80},{1... | collective-permute-start | bytes 393224 | tf_op jit(solution)/shard_map/ppermute | solution.py:13
  54.0 6.9 %collective-permute-start.14 = (f32[16,16,128]{2,1,0:T(8,128)S(1)}, f32[16,16,128]{2,1,0:T(8,128)S(1)}, u32[]{:S(2)}, u32[]{:S(2)}) collective-permute-start(f32[16,16,128]{2,1,0:T(8,128)S(1)} %add.290), channel_id=1, source_target_pairs={{0,64},{16,80},{32,96},{48,112},{64,0},{80,16},{96,32},{112,48},{1... | collective-permute-start | bytes 393224 | tf_op jit(solution)/shard_map/ppermute | solution.py:13
  62.3 8.3 %collective-permute-start.16 = (f32[16,896]{1,0:T(8,128)S(1)}, f32[16,896]{1,0:T(8,128)S(1)}, u32[]{:S(2)}, u32[]{:S(2)}) collective-permute-start(f32[16,896]{1,0:T(8,128)S(1)} %pad_maximum_fusion.17), channel_id=1, source_target_pairs={{0,4},{1,5},{2,6},{3,7},{4,8},{5,9},{6,10},{7,11},{8,12},{9,13},{1... | collective-permute-start | bytes 172040 | tf_op jit(solution)/shard_map/ppermute | solution.py:13
  63.5 7.2 %collective-permute-start.17 = (f32[16,896]{1,0:T(8,128)S(1)}, f32[16,896]{1,0:T(8,128)S(1)}, u32[]{:S(2)}, u32[]{:S(2)}) collective-permute-start(f32[16,896]{1,0:T(8,128)S(1)} %pad_maximum_fusion.17), channel_id=1, source_target_pairs={{0,12},{1,13},{2,14},{3,15},{4,0},{5,1},{6,2},{7,3},{8,4},{9,5},{1... | collective-permute-start | bytes 172040 | tf_op jit(solution)/shard_map/ppermute | solution.py:13
  66.0 6.9 %collective-permute-start.18 = (f32[16,896]{1,0:T(8,128)S(1)}, f32[16,896]{1,0:T(8,128)S(1)}, u32[]{:S(2)}, u32[]{:S(2)}) collective-permute-start(f32[16,896]{1,0:T(8,128)S(1)} %pad_maximum_fusion.17), channel_id=1, source_target_pairs={{0,8},{1,9},{2,10},{3,11},{4,12},{5,13},{6,14},{7,15},{8,0},{9,1},... | collective-permute-start | bytes 172040 | tf_op jit(solution)/shard_map/ppermute | solution.py:13
  74.3 4.0 %collective-permute-start.19 = (f32[17,16,128]{2,1,0:T(8,128)S(1)}, f32[17,16,128]{2,1,0:T(8,128)S(1)}, u32[]{:S(2)}, u32[]{:S(2)}) collective-permute-start(f32[17,16,128]{2,1,0:T(8,128)S(1)} %pad_maximum_fusion.9), channel_id=1, source_target_pairs={{0,128},{16,144},{32,160},{48,176},{64,192},{80,208},{96,224},{112... | collective-permute-start | bytes 417800 | tf_op jit(solution)/shard_map/ppermute | solution.py:13
  78.3 5.3 %collective-permute-start.20 = (f32[17,16,128]{2,1,0:T(8,128)S(1)}, f32[17,16,128]{2,1,0:T(8,128)}, u32[]{:S(2)}, u32[]{:S(2)}) collective-permute-start(f32[17,16,128]{2,1,0:T(8,128)S(1)} %fusion.83), channel_id=1, source_target_pairs={{0,32},{16,48},{32,64},{48,80},{64,96},{80,112},{96,0},{112,16},{1... | collective-permute-start | bytes 417800 | tf_op jit(solution)/shard_map/ppermute | solution.py:13
  78.4 6.2 %collective-permute-start.21 = (f32[17,16,128]{2,1,0:T(8,128)S(1)}, f32[17,16,128]{2,1,0:T(8,128)}, u32[]{:S(2)}, u32[]{:S(2)}) collective-permute-start(f32[17,16,128]{2,1,0:T(8,128)S(1)} %fusion.83), channel_id=1, source_target_pairs={{0,96},{16,112},{32,0},{48,16},{64,32},{80,48},{96,64},{112,80},{1... | collective-permute-start | bytes 417800 | tf_op jit(solution)/shard_map/ppermute | solution.py:13
  81.1 5.5 %collective-permute-start.22 = (f32[17,16,128]{2,1,0:T(8,128)S(1)}, f32[17,16,128]{2,1,0:T(8,128)}, u32[]{:S(2)}, u32[]{:S(2)}) collective-permute-start(f32[17,16,128]{2,1,0:T(8,128)S(1)} %fusion.83), channel_id=1, source_target_pairs={{0,64},{16,80},{32,96},{48,112},{64,0},{80,16},{96,32},{112,48},{1... | collective-permute-start | bytes 417800 | tf_op jit(solution)/shard_map/ppermute | solution.py:13
  89.4 8.6 %collective-permute-start.23 = (f32[16,896]{1,0:T(8,128)S(1)}, f32[16,896]{1,0:T(8,128)S(1)}, u32[]{:S(2)}, u32[]{:S(2)}) collective-permute-start(f32[16,896]{1,0:T(8,128)S(1)} %pad_maximum_fusion.18), channel_id=1, source_target_pairs={{0,4},{1,5},{2,6},{3,7},{4,8},{5,9},{6,10},{7,11},{8,12},{9,13},{1... | collective-permute-start | bytes 172040 | tf_op jit(solution)/shard_map/ppermute | solution.py:13
  91.0 7.0 %collective-permute-start.24 = (f32[16,896]{1,0:T(8,128)S(1)}, f32[16,896]{1,0:T(8,128)S(1)}, u32[]{:S(2)}, u32[]{:S(2)}) collective-permute-start(f32[16,896]{1,0:T(8,128)S(1)} %pad_maximum_fusion.18), channel_id=1, source_target_pairs={{0,12},{1,13},{2,14},{3,15},{4,0},{5,1},{6,2},{7,3},{8,4},{9,5},{1... | collective-permute-start | bytes 172040 | tf_op jit(solution)/shard_map/ppermute | solution.py:13
  93.0 7.3 %collective-permute-start.25 = (f32[16,896]{1,0:T(8,128)S(1)}, f32[16,896]{1,0:T(8,128)S(1)}, u32[]{:S(2)}, u32[]{:S(2)}) collective-permute-start(f32[16,896]{1,0:T(8,128)S(1)} %pad_maximum_fusion.18), channel_id=1, source_target_pairs={{0,8},{1,9},{2,10},{3,11},{4,12},{5,13},{6,14},{7,15},{8,0},{9,1},... | collective-permute-start | bytes 172040 | tf_op jit(solution)/shard_map/ppermute | solution.py:13
  103.1 17.3 %all-to-all-start = ((f32[16,24,128]{2,1,0:T(8,128)}), f32[16,24,128]{2,1,0:T(8,128)S(1)}, u32[]{:S(2)}, u32[]{:S(2)}) async-start(f32[16,24,128]{2,1,0:T(8,128)} %pad_maximum_fusion.8), calls=%async_computation | async-start | bytes 393216 | tf_op jit(solution)/shard_map/all_to_all | solution.py:170
  113.8 1.6 %collective-permute-start.26 = (f32[9,16,128]{2,1,0:T(8,128)S(1)}, f32[9,16,128]{2,1,0:T(8,128)S(1)}, u32[]{:S(2)}, u32[]{:S(2)}) collective-permute-start(f32[9,16,128]{2,1,0:T(8,128)S(1)} %get-tuple-element.49), channel_id=1, source_target_pairs={{0,16},{16,0},{32,48},{48,32},{64,80},{80,64},{96,112},{112,96},{1... | collective-permute-start | bytes 221192 | tf_op jit(solution)/shard_map/ppermute | solution.py:13
  121.9 2.8 %collective-permute-start.27 = (f32[64,128]{1,0:T(8,128)S(1)}, f32[64,128]{1,0:T(8,128)S(1)}, u32[]{:S(2)}, u32[]{:S(2)}) collective-permute-start(f32[64,128]{1,0:T(8,128)S(1)} %get-tuple-element.62), channel_id=1, source_target_pairs={{0,3},{1,0},{2,1},{3,2},{4,7},{5,4},{6,5},{7,6},{8,11},{9,8},{10,9... | collective-permute-start | bytes 98312 | tf_op jit(solution)/shard_map/ppermute | solution.py:13
  122.0 4.4 %collective-permute-start.28 = (f32[64,128]{1,0:T(8,128)S(1)}, f32[64,128]{1,0:T(8,128)S(1)}, u32[]{:S(2)}, u32[]{:S(2)}) collective-permute-start(f32[64,128]{1,0:T(8,128)S(1)} %get-tuple-element.64), channel_id=1, source_target_pairs={{0,2},{1,3},{2,0},{3,1},{4,6},{5,7},{6,4},{7,5},{8,10},{9,11},{10,... | collective-permute-start | bytes 98312 | tf_op jit(solution)/shard_map/ppermute | solution.py:13
  122.7 4.4 %collective-permute-start.29 = (f32[64,128]{1,0:T(8,128)S(1)}, f32[64,128]{1,0:T(8,128)S(1)}, u32[]{:S(2)}, u32[]{:S(2)}) collective-permute-start(f32[64,128]{1,0:T(8,128)S(1)} %get-tuple-element.63), channel_id=1, source_target_pairs={{0,1},{1,2},{2,3},{3,0},{4,5},{5,6},{6,7},{7,4},{8,9},{9,10},{10,1... | collective-permute-start | bytes 98312 | tf_op jit(solution)/shard_map/ppermute | solution.py:13
